TPU v7x, 32 devices: a whole 2x2x4 slice. The times are simulated.
32 devices in a mesh: rep: 2 (over y), seq: 16 (over z, x, core).
Axes of the slice: x: 2, y: 2, z: 4, core: 2. Of those that a mesh axis runs over, the one named last changes fastest.
Arguments:
- samples: bfloat16 [2, 8192, 512], P('rep', 'seq'), may hold values from -6 to 6
- clip_lengths: int32 [2, 4], P('rep'), may hold values from 1 to 1536, 4096 in all within a row
- stem_weight: bfloat16 [1536, 512], replicated, may hold values from -0.15625 to 0.15625
- stem_gain: float32 [512], replicated, may hold values from 0.5 to 1.5
- stem_bias: float32 [512], replicated, may hold values from -1.5 to 1.5
- proj_weight: bfloat16 [512, 768], replicated, may hold values from -0.25 to 0.25
- pos_weight: bfloat16 [6144, 768], replicated, may hold values from -0.078125 to 0.078125
- norm_gains: float32 [768, 3], replicated, may hold values from 0.5 to 1.5
- biases: float32 [768, 9], replicated, may hold values from -1.5 to 1.5
- attn_in: bfloat16 [768, 2304], replicated, may hold values from -0.21875 to 0.21875
- attn_out: bfloat16 [768, 768], replicated, may hold values from -1.75 to 1.75
- ffn_in: bfloat16 [768, 3072], replicated, may hold values from -0.21875 to 0.21875
- ffn_in_bias: float32 [3072], replicated, may hold values from -1.5 to 1.5
- ffn_out: bfloat16 [3072, 768], replicated, may hold values from -0.109375 to 0.109375
- out_grad: bfloat16 [2, 4096, 768], P('rep', 'seq'), may hold values from -6 to 6
Outputs:
- layer_out: bfloat16 [2, 4096, 768], P('rep', 'seq')
- sample_grad: float32 [2, 8192, 512], P('rep', 'seq')
- stem_weight_grad: float32 [1536, 512], P('seq')
- stem_gain_grad: float32 [512], P('seq')
- stem_bias_grad: float32 [512], P('seq')
- proj_weight_grad: float32 [512, 768], P('seq')
- pos_weight_grad: float32 [6144, 768], P('seq')
- norm_gains_grad: float32 [768, 3], P('seq')
- biases_grad: float32 [768, 9], P('seq')
- attn_in_grad: float32 [768, 2304], P('seq')
- attn_out_grad: float32 [768, 768], P('seq')
- ffn_in_grad: float32 [768, 3072], P('seq')
- ffn_in_bias_grad: float32 [3072], P('seq')
- ffn_out_grad: float32 [3072, 768], P('seq')
Inputs may be any that keep to these rules, and one draw needn't show every extreme that they name: `clip_lengths`: A stream's 4 clip lengths add up to 4096; the longest is exactly 1536.
All inputs are finite; a program needn't handle non-finite values.
Results may differ from a plain program's by a relative error of at most 0.018.
Values may be sent and summed in bfloat16 or wider, within the bound.
No kernel may reach another device: no remote copies, remote signals or barrier semaphores. Data moves between devices by JAX's collectives and lax.ppermute only.
A program may use at most 256 MiB of HBM per device.

v0:
```python
import jax
import jax.numpy as jnp
from jax import lax
from jax.sharding import PartitionSpec as P

HEADS = 12
KERNEL = 128
GROUPS = 16
MAXLEN = 1536


def from_behind(value, axis, steps):
    count = lax.axis_size(axis)
    initial, last = (max(0, -steps), min(count, count - steps))
    return lax.ppermute(value, axis, [(source, source + steps) for source in range(initial, last)])


def padded_2(value, sides, width):
    for axis, dim in sides:
        size, length = (lax.axis_size(axis), value.shape[dim])
        up = [(i, (i + 1) % size) for i in range(size - 1)]
        down = [(j, i) for i, j in up]
        last = lax.slice_in_dim(value, length - width, length, axis=dim)
        initial = lax.slice_in_dim(value, 0, width, axis=dim)
        before = lax.ppermute(last, axis, up)
        after = lax.ppermute(initial, axis, down)
        value = jnp.concatenate([before, value, after], axis=dim)
    return value


def norm_rows(values, scales, shifts):
    center = values - jnp.mean(values, axis=-1, keepdims=True)
    spread = jnp.mean(center * center, axis=-1, keepdims=True)
    return center * lax.rsqrt(spread + 1e-05) * scales + shifts


def gelu_exact(values):
    return jax.nn.gelu(values, approximate=False)


def dot_plain(left, right):
    return jnp.dot(left, right, preferred_element_type=jnp.float32)


def dot_over_rows(left, right):
    return lax.dot_general(
        left, right, (((0,), (0,)), ((), ())), preferred_element_type=jnp.float32
    )


def dot_by_rows(left, right):
    return lax.dot_general(
        left, right, (((1,), (1,)), ((), ())), preferred_element_type=jnp.float32
    )


def clip_span(ends, begin, count, total):
    places = begin + jnp.arange(count, dtype=jnp.int32)
    found = jnp.sum((places[:, None] >= ends[None, :]).astype(jnp.int32), axis=1)
    inside = jnp.logical_and(places >= 0, places < total)
    return jnp.where(inside, found, -1)


def local(
    samples,
    clip_lengths,
    stem_weight,
    stem_gain,
    stem_bias,
    proj_weight,
    pos_weight,
    norm_gains,
    biases,
    attn_in,
    attn_out,
    ffn_in,
    ffn_in_bias,
    ffn_out,
    out_grad,
):
    rows_dev = out_grad.shape[1]
    width = attn_out.shape[0]
    chans = stem_weight.shape[1]
    group_width = width // GROUPS
    head_dim = width // HEADS
    scale = float(head_dim) ** (-0.5)
    total = rows_dev * lax.axis_size("seq")
    begin = lax.axis_index("seq") * rows_dev
    ends = jnp.cumsum(clip_lengths[0])
    own_ids = clip_span(ends, begin, rows_dev, total)
    half = KERNEL // 2
    reach = (MAXLEN - 2) // rows_dev + 1
    frames = samples[0].reshape(rows_dev, 2 * chans)
    next_row = from_behind(frames[:1, :chans], "seq", -1)
    same_next = clip_span(ends, begin + 1, rows_dev, total) == own_ids
    following = jnp.concatenate([frames[1:, :chans], next_row], axis=0)
    following = jnp.where(same_next[:, None], following, jnp.zeros_like(following))
    unfold = jnp.concatenate([frames, following], axis=1)
    stem_pre = dot_plain(unfold, stem_weight)
    feature = gelu_exact(stem_pre)
    normed_b = norm_rows(feature, stem_gain, stem_bias).astype(jnp.bfloat16)
    start_x = dot_plain(normed_b, proj_weight) + biases[:, 0]
    start_b = start_x.astype(jnp.bfloat16)
    padded = padded_2(start_b, (("seq", 0),), half)
    padded_ids = clip_span(ends, begin - half, rows_dev + 2 * half, total)

    def tap_stack(source, first_tap, forward):
        columns = []
        for inner in range(8):
            where_at = first_tap + inner if forward else 2 * half - first_tap - inner
            piece = lax.dynamic_slice_in_dim(source, where_at, rows_dev, 0)
            keep = lax.dynamic_slice_in_dim(padded_ids, where_at, rows_dev, 0) == own_ids
            columns.append(jnp.where(keep[:, None], piece, jnp.zeros_like(piece)))
        return jnp.stack(columns, axis=1).reshape(rows_dev, 8, GROUPS, group_width)

    def tap_kernel(first_tap):
        block = lax.dynamic_slice_in_dim(pos_weight, first_tap * group_width, 8 * group_width, 0)
        return block.reshape(8, group_width, GROUPS, group_width)

    def conv_step(index, running):
        first_tap = index * 8
        return running + jnp.einsum(
            "tjgi,jigo->tgo",
            tap_stack(padded, first_tap, True),
            tap_kernel(first_tap),
            preferred_element_type=jnp.float32,
        )

    conv_sum = lax.fori_loop(
        0, KERNEL // 8, conv_step, jnp.zeros((rows_dev, GROUPS, group_width), jnp.float32)
    )
    conv_out = conv_sum.reshape(rows_dev, width) + biases[:, 1]
    mixed = start_x + gelu_exact(conv_out)
    hidden = norm_rows(mixed, norm_gains[:, 0], biases[:, 2])
    hidden_b = hidden.astype(jnp.bfloat16)
    project = dot_plain(hidden_b, attn_in)
    query_b = (project[:, :width] + biases[:, 3]).astype(jnp.bfloat16)
    keys_b = project[:, width : 2 * width].astype(jnp.bfloat16)
    values_b = (project[:, 2 * width :] + biases[:, 4]).astype(jnp.bfloat16)
    pair = jnp.concatenate([keys_b, values_b], axis=1)
    query3 = query_b.reshape(rows_dev, HEADS, head_dim)
    arrived = {0: pair}
    from_below = pair
    from_above = pair
    for step in range(1, reach + 1):
        from_below = from_behind(from_below, "seq", 1)
        from_above = from_behind(from_above, "seq", -1)
        arrived[step] = from_below
        arrived[-step] = from_above
    offsets = [0] + [step for step in range(1, reach + 1)] + [-step for step in range(1, reach + 1)]
    blocks = []
    for offset in offsets:
        keys3 = arrived[offset][:, :width].reshape(rows_dev, HEADS, head_dim)
        values3 = arrived[offset][:, width:].reshape(rows_dev, HEADS, head_dim)
        allowed = (
            own_ids[:, None] == clip_span(ends, begin - offset * rows_dev, rows_dev, total)[None, :]
        )
        blocks.append((offset, keys3, values3, allowed, jnp.any(allowed)))

    def scores_of(keys3, allowed):
        raw = jnp.einsum("qhd,khd->hqk", query3, keys3, preferred_element_type=jnp.float32)
        return jnp.where(allowed[None], raw * scale, -1e30)

    top = jnp.full((HEADS, rows_dev), -1e30, jnp.float32)
    mass = jnp.zeros((HEADS, rows_dev), jnp.float32)
    for offset, keys3, values3, allowed, live in blocks:
        stats_top = top
        stats_mass = mass
        scores = scores_of(keys3, allowed)
        new_top = jnp.maximum(stats_top, jnp.max(scores, axis=-1))
        weight = jnp.where(allowed[None], jnp.exp(scores - new_top[:, :, None]), 0.0)
        top = new_top
        mass = stats_mass * jnp.exp(stats_top - new_top) + jnp.sum(weight, axis=-1)
    log_total = top + jnp.log(mass)

    def probs_of(keys3, allowed):
        return jnp.where(
            allowed[None], jnp.exp(scores_of(keys3, allowed) - log_total[:, :, None]), 0.0
        )

    attended = jnp.zeros((rows_dev, HEADS, head_dim), jnp.float32)
    for offset, keys3, values3, allowed, live in blocks:
        output_running = attended
        probs_b = probs_of(keys3, allowed).astype(jnp.bfloat16)
        attended = output_running + jnp.einsum(
            "hqk,khd->qhd", probs_b, values3, preferred_element_type=jnp.float32
        )
    attended_b = attended.reshape(rows_dev, width).astype(jnp.bfloat16)
    pre_second = hidden + dot_plain(attended_b, attn_out) + biases[:, 5]
    second = norm_rows(pre_second, norm_gains[:, 1], biases[:, 6])
    second_b = second.astype(jnp.bfloat16)
    inner = dot_plain(second_b, ffn_in) + ffn_in_bias
    inner_b = gelu_exact(inner).astype(jnp.bfloat16)
    pre_last = second + dot_plain(inner_b, ffn_out) + biases[:, 7]
    layer_out = norm_rows(pre_last, norm_gains[:, 2], biases[:, 8]).astype(jnp.bfloat16)[None]
    grad_last, gain_grad_c, bias_grad_c = jax.vjp(
        norm_rows, pre_last, norm_gains[:, 2], biases[:, 8]
    )[1](out_grad[0].astype(jnp.float32))
    grad_last_b = grad_last.astype(jnp.bfloat16)
    grad_ffn_out = dot_over_rows(inner_b, grad_last_b)
    grad_inner = jax.vjp(gelu_exact, inner)[1](dot_by_rows(grad_last_b, ffn_out))[0]
    grad_inner_b = grad_inner.astype(jnp.bfloat16)
    grad_ffn_in = dot_over_rows(second_b, grad_inner_b)
    grad_second = grad_last + dot_by_rows(grad_inner_b, ffn_in)
    grad_pre_second, gain_grad_b, bias_grad_b = jax.vjp(
        norm_rows, pre_second, norm_gains[:, 1], biases[:, 6]
    )[1](grad_second)
    grad_branch_b = grad_pre_second.astype(jnp.bfloat16)
    grad_attn_out = dot_over_rows(attended_b, grad_branch_b)
    grad_out3 = (
        dot_by_rows(grad_branch_b, attn_out).astype(jnp.bfloat16).reshape(rows_dev, HEADS, head_dim)
    )
    delta = jnp.zeros((HEADS, rows_dev), jnp.float32)
    for offset, keys3, values3, allowed, live in blocks:
        delta_running = delta
        delta_prob_grad = jnp.einsum(
            "qhd,khd->hqk", grad_out3, values3, preferred_element_type=jnp.float32
        )
        delta = delta_running + jnp.sum(probs_of(keys3, allowed) * delta_prob_grad, axis=-1)
    grad_query3 = jnp.zeros((rows_dev, HEADS, head_dim), jnp.float32)
    returned = {}
    for offset, keys3, values3, allowed, live in blocks:
        grad_running = grad_query3
        probs = probs_of(keys3, allowed)
        prob_grad = jnp.einsum(
            "qhd,khd->hqk", grad_out3, values3, preferred_element_type=jnp.float32
        )
        score_grad_b = (probs * (prob_grad - delta[:, :, None]) * scale).astype(jnp.bfloat16)
        grad_running = grad_running + jnp.einsum(
            "hqk,khd->qhd", score_grad_b, keys3, preferred_element_type=jnp.float32
        )
        key_grad = jnp.einsum(
            "hqk,qhd->khd", score_grad_b, query3, preferred_element_type=jnp.float32
        )
        value_grad = jnp.einsum(
            "hqk,qhd->khd",
            probs.astype(jnp.bfloat16),
            grad_out3,
            preferred_element_type=jnp.float32,
        )
        grad_query3, returned[offset] = (
            grad_running,
            jnp.concatenate(
                [key_grad.reshape(rows_dev, width), value_grad.reshape(rows_dev, width)], axis=1
            ),
        )
    moving = returned[reach]
    upward = returned[-reach]
    for step in range(reach - 1, -1, -1):
        moving = from_behind(moving.astype(jnp.bfloat16), "seq", -1).astype(moving.dtype)
        upward = from_behind(upward.astype(jnp.bfloat16), "seq", 1).astype(upward.dtype)
        if step > 0:
            moving = moving + returned[step]
            upward = upward + returned[-step]
    pair_grad = returned[0] + moving + upward
    grad_query = grad_query3.reshape(rows_dev, width)
    grad_project_b = jnp.concatenate([grad_query, pair_grad], axis=1).astype(jnp.bfloat16)
    grad_attn_in = dot_over_rows(hidden_b, grad_project_b)
    grad_hidden = grad_pre_second + dot_by_rows(grad_project_b, attn_in)
    grad_mixed, gain_grad_a, bias_grad_a = jax.vjp(
        norm_rows, mixed, norm_gains[:, 0], biases[:, 2]
    )[1](grad_hidden)
    grad_conv = jax.vjp(gelu_exact, conv_out)[1](grad_mixed)[0]
    grad_conv_b = grad_conv.astype(jnp.bfloat16)
    padded_grad = padded_2(grad_conv_b, (("seq", 0),), half)
    grad_conv3 = grad_conv_b.reshape(rows_dev, GROUPS, group_width)

    def conv_back(index, carry):
        weight_grad, input_grad = carry
        first_tap = index * 8
        block_grad = jnp.einsum(
            "tjgi,tgo->jigo",
            tap_stack(padded, first_tap, True),
            grad_conv3,
            preferred_element_type=jnp.float32,
        )
        weight_grad = lax.dynamic_update_slice_in_dim(
            weight_grad, block_grad.reshape(8 * group_width, width), first_tap * group_width, 0
        )
        input_grad = input_grad + jnp.einsum(
            "tjgo,jigo->tgi",
            tap_stack(padded_grad, first_tap, False),
            tap_kernel(first_tap),
            preferred_element_type=jnp.float32,
        )
        return (weight_grad, input_grad)

    pos_grad, input_grad = lax.fori_loop(
        0,
        KERNEL // 8,
        conv_back,
        (
            jnp.zeros((KERNEL * group_width, width), jnp.float32),
            jnp.zeros((rows_dev, GROUPS, group_width), jnp.float32),
        ),
    )
    grad_start = grad_mixed + input_grad.reshape(rows_dev, width)
    grad_start_b = grad_start.astype(jnp.bfloat16)
    grad_proj = dot_over_rows(normed_b, grad_start_b)
    grad_feature, stem_gain_grad, stem_bias_grad = jax.vjp(
        norm_rows, feature, stem_gain, stem_bias
    )[1](dot_by_rows(grad_start_b, proj_weight))
    grad_pre_b = jax.vjp(gelu_exact, stem_pre)[1](grad_feature)[0].astype(jnp.bfloat16)
    grad_stem = dot_over_rows(unfold, grad_pre_b)
    grad_unfold = dot_by_rows(grad_pre_b, stem_weight)
    grad_follow = jnp.where(same_next[:, None], grad_unfold[:, 2 * chans :], 0.0)
    carried = from_behind(grad_follow[-1:], "seq", 1)
    shifted_back = jnp.concatenate([carried, grad_follow[:-1]], axis=0)
    grad_frames = grad_unfold[:, : 2 * chans] + jnp.concatenate(
        [shifted_back, jnp.zeros((rows_dev, chans), jnp.float32)], axis=1
    )
    sample_grad = grad_frames.reshape(1, 2 * rows_dev, chans)
    gains_grad = jnp.stack([gain_grad_a, gain_grad_b, gain_grad_c], axis=1)
    bias_table = jnp.stack(
        [
            jnp.sum(grad_start, axis=0),
            jnp.sum(grad_conv, axis=0),
            bias_grad_a,
            jnp.sum(grad_query, axis=0),
            jnp.sum(pair_grad[:, width:], axis=0),
            jnp.sum(grad_pre_second, axis=0),
            bias_grad_b,
            jnp.sum(grad_last, axis=0),
            bias_grad_c,
        ],
        axis=1,
    )
    inner_bias_grad = jnp.sum(grad_inner, axis=0)
    shares = (
        lax.psum_scatter(grad_stem, "seq", scatter_dimension=0, tiled=True),
        lax.psum_scatter(stem_gain_grad, "seq", scatter_dimension=0, tiled=True),
        lax.psum_scatter(stem_bias_grad, "seq", scatter_dimension=0, tiled=True),
        lax.psum_scatter(grad_proj, "seq", scatter_dimension=0, tiled=True),
        lax.psum_scatter(pos_grad, "seq", scatter_dimension=0, tiled=True),
        lax.psum_scatter(gains_grad, "seq", scatter_dimension=0, tiled=True),
        lax.psum_scatter(bias_table, "seq", scatter_dimension=0, tiled=True),
        lax.psum_scatter(grad_attn_in, "seq", scatter_dimension=0, tiled=True),
        lax.psum_scatter(grad_attn_out, "seq", scatter_dimension=0, tiled=True),
        lax.psum_scatter(grad_ffn_in, "seq", scatter_dimension=0, tiled=True),
        lax.psum_scatter(inner_bias_grad, "seq", scatter_dimension=0, tiled=True),
        lax.psum_scatter(grad_ffn_out, "seq", scatter_dimension=0, tiled=True),
    )
    summed = (
        lax.psum(shares[0].astype(jnp.bfloat16), "rep").astype(jnp.float32),
        lax.psum(shares[1].astype(jnp.bfloat16), "rep").astype(jnp.float32),
        lax.psum(shares[2].astype(jnp.bfloat16), "rep").astype(jnp.float32),
        lax.psum(shares[3].astype(jnp.bfloat16), "rep").astype(jnp.float32),
        lax.psum(shares[4].astype(jnp.bfloat16), "rep").astype(jnp.float32),
        lax.psum(shares[5].astype(jnp.bfloat16), "rep").astype(jnp.float32),
        lax.psum(shares[6].astype(jnp.bfloat16), "rep").astype(jnp.float32),
        lax.psum(shares[7].astype(jnp.bfloat16), "rep").astype(jnp.float32),
        lax.psum(shares[8].astype(jnp.bfloat16), "rep").astype(jnp.float32),
        lax.psum(shares[9].astype(jnp.bfloat16), "rep").astype(jnp.float32),
        lax.psum(shares[10].astype(jnp.bfloat16), "rep").astype(jnp.float32),
        lax.psum(shares[11].astype(jnp.bfloat16), "rep").astype(jnp.float32),
    )
    return (
        layer_out,
        sample_grad,
        summed[0],
        summed[1],
        summed[2],
        summed[3],
        summed[4],
        summed[5],
        summed[6],
        summed[7],
        summed[8],
        summed[9],
        summed[10],
        summed[11],
    )


def solution(mesh):
    placed = (
        P("rep", "seq", None),
        P("rep", None),
        P(),
        P(),
        P(),
        P(),
        P(),
        P(),
        P(),
        P(),
        P(),
        P(),
        P(),
        P(),
        P("rep", "seq", None),
    )
    return jax.shard_map(
        local,
        mesh=mesh,
        in_specs=placed,
        out_specs=(
            P("rep", "seq", None),
            P("rep", "seq", None),
            P("seq", None),
            P("seq"),
            P("seq"),
            P("seq", None),
            P("seq", None),
            P("seq", None),
            P("seq", None),
            P("seq", None),
            P("seq", None),
            P("seq", None),
            P("seq"),
            P("seq", None),
        ),
        check_vma=False,
    )
```

profile of v0, /device:TPU:16, one launch (start us, length us, event | category | flops | bytes accessed | tf_op | source)
XLA Modules:
  0.0 2351.0 jit_solution(12549075094031599434)
XLA Ops:
  48.1 338.9 %while.36 = (s32[]{:T(128)}, f32[256,16,48]{0,2,1:T(8,128)}, bf16[6144,768]{1,0:T(8,128)(2,1)}, s32[384]{0:T(512)S(1)}, s32[256]{0:T(256)S(1)}, /*index=5*/bf16[...) while((s32[]{:T(128)}, f32[256,16,48]{0,2,1:T(8,128)}, ...), condition=%wide.region_7.8_spmd.clone, body=%wide.region_6.7_spmd.clone.sunk | while | flops 152963104 | bytes 20264640 | solution.py:129
  600.1 8.1 multiply_convert_fusion.13
  650.4 14.6 multiply_reduce_fusion.12
  665.1 15.0 multiply_reduce_fusion.11
  680.0 15.0 multiply_convert_fusion.6
  695.1 10.7 multiply_convert_fusion
  727.4 14.1 multiply_convert_fusion.12
  774.5 10.7 collective-permute-start.22
  789.2 25.4 %collective-permute-start.23 = (bf16[256,1536]{0,1:T(8,128)(2,1)S(1)}, bf16[256,1536]{0,1:T(8,128)(2,1)S(1)}, u32[]{:S(2)}, u32[]{:S(2)}) collective-permute-start(bf16[256,1536]{0,1:T(8,128)(2,1)S(1)} %fusion.43), channel_id=1, source_target_pairs={{0,1},{1,2},{2,3},{3,4},{4,5},{5,6},{6,7},{7,8},{8,9},{9,10},{10,1... | collective-permute-start | bytes 2359304 | tf_op jit(solution)/shard_map/ppermute | solution.py:15
  817.8 10.5 collective-permute-start.24
  832.5 20.2 collective-permute-start.25
  855.9 18.9 collective-permute-start.26
  884.7 9.9 collective-permute-start.27
  912.5 584.7 %while.37 = (s32[]{:T(128)}, f32[6144,768]{1,0:T(8,128)}, f32[256,16,48]{0,2,1:T(8,128)}, s32[384]{0:T(512)S(1)}, s32[256]{0:T(256)S(1)}, /*index=5*/bf16[384,76...) while((s32[]{:T(128)}, f32[6144,768]{1,0:T(8,128)}, ...), condition=%wide.region_72.73_spmd.clone, body=%wide.region_71.72_spmd.clone.sunk | while | flops 305532992 | bytes 48596484 | solution.py:288
  1556.1 21.2 reduce-scatter.14.cloned.1.call-done
  1578.9 114.2 %reduce-scatter.26.cloned.1.call-done = f32[192,768]{1,0:T(8,128)} async-done(((f32[3072,768]{1,0:T(8,128)}), f32[192,768]{1,0:T(8,128)}) %reduce-scatter.26.cloned.1.call-update) | async-done | bytes 589840 | tf_op jit(solution)/shard_map/reduce_scatter | solution.py:341
  1694.9 113.3 %reduce-scatter.24.cloned.1.call-done = f32[48,3072]{1,0:T(8,128)} async-done(((f32[768,3072]{1,0:T(8,128)}), f32[48,3072]{1,0:T(8,128)}) %reduce-scatter.24.cloned.1.call-update) | async-done | bytes 589840 | tf_op jit(solution)/shard_map/reduce_scatter | solution.py:339
  1810.0 92.2 %reduce-scatter.20.cloned.1.call-done = f32[48,2304]{1,0:T(8,128)} async-done(((f32[768,2304]{1,0:T(8,128)}), f32[48,2304]{1,0:T(8,128)}) %reduce-scatter.20.cloned.1.call-update) | async-done | bytes 442384 | tf_op jit(solution)/shard_map/reduce_scatter | solution.py:337
  1903.9 196.3 %reduce-scatter.18.cloned.1.call-done = f32[384,768]{1,0:T(8,128)} async-done(((f32[6144,768]{1,0:T(8,128)}), f32[384,768]{1,0:T(8,128)}) %reduce-scatter.18.cloned.1.call-update) | async-done | bytes 1179664 | tf_op jit(solution)/shard_map/reduce_scatter | solution.py:334
  2112.3 46.7 %reduce-scatter.28.cloned.1.call-done = f32[48,3]{1,0:T(8,128)} async-done(((f32[768,3]{1,0:T(8,128)}), f32[48,3]{1,0:T(8,128)}) %reduce-scatter.28.cloned.1.call-update) | async-done | bytes 592
  2160.4 44.2 %all-reduce.4 = (bf16[512]{0:T(512)(128)(2,1)}, bf16[512]{0:T(512)(128)(2,1)}, bf16[3072]{0:T(1024)(128)(2,1)}) all-reduce(f32[512]{0:T(512)} %get-tuple-element.603, f32[512]{0:T(512)S(1)} %copy-done.254, f32[3072]{0:T(1024)S(1)} %copy-done.247), channel_id=3, replica_groups=mesh['rep'=2,'seq'=16] {'seq'}, use_global_device_ids=true, to_apply=%region_78.79.clone | all-reduce | flops 4096 | bytes 24576
  2218.3 61.4 %reduce-scatter.16.cloned.1.call-done = f32[32,768]{1,0:T(8,128)} async-done(((f32[512,768]{1,0:T(8,128)}), f32[32,768]{1,0:T(8,128)}) %reduce-scatter.16.cloned.1.call-update) | async-done | bytes 98320 | tf_op jit(solution)/shard_map/reduce_scatter | solution.py:333
  2281.3 9.9 all-reduce.5
  2297.3 38.6 %all-reduce.9.cloned.1.call-done = (bf16[96,512]{1,0:T(8,128)(2,1)}, bf16[384,768]{1,0:T(8,128)(2,1)}, bf16[48,2304]{1,0:T(8,128)(2,1)}, bf16[48,768]{1,0:T(8,12...) async-done(((bf16[96,512]{1,0:T(8,128)(2,1)}, bf16[384,768]{1,0:T(8,128)(2,1)}, bf16[48,2304]{1,0:T(8,128)(2,1)}, bf16[48,768]{1,0:T(8,128)(2,1)}, ...) | async-done | bytes 1572880 | tf_op jit(solution)/shard_map/psum | solution.py:344
  (1815 shorter events, 1417.5 us)
Async XLA Ops:
  7.2 1547.4 %reduce-scatter.22.cloned.1.call-start = ((), (), s32[]{:S(2)}) async-start(), calls=%async_computation.13 | async-start | bytes 2506752 | tf_op jit(solution)/shard_map/reduce_scatter | solution.py:338
  402.7 21.7 collective-permute-start.3
  419.9 23.0 collective-permute-start.10
  446.9 20.5 collective-permute-start.11
  472.4 21.6 collective-permute-start.6
  498.0 21.4 collective-permute-start.7
  523.3 21.5 collective-permute-start.8
  765.3 20.6 collective-permute-start.16
  786.1 29.1 %collective-permute-start.17 = (bf16[256,1536]{0,1:T(8,128)(2,1)S(1)}, bf16[256,1536]{0,1:T(8,128)(2,1)S(1)}, u32[]{:S(2)}, u32[]{:S(2)}) collective-permute-start(bf16[256,1536]{0,1:T(8,128)(2,1)S(1)} %fusion.38), channel_id=1, source_target_pairs={{1,0},{2,1},{3,2},{4,3},{5,4},{6,5},{7,6},{8,7},{9,8},{10,9},{11,1... | collective-permute-start | bytes 2359304 | tf_op jit(solution)/shard_map/ppermute | solution.py:15
  789.2 28.3 %collective-permute-start.23 = (bf16[256,1536]{0,1:T(8,128)(2,1)S(1)}, bf16[256,1536]{0,1:T(8,128)(2,1)S(1)}, u32[]{:S(2)}, u32[]{:S(2)}) collective-permute-start(bf16[256,1536]{0,1:T(8,128)(2,1)S(1)} %fusion.43), channel_id=1, source_target_pairs={{0,1},{1,2},{2,3},{3,4},{4,5},{5,6},{6,7},{7,8},{8,9},{9,10},{10,1... | collective-permute-start | bytes 2359304 | tf_op jit(solution)/shard_map/ppermute | solution.py:15
  829.2 24.2 %collective-permute-start.19 = (bf16[256,1536]{0,1:T(8,128)(2,1)S(1)}, bf16[256,1536]{0,1:T(8,128)(2,1)S(1)}, u32[]{:S(2)}, u32[]{:S(2)}) collective-permute-start(bf16[256,1536]{0,1:T(8,128)(2,1)S(1)} %fusion.40), channel_id=1, source_target_pairs={{1,0},{2,1},{3,2},{4,3},{5,4},{6,5},{7,6},{8,7},{9,8},{10,9},{11,1... | collective-permute-start | bytes 2359304 | tf_op jit(solution)/shard_map/ppermute | solution.py:15
  832.5 23.2 collective-permute-start.25
  853.6 23.8 %collective-permute-start.20 = (bf16[256,1536]{0,1:T(8,128)(2,1)S(1)}, bf16[256,1536]{0,1:T(8,128)(2,1)S(1)}, u32[]{:S(2)}, u32[]{:S(2)}) collective-permute-start(bf16[256,1536]{0,1:T(8,128)(2,1)S(1)} %fusion.41), channel_id=1, source_target_pairs={{1,0},{2,1},{3,2},{4,3},{5,4},{6,5},{7,6},{8,7},{9,8},{10,9},{11,1... | collective-permute-start | bytes 2359304 | tf_op jit(solution)/shard_map/ppermute | solution.py:15
  855.9 21.5 collective-permute-start.26
  898.5 678.8 %reduce-scatter.14.cloned.1.call-start = ((), (), s32[]{:S(2)}) async-start(), calls=%async_computation.9 | async-start | bytes 3342336 | tf_op jit(solution)/shard_map/reduce_scatter | solution.py:330
  1509.3 183.9 %reduce-scatter.26.cloned.1.call-start = ((), (), s32[]{:S(2)}) async-start(), calls=%async_computation.15 | async-start | bytes 10027008 | tf_op jit(solution)/shard_map/reduce_scatter | solution.py:341
  1516.2 292.0 %reduce-scatter.24.cloned.1.call-start = ((), (), s32[]{:S(2)}) async-start(), calls=%async_computation.14 | async-start | bytes 10027008 | tf_op jit(solution)/shard_map/reduce_scatter | solution.py:339
  1523.9 378.3 %reduce-scatter.20.cloned.1.call-start = ((), (), s32[]{:S(2)}) async-start(), calls=%async_computation.12 | async-start | bytes 7520256 | tf_op jit(solution)/shard_map/reduce_scatter | solution.py:337
  1530.2 570.0 %reduce-scatter.18.cloned.1.call-start = ((), (), s32[]{:S(2)}) async-start(), calls=%async_computation.11 | async-start | bytes 20054016 | tf_op jit(solution)/shard_map/reduce_scatter | solution.py:334
  1530.8 628.2 %reduce-scatter.28.cloned.1.call-start = ((), (), s32[]{:S(2)}) async-start(), calls=%async_computation.16 | async-start | bytes 417792
  1541.9 675.6 %reduce-scatter.30.cloned.1.call-start = ((), (), s32[]{:S(2)}) async-start(), calls=%async_computation.17 | async-start | bytes 417792
  1551.6 728.2 %reduce-scatter.16.cloned.1.call-start = ((), (), s32[]{:S(2)}) async-start(), calls=%async_computation.10 | async-start | bytes 1671168 | tf_op jit(solution)/shard_map/reduce_scatter | solution.py:333
  1554.5 781.4 %all-reduce.9.cloned.1.call-start = ((), (), s32[]{:S(2)}) async-start(), calls=%async_computation.18 | async-start | bytes 3145728 | tf_op jit(solution)/shard_map/psum | solution.py:344
  2107.8 100.6 %collective-permute-start.29 = (f32[1,512]{1,0:T(1,128)}, f32[1,512]{1,0:T(1,128)}, u32[]{:S(2)}, u32[]{:S(2)}) collective-permute-start(f32[1,512]{1,0:T(1,128)} %slice.239), channel_id=1, source_target_pairs={{0,1},{1,2},{2,3},{3,4},{4,5},{5,6},{6,7},{7,8},{8,9},{9,10},{10,1... | collective-permute-start | bytes 6152 | tf_op jit(solution)/shard_map/ppermute | solution.py:15
  (429 other events, 3549.9 us)
Sparse Core Ops, SparseCore 0:
  898.6 64.6 reduce-scatter.21
  1509.4 67.9 reduce-scatter.13
  1582.0 111.0 reduce-scatter.25
  1697.1 111.0 reduce-scatter.23
  1812.6 89.5 reduce-scatter.19
  1906.2 194.0 reduce-scatter.17
  2104.3 54.6 reduce-scatter.27
  2162.9 54.5 reduce-scatter.29
  2221.2 58.4 reduce-scatter.15
  2283.5 52.3 all-reduce.8
where the time goes:
time: 2370 us; the launch traced here: 2350 us
  local copies, waits for them, and re-layouts  712 us (30%)
  waiting for transfers between devices  698 us (29%)
  matrix products  358 us (15%)
  other arithmetic  338 us (14%)
  starting transfers between devices  170 us (7%)
  blocking collectives  54.1 us (2%)
    select_n x48, other arithmetic, tap_stack(): columns.append(jnp.where(keep[:, None], piece, jnp.zeros_like(piece)))  204 us
    reduce_scatter x1, waiting for transfers between devices, local(): lax.psum_scatter(pos_grad, 'seq', scatter_dimension=0, tiled=True)  196 us
    while x624, local copies, waits for them, and re-layouts  195 us
    ppermute x26, starting transfers between devices, from_behind(): lax.ppermute(value, axis, [(source, source + steps) for source in range(i...  151 us
    reshape x32, local copies, waits for them, and re-layouts, tap_kernel(): return block.reshape(8, group_width, GROUPS, group_width)  118 us
    reduce_scatter x1, waiting for transfers between devices, local(): lax.psum_scatter(grad_ffn_out, 'seq', scatter_dimension=0, tiled=True)  114 us
    reduce_scatter x1, waiting for transfers between devices, local(): lax.psum_scatter(grad_ffn_in, 'seq', scatter_dimension=0, tiled=True)  113 us
    reduce_scatter x1, waiting for transfers between devices, local(): lax.psum_scatter(grad_attn_in, 'seq', scatter_dimension=0, tiled=True)  92.2 us
  transfers between devices with their start and end apart: 40, of which 14 were waited for; matrix products, arithmetic and copies ran while one was open for 34% of the time, Pallas kernels for 0%

commit v1 on v0

v1 whole, which is shorter than its diff:
```python
import functools

import jax
import jax.numpy as jnp
from jax import lax
from jax.experimental import pallas as pl
from jax.experimental.pallas import tpu as pltpu
from jax.sharding import PartitionSpec as P

HEADS = 12
KERNEL = 128
GROUPS = 16
MAXLEN = 1536
RING = 16

def row_dot(left, right):
    return lax.dot_general(left, right, (((1,), (1,)), ((), ())), preferred_element_type=jnp.float32)


def plain_dot(left, right):
    return lax.dot_general(left, right, (((1,), (0,)), ((), ())), preferred_element_type=jnp.float32)


def over_rows_dot(left, right):
    return lax.dot_general(left, right, (((0,), (0,)), ((), ())), preferred_element_type=jnp.float32)


VMEM_WHOLE = pl.BlockSpec(memory_space=pltpu.VMEM)
SMEM_WHOLE = pl.BlockSpec(memory_space=pltpu.SMEM)
HEAD_DIM = 64
Q_TILE = 512
K_TILE = 512
LOW = -1e30


def unpack_heads(packed_ref, targets, factor):
    blocks, half, lanes = packed_ref.shape
    share = lanes // 2

    def one(block, carry):
        tile = packed_ref[block]
        for side in range(2):
            row = pl.multiple_of(block * 2 * half + side * half, half)
            for place, target in enumerate(targets):
                begin = side * share + place * HEAD_DIM
                piece = tile[:, begin : begin + HEAD_DIM]
                if place == 0 and factor != 1.0:
                    piece = piece * jnp.bfloat16(factor)
                target[pl.ds(row, half), :] = piece
        return carry

    lax.fori_loop(0, blocks, one, 0)


def attend_kernel(
    halo, low_ref, high_ref, packed_ref, query_ids_ref, key_ids_ref, out_ref, wide_ref, log_ref,
    query, keys, values,
):
    scale = HEAD_DIM ** (-0.5)
    unpack_heads(packed_ref, (query, keys, values), scale)
    rows = query_ids_ref.shape[0]
    half = packed_ref.shape[1]
    block = 2 * half

    def query_tile(index, carry):
        first = pl.multiple_of(index * Q_TILE, Q_TILE)
        q = query[pl.ds(halo * block + first, Q_TILE), :]
        q_ids = query_ids_ref[pl.ds(first, Q_TILE), :]

        def key_tile(at, state):
            top, mass, total = state
            column = pl.multiple_of(at * K_TILE, K_TILE)
            scores = row_dot(q, keys[pl.ds(column, K_TILE), :])
            scores = jnp.where(q_ids == key_ids_ref[:, pl.ds(column, K_TILE)], scores, LOW)
            new_top = jnp.maximum(top, jnp.max(scores, axis=1, keepdims=True))
            weight = jnp.exp(scores - new_top)
            fade = jnp.exp(top - new_top)
            mass = fade * mass + jnp.sum(weight, axis=1, keepdims=True)
            total = fade * total + plain_dot(
                weight.astype(jnp.bfloat16), values[pl.ds(column, K_TILE), :]
            )
            return new_top, mass, total

        top, mass, total = lax.fori_loop(
            low_ref[index],
            high_ref[index],
            key_tile,
            (
                jnp.full((Q_TILE, 1), 0.5 * LOW, jnp.float32),
                jnp.zeros((Q_TILE, 1), jnp.float32),
                jnp.zeros((Q_TILE, HEAD_DIM), jnp.float32),
            ),
        )
        mass = jnp.maximum(mass, 1e-37)
        attended = total / mass
        wide_ref[pl.ds(first, Q_TILE), :] = attended
        log_ref[pl.ds(first, Q_TILE), :] = top + jnp.log(mass)
        narrow = attended.astype(jnp.bfloat16)
        for inner in range(Q_TILE // block):
            spot = index * (Q_TILE // block) + inner
            out_ref[spot, :, 0:HEAD_DIM] = narrow[inner * block : inner * block + half]
            out_ref[spot, :, HEAD_DIM:] = narrow[inner * block + half : (inner + 1) * block]
        return carry

    lax.fori_loop(0, rows // Q_TILE, query_tile, 0)


def attend(low, high, packed, query_ids, key_ids, halo):
    blocks, half, _ = packed.shape
    rows = query_ids.shape[0]
    key_rows = blocks * 2 * half
    return pl.pallas_call(
        functools.partial(attend_kernel, halo),
        out_shape=(
            jax.ShapeDtypeStruct((blocks - 2 * halo, half, 2 * HEAD_DIM), jnp.bfloat16),
            jax.ShapeDtypeStruct((rows, HEAD_DIM), jnp.float32),
            jax.ShapeDtypeStruct((rows, 1), jnp.float32),
        ),
        in_specs=[SMEM_WHOLE] * 2 + [VMEM_WHOLE] * 3,
        out_specs=(VMEM_WHOLE,) * 3,
        scratch_shapes=[pltpu.VMEM((key_rows, HEAD_DIM), jnp.bfloat16)] * 3,
        compiler_params=pltpu.CompilerParams(vmem_limit_bytes=56 << 20),
        name="attend",
    )(low, high, packed, query_ids, key_ids)


def attend_back_kernel(
    halo, low_ref, high_ref, packed_ref, grad_ref, wide_ref, log_ref, query_ids_ref, key_ids_ref,
    out_ref, query, keys, values, grads, key_grads, value_grads,
):
    scale = HEAD_DIM ** (-0.5)
    unpack_heads(packed_ref, (query, keys, values), scale)
    unpack_heads(grad_ref, (grads,), 1.0)
    blocks, half, _ = packed_ref.shape
    rows = query_ids_ref.shape[0]
    block = 2 * half
    key_grads[...] = jnp.zeros_like(key_grads)
    value_grads[...] = jnp.zeros_like(value_grads)
    if halo:
        out_ref[...] = jnp.zeros_like(out_ref)

    def query_tile(index, carry):
        first = pl.multiple_of(index * Q_TILE, Q_TILE)
        q = query[pl.ds(halo * block + first, Q_TILE), :]
        g = grads[pl.ds(first, Q_TILE), :]
        q_ids = query_ids_ref[pl.ds(first, Q_TILE), :]
        log_total = log_ref[pl.ds(first, Q_TILE), :]
        delta = jnp.sum(
            g.astype(jnp.float32) * wide_ref[pl.ds(first, Q_TILE), :], axis=1, keepdims=True
        )

        def key_tile(at, running):
            column = pl.multiple_of(at * K_TILE, K_TILE)
            k = keys[pl.ds(column, K_TILE), :]
            v = values[pl.ds(column, K_TILE), :]
            probs = jnp.where(
                q_ids == key_ids_ref[:, pl.ds(column, K_TILE)],
                jnp.exp(row_dot(q, k) - log_total),
                0.0,
            )
            prob_grad = row_dot(g, v)
            score_grad = (probs * (prob_grad - delta) * scale).astype(jnp.bfloat16)
            value_grads[pl.ds(column, K_TILE), :] += over_rows_dot(probs.astype(jnp.bfloat16), g)
            key_grads[pl.ds(column, K_TILE), :] += over_rows_dot(score_grad, q)
            return running + plain_dot(score_grad, k)

        query_grad = lax.fori_loop(
            low_ref[index], high_ref[index], key_tile, jnp.zeros((Q_TILE, HEAD_DIM), jnp.float32)
        ).astype(jnp.bfloat16)
        for inner in range(Q_TILE // block):
            spot = halo + index * (Q_TILE // block) + inner
            out_ref[spot, :, 0:HEAD_DIM] = query_grad[inner * block : inner * block + half]
            out_ref[spot, :, 3 * HEAD_DIM : 4 * HEAD_DIM] = query_grad[
                inner * block + half : (inner + 1) * block
            ]
        return carry

    lax.fori_loop(0, rows // Q_TILE, query_tile, 0)

    def finish(spot, carry):
        for side in range(2):
            row = pl.multiple_of(spot * block + side * half, half)
            begin = (3 * side + 1) * HEAD_DIM
            out_ref[spot, :, begin : begin + HEAD_DIM] = (
                key_grads[pl.ds(row, half), :] * (1.0 / scale)
            ).astype(jnp.bfloat16)
            out_ref[spot, :, begin + HEAD_DIM : begin + 2 * HEAD_DIM] = value_grads[
                pl.ds(row, half), :
            ].astype(jnp.bfloat16)
        return carry

    lax.fori_loop(0, blocks, finish, 0)


def attend_back(low, high, packed, grad, wide, log_total, query_ids, key_ids, halo):
    blocks, half, lanes = packed.shape
    rows = query_ids.shape[0]
    key_rows = blocks * 2 * half
    return pl.pallas_call(
        functools.partial(attend_back_kernel, halo),
        out_shape=jax.ShapeDtypeStruct((blocks, half, lanes), jnp.bfloat16),
        in_specs=[SMEM_WHOLE] * 2 + [VMEM_WHOLE] * 6,
        out_specs=VMEM_WHOLE,
        scratch_shapes=[pltpu.VMEM((key_rows, HEAD_DIM), jnp.bfloat16)] * 3
        + [pltpu.VMEM((rows, HEAD_DIM), jnp.bfloat16)]
        + [pltpu.VMEM((key_rows, HEAD_DIM), jnp.float32)] * 2,
        compiler_params=pltpu.CompilerParams(vmem_limit_bytes=60 << 20),
        name="attend_back",
    )(low, high, packed, grad, wide, log_total, query_ids, key_ids)

TAPS = 16
PARTS = 4


def conv_kernel(back, rows_ref, ids_ref, weight_ref, out_ref, planes, shifted, block, total):
    step = pl.program_id(0)
    rows, width = out_ref.shape
    group_width = width // GROUPS
    part = width // PARTS
    held = GROUPS // PARTS
    long = planes.shape[1]

    @pl.when(step == 0)
    def _():
        for at in range(PARTS):
            planes[at] = rows_ref[:, at * part : (at + 1) * part].astype(jnp.float32)
        planes[PARTS] = jnp.broadcast_to(ids_ref[...], (long, part))

        def plane(at, carry):
            tile = planes[at]

            def pair(two, inner_carry):
                if back:
                    first, second = TAPS - 2 * two, TAPS - 2 * two - 1
                else:
                    first, second = 2 * two, 2 * two + 1
                both = jnp.concatenate(
                    [
                        pltpu.roll(tile, lax.rem(long - first, long), 0),
                        pltpu.roll(tile, lax.rem(long - second, long), 0),
                    ],
                    axis=1,
                ).astype(jnp.bfloat16)
                lanes = pl.multiple_of(two * 2 * part, 128)
                shifted[at, :, pl.ds(lanes, 2 * part)] = both[: long - TAPS]
                return inner_carry

            return lax.fori_loop(0, TAPS // 2, pair, carry)

        lax.fori_loop(0, PARTS + 1, plane, 0)

    turn = (KERNEL // TAPS - 1 - step) if back else step
    base = pl.multiple_of(turn * TAPS, TAPS)
    own = ids_ref[pl.ds(KERNEL // 2, rows), :].astype(jnp.bfloat16)
    keep = shifted[PARTS, pl.ds(base, rows), :] == jnp.broadcast_to(own, (rows, TAPS * part))
    lane = lax.broadcasted_iota(jnp.int32, (group_width, 2 * part), 1)
    lane = jnp.where(lane >= part, lane - part, lane)
    nothing = jnp.bfloat16(0)
    for at in range(PARTS):

        def fill(two, carry):
            row = pl.multiple_of(2 * two * group_width, 16)
            own_lanes = slice(at * part, (at + 1) * part)
            one = weight_ref[pl.ds(row, group_width), own_lanes]
            other = weight_ref[pl.ds(pl.multiple_of(row + group_width, 16), group_width), own_lanes]
            for group in range(held):
                inside = (lane >= group * group_width) & (lane < (group + 1) * group_width)
                if back:
                    both = jnp.concatenate([one, other], axis=1)
                    lanes = pl.multiple_of(two * 2 * part, 128)
                    block[
                        group * group_width : (group + 1) * group_width, pl.ds(lanes, 2 * part)
                    ] = jnp.where(inside, both, nothing)
                else:
                    for side, piece in enumerate((one, other)):
                        place = pl.multiple_of((2 * two + side) * part + group * group_width, 16)
                        block[pl.ds(place, group_width), :] = jnp.where(
                            inside[:, :part], piece, nothing
                        )
            return carry

        lax.fori_loop(0, TAPS // 2, fill, 0)
        taken = jnp.where(keep, shifted[at, pl.ds(base, rows), :], nothing)
        result = (row_dot if back else plain_dot)(taken, block[...])

        @pl.when(step == 0)
        def _():
            total[at] = result

        @pl.when(step > 0)
        def _():
            total[at] += result

    @pl.when(step == pl.num_programs(0) - 1)
    def _():
        for at in range(PARTS):
            out_ref[:, at * part : (at + 1) * part] = total[at]


def conv_rows(back, padded, padded_ids, weight):
    long, width = padded.shape
    rows = long - KERNEL
    part = width // PARTS
    group_width = width // GROUPS
    return pl.pallas_call(
        functools.partial(conv_kernel, back),
        grid=(KERNEL // TAPS,),
        out_shape=jax.ShapeDtypeStruct((rows, width), jnp.float32),
        in_specs=[
            pl.BlockSpec((long, width), lambda step: (0, 0)),
            pl.BlockSpec((long, 1), lambda step: (0, 0)),
            pl.BlockSpec((TAPS * group_width, width), lambda step: (step, 0)),
        ],
        out_specs=pl.BlockSpec((rows, width), lambda step: (0, 0)),
        scratch_shapes=[
            pltpu.VMEM((PARTS + 1, long, part), jnp.float32),
            pltpu.VMEM((PARTS + 1, long - TAPS, TAPS * part), jnp.bfloat16),
            pltpu.VMEM((part, TAPS * part) if back else (TAPS * part, part), jnp.bfloat16),
            pltpu.VMEM((PARTS, rows, part), jnp.float32),
        ],
        compiler_params=pltpu.CompilerParams(vmem_limit_bytes=56 << 20),
        name="conv_back" if back else "conv",
    )(padded, padded_ids, weight)


CHUNKS = 8


def taps_grad_kernel(
    clips, halo, input_ref, grad_ref, input_ids_ref, grad_ids_ref, out_ref,
    inputs, grads, spaced_inputs, spaced_grads, input_cols, grad_cols,
):
    half = KERNEL // 2
    group_width = inputs.shape[1]

    def unpack(packed_ref, target):
        blocks, rows, _ = packed_ref.shape

        def one(block, carry):
            tile = packed_ref[block]
            for chunk in range(CHUNKS):
                row = pl.multiple_of((block * CHUNKS + chunk) * rows, rows)
                target[pl.ds(row, rows), :] = tile[:, chunk * group_width : (chunk + 1) * group_width]
            return carry

        lax.fori_loop(0, blocks, one, 0)

    unpack(input_ref, inputs)
    unpack(grad_ref, grads)
    spaced_inputs[...] = jnp.zeros_like(spaced_inputs)
    spaced_grads[...] = jnp.zeros_like(spaced_grads)
    input_rows, grad_rows = inputs.shape[0], grads.shape[0]
    halo_rows = (input_rows - grad_rows) // 2

    def place(clip, carry):
        at = pl.multiple_of(half + half * clip, half)
        number = clip.astype(jnp.float32)
        spaced_inputs[pl.ds(at, input_rows), :] += jnp.where(
            input_ids_ref[...] == number, inputs[...].astype(jnp.float32), 0.0
        )
        spaced_grads[pl.ds(at + halo_rows, grad_rows), :] += jnp.where(
            grad_ids_ref[...] == number, grads[...].astype(jnp.float32), 0.0
        )
        return carry

    lax.fori_loop(0, clips, place, 0)
    origin = half + halo_rows
    span = input_cols.shape[0]
    spaced = spaced_grads[...]
    for tap in range(TAPS):
        moved = pltpu.roll(spaced, tap, 0) if tap else spaced
        grad_cols[:, tap * group_width : (tap + 1) * group_width] = moved[
            origin : origin + span
        ].astype(jnp.bfloat16)
    for turn in range(KERNEL // TAPS):
        begin = origin - half + turn * TAPS
        input_cols[:, turn * group_width : (turn + 1) * group_width] = spaced_inputs[
            begin : begin + span, :
        ].astype(jnp.bfloat16)
    result = over_rows_dot(input_cols[...], grad_cols[...]).astype(jnp.bfloat16)
    for place_at in range(2 * KERNEL // TAPS):
        turn, side = place_at // 2, place_at % 2
        out_ref[place_at] = result[
            turn * group_width : (turn + 1) * group_width,
            side * CHUNKS * group_width : (side + 1) * CHUNKS * group_width,
        ]


def taps_grad(inputs, grads, input_ids, grad_ids, clips, halo, group_width):
    _, rows, lanes = grads.shape
    half = KERNEL // 2
    grad_rows = grad_ids.shape[0]
    input_rows = input_ids.shape[0]
    long = input_rows + half * clips + KERNEL + (input_rows - grad_rows) // 2
    span = grad_rows + half * clips
    return pl.pallas_call(
        functools.partial(taps_grad_kernel, clips, halo),
        out_shape=jax.ShapeDtypeStruct((2 * KERNEL // TAPS, group_width, lanes), jnp.bfloat16),
        in_specs=[VMEM_WHOLE] * 4,
        out_specs=VMEM_WHOLE,
        scratch_shapes=[
            pltpu.VMEM((input_rows, group_width), jnp.bfloat16),
            pltpu.VMEM((grad_rows, group_width), jnp.bfloat16),
            pltpu.VMEM((long, group_width), jnp.float32),
            pltpu.VMEM((long, group_width), jnp.float32),
            pltpu.VMEM((span, KERNEL // TAPS * group_width), jnp.bfloat16),
            pltpu.VMEM((span, TAPS * group_width), jnp.bfloat16),
        ],
        compiler_params=pltpu.CompilerParams(vmem_limit_bytes=60 << 20),
        name="taps_grad",
    )(inputs, grads, input_ids, grad_ids)


def from_behind(value, axis, steps):
    count = lax.axis_size(axis)
    initial, last = (max(0, -steps), min(count, count - steps))
    return lax.ppermute(value, axis, [(source, source + steps) for source in range(initial, last)])


def padded_2(value, width):
    length = value.shape[0]
    before = from_behind(value[length - width :], "seq", 1)
    after = from_behind(value[:width], "seq", -1)
    return jnp.concatenate([before, value, after], axis=0)


def norm_rows(values, scales, shifts):
    center = values - jnp.mean(values, axis=-1, keepdims=True)
    spread = jnp.mean(center * center, axis=-1, keepdims=True)
    return center * lax.rsqrt(spread + 1e-05) * scales + shifts


def gelu_exact(values):
    return jax.nn.gelu(values, approximate=False)


def clip_span(ends, begin, count, total):
    places = begin + jnp.arange(count, dtype=jnp.int32)
    found = jnp.sum((places[:, None] >= ends[None, :]).astype(jnp.int32), axis=1)
    inside = jnp.logical_and(places >= 0, places < total)
    return jnp.where(inside, found, -1)


def near_groups():
    size = lax.axis_size("seq")
    return [[base + i for i in range(RING)] for base in range(0, size, RING)]


def swap(value):
    groups = None if lax.axis_size("seq") == RING else near_groups()
    return lax.all_to_all(value, "seq", 0, 0, axis_index_groups=groups)


def with_far_blocks(value, count):
    if lax.axis_size("seq") == RING or count == 0:
        return value
    before = from_behind(value[value.shape[0] - count :], "seq", RING)
    after = from_behind(value[:count], "seq", -RING)
    return jnp.concatenate([before, value, after], axis=0)


def fold_far_blocks(value, count):
    if lax.axis_size("seq") == RING or count == 0:
        return value
    own = value[count : value.shape[0] - count]
    to_before = from_behind(value[:count], "seq", -RING)
    to_after = from_behind(value[value.shape[0] - count :], "seq", RING)
    wide = own.astype(jnp.float32)
    wide = wide.at[wide.shape[0] - count :].add(to_before.astype(jnp.float32))
    wide = wide.at[:count].add(to_after.astype(jnp.float32))
    return wide.astype(value.dtype)


def pack_halves(parts):
    frames, heads, _ = parts[0].shape
    joined = jnp.concatenate(parts, axis=2)
    lanes = joined.shape[2]
    moved = joined.reshape(2, frames // 2, heads, lanes).transpose(2, 1, 0, 3)
    moved = moved.reshape(heads, frames // 2, 2 * lanes)
    return jnp.pad(moved, ((0, RING - heads), (0, 0), (0, 0)))


def unpack_halves(packed, heads, count):
    half = packed.shape[1]
    lanes = packed.shape[2] // (2 * count)
    parts = packed[:heads].reshape(heads, half, 2, count, lanes).transpose(2, 1, 3, 0, 4)
    return parts.reshape(2 * half, count * heads * lanes)


def pack_groups(value):
    frames, width = value.shape
    group_width = width // GROUPS
    moved = value.reshape(CHUNKS, frames // CHUNKS, GROUPS, group_width).transpose(2, 1, 0, 3)
    return moved.reshape(GROUPS, frames // CHUNKS, CHUNKS * group_width)


LANES = 256


def flat_share(grad, count):
    rows, columns = grad.shape
    share = grad.astype(jnp.bfloat16).reshape(count, rows // count, columns)
    return [share[:, :, at : at + LANES] for at in range(0, columns, LANES)]


def reduce_shares(grads, extra=None):
    count = lax.axis_size("seq")
    pieces, sizes = [], []
    for grad in grads:
        pieces += flat_share(grad, count)
        sizes.append((grad.shape[0] // count, grad.shape[1]))
    if extra is not None:
        pieces.append(extra.astype(jnp.bfloat16))
    share = lax.psum_scatter(
        jnp.concatenate(pieces, axis=1), "seq", scatter_dimension=0, tiled=False
    ).astype(jnp.bfloat16)
    total = sum_pair(share)
    out, at = [], 0
    for rows, columns in sizes:
        parts = []
        for _ in range(columns // LANES):
            parts.append(total[at : at + rows])
            at += rows
        out.append(jnp.concatenate(parts, axis=1))
    if extra is not None:
        out.append(total[at:])
    return out


def sum_pair(share):
    count = lax.axis_size("rep")
    total = share.astype(jnp.float32)
    if count == 2:
        other = lax.ppermute(share, "rep", [(0, 1), (1, 0)])
        return total + other.astype(jnp.float32)
    return lax.psum(share, "rep").astype(jnp.float32)


def local(
    samples,
    clip_lengths,
    stem_weight,
    stem_gain,
    stem_bias,
    proj_weight,
    pos_weight,
    norm_gains,
    biases,
    attn_in,
    attn_out,
    ffn_in,
    ffn_in_bias,
    ffn_out,
    out_grad,
):
    rows_dev = out_grad.shape[1]
    width = attn_out.shape[0]
    chans = stem_weight.shape[1]
    group_width = width // GROUPS
    count = lax.axis_size("seq")
    place = lax.axis_index("seq")
    total = rows_dev * count
    begin = place * rows_dev
    ends = jnp.cumsum(clip_lengths[0])
    clips = ends.shape[0]
    own_ids = clip_span(ends, begin, rows_dev, total)
    half = KERNEL // 2
    frames = samples[0].reshape(rows_dev, 2 * chans)
    next_row = from_behind(frames[:1, :chans], "seq", -1)
    same_next = clip_span(ends, begin + 1, rows_dev, total) == own_ids
    following = jnp.concatenate([frames[1:, :chans], next_row], axis=0)
    following = jnp.where(same_next[:, None], following, jnp.zeros_like(following))
    unfold = jnp.concatenate([frames, following], axis=1)
    stem_pre = plain_dot(unfold, stem_weight)
    feature = gelu_exact(stem_pre)
    normed_b = norm_rows(feature, stem_gain, stem_bias).astype(jnp.bfloat16)
    start_x = plain_dot(normed_b, proj_weight) + biases[:, 0]
    start_b = start_x.astype(jnp.bfloat16)
    padded = padded_2(start_b, half)
    padded_ids = clip_span(ends, begin - half, rows_dev + 2 * half, total)
    padded_ids = padded_ids.astype(jnp.float32)[:, None]
    start_groups = swap(pack_groups(start_b))
    conv_out = conv_rows(False, padded, padded_ids, pos_weight) + biases[:, 1]
    mixed = start_x + gelu_exact(conv_out)
    hidden = norm_rows(mixed, norm_gains[:, 0], biases[:, 2])
    hidden_b = hidden.astype(jnp.bfloat16)
    project = plain_dot(hidden_b, attn_in)
    query_b = (project[:, :width] + biases[:, 3]).astype(jnp.bfloat16)
    keys_b = project[:, width : 2 * width].astype(jnp.bfloat16)
    values_b = (project[:, 2 * width :] + biases[:, 4]).astype(jnp.bfloat16)
    by_head = [piece.reshape(rows_dev, HEADS, HEAD_DIM) for piece in (query_b, keys_b, values_b)]

    segment = RING * rows_dev
    far = 0 if count == RING else -(-MAXLEN // rows_dev)
    segment_begin = (place // RING) * segment
    key_begin = segment_begin - far * rows_dev
    query_ids = clip_span(ends, segment_begin, segment, total)
    key_ids = clip_span(ends, key_begin, segment + 2 * far * rows_dev, total)
    firsts = segment_begin + Q_TILE * jnp.arange(segment // Q_TILE, dtype=jnp.int32)
    lasts = firsts + (Q_TILE - 1)
    low = jnp.max(jnp.where(ends[None] <= firsts[:, None], ends[None], 0), axis=1)
    high = jnp.min(jnp.where(ends[None] > lasts[:, None], ends[None], total), axis=1)
    low = (low - key_begin) // K_TILE
    high = (high - key_begin + (K_TILE - 1)) // K_TILE
    high = jnp.where(place % RING < HEADS, high, low)
    packed = with_far_blocks(swap(pack_halves(by_head)), far)
    attended_heads, wide, log_total = attend(
        low, high, packed, query_ids[:, None], key_ids[None, :], far
    )
    attended_b = unpack_halves(swap(attended_heads), HEADS, 1)
    pre_second = hidden + plain_dot(attended_b, attn_out) + biases[:, 5]
    second = norm_rows(pre_second, norm_gains[:, 1], biases[:, 6])
    second_b = second.astype(jnp.bfloat16)
    inner = plain_dot(second_b, ffn_in) + ffn_in_bias
    inner_b = gelu_exact(inner).astype(jnp.bfloat16)
    pre_last = second + plain_dot(inner_b, ffn_out) + biases[:, 7]
    layer_out = norm_rows(pre_last, norm_gains[:, 2], biases[:, 8]).astype(jnp.bfloat16)[None]
    grad_last, gain_grad_c, bias_grad_c = jax.vjp(
        norm_rows, pre_last, norm_gains[:, 2], biases[:, 8]
    )[1](out_grad[0].astype(jnp.float32))
    grad_last_b = grad_last.astype(jnp.bfloat16)
    grad_ffn_out = over_rows_dot(inner_b, grad_last_b)
    grad_inner = jax.vjp(gelu_exact, inner)[1](row_dot(grad_last_b, ffn_out))[0]
    grad_inner_b = grad_inner.astype(jnp.bfloat16)
    grad_ffn_in = over_rows_dot(second_b, grad_inner_b)
    ffn_grads = reduce_shares([grad_ffn_in, grad_ffn_out])
    grad_second = grad_last + row_dot(grad_inner_b, ffn_in)
    grad_pre_second, gain_grad_b, bias_grad_b = jax.vjp(
        norm_rows, pre_second, norm_gains[:, 1], biases[:, 6]
    )[1](grad_second)
    grad_branch_b = grad_pre_second.astype(jnp.bfloat16)
    grad_attn_out = over_rows_dot(attended_b, grad_branch_b)
    grad_out = row_dot(grad_branch_b, attn_out).astype(jnp.bfloat16)
    grad_heads = swap(pack_halves([grad_out.reshape(rows_dev, HEADS, HEAD_DIM)]))
    packed_grad = attend_back(
        low, high, packed, grad_heads, wide, log_total, query_ids[:, None], key_ids[None, :], far
    )
    grad_project_b = unpack_halves(swap(fold_far_blocks(packed_grad, far)), HEADS, 3)
    grad_attn_in = over_rows_dot(hidden_b, grad_project_b)
    attn_grads = reduce_shares([grad_attn_in, grad_attn_out])
    grad_hidden = grad_pre_second + row_dot(grad_project_b, attn_in)
    grad_mixed, gain_grad_a, bias_grad_a = jax.vjp(
        norm_rows, mixed, norm_gains[:, 0], biases[:, 2]
    )[1](grad_hidden)
    grad_conv = jax.vjp(gelu_exact, conv_out)[1](grad_mixed)[0]
    grad_conv_b = grad_conv.astype(jnp.bfloat16)
    padded_grad = padded_2(grad_conv_b, half)
    grad_groups = swap(pack_groups(grad_conv_b))
    input_grad = conv_rows(True, padded_grad, padded_ids, pos_weight)

    near = 0 if count == RING else 1
    first_clip = query_ids[0]
    input_ids = clip_span(ends, segment_begin - near * rows_dev, segment + 2 * near * rows_dev, total)
    taps = taps_grad(
        with_far_blocks(start_groups, near),
        grad_groups,
        (input_ids - first_clip).astype(jnp.float32)[:, None],
        (query_ids - first_clip).astype(jnp.float32)[:, None],
        clips,
        near,
        group_width,
    )
    own_taps = KERNEL // count
    if count == RING:
        pos_pieces = swap(taps)
    else:
        segments = count // RING
        by_tap = taps.reshape(2 * KERNEL // TAPS, group_width, CHUNKS, group_width)
        by_tap = by_tap.transpose(0, 2, 1, 3).reshape(segments, -1, LANES)
        across = [[low_at + RING * j for j in range(segments)] for low_at in range(RING)]
        by_tap = lax.all_to_all(by_tap, "seq", 0, 0, axis_index_groups=across)
        by_tap = jnp.sum(by_tap.astype(jnp.float32), axis=0).astype(jnp.bfloat16)
        by_tap = by_tap.reshape(RING, own_taps, group_width, group_width).transpose(0, 2, 1, 3)
        pos_pieces = swap(by_tap.reshape(RING, group_width, own_taps * group_width))
    pos_total = sum_pair(pos_pieces).reshape(GROUPS, group_width, own_taps, group_width)
    pos_grad = pos_total.transpose(2, 1, 0, 3).reshape(own_taps * group_width, width)

    grad_start = grad_mixed + input_grad
    grad_start_b = grad_start.astype(jnp.bfloat16)
    grad_proj = over_rows_dot(normed_b, grad_start_b)
    grad_feature, stem_gain_grad, stem_bias_grad = jax.vjp(
        norm_rows, feature, stem_gain, stem_bias
    )[1](row_dot(grad_start_b, proj_weight))
    grad_pre_b = jax.vjp(gelu_exact, stem_pre)[1](grad_feature)[0].astype(jnp.bfloat16)
    grad_stem = over_rows_dot(unfold, grad_pre_b)
    grad_unfold = row_dot(grad_pre_b, stem_weight)
    grad_follow = jnp.where(same_next[:, None], grad_unfold[:, 2 * chans :], 0.0)
    carried = from_behind(grad_follow[-1:], "seq", 1)
    shifted_back = jnp.concatenate([carried, grad_follow[:-1]], axis=0)
    grad_frames = grad_unfold[:, : 2 * chans] + jnp.concatenate(
        [shifted_back, jnp.zeros((rows_dev, chans), jnp.float32)], axis=1
    )
    sample_grad = grad_frames.reshape(1, 2 * rows_dev, chans)

    gains_grad = jnp.stack([gain_grad_a, gain_grad_b, gain_grad_c], axis=0)
    project_sums = jnp.sum(grad_project_b.astype(jnp.float32), axis=0)
    bias_table = jnp.stack(
        [
            jnp.sum(grad_start, axis=0),
            jnp.sum(grad_conv, axis=0),
            bias_grad_a,
            project_sums[:width],
            project_sums[2 * width :],
            jnp.sum(grad_pre_second, axis=0),
            bias_grad_b,
            jnp.sum(grad_last, axis=0),
            bias_grad_c,
        ],
        axis=0,
    )
    inner_bias_grad = jnp.sum(grad_inner, axis=0)
    small = jnp.concatenate(
        [
            jnp.concatenate([gains_grad, bias_table], axis=0)
            .reshape(12, count, width // count)
            .transpose(1, 0, 2)
            .reshape(count, -1),
            inner_bias_grad.reshape(count, -1),
            stem_gain_grad.reshape(count, -1),
            stem_bias_grad.reshape(count, -1),
        ],
        axis=1,
    )
    length = small.shape[1]
    small = jnp.pad(small, ((0, 0), (0, -length % LANES))).reshape(count, -1, LANES)
    grad_proj_sum, grad_stem_sum, small_sum = reduce_shares([grad_proj, grad_stem], small)
    flat = small_sum.reshape(-1)
    own = width // count
    table = flat[: 12 * own].reshape(12, own)
    at = 12 * own
    own_inner = inner_bias_grad.shape[0] // count
    own_chans = chans // count
    inner_sum = flat[at : at + own_inner]
    at += own_inner
    return (
        layer_out,
        sample_grad,
        grad_stem_sum,
        flat[at : at + own_chans],
        flat[at + own_chans : at + 2 * own_chans],
        grad_proj_sum,
        pos_grad,
        table[:3].T,
        table[3:].T,
        attn_grads[0],
        attn_grads[1],
        ffn_grads[0],
        inner_sum,
        ffn_grads[1],
    )


def solution(mesh):
    streams = P("rep", "seq", None)
    rows = P("seq", None)
    return jax.shard_map(
        local,
        mesh=mesh,
        in_specs=(streams, P("rep", None)) + (P(),) * 12 + (streams,),
        out_specs=(streams, streams, rows, P("seq"), P("seq"))
        + (rows,) * 7
        + (P("seq"), rows),
        check_vma=False,
    )
```

time: 2370 us -> 793 us (0.33)
  local copies, waits for them, and re-layouts: 712 us -> 143 us
  waiting for transfers between devices: 698 us -> 179 us
  matrix products: 358 us -> 39.5 us
  other arithmetic: 338 us -> 44.7 us
  Pallas kernels: 0 us -> 230 us
  starting transfers between devices: 170 us -> 34.6 us
  blocking collectives: 54.1 us -> 90.6 us
    reduce_scatter x7 -> x3, waiting for transfers between devices: 599 us -> 96.9 us  [reduce_shares(): lax.psum_scatter(jnp.concatenate(pieces, axis=1), 'seq', scatter_dimensio...]
    dot_general x144 -> x18, matrix products: 358 us -> 39.5 us  [the longest x6 19.4 us: plain_dot(): lax.dot_general(left, right, (((1,), (0,)), ((), ())), preferred_element_...]
    pallas_call x0 -> x5, Pallas kernels: none -> 230 us  [the longest x2 138 us: conv_rows(): pl.pallas_call(functools.partial(conv_kernel, back), grid=(KERNEL // TAPS...]
    select_n x48 -> x1, other arithmetic: 204 us -> 0.53 us  [local(): high = jnp.where(place % RING < HEADS, high, low)]
    while x624 -> x0, local copies, waits for them, and re-layouts: 195 us -> none
    reshape x50 -> x14, local copies, waits for them, and re-layouts: 180 us -> 22 us  [the longest x2 4.28 us: pack_halves(): moved = moved.reshape(heads, frames // 2, 2 * lanes)]
    ppermute x26 -> x6, starting transfers between devices: 151 us -> 14.2 us  [from_behind(): lax.ppermute(value, axis, [(source, source + steps) for source in range(i...]
    all_to_all x0 -> x4, blocking collectives: none -> 90.6 us  [swap(): return lax.all_to_all(value, 'seq', 0, 0, axis_index_groups=groups)]
  transfers between devices with their start and end apart: 40 -> 16, of which waited for: 14 -> 10; matrix products, arithmetic and copies ran while one was open for 34% -> 13% of each run, Pallas kernels for 0% -> 3%
where the time goes in v1:
time: 793 us; the launch traced here: 779 us
  Pallas kernels  230 us (29%)
  waiting for transfers between devices  179 us (23%)
  local copies, waits for them, and re-layouts  143 us (18%)
  blocking collectives  90.6 us (11%)
  other arithmetic  44.7 us (6%)
  matrix products  39.5 us (5%)
  starting transfers between devices  34.6 us (4%)
  between operations  17.2 us (2%)
    pallas_call x2, Pallas kernels, conv_rows(): pl.pallas_call(functools.partial(conv_kernel, back), grid=(KERNEL // TAPS...  138 us
    reduce_scatter x3, waiting for transfers between devices, reduce_shares(): lax.psum_scatter(jnp.concatenate(pieces, axis=1), 'seq', scatter_dimensio...  96.9 us
    all_to_all x4, blocking collectives, swap(): return lax.all_to_all(value, 'seq', 0, 0, axis_index_groups=groups)  90.6 us
    all_to_all x3, waiting for transfers between devices, swap(): return lax.all_to_all(value, 'seq', 0, 0, axis_index_groups=groups)  53.9 us
    unnamed x232, local copies, waits for them, and re-layouts  46.8 us
    pallas_call x1, Pallas kernels, attend_back(): pl.pallas_call(functools.partial(attend_back_kernel, halo), out_shape=jax...  37 us
    pallas_call x1, Pallas kernels, attend(): pl.pallas_call(functools.partial(attend_kernel, halo), out_shape=(jax.Sha...  28 us
    pallas_call x1, Pallas kernels, taps_grad(): pl.pallas_call(functools.partial(taps_grad_kernel, clips, halo), out_shap...  27.1 us
  transfers between devices with their start and end apart: 16, of which 10 were waited for; matrix products, arithmetic and copies ran while one was open for 13% of the time, Pallas kernels for 3%

profile of v1, /device:TPU:16, one launch (start us, length us, event | category | flops | bytes accessed | tf_op | source)
XLA Modules:
  0.0 779.1 jit_solution(16690783731153203135)
XLA Ops:
  20.1 4.1 fusion.82
  30.9 4.1 collective-permute-done.1
  35.8 64.3 %conv.1 = f32[256,768]{1,0:T(8,128)} custom-call(bf16[384,768]{1,0:T(8,128)(2,1)} %pad_maximum_fusion.1.rows_ref, f32[384,1]{1,0:T(8,128)} %fusion.46.ids_ref, bf16[6144,768]{1,0:T(8,128)(2,1)} %weight_ref.3), custom_call_target="tpu_custom_call" | custom-call | tf_op jit(solution)/shard_map/conv/pallas_call | solution.py:305
  128.0 5.2 all-to-all-start
  142.9 4.1 subtract_convert_fusion
  147.1 22.7 %all-to-all-done.packed_ref = bf16[16,128,384]{2,1,0:T(8,128)(2,1)} async-done(((bf16[16,128,384]{2,1,0:T(8,128)(2,1)}), bf16[16,128,384]{2,1,0:T(8,128)(2,1)}, u32[]{:S(2)}, u32[]{:S(2)}) %all-to-all-start) | async-done | bytes 1572896 | tf_op jit(solution)/shard_map/all_to_all | solution.py:451
  169.8 28.0 %attend.1 = (bf16[16,128,128]{2,1,0:T(8,128)(2,1)}, f32[4096,64]{1,0:T(8,128)}, f32[4096,1]{1,0:T(8,128)}) custom-call(s32[8]{0:T(128)} %get-tuple-element.64.low_ref, s32[8]{0:T(128)} %get-tuple-element.63.high_ref, bf16[16,128,384]{2,1,0:T(8,128)(2,1)} %all-to-all-done.packed_ref, s32[4096,1]{1,0:T(8,128)} %get-tuple-element.50.query_ids_ref, ...), custom_call_target="tpu_custom_call" | custom-call | tf_op jit(solution)/shard_map/attend/pallas_call | solution.py:112
  197.8 18.6 %all_to_all.35 = bf16[16,128,128]{2,1,0:T(8,128)(2,1)S(1)} all-to-all(bf16[16,128,128]{2,1,0:T(8,128)(2,1)} %get-tuple-element.17), channel_id=1, replica_groups=mesh['rep'=2,'seq'=16] {'seq'}, dimensions={0} | all-to-all | bytes 1048576 | tf_op jit(solution)/shard_map/all_to_all | solution.py:451
  223.1 9.8 %multiply_convert_fusion = (bf16[256,3072]{1,0:T(8,128)(2,1)S(1)}, f32[256,3072]{1,0:T(8,128)S(1)}, f32[256,3072]{1,0:T(8,128)S(1)}) fusion(f32[3072]{0:T(1024)S(1)} %copy-done.80, bf16[768,3072]{1,0:T(8,128)(2,1)} %param.26, f32[256,768]{1,0:T(8,128)S(1)} %get-tuple-element.96, f32[768]{0:T(1024)S(1)} %get-tuple-element.32, f32[768]{0:T(1024)S(1)} %get-tuple-element.44, ...), kind=kOutput, calls=%fused_computation.7 | convolution fusion | flops 1260847104 | bytes 13389824 | tf_op jit(solution)/shard_map/dot_general | solution.py:21
  253.1 18.5 %all_to_all.36.grad_ref = bf16[16,128,128]{2,1,0:T(8,128)(2,1)} all-to-all(bf16[16,128,128]{2,1,0:T(8,128)(2,1)S(1)} %pad.15), channel_id=1, replica_groups=mesh['rep'=2,'seq'=16] {'seq'}, dimensions={0} | all-to-all | bytes 1048576 | tf_op jit(solution)/shard_map/all_to_all | solution.py:451
  271.6 37.0 %attend_back.1 = bf16[16,128,384]{2,1,0:T(8,128)(2,1)} custom-call(s32[8]{0:T(128)} %get-tuple-element.64.low_ref, s32[8]{0:T(128)} %get-tuple-element.63.high_ref, bf16[16,128,384]{2,1,0:T(8,128)(2,1)} %all-to-all-done.packed_ref, bf16[16,128,128]{2,1,0:T(8,128)(2,1)} %all_to_all.36.grad_ref, f32[4096,64]{1,0:T(8,128)} %get-tuple-element.18.wide_ref, ...), custom_call_target="tpu_custom_call" | custom-call | tf_op jit(solution)/shard_map/attend_back/pallas_call | solution.py:199
  308.6 4.9 all-to-all-start.3
  328.3 21.7 %all-to-all-done.3 = bf16[16,128,384]{2,1,0:T(8,128)(2,1)} async-done(((bf16[16,128,384]{2,1,0:T(8,128)(2,1)}), bf16[16,128,384]{2,1,0:T(8,128)(2,1)}, u32[]{:S(2)}, u32[]{:S(2)}) %all-to-all-start.3) | async-done | bytes 1572896 | tf_op jit(solution)/shard_map/all_to_all | solution.py:451
  360.7 3.9 multiply_reduce_fusion.1
  376.1 73.5 %conv_back.1 = f32[256,768]{1,0:T(8,128)} custom-call(bf16[384,768]{1,0:T(8,128)(2,1)} %pad_maximum_fusion.2.rows_ref, f32[384,1]{1,0:T(8,128)} %fusion.46.ids_ref, bf16[6144,768]{1,0:T(8,128)(2,1)} %weight_ref.3), custom_call_target="tpu_custom_call" | custom-call | tf_op jit(solution)/shard_map/conv_back/pallas_call | solution.py:305
  516.4 5.0 all-to-all-start.4
  524.0 9.5 %all-to-all-done.4.input_ref = bf16[16,32,384]{2,1,0:T(8,128)(2,1)S(1)} async-done(((bf16[16,32,384]{2,1,0:T(8,128)(2,1)}), bf16[16,32,384]{2,1,0:T(8,128)(2,1)S(1)}, u32[]{:S(2)}, u32[]{:S(2)}) %all-to-all-start.4) | async-done | bytes 393248 | tf_op jit(solution)/shard_map/all_to_all | solution.py:451
  533.6 19.3 %all_to_all.37.grad_ref = bf16[16,32,384]{2,1,0:T(8,128)(2,1)} all-to-all(bf16[16,32,384]{2,1,0:T(8,128)(2,1)S(1)} %reshape.466), channel_id=1, replica_groups=mesh['rep'=2,'seq'=16] {'seq'}, dimensions={0} | all-to-all | bytes 786432 | tf_op jit(solution)/shard_map/all_to_all | solution.py:451
  552.8 27.1 %taps_grad.1 = bf16[16,48,384]{2,1,0:T(8,128)(2,1)} custom-call(bf16[16,32,384]{2,1,0:T(8,128)(2,1)} %copy-done.28, bf16[16,32,384]{2,1,0:T(8,128)(2,1)} %all_to_all.37.grad_ref, f32[4096,1]{1,0:T(8,128)} %get-tuple-element.49.input_ids_ref.grad_ids_ref, f32[4096,1]{1,0:T(8,128)} %get-tuple-element.49.input_ids_ref.grad_ids_ref), custom_call_target="tpu_custom_call" | custom-call | tf_op jit(solution)/shard_map/taps_grad/pallas_call | solution.py:396
  579.9 34.3 %all_to_all.38 = bf16[16,48,384]{2,1,0:T(8,128)(2,1)S(1)} all-to-all(bf16[16,48,384]{2,1,0:T(8,128)(2,1)} %taps_grad.1), channel_id=1, replica_groups=mesh['rep'=2,'seq'=16] {'seq'}, dimensions={0} | all-to-all | bytes 1179648 | tf_op jit(solution)/shard_map/all_to_all | solution.py:451
  625.5 5.0 collective-permute-done.7
  647.8 5.1 collective-permute-done.8
  657.7 96.9 %reduce-scatter.8.cloned.1.call-done = bf16[1,1152,256]{2,1,0:T(8,128)(2,1)} async-done(((bf16[16,1152,256]{2,1,0:T(8,128)(2,1)}), bf16[1,1152,256]{2,1,0:T(8,128)(2,1)}) %reduce-scatter.8.cloned.1.call-update) | async-done | bytes 589840 | tf_op jit(solution)/shard_map/reduce_scatter | solution.py:514
  759.6 10.3 %collective-permute-done.9 = bf16[1152,256]{1,0:T(8,128)(2,1)S(1)} collective-permute-done((bf16[1152,256]{1,0:T(8,128)(2,1)}, bf16[1152,256]{1,0:T(8,128)(2,1)S(1)}, u32[]{:S(2)}, u32[]{:S(2)}) %collective-permute-start.9) | collective-permute-done | bytes 589856 | tf_op jit(solution)/shard_map/ppermute | solution.py:534
  (411 shorter events, 229.1 us)
Async XLA Ops:
  7.2 97.6 %copy-start = (bf16[768,2304]{1,0:T(8,128)(2,1)S(1)}, bf16[768,2304]{1,0:T(8,128)(2,1)}, u32[]{:S(2)}) copy-start(bf16[768,2304]{1,0:T(8,128)(2,1)} %param.24) | copy-start | bytes 10616836
  10.6 8.5 %collective-permute-start = (bf16[1,512]{1,0:T(2,128)(2,1)}, bf16[1,512]{1,0:T(2,128)(2,1)}, u32[]{:S(2)}, u32[]{:S(2)}) collective-permute-start(bf16[1,512]{1,0:T(2,128)(2,1)} %slice.424), channel_id=1, source_target_pairs={{1,0},{2,1},{3,2},{4,3},{5,4},{6,5},{7,6},{8,7},{9,8},{10,9},{11,1... | collective-permute-start | bytes 3080 | tf_op jit(solution)/shard_map/ppermute | solution.py:417
  25.5 5.4 collective-permute-start.2
  28.1 6.8 collective-permute-start.1
  35.8 64.3 %copy-start.45 = (f32[768]{0:T(1024)S(1)}, f32[768]{0:T(1024)}, u32[]{:S(2)}) copy-start(f32[768]{0:T(1024)} %get-tuple-element.37) | copy-start | bytes 9220
  128.0 41.7 %all-to-all-start = ((bf16[16,128,384]{2,1,0:T(8,128)(2,1)}), bf16[16,128,384]{2,1,0:T(8,128)(2,1)}, u32[]{:S(2)}, u32[]{:S(2)}) async-start(bf16[16,128,384]{2,1,0:T(8,128)(2,1)} %pad.14), calls=%async_computation | async-start | bytes 3145728 | tf_op jit(solution)/shard_map/all_to_all | solution.py:451
  308.6 41.4 %all-to-all-start.3 = ((bf16[16,128,384]{2,1,0:T(8,128)(2,1)}), bf16[16,128,384]{2,1,0:T(8,128)(2,1)}, u32[]{:S(2)}, u32[]{:S(2)}) async-start(bf16[16,128,384]{2,1,0:T(8,128)(2,1)} %attend_back.1), calls=%async_computation.3 | async-start | bytes 3145728 | tf_op jit(solution)/shard_map/all_to_all | solution.py:451
  313.4 311.3 %reduce-scatter.4.cloned.1.call-start = ((), (), s32[]{:S(2)}) async-start(), calls=%async_computation.10 | async-start | bytes 2576384 | tf_op jit(solution)/shard_map/reduce_scatter | solution.py:514
  365.5 9.5 %collective-permute-start.4 = (bf16[64,768]{1,0:T(8,128)(2,1)S(1)}, bf16[64,768]{1,0:T(8,128)(2,1)S(1)}, u32[]{:S(2)}, u32[]{:S(2)}) collective-permute-start(bf16[64,768]{1,0:T(8,128)(2,1)S(1)} %get-tuple-element.82), channel_id=1, source_target_pairs={{1,0},{2,1},{3,2},{4,3},{5,4},{6,5},{7,6},{8,7},{9,8},{10,9},{11,1... | collective-permute-start | bytes 294920 | tf_op jit(solution)/shard_map/ppermute | solution.py:417
  368.4 6.8 collective-permute-start.3
  376.1 75.4 %copy-start.6 = (f32[256,512]{1,0:T(8,128)S(1)}, f32[256,512]{1,0:T(8,128)}, u32[]{:S(2)}) copy-start(f32[256,512]{1,0:T(8,128)} %copy-done.5) | copy-start | bytes 1572868
  376.1 75.4 %copy-start.21 = (bf16[512,768]{1,0:T(8,128)(2,1)S(1)}, bf16[512,768]{1,0:T(8,128)(2,1)}, u32[]{:S(2)}) copy-start(bf16[512,768]{1,0:T(8,128)(2,1)} %param.20) | copy-start | bytes 2359300
  376.1 75.4 %copy-start.41 = (f32[256]{0:T(256)S(1)}, f32[256]{0:T(256)}, u32[]{:S(2)}) copy-start(f32[256]{0:T(256)} %copy-done.40) | copy-start | bytes 3076
  481.5 163.7 %reduce-scatter.6.cloned.1.call-start = ((), (), s32[]{:S(2)}) async-start(), calls=%async_computation.11 | async-start | bytes 5013504 | tf_op jit(solution)/shard_map/reduce_scatter | solution.py:514
  494.8 259.8 %reduce-scatter.8.cloned.1.call-start = ((), (), s32[]{:S(2)}) async-start(), calls=%async_computation.12 | async-start | bytes 10027008 | tf_op jit(solution)/shard_map/reduce_scatter | solution.py:514
  516.4 17.2 %all-to-all-start.4 = ((bf16[16,32,384]{2,1,0:T(8,128)(2,1)}), bf16[16,32,384]{2,1,0:T(8,128)(2,1)S(1)}, u32[]{:S(2)}, u32[]{:S(2)}) async-start(bf16[16,32,384]{2,1,0:T(8,128)(2,1)} %reshape.464), calls=%async_computation.5 | async-start | bytes 786432 | tf_op jit(solution)/shard_map/all_to_all | solution.py:451
  552.8 62.7 %copy-start.32 = (bf16[256,512]{1,0:T(8,128)(2,1)S(1)}, bf16[256,512]{1,0:T(8,128)(2,1)}, u32[]{:S(2)}) copy-start(bf16[256,512]{1,0:T(8,128)(2,1)} %copy-done.31) | copy-start | bytes 786436
  579.9 37.6 %copy-start.75 = (pred[256]{0:T(512)(128)(4,1)S(1)}, pred[256]{0:T(512)(128)(4,1)}, u32[]{:S(2)}) copy-start(pred[256]{0:T(512)(128)(4,1)} %copy-done.74) | copy-start | bytes 772
  614.2 16.3 %collective-permute-start.7 = (bf16[16,48,384]{2,1,0:T(8,128)(2,1)S(1)}, bf16[16,48,384]{2,1,0:T(8,128)(2,1)}, u32[]{:S(2)}, u32[]{:S(2)}) collective-permute-start(bf16[16,48,384]{2,1,0:T(8,128)(2,1)S(1)} %all_to_all.38), channel_id=1, source_target_pairs={{0,16},{16,0},{1,17},{17,1},{2,18},{18,2},{3,19},{19,3},{4,20},{20... | collective-permute-start | bytes 1769480 | tf_op jit(solution)/shard_map/ppermute | solution.py:534
  617.7 5.8 collective-permute-start.5
  624.8 17.6 %collective-permute-start.6 = (bf16[292,256]{1,0:T(8,128)(2,1)}, bf16[292,256]{1,0:T(8,128)(2,1)S(1)}, u32[]{:S(2)}, u32[]{:S(2)}) collective-permute-start(bf16[292,256]{1,0:T(8,128)(2,1)} %bitcast.157), channel_id=1, source_target_pairs={{0,16},{16,0},{1,17},{17,1},{2,18},{18,2},{3,19},{19,3},{4,20},{20... | collective-permute-start | bytes 448520 | tf_op jit(solution)/shard_map/ppermute | solution.py:534
  645.2 7.6 collective-permute-start.8
  653.9 102.8 %copy-start.23 = (f32[576,256]{1,0:T(8,128)}, f32[576,256]{1,0:T(8,128)S(1)}, u32[]{:S(2)}) copy-start(f32[576,256]{1,0:T(8,128)S(1)} %convert_add_fusion.2) | copy-start | bytes 1769476
  754.6 15.3 %collective-permute-start.9 = (bf16[1152,256]{1,0:T(8,128)(2,1)}, bf16[1152,256]{1,0:T(8,128)(2,1)S(1)}, u32[]{:S(2)}, u32[]{:S(2)}) collective-permute-start(bf16[1152,256]{1,0:T(8,128)(2,1)} %bitcast.155), channel_id=1, source_target_pairs={{0,16},{16,0},{1,17},{17,1},{2,18},{18,2},{3,19},{19,3},{4,20},{20... | collective-permute-start | bytes 1769480 | tf_op jit(solution)/shard_map/ppermute | solution.py:534
  (77 other events, 498.3 us)
Sparse Core Ops, SparseCore 0:
  481.6 69.3 reduce-scatter.3
  554.9 83.7 reduce-scatter.5
  643.3 111.2 reduce-scatter.7

commit v2 on v1

--- a/solution.py
+++ b/solution.py
@@ -209,121 +209,130 @@
     )(low, high, packed, grad, wide, log_total, query_ids, key_ids)
 
 TAPS = 16
-PARTS = 4
-
-
-def conv_kernel(back, rows_ref, ids_ref, weight_ref, out_ref, planes, shifted, block, total):
-    step = pl.program_id(0)
-    rows, width = out_ref.shape
+SHOT = 384
+
+
+def conv_weights_kernel(back, weight_ref, out_ref):
+    group_width = out_ref.shape[1]
+    if back:
+        for group in range(GROUPS):
+            lanes = slice(group_width * group, group_width * (group + 1))
+            out_ref[group] = jnp.concatenate(
+                [weight_ref[group_width * tap : group_width * (tap + 1), lanes] for tap in range(TAPS)],
+                axis=1,
+            )
+    else:
+        turned = weight_ref[...].T
+        for group in range(GROUPS):
+            out_ref[group] = turned[group_width * group : group_width * (group + 1)]
+
+
+def conv_weights(back, weight):
+    rows, width = weight.shape
     group_width = width // GROUPS
-    part = width // PARTS
-    held = GROUPS // PARTS
-    long = planes.shape[1]
-
-    @pl.when(step == 0)
+    turns = KERNEL // TAPS
+    return pl.pallas_call(
+        functools.partial(conv_weights_kernel, back),
+        grid=(turns,),
+        out_shape=jax.ShapeDtypeStruct((GROUPS, turns * group_width, TAPS * group_width), weight.dtype),
+        in_specs=[pl.BlockSpec((TAPS * group_width, width), lambda turn: (turn, 0))],
+        out_specs=pl.BlockSpec((GROUPS, group_width, TAPS * group_width), lambda turn: (0, turn, 0)),
+        cost_estimate=pl.CostEstimate(flops=0, bytes_accessed=4 * rows * width, transcendentals=0),
+        name="conv_weights_back" if back else "conv_weights",
+    )(weight)
+
+
+def conv_kernel(back, rows_ref, ids_ref, weight_ref, out_ref, spaced, total):
+    group = pl.program_id(0)
+    long, width = rows_ref.shape
+    rows = out_ref.shape[0]
+    half = KERNEL // 2
+    turns = KERNEL // TAPS
+    group_width = width // GROUPS
+    room = spaced.shape[1]
+    own = ids_ref[:, half : half + rows]
+    first = jnp.min(own)
+    count = jnp.max(own) - first + 1
+
+    @pl.when(group == 0)
     def _():
-        for at in range(PARTS):
-            planes[at] = rows_ref[:, at * part : (at + 1) * part].astype(jnp.float32)
-        planes[PARTS] = jnp.broadcast_to(ids_ref[...], (long, part))
-
-        def plane(at, carry):
-            tile = planes[at]
-
-            def pair(two, inner_carry):
-                if back:
-                    first, second = TAPS - 2 * two, TAPS - 2 * two - 1
-                else:
-                    first, second = 2 * two, 2 * two + 1
-                both = jnp.concatenate(
-                    [
-                        pltpu.roll(tile, lax.rem(long - first, long), 0),
-                        pltpu.roll(tile, lax.rem(long - second, long), 0),
-                    ],
-                    axis=1,
-                ).astype(jnp.bfloat16)
-                lanes = pl.multiple_of(two * 2 * part, 128)
-                shifted[at, :, pl.ds(lanes, 2 * part)] = both[: long - TAPS]
-                return inner_carry
-
-            return lax.fori_loop(0, TAPS // 2, pair, carry)
-
-        lax.fori_loop(0, PARTS + 1, plane, 0)
-
-    turn = (KERNEL // TAPS - 1 - step) if back else step
-    base = pl.multiple_of(turn * TAPS, TAPS)
-    own = ids_ref[pl.ds(KERNEL // 2, rows), :].astype(jnp.bfloat16)
-    keep = shifted[PARTS, pl.ds(base, rows), :] == jnp.broadcast_to(own, (rows, TAPS * part))
-    lane = lax.broadcasted_iota(jnp.int32, (group_width, 2 * part), 1)
-    lane = jnp.where(lane >= part, lane - part, lane)
-    nothing = jnp.bfloat16(0)
-    for at in range(PARTS):
-
-        def fill(two, carry):
-            row = pl.multiple_of(2 * two * group_width, 16)
-            own_lanes = slice(at * part, (at + 1) * part)
-            one = weight_ref[pl.ds(row, group_width), own_lanes]
-            other = weight_ref[pl.ds(pl.multiple_of(row + group_width, 16), group_width), own_lanes]
-            for group in range(held):
-                inside = (lane >= group * group_width) & (lane < (group + 1) * group_width)
-                if back:
-                    both = jnp.concatenate([one, other], axis=1)
-                    lanes = pl.multiple_of(two * 2 * part, 128)
-                    block[
-                        group * group_width : (group + 1) * group_width, pl.ds(lanes, 2 * part)
-                    ] = jnp.where(inside, both, nothing)
-                else:
-                    for side, piece in enumerate((one, other)):
-                        place = pl.multiple_of((2 * two + side) * part + group * group_width, 16)
-                        block[pl.ds(place, group_width), :] = jnp.where(
-                            inside[:, :part], piece, nothing
-                        )
+        turned = rows_ref[...].astype(jnp.float32).T
+        ids = ids_ref[...]
+        rest = jnp.zeros((width, room - long), jnp.float32)
+
+        def of_clip(clip):
+            return jnp.concatenate([jnp.where(ids == first + clip, turned, 0.0), rest], axis=1)
+
+        spaced[...] = of_clip(0).astype(jnp.bfloat16)
+
+        def place(clip, carry):
+            spaced[...] += pltpu.roll(of_clip(clip), clip * half, 1).astype(jnp.bfloat16)
             return carry
 
-        lax.fori_loop(0, TAPS // 2, fill, 0)
-        taken = jnp.where(keep, shifted[at, pl.ds(base, rows), :], nothing)
-        result = (row_dot if back else plain_dot)(taken, block[...])
-
-        @pl.when(step == 0)
-        def _():
-            total[at] = result
-
-        @pl.when(step > 0)
-        def _():
-            total[at] += result
-
-    @pl.when(step == pl.num_programs(0) - 1)
+        lax.fori_loop(1, count, place, 0)
+
+    row = pl.multiple_of(group * group_width, group_width)
+    shots = lax.div(rows + half * (count - 1) + SHOT - 1, SHOT)
+
+    def shot(index, carry):
+        base = pl.multiple_of(index * SHOT, 128)
+        tile = spaced[pl.ds(row, group_width), pl.ds(base, SHOT + 2 * KERNEL)]
+        moved = []
+        for tap in range(TAPS):
+            begin = TAPS - tap if back else tap
+            moved.append(tile[:, begin : begin + SHOT + KERNEL])
+        product = plain_dot(weight_ref[0], jnp.concatenate(moved, axis=0))
+        result = None
+        for turn in range(turns):
+            begin = (turns - 1 - turn if back else turn) * TAPS
+            piece = product[turn * group_width : (turn + 1) * group_width, begin : begin + SHOT]
+            result = piece if result is None else result + piece
+        total[pl.ds(row, group_width), pl.ds(base, SHOT)] = result
+        return carry
+
+    lax.fori_loop(0, shots, shot, 0)
+
+    @pl.when(group == GROUPS - 1)
     def _():
-        for at in range(PARTS):
-            out_ref[:, at * part : (at + 1) * part] = total[at]
-
-
-def conv_rows(back, padded, padded_ids, weight):
+        wide = total.shape[1]
+
+        def collect(clip, carry):
+            moved = pltpu.roll(total[...], lax.rem(wide - clip * half, wide), 1)[:, :rows]
+            total[:, :rows] = jnp.where(own == first + clip, moved, total[:, :rows])
+            return carry
+
+        lax.fori_loop(1, count, collect, 0)
+        out_ref[...] = total[:, :rows].T
+
+
+def conv_rows(back, padded, padded_ids, weight, clips):
     long, width = padded.shape
     rows = long - KERNEL
-    part = width // PARTS
-    group_width = width // GROUPS
+    shots = -(-(rows + KERNEL // 2 * (clips - 1)) // SHOT)
     return pl.pallas_call(
         functools.partial(conv_kernel, back),
-        grid=(KERNEL // TAPS,),
+        grid=(GROUPS,),
         out_shape=jax.ShapeDtypeStruct((rows, width), jnp.float32),
         in_specs=[
-            pl.BlockSpec((long, width), lambda step: (0, 0)),
-            pl.BlockSpec((long, 1), lambda step: (0, 0)),
-            pl.BlockSpec((TAPS * group_width, width), lambda step: (step, 0)),
+            pl.BlockSpec((long, width), lambda group: (0, 0)),
+            pl.BlockSpec((1, long), lambda group: (0, 0)),
+            pl.BlockSpec((1,) + weight.shape[1:], lambda group: (group, 0, 0)),
         ],
-        out_specs=pl.BlockSpec((rows, width), lambda step: (0, 0)),
+        out_specs=pl.BlockSpec((rows, width), lambda group: (0, 0)),
         scratch_shapes=[
-            pltpu.VMEM((PARTS + 1, long, part), jnp.float32),
-            pltpu.VMEM((PARTS + 1, long - TAPS, TAPS * part), jnp.bfloat16),
-            pltpu.VMEM((part, TAPS * part) if back else (TAPS * part, part), jnp.bfloat16),
-            pltpu.VMEM((PARTS, rows, part), jnp.float32),
+            pltpu.VMEM((width, SHOT * shots + 2 * KERNEL), jnp.bfloat16),
+            pltpu.VMEM((width, SHOT * shots), jnp.float32),
         ],
-        compiler_params=pltpu.CompilerParams(vmem_limit_bytes=56 << 20),
+        compiler_params=pltpu.CompilerParams(vmem_limit_bytes=48 << 20),
+        cost_estimate=pl.CostEstimate(
+            flops=16 * 2 * 384 * 768 * 512, bytes_accessed=2 * weight.size, transcendentals=0
+        ),
         name="conv_back" if back else "conv",
     )(padded, padded_ids, weight)
 
 
 CHUNKS = 8
+LANES = 256
 
 
 def taps_grad_kernel(
@@ -410,6 +419,454 @@
         name="taps_grad",
     )(inputs, grads, input_ids, grad_ids)
 
+EPS = 1e-05
+BF = jnp.bfloat16
+SHARE = 384
+
+
+def norm_parts(values):
+    center = values - jnp.mean(values, axis=-1, keepdims=True)
+    inverse = lax.rsqrt(jnp.mean(center * center, axis=-1, keepdims=True) + EPS)
+    return center * inverse, inverse
+
+
+def norm_back(unit, inverse, scales, grad):
+    scaled = grad * scales
+    back = inverse * (
+        scaled
+        - jnp.mean(scaled, axis=-1, keepdims=True)
+        - unit * jnp.mean(scaled * unit, axis=-1, keepdims=True)
+    )
+    return back, row_sum(grad * unit), row_sum(grad)
+
+
+def row_sum(values):
+    return jnp.sum(values, axis=0, keepdims=True)
+
+
+def gelu_both(values):
+    below = 0.5 + 0.5 * lax.erf(values * 0.7071067811865476)
+    bell = jnp.exp(-0.5 * values * values) * 0.3989422804014327
+    return values * below, below + values * bell
+
+
+def call(kernel, outs, scratch, args, name, flops, grid=None, in_specs=None, out_specs=None, limit=56):
+    size = sum(a.size * a.dtype.itemsize for a in args)
+    size += sum(o.size * o.dtype.itemsize for o in outs)
+    extra = {} if grid is None else {"grid": grid}
+    return pl.pallas_call(
+        kernel,
+        out_shape=tuple(outs),
+        in_specs=in_specs or [VMEM_WHOLE] * len(args),
+        out_specs=out_specs or (VMEM_WHOLE,) * len(outs),
+        scratch_shapes=scratch,
+        compiler_params=pltpu.CompilerParams(vmem_limit_bytes=limit << 20),
+        cost_estimate=pl.CostEstimate(flops=flops, bytes_accessed=size, transcendentals=0),
+        name=name,
+        **extra,
+    )(*args)
+
+
+def like(shape, dtype=jnp.float32):
+    return jax.ShapeDtypeStruct(shape, dtype)
+
+
+def store_groups(values_b, out_ref):
+    rows, width = values_b.shape
+    group_width = width // GROUPS
+    part = rows // CHUNKS
+    for group in range(GROUPS):
+        lanes = slice(group * group_width, (group + 1) * group_width)
+        out_ref[group] = jnp.concatenate(
+            [values_b[part * e : part * (e + 1), lanes] for e in range(CHUNKS)], axis=1
+        )
+
+
+def stem_kernel(
+    frames_ref, next_ref, same_ref, weight_ref, gain_ref, bias_ref, proj_ref, gains_ref, biases_ref,
+    start_ref, start_b_ref, groups_ref, pre_ref, normed_ref, follow_ref, table_ref,
+):
+    rows, chans = pre_ref.shape
+    table_ref[0:3] = gains_ref[...].T
+    table_ref[3:12] = biases_ref[...].T
+    moved = pltpu.roll(frames_ref[:, :chans].astype(jnp.float32), rows - 1, 0)
+    last = lax.broadcasted_iota(jnp.int32, (rows, 1), 0) == rows - 1
+    moved = jnp.where(last, next_ref[...].astype(jnp.float32), moved)
+    follow = jnp.where(same_ref[...] > 0.0, moved, 0.0).astype(BF)
+    follow_ref[...] = follow
+    pre = plain_dot(frames_ref[...], weight_ref[: 2 * chans]) + plain_dot(follow, weight_ref[2 * chans :])
+    pre_ref[...] = pre
+    unit, _ = norm_parts(gelu_both(pre)[0])
+    normed = (unit * gain_ref[...] + bias_ref[...]).astype(BF)
+    normed_ref[...] = normed
+    start = plain_dot(normed, proj_ref[...]) + table_ref[3:4]
+    start_ref[...] = start
+    start_b = start.astype(BF)
+    start_b_ref[...] = start_b
+    store_groups(start_b, groups_ref)
+
+
+def stem(frames, next_row, same_next, weight, gain, bias, proj, gains, biases):
+    rows = frames.shape[0]
+    chans, width = proj.shape
+    part = rows // CHUNKS
+    return call(
+        stem_kernel,
+        [
+            like((rows, width)), like((rows, width), BF),
+            like((GROUPS, part, CHUNKS * width // GROUPS), BF),
+            like((rows, chans)), like((rows, chans), BF), like((rows, chans), BF), like((12, width)),
+        ],
+        [],
+        (frames, next_row, same_next, weight, gain, bias, proj, gains, biases),
+        "stem",
+        6 * 10**9,
+    )
+
+
+def project_kernel(conv_ref, start_ref, table_ref, weight_ref, hidden_ref, packed_ref):
+    rows, width = start_ref.shape
+    half = rows // 2
+    mixed = start_ref[...] + gelu_both(conv_ref[...] + table_ref[4:5])[0]
+    unit, _ = norm_parts(mixed)
+    hidden = unit * table_ref[0:1] + table_ref[5:6]
+    hidden_ref[...] = hidden
+    hidden_b = hidden.astype(BF)
+    shifts = (table_ref[6:7], jnp.zeros((1, width), jnp.float32), table_ref[7:8])
+    parts = [
+        (plain_dot(hidden_b, weight_ref[:, at * width : (at + 1) * width]) + shift).astype(BF)
+        for at, shift in enumerate(shifts)
+    ]
+    heads = width // HEAD_DIM
+    for head in range(heads):
+        lanes = slice(head * HEAD_DIM, (head + 1) * HEAD_DIM)
+        packed_ref[head] = jnp.concatenate(
+            [part[:half, lanes] for part in parts] + [part[half:, lanes] for part in parts], axis=1
+        )
+    for head in range(heads, RING):
+        packed_ref[head] = jnp.zeros_like(packed_ref[head])
+
+
+def project_heads(conv_sum, start, table, weight):
+    rows, width = start.shape
+    return call(
+        project_kernel,
+        [like((rows, width)), like((RING, rows // 2, 6 * HEAD_DIM), BF)],
+        [],
+        (conv_sum, start, table, weight),
+        "project_heads",
+        6 * 10**9,
+    )
+
+
+def middle_kernel(
+    heads_ref, hidden_ref, table_ref, out_weight_ref, in_ref, in_bias_ref, back_ref, out_grad_ref,
+    layer_ref, grad_heads_ref, grad_second_ref, out_part_ref, sums_ref, in_bias_grad_ref, joined_ref,
+    attended, before, second, second_b, second_t, inner_b, slope, total, grad_last, grad_last_b,
+    joined, sems,
+):
+    step = pl.program_id(0)
+    rows, width = hidden_ref.shape
+    half = rows // 2
+    chunk = in_ref.shape[1]
+    chunks = pl.num_programs(0) // 2
+    heads = width // HEAD_DIM
+    shares = joined_ref.shape[0]
+    in_rows = width // shares
+    back_rows = chunk * chunks // shares
+    owners = chunk // back_rows
+
+    def in_copy(at):
+        place = (slice(None), pl.ds(pl.multiple_of(at * in_rows, 16), in_rows))
+        return pltpu.make_async_copy(joined.at[place], joined_ref.at[place], sems.at[0, at])
+
+    def back_copy(at):
+        place = (pl.ds(at * owners, owners), pl.ds(in_rows * chunks, joined_ref.shape[1] - in_rows * chunks))
+        return pltpu.make_async_copy(joined.at[place], joined_ref.at[place], sems.at[1, at])
+
+    @pl.when(step == 0)
+    def _():
+        for head in range(heads):
+            lanes = slice(head * HEAD_DIM, (head + 1) * HEAD_DIM)
+            attended[:half, lanes] = heads_ref[head, :, :HEAD_DIM]
+            attended[half:, lanes] = heads_ref[head, :, HEAD_DIM:]
+        value = hidden_ref[...] + plain_dot(attended[...], out_weight_ref[...]) + table_ref[8:9]
+        before[...] = value
+        unit, _ = norm_parts(value)
+        value = unit * table_ref[1:2] + table_ref[9:10]
+        second[...] = value
+        second_b[...] = value.astype(BF)
+        second_t[...] = value.T.astype(BF)
+        total[...] = jnp.zeros_like(total)
+
+    @pl.when(step < chunks)
+    def _():
+        at = pl.multiple_of(step * chunk, chunk)
+        value, back = gelu_both(plain_dot(second_b[...], in_ref[...]) + in_bias_ref[:, pl.ds(at, chunk)])
+        value_b = value.astype(BF)
+        inner_b[step] = value_b
+        slope[step] = back
+        total[...] += plain_dot(value_b, back_ref[...])
+
+    @pl.when(step == chunks - 1)
+    def _():
+        unit, inverse = norm_parts(second[...] + total[...] + table_ref[10:11])
+        layer_ref[...] = (unit * table_ref[2:3] + table_ref[11:12]).astype(BF)
+        back, gain, bias = norm_back(unit, inverse, table_ref[2:3], out_grad_ref[...].astype(jnp.float32))
+        grad_last[...] = back
+        grad_last_b[...] = back.astype(BF)
+        total[...] = back
+        sums_ref[0:1] = gain
+        sums_ref[1:2] = bias
+        sums_ref[2:3] = row_sum(back)
+
+    @pl.when(step >= chunks)
+    def _():
+        turn = step - chunks
+        at = pl.multiple_of(turn * chunk, chunk)
+        grad = row_dot(grad_last_b[...], back_ref[...]) * slope[turn]
+        in_bias_grad_ref[:, pl.ds(at, chunk)] = row_sum(grad)
+        grad_b = grad.astype(BF)
+        total[...] += row_dot(grad_b, in_ref[...])
+        product = plain_dot(second_t[...], grad_b).astype(BF)
+        for share in range(shares):
+            joined[share, pl.ds(pl.multiple_of(turn * in_rows, 16), in_rows), :] = product[
+                share * in_rows : (share + 1) * in_rows
+            ]
+        in_copy(turn).start()
+        product = over_rows_dot(inner_b[turn], grad_last_b[...]).astype(BF)
+        for owner in range(owners):
+            for place in range(width // SHARE):
+                begin = in_rows * chunks + place * back_rows
+                joined[turn * owners + owner, begin : begin + back_rows, :] = product[
+                    owner * back_rows : (owner + 1) * back_rows, place * SHARE : (place + 1) * SHARE
+                ]
+        back_copy(turn).start()
+
+    @pl.when(step == 2 * chunks - 1)
+    def _():
+        unit, inverse = norm_parts(before[...])
+        back, gain, bias = norm_back(unit, inverse, table_ref[1:2], total[...])
+        grad_second_ref[...] = back
+        sums_ref[3:4] = row_sum(back)
+        sums_ref[4:5] = gain
+        sums_ref[5:6] = bias
+        sums_ref[6:8] = jnp.zeros((2, width), jnp.float32)
+        back_b = back.astype(BF)
+        grads = row_dot(back_b, out_weight_ref[...]).astype(BF)
+        for head in range(heads):
+            lanes = slice(head * HEAD_DIM, (head + 1) * HEAD_DIM)
+            grad_heads_ref[head] = jnp.concatenate([grads[:half, lanes], grads[half:, lanes]], axis=1)
+        for head in range(heads, RING):
+            grad_heads_ref[head] = jnp.zeros_like(grad_heads_ref[head])
+        product = over_rows_dot(attended[...], back_b).astype(BF)
+        for share in range(shares):
+            for place in range(width // SHARE):
+                out_part_ref[share, place * in_rows : (place + 1) * in_rows, :] = product[
+                    share * in_rows : (share + 1) * in_rows, place * SHARE : (place + 1) * SHARE
+                ]
+
+        def finish(at, carry):
+            in_copy(at).wait()
+            back_copy(at).wait()
+            return carry
+
+        lax.fori_loop(0, chunks, finish, 0)
+
+
+def middle(heads, hidden, table, out_weight, ffn_in, in_bias, ffn_out, out_grad, count):
+    rows, width = hidden.shape
+    inner = ffn_in.shape[1]
+    chunk = SHARE
+    chunks = inner // chunk
+    own = lambda shape: pl.BlockSpec(shape, lambda step: (0,) * len(shape))
+    outs = [
+        like((rows, width), BF),
+        like((RING, rows // 2, 2 * HEAD_DIM), BF),
+        like((rows, width)),
+        like((count, width // count * width // SHARE, SHARE), BF),
+        like((8, width)),
+        like((1, inner)),
+        like((count, 2 * width // count * inner // SHARE, SHARE), BF),
+    ]
+    args = (heads, hidden, table, out_weight, ffn_in, in_bias, ffn_out, out_grad)
+    in_specs = [own(a.shape) for a in args]
+    in_specs[4] = pl.BlockSpec((width, chunk), lambda step: (0, step % chunks))
+    in_specs[6] = pl.BlockSpec((chunk, width), lambda step: (step % chunks, 0))
+    out_specs = [own(o.shape) for o in outs]
+    out_specs[6] = pl.BlockSpec(memory_space=pl.ANY)
+    scratch = [
+        pltpu.VMEM((rows, width), BF),
+        pltpu.VMEM((rows, width), jnp.float32),
+        pltpu.VMEM((rows, width), jnp.float32),
+        pltpu.VMEM((rows, width), BF),
+        pltpu.VMEM((width, rows), BF),
+        pltpu.VMEM((chunks, rows, chunk), BF),
+        pltpu.VMEM((chunks, rows, chunk), jnp.float32),
+        pltpu.VMEM((rows, width), jnp.float32),
+        pltpu.VMEM((rows, width), jnp.float32),
+        pltpu.VMEM((rows, width), BF),
+        pltpu.VMEM(outs[6].shape, BF),
+        pltpu.SemaphoreType.DMA((2, chunks)),
+    ]
+    return call(
+        middle_kernel, outs, scratch, args, "middle", 2 * 10**10, (2 * chunks,), in_specs, tuple(out_specs)
+    )
+
+
+def after_heads_kernel(
+    packed_ref, grad_second_ref, hidden_ref, conv_ref, start_ref, table_ref, weight_ref, out_part_ref,
+    mixed_ref, conv_b_ref, groups_ref, joined_ref, sums_ref, grads,
+):
+    rows, width = hidden_ref.shape
+    half = rows // 2
+    heads = width // HEAD_DIM
+    shares = joined_ref.shape[0]
+    own_rows = width // shares
+    for head in range(heads):
+        tile = packed_ref[head]
+        for part in range(3):
+            lanes = slice(part * width + head * HEAD_DIM, part * width + (head + 1) * HEAD_DIM)
+            grads[:half, lanes] = tile[:, part * HEAD_DIM : (part + 1) * HEAD_DIM]
+            grads[half:, lanes] = tile[:, (part + 3) * HEAD_DIM : (part + 4) * HEAD_DIM]
+    hidden_t = hidden_ref[...].T.astype(BF)
+    blocks = 3 * width // SHARE
+    for place in range(blocks):
+        lanes = slice(place * SHARE, (place + 1) * SHARE)
+        product = plain_dot(hidden_t, grads[:, lanes]).astype(BF)
+        for share in range(shares):
+            joined_ref[share, place * own_rows : (place + 1) * own_rows, :] = product[
+                share * own_rows : (share + 1) * own_rows
+            ]
+    for share in range(shares):
+        joined_ref[share, blocks * own_rows :, :] = out_part_ref[share]
+    back = grad_second_ref[...] + row_dot(grads[...], weight_ref[...])
+    value, slope = gelu_both(conv_ref[...] + table_ref[4:5])
+    unit, inverse = norm_parts(start_ref[...] + value)
+    mixed, gain, bias = norm_back(unit, inverse, table_ref[0:1], back)
+    mixed_ref[...] = mixed
+    conv = mixed * slope
+    conv_b = conv.astype(BF)
+    conv_b_ref[...] = conv_b
+    store_groups(conv_b, groups_ref)
+    sums_ref[0:1] = gain
+    sums_ref[1:2] = bias
+    sums_ref[2:3] = row_sum(conv)
+    sums_ref[3:4] = row_sum(grads[:, :width].astype(jnp.float32))
+    sums_ref[4:5] = row_sum(grads[:, 2 * width :].astype(jnp.float32))
+    sums_ref[5:8] = jnp.zeros((3, width), jnp.float32)
+
+
+def after_heads(packed, grad_second, hidden, conv_sum, start, table, weight, out_part):
+    rows, width = hidden.shape
+    shares = out_part.shape[0]
+    return call(
+        after_heads_kernel,
+        [
+            like((rows, width)), like((rows, width), BF),
+            like((GROUPS, rows // CHUNKS, CHUNKS * width // GROUPS), BF),
+            like((shares, out_part.shape[1] + width // shares * 3 * width // SHARE, SHARE), BF),
+            like((8, width)),
+        ],
+        [pltpu.VMEM((rows, 3 * width), BF)],
+        (packed, grad_second, hidden, conv_sum, start, table, weight, out_part),
+        "after_heads",
+        6 * 10**9,
+    )
+
+
+PIECE = 128
+
+
+def stem_back_kernel(
+    input_ref, mixed_ref, normed_ref, pre_ref, frames_ref, follow_ref, same_ref, weight_ref, gain_ref,
+    proj_ref, middle_sums_ref, inner_sums_ref, after_sums_ref,
+    samples_ref, carried_ref, joined_ref, table, spread, woven,
+):
+    rows, chans = pre_ref.shape
+    width = input_ref.shape[1]
+    shares = joined_ref.shape[0]
+    start = mixed_ref[...] + input_ref[...]
+    start_b = start.astype(BF)
+
+    def share_out(product, begin):
+        own, columns = product.shape[0] // shares, product.shape[1]
+        for share in range(shares):
+            for place in range(columns // PIECE):
+                at = begin + place * own
+                joined_ref[share, at : at + own, :] = product[
+                    share * own : (share + 1) * own, place * PIECE : (place + 1) * PIECE
+                ]
+        return begin + own * columns // PIECE
+
+    at = share_out(over_rows_dot(normed_ref[...], start_b).astype(BF), 0)
+    value, slope = gelu_both(pre_ref[...])
+    unit, inverse = norm_parts(value)
+    feature, gain_sum, bias_sum = norm_back(
+        unit, inverse, gain_ref[...], row_dot(start_b, proj_ref[...])
+    )
+    pre_b = (feature * slope).astype(BF)
+    taps_t = jnp.concatenate(
+        [
+            over_rows_dot(frames_ref[:, :chans], pre_b),
+            over_rows_dot(frames_ref[:, chans:], pre_b),
+            over_rows_dot(follow_ref[...], pre_b),
+        ],
+        axis=0,
+    ).astype(BF)
+    at = share_out(taps_t, at)
+    first = row_dot(pre_b, weight_ref[:chans])
+    follow = jnp.where(same_ref[...] > 0.0, row_dot(pre_b, weight_ref[2 * chans :]), 0.0)
+    carried_ref[...] = follow[rows - 1 :]
+    moved = pltpu.roll(follow, 1, 0)
+    top = lax.broadcasted_iota(jnp.int32, (rows, 1), 0) == 0
+    even = first + jnp.where(top, 0.0, moved)
+    odd = row_dot(pre_b, weight_ref[chans : 2 * chans])
+    for lane in range(0, chans, PIECE):
+        woven[pl.ds(0, rows, stride=2), :] = even[:, lane : lane + PIECE]
+        woven[pl.ds(1, rows, stride=2), :] = odd[:, lane : lane + PIECE]
+        samples_ref[:, lane : lane + PIECE] = woven[...]
+    table[0:1] = after_sums_ref[0:1]
+    table[1:2] = middle_sums_ref[4:5]
+    table[2:3] = middle_sums_ref[0:1]
+    table[3:4] = row_sum(start)
+    table[4:5] = after_sums_ref[2:3]
+    table[5:6] = after_sums_ref[1:2]
+    table[6:7] = after_sums_ref[3:4]
+    table[7:8] = after_sums_ref[4:5]
+    table[8:9] = middle_sums_ref[3:4]
+    table[9:10] = middle_sums_ref[5:6]
+    table[10:11] = middle_sums_ref[2:3]
+    table[11:12] = middle_sums_ref[1:2]
+    spread[...] = jnp.zeros_like(spread)
+    own, own_chans = width // shares, chans // shares
+    own_inner = inner_sums_ref.shape[1] // shares
+    for share in range(shares):
+        spread[share, 0:12, 0:own] = table[:, share * own : (share + 1) * own]
+        for place in range(-(-own_inner // PIECE)):
+            length = min(PIECE, own_inner - place * PIECE)
+            begin = share * own_inner + place * PIECE
+            spread[share, 12 + place : 13 + place, 0:length] = inner_sums_ref[:, begin : begin + length]
+        lanes = slice(share * own_chans, (share + 1) * own_chans)
+        spread[share, 14:15, 0:own_chans] = gain_sum[:, lanes]
+        spread[share, 15:16, 0:own_chans] = bias_sum[:, lanes]
+        joined_ref[share, at:, :] = spread[share].astype(BF)
+
+
+def stem_back(input_grad, mixed, normed, pre, frames, follow, same_next, weight, gain, proj, sums, shares):
+    rows, chans = pre.shape
+    width = input_grad.shape[1]
+    pieces = (chans // shares * width + 3 * chans // shares * chans) // PIECE + 16
+    return call(
+        stem_back_kernel,
+        [like((2 * rows, chans)), like((1, chans)), like((shares, pieces, PIECE), BF)],
+        [pltpu.VMEM((12, width), jnp.float32), pltpu.VMEM((shares, 16, PIECE), jnp.float32),
+         pltpu.VMEM((2 * rows, PIECE), jnp.float32)],
+        (input_grad, mixed, normed, pre, frames, follow, same_next, weight, gain, proj) + sums,
+        "stem_back",
+        6 * 10**9,
+    )
+
 
 def from_behind(value, axis, steps):
     count = lax.axis_size(axis)
@@ -422,16 +879,6 @@
     before = from_behind(value[length - width :], "seq", 1)
     after = from_behind(value[:width], "seq", -1)
     return jnp.concatenate([before, value, after], axis=0)
-
-
-def norm_rows(values, scales, shifts):
-    center = values - jnp.mean(values, axis=-1, keepdims=True)
-    spread = jnp.mean(center * center, axis=-1, keepdims=True)
-    return center * lax.rsqrt(spread + 1e-05) * scales + shifts
-
-
-def gelu_exact(values):
-    return jax.nn.gelu(values, approximate=False)
 
 
 def clip_span(ends, begin, count, total):
@@ -471,69 +918,58 @@
     return wide.astype(value.dtype)
 
 
-def pack_halves(parts):
-    frames, heads, _ = parts[0].shape
-    joined = jnp.concatenate(parts, axis=2)
-    lanes = joined.shape[2]
-    moved = joined.reshape(2, frames // 2, heads, lanes).transpose(2, 1, 0, 3)
-    moved = moved.reshape(heads, frames // 2, 2 * lanes)
-    return jnp.pad(moved, ((0, RING - heads), (0, 0), (0, 0)))
-
-
-def unpack_halves(packed, heads, count):
-    half = packed.shape[1]
-    lanes = packed.shape[2] // (2 * count)
-    parts = packed[:heads].reshape(heads, half, 2, count, lanes).transpose(2, 1, 3, 0, 4)
-    return parts.reshape(2 * half, count * heads * lanes)
-
-
-def pack_groups(value):
-    frames, width = value.shape
-    group_width = width // GROUPS
-    moved = value.reshape(CHUNKS, frames // CHUNKS, GROUPS, group_width).transpose(2, 1, 0, 3)
-    return moved.reshape(GROUPS, frames // CHUNKS, CHUNKS * group_width)
-
-
-LANES = 256
-
-
-def flat_share(grad, count):
-    rows, columns = grad.shape
-    share = grad.astype(jnp.bfloat16).reshape(count, rows // count, columns)
-    return [share[:, :, at : at + LANES] for at in range(0, columns, LANES)]
-
-
-def reduce_shares(grads, extra=None):
-    count = lax.axis_size("seq")
-    pieces, sizes = [], []
-    for grad in grads:
-        pieces += flat_share(grad, count)
-        sizes.append((grad.shape[0] // count, grad.shape[1]))
-    if extra is not None:
-        pieces.append(extra.astype(jnp.bfloat16))
-    share = lax.psum_scatter(
-        jnp.concatenate(pieces, axis=1), "seq", scatter_dimension=0, tiled=False
-    ).astype(jnp.bfloat16)
-    total = sum_pair(share)
+def sum_pair(share):
+    count = lax.axis_size("rep")
+    if count == 2:
+        other = lax.ppermute(share, "rep", [(0, 1), (1, 0)])
+        return share.astype(jnp.float32) + other.astype(jnp.float32)
+    return lax.psum(share, "rep").astype(jnp.float32)
+
+
+def spread_out(total, sizes, lanes):
     out, at = [], 0
     for rows, columns in sizes:
         parts = []
-        for _ in range(columns // LANES):
+        for _ in range(columns // lanes):
             parts.append(total[at : at + rows])
             at += rows
         out.append(jnp.concatenate(parts, axis=1))
-    if extra is not None:
-        out.append(total[at:])
     return out
 
 
-def sum_pair(share):
-    count = lax.axis_size("rep")
-    total = share.astype(jnp.float32)
-    if count == 2:
-        other = lax.ppermute(share, "rep", [(0, 1), (1, 0)])
-        return total + other.astype(jnp.float32)
-    return lax.psum(share, "rep").astype(jnp.float32)
+def regroup(joined, blocks):
+    count = lax.axis_size("seq")
+    if count == RING:
+        return joined
+    parts = count // RING
+    lanes = joined.shape[2]
+    out, at = [], 0
+    for number, rows in blocks:
+        piece = joined[:, at : at + number * rows]
+        at += number * rows
+        piece = piece.reshape(RING, number, parts, rows // parts, lanes).transpose(0, 2, 1, 3, 4)
+        out.append(piece.reshape(count, number * rows // parts, lanes))
+    return jnp.concatenate(out, axis=1)
+
+
+def regroup_small(small, widths):
+    count = lax.axis_size("seq")
+    if count == RING:
+        return small
+    parts = count // RING
+    own, own_inner, own_chans = widths
+    lanes = small.shape[2]
+    table = small[:, :12, : own * parts].reshape(RING, 12, parts, own).transpose(0, 2, 1, 3)
+    table = jnp.pad(table.reshape(count, 12, own), ((0, 0), (0, 0), (0, lanes - own)))
+    wide = small[:, 12:14].reshape(RING, 2 * lanes)[:, : own_inner * parts].reshape(count, own_inner)
+    wide = jnp.pad(wide, ((0, 0), (0, 2 * lanes - own_inner))).reshape(count, 2, lanes)
+    stems = small[:, 14:16, : own_chans * parts].reshape(RING, 2, parts, own_chans).transpose(0, 2, 1, 3)
+    stems = jnp.pad(stems.reshape(count, 2, own_chans), ((0, 0), (0, 0), (0, lanes - own_chans)))
+    return jnp.concatenate([table, wide, stems], axis=1)
+
+
+def over_seq(joined):
+    return lax.psum_scatter(joined, "seq", scatter_dimension=0, tiled=False).astype(jnp.bfloat16)
 
 
 def local(
@@ -556,6 +992,7 @@
     rows_dev = out_grad.shape[1]
     width = attn_out.shape[0]
     chans = stem_weight.shape[1]
+    inner = ffn_in.shape[1]
     group_width = width // GROUPS
     count = lax.axis_size("seq")
     place = lax.axis_index("seq")
@@ -563,32 +1000,23 @@
     begin = place * rows_dev
     ends = jnp.cumsum(clip_lengths[0])
     clips = ends.shape[0]
-    own_ids = clip_span(ends, begin, rows_dev, total)
     half = KERNEL // 2
+    padded_ids = clip_span(ends, begin - half, rows_dev + 2 * half, total)
+    own_ids = padded_ids[half : half + rows_dev]
+    same_next = (padded_ids[half + 1 : half + 1 + rows_dev] == own_ids).astype(jnp.float32)[:, None]
     frames = samples[0].reshape(rows_dev, 2 * chans)
-    next_row = from_behind(frames[:1, :chans], "seq", -1)
-    same_next = clip_span(ends, begin + 1, rows_dev, total) == own_ids
-    following = jnp.concatenate([frames[1:, :chans], next_row], axis=0)
-    following = jnp.where(same_next[:, None], following, jnp.zeros_like(following))
-    unfold = jnp.concatenate([frames, following], axis=1)
-    stem_pre = plain_dot(unfold, stem_weight)
-    feature = gelu_exact(stem_pre)
-    normed_b = norm_rows(feature, stem_gain, stem_bias).astype(jnp.bfloat16)
-    start_x = plain_dot(normed_b, proj_weight) + biases[:, 0]
-    start_b = start_x.astype(jnp.bfloat16)
+    next_row = from_behind(samples[0, :1], "seq", -1)
+    fore_weights = conv_weights(False, pos_weight)
+    next_row, fore_weights = lax.optimization_barrier((next_row, fore_weights))
+    start_x, start_b, start_packed, stem_pre, normed_b, follow, table = stem(
+        frames, next_row, same_next, stem_weight, stem_gain[None], stem_bias[None], proj_weight,
+        norm_gains, biases,
+    )
     padded = padded_2(start_b, half)
-    padded_ids = clip_span(ends, begin - half, rows_dev + 2 * half, total)
-    padded_ids = padded_ids.astype(jnp.float32)[:, None]
-    start_groups = swap(pack_groups(start_b))
-    conv_out = conv_rows(False, padded, padded_ids, pos_weight) + biases[:, 1]
-    mixed = start_x + gelu_exact(conv_out)
-    hidden = norm_rows(mixed, norm_gains[:, 0], biases[:, 2])
-    hidden_b = hidden.astype(jnp.bfloat16)
-    project = plain_dot(hidden_b, attn_in)
-    query_b = (project[:, :width] + biases[:, 3]).astype(jnp.bfloat16)
-    keys_b = project[:, width : 2 * width].astype(jnp.bfloat16)
-    values_b = (project[:, 2 * width :] + biases[:, 4]).astype(jnp.bfloat16)
-    by_head = [piece.reshape(rows_dev, HEADS, HEAD_DIM) for piece in (query_b, keys_b, values_b)]
+    start_groups = swap(start_packed)
+    conv_sum = conv_rows(False, padded, padded_ids[None], fore_weights, clips)
+    conv_sum, start_groups = lax.optimization_barrier((conv_sum, start_groups))
+    hidden, packed = project_heads(conv_sum, start_x, table, attn_in)
 
     segment = RING * rows_dev
     far = 0 if count == RING else -(-MAXLEN // rows_dev)
@@ -603,50 +1031,39 @@
     low = (low - key_begin) // K_TILE
     high = (high - key_begin + (K_TILE - 1)) // K_TILE
     high = jnp.where(place % RING < HEADS, high, low)
-    packed = with_far_blocks(swap(pack_halves(by_head)), far)
+    packed = with_far_blocks(swap(packed), far)
+    back_weights = conv_weights(True, pos_weight)
+    packed, back_weights = lax.optimization_barrier((packed, back_weights))
     attended_heads, wide, log_total = attend(
         low, high, packed, query_ids[:, None], key_ids[None, :], far
     )
-    attended_b = unpack_halves(swap(attended_heads), HEADS, 1)
-    pre_second = hidden + plain_dot(attended_b, attn_out) + biases[:, 5]
-    second = norm_rows(pre_second, norm_gains[:, 1], biases[:, 6])
-    second_b = second.astype(jnp.bfloat16)
-    inner = plain_dot(second_b, ffn_in) + ffn_in_bias
-    inner_b = gelu_exact(inner).astype(jnp.bfloat16)
-    pre_last = second + plain_dot(inner_b, ffn_out) + biases[:, 7]
-    layer_out = norm_rows(pre_last, norm_gains[:, 2], biases[:, 8]).astype(jnp.bfloat16)[None]
-    grad_last, gain_grad_c, bias_grad_c = jax.vjp(
-        norm_rows, pre_last, norm_gains[:, 2], biases[:, 8]
-    )[1](out_grad[0].astype(jnp.float32))
-    grad_last_b = grad_last.astype(jnp.bfloat16)
-    grad_ffn_out = over_rows_dot(inner_b, grad_last_b)
-    grad_inner = jax.vjp(gelu_exact, inner)[1](row_dot(grad_last_b, ffn_out))[0]
-    grad_inner_b = grad_inner.astype(jnp.bfloat16)
-    grad_ffn_in = over_rows_dot(second_b, grad_inner_b)
-    ffn_grads = reduce_shares([grad_ffn_in, grad_ffn_out])
-    grad_second = grad_last + row_dot(grad_inner_b, ffn_in)
-    grad_pre_second, gain_grad_b, bias_grad_b = jax.vjp(
-        norm_rows, pre_second, norm_gains[:, 1], biases[:, 6]
-    )[1](grad_second)
-    grad_branch_b = grad_pre_second.astype(jnp.bfloat16)
-    grad_attn_out = over_rows_dot(attended_b, grad_branch_b)
-    grad_out = row_dot(grad_branch_b, attn_out).astype(jnp.bfloat16)
-    grad_heads = swap(pack_halves([grad_out.reshape(rows_dev, HEADS, HEAD_DIM)]))
+    layer_out, grad_heads, grad_pre_second, out_part, middle_sums, inner_sums, ffn_joined = middle(
+        swap(attended_heads), hidden, table, attn_out, ffn_in, ffn_in_bias[None], ffn_out, out_grad[0],
+        RING,
+    )
+    near_rows, near_chans, near_inner = width // RING, chans // RING, inner // RING
+    grad_heads = swap(grad_heads)
+    ffn_share = over_seq(
+        regroup(ffn_joined, [(inner // SHARE, near_rows), (width // SHARE, near_inner)])
+    )
     packed_grad = attend_back(
         low, high, packed, grad_heads, wide, log_total, query_ids[:, None], key_ids[None, :], far
     )
-    grad_project_b = unpack_halves(swap(fold_far_blocks(packed_grad, far)), HEADS, 3)
-    grad_attn_in = over_rows_dot(hidden_b, grad_project_b)
-    attn_grads = reduce_shares([grad_attn_in, grad_attn_out])
-    grad_hidden = grad_pre_second + row_dot(grad_project_b, attn_in)
-    grad_mixed, gain_grad_a, bias_grad_a = jax.vjp(
-        norm_rows, mixed, norm_gains[:, 0], biases[:, 2]
-    )[1](grad_hidden)
-    grad_conv = jax.vjp(gelu_exact, conv_out)[1](grad_mixed)[0]
-    grad_conv_b = grad_conv.astype(jnp.bfloat16)
+    grad_mixed, grad_conv_b, grad_packed, attn_joined, after_sums = after_heads(
+        swap(fold_far_blocks(packed_grad, far)), grad_pre_second, hidden, conv_sum, start_x, table,
+        attn_in, out_part,
+    )
     padded_grad = padded_2(grad_conv_b, half)
-    grad_groups = swap(pack_groups(grad_conv_b))
-    input_grad = conv_rows(True, padded_grad, padded_ids, pos_weight)
+    grad_groups = swap(grad_packed)
+    input_grad = conv_rows(True, padded_grad, padded_ids[None], back_weights, clips)
+    input_grad, grad_groups, ffn_share = lax.optimization_barrier((input_grad, grad_groups, ffn_share))
+    attn_share = over_seq(regroup(attn_joined, [(4 * width // SHARE, near_rows)]))
+    sample_grad, carried, stem_joined = stem_back(
+        input_grad, grad_mixed, normed_b, stem_pre, frames, follow, same_next, stem_weight,
+        stem_gain[None], proj_weight, (middle_sums, inner_sums, after_sums), RING,
+    )
+    carried = from_behind(carried, "seq", 1)
+    stem_joined, grad_groups = lax.optimization_barrier((stem_joined, grad_groups))
 
     near = 0 if count == RING else 1
     first_clip = query_ids[0]
@@ -675,78 +1092,47 @@
     pos_total = sum_pair(pos_pieces).reshape(GROUPS, group_width, own_taps, group_width)
     pos_grad = pos_total.transpose(2, 1, 0, 3).reshape(own_taps * group_width, width)
 
-    grad_start = grad_mixed + input_grad
-    grad_start_b = grad_start.astype(jnp.bfloat16)
-    grad_proj = over_rows_dot(normed_b, grad_start_b)
-    grad_feature, stem_gain_grad, stem_bias_grad = jax.vjp(
-        norm_rows, feature, stem_gain, stem_bias
-    )[1](row_dot(grad_start_b, proj_weight))
-    grad_pre_b = jax.vjp(gelu_exact, stem_pre)[1](grad_feature)[0].astype(jnp.bfloat16)
-    grad_stem = over_rows_dot(unfold, grad_pre_b)
-    grad_unfold = row_dot(grad_pre_b, stem_weight)
-    grad_follow = jnp.where(same_next[:, None], grad_unfold[:, 2 * chans :], 0.0)
-    carried = from_behind(grad_follow[-1:], "seq", 1)
-    shifted_back = jnp.concatenate([carried, grad_follow[:-1]], axis=0)
-    grad_frames = grad_unfold[:, : 2 * chans] + jnp.concatenate(
-        [shifted_back, jnp.zeros((rows_dev, chans), jnp.float32)], axis=1
-    )
-    sample_grad = grad_frames.reshape(1, 2 * rows_dev, chans)
-
-    gains_grad = jnp.stack([gain_grad_a, gain_grad_b, gain_grad_c], axis=0)
-    project_sums = jnp.sum(grad_project_b.astype(jnp.float32), axis=0)
-    bias_table = jnp.stack(
-        [
-            jnp.sum(grad_start, axis=0),
-            jnp.sum(grad_conv, axis=0),
-            bias_grad_a,
-            project_sums[:width],
-            project_sums[2 * width :],
-            jnp.sum(grad_pre_second, axis=0),
-            bias_grad_b,
-            jnp.sum(grad_last, axis=0),
-            bias_grad_c,
-        ],
-        axis=0,
-    )
-    inner_bias_grad = jnp.sum(grad_inner, axis=0)
-    small = jnp.concatenate(
-        [
-            jnp.concatenate([gains_grad, bias_table], axis=0)
-            .reshape(12, count, width // count)
-            .transpose(1, 0, 2)
-            .reshape(count, -1),
-            inner_bias_grad.reshape(count, -1),
-            stem_gain_grad.reshape(count, -1),
-            stem_bias_grad.reshape(count, -1),
-        ],
-        axis=1,
-    )
-    length = small.shape[1]
-    small = jnp.pad(small, ((0, 0), (0, -length % LANES))).reshape(count, -1, LANES)
-    grad_proj_sum, grad_stem_sum, small_sum = reduce_shares([grad_proj, grad_stem], small)
-    flat = small_sum.reshape(-1)
     own = width // count
-    table = flat[: 12 * own].reshape(12, own)
-    at = 12 * own
-    own_inner = inner_bias_grad.shape[0] // count
     own_chans = chans // count
-    inner_sum = flat[at : at + own_inner]
-    at += own_inner
+    if count != RING:
+        stem_joined = jnp.concatenate(
+            [
+                regroup(
+                    stem_joined[:, :-16],
+                    [(width // PIECE, near_chans), (chans // PIECE, 3 * near_chans)],
+                ),
+                regroup_small(stem_joined[:, -16:], (own, inner // count, own_chans)),
+            ],
+            axis=1,
+        )
+    received = lax.all_to_all(stem_joined, "seq", 0, 0)
+    stem_total = sum_pair(jnp.sum(received.astype(jnp.float32), axis=0).astype(jnp.bfloat16))
+    grad_proj, grad_stem = spread_out(
+        stem_total[:-16], [(own_chans, width), (3 * own_chans, chans)], PIECE
+    )
+    small = stem_total[-16:]
+    grad_ffn_in, grad_ffn_out = spread_out(
+        sum_pair(ffn_share), [(own, inner), (inner // count, width)], SHARE
+    )
+    grad_attn_in, grad_attn_out = spread_out(
+        sum_pair(attn_share), [(own, 3 * width), (own, width)], SHARE
+    )
+    sample_grad = sample_grad.at[:1].add(carried)
     return (
-        layer_out,
-        sample_grad,
-        grad_stem_sum,
-        flat[at : at + own_chans],
-        flat[at + own_chans : at + 2 * own_chans],
-        grad_proj_sum,
+        layer_out[None],
+        sample_grad[None],
+        grad_stem,
+        small[14, :own_chans],
+        small[15, :own_chans],
+        grad_proj,
         pos_grad,
-        table[:3].T,
-        table[3:].T,
-        attn_grads[0],
-        attn_grads[1],
-        ffn_grads[0],
-        inner_sum,
-        ffn_grads[1],
+        small[:3, :own].T,
+        small[3:12, :own].T,
+        grad_attn_in,
+        grad_attn_out,
+        grad_ffn_in,
+        small[12:14].reshape(-1)[: inner // count],
+        grad_ffn_out,
     )
 
 

time: 793 us -> 515 us (0.65)
  local copies, waits for them, and re-layouts: 143 us -> 32.9 us
  waiting for transfers between devices: 179 us -> 102 us
  matrix products: 39.5 us -> 0 us
  other arithmetic: 44.7 us -> 15.5 us
  Pallas kernels: 230 us -> 203 us
  starting transfers between devices: 34.6 us -> 47.5 us
    reduce_scatter x3 -> x2, waiting for transfers between devices: 96.9 us -> 20.4 us  [over_seq(): lax.psum_scatter(joined, 'seq', scatter_dimension=0, tiled=False)]
    ppermute x6, waiting for transfers between devices: 8.2 us -> 61.9 us  [from_behind(): lax.ppermute(value, axis, [(source, source + steps) for source in range(i...]
    dot_general x18 -> x0, matrix products: 39.5 us -> none  [the longest x6 19.4 us: plain_dot(): lax.dot_general(left, right, (((1,), (0,)), ((), ())), preferred_element_...]
    all_to_all x3 -> x4, waiting for transfers between devices: 53.9 us -> 15 us  [swap(): return lax.all_to_all(value, 'seq', 0, 0, axis_index_groups=groups)]
    unnamed x232 -> x45, local copies, waits for them, and re-layouts: 46.8 us -> 11.6 us
    pallas_call x2 -> x9, Pallas kernels: 138 us -> 114 us  [the longest x5 51.1 us: call(): pl.pallas_call(kernel, out_shape=tuple(outs), in_specs=in_specs or [VMEM_...]
    concatenate x20 -> x2, local copies, waits for them, and re-layouts: 22.5 us -> 0.64 us  [spread_out(): out.append(jnp.concatenate(parts, axis=1))]
    slice x22 -> x3, local copies, waits for them, and re-layouts: 19.3 us -> 0.07 us  [spread_out(): parts.append(total[at:at + rows])]
  transfers between devices with their start and end apart: 16 -> 17, of which waited for: 10 -> 7; matrix products, arithmetic and copies ran while one was open for 13% -> 8% of each run, Pallas kernels for 3% -> 28%
where the time goes in v2:
time: 515 us; the launch traced here: 507 us
  Pallas kernels  203 us (39%)
  waiting for transfers between devices  102 us (20%)
  blocking collectives  88.7 us (17%)
  starting transfers between devices  47.5 us (9%)
  local copies, waits for them, and re-layouts  32.9 us (6%)
  between operations  16.6 us (3%)
  other arithmetic  15.5 us (3%)
    all_to_all x3, blocking collectives, swap(): return lax.all_to_all(value, 'seq', 0, 0, axis_index_groups=groups)  88.7 us
    ppermute x6, waiting for transfers between devices, from_behind(): lax.ppermute(value, axis, [(source, source + steps) for source in range(i...  61.9 us
    pallas_call x5, Pallas kernels, call(): pl.pallas_call(kernel, out_shape=tuple(outs), in_specs=in_specs or [VMEM_...  51.1 us
    pallas_call x2, Pallas kernels, conv_rows(): pl.pallas_call(functools.partial(conv_kernel, back), grid=(GROUPS,), out_...  39.9 us
    pallas_call x1, Pallas kernels, attend_back(): pl.pallas_call(functools.partial(attend_back_kernel, halo), out_shape=jax...  35.8 us
    pallas_call x1, Pallas kernels, taps_grad(): pl.pallas_call(functools.partial(taps_grad_kernel, clips, halo), out_shap...  27.3 us
    pallas_call x1, Pallas kernels, attend(): pl.pallas_call(functools.partial(attend_kernel, halo), out_shape=(jax.Sha...  26.3 us
    pallas_call x2, Pallas kernels, conv_weights(): pl.pallas_call(functools.partial(conv_weights_kernel, back), grid=(turns,...  23.1 us
  transfers between devices with their start and end apart: 17, of which 7 were waited for; matrix products, arithmetic and copies ran while one was open for 8% of the time, Pallas kernels for 28%

profile of v2, /device:TPU:16, one launch (start us, length us, event | category | flops | bytes accessed | tf_op | source)
XLA Modules:
  0.0 506.8 jit_solution(11982908982331965196)
XLA Ops:
  17.0 10.6 %conv_weights.1.weight_ref = bf16[16,384,768]{2,1,0:T(8,128)(2,1)} custom-call(bf16[6144,768]{1,0:T(8,128)(2,1)} %weight_ref.9), custom_call_target="tpu_custom_call" | custom-call | bytes 18874368 | tf_op jit(solution)/shard_map/conv_weights/pallas_call | solution.py:234
  28.2 4.7 stem.1
  32.9 5.5 %all-to-all-start = ((bf16[16,32,384]{2,1,0:T(8,128)(2,1)}), bf16[16,32,384]{2,1,0:T(8,128)(2,1)S(1)}, u32[]{:S(2)}, u32[]{:S(2)}) async-start(bf16[16,32,384]{2,1,0:T(8,128)(2,1)} %get-tuple-element.67), calls=%async_computation | async-start | bytes 786432 | tf_op jit(solution)/shard_map/all_to_all | solution.py:898
  45.8 4.7 collective-permute-done.1
  51.5 17.9 %conv.1.conv_ref = f32[256,768]{1,0:T(8,128)S(1)} custom-call(bf16[384,768]{1,0:T(8,128)(2,1)S(1)} %pad_maximum_fusion.rows_ref, s32[1,384]{1,0:T(1,128)S(1)} %and_select_fusion.1.ids_ref, bf16[16,384,768]{2,1,0:T(8,128)(2,1)} %conv_weights.1.weight_ref), custom_call_target="tpu_custom_call" | custom-call | flops 4831838208 | bytes 9437184 | tf_op jit(solution)/shard_map/conv/pallas_call | solution.py:312
  70.3 5.3 %project_heads.1 = (f32[256,768]{1,0:T(8,128)}, bf16[16,128,384]{2,1,0:T(8,128)(2,1)}) custom-call(f32[256,768]{1,0:T(8,128)} %copy-done, f32[256,768]{1,0:T(8,128)} %get-tuple-element.69.start_ref, f32[12,768]{1,0:T(8,128)} %get-tuple-element.70.table_ref, bf16[768,2304]{1,0:T(8,128)(2,1)} %weight_ref.10), custom_call_target="tpu_custom_call" | custom-call | flops 6000000000 | bytes 7507968 | tf_op jit(solution)/shard_map/project_heads/pallas_call | solution.py:457
  79.8 12.5 %conv_weights_back.1.weight_ref = bf16[16,384,768]{2,1,0:T(8,128)(2,1)} custom-call(bf16[6144,768]{1,0:T(8,128)(2,1)} %weight_ref.9), custom_call_target="tpu_custom_call" | custom-call | bytes 18874368 | tf_op jit(solution)/shard_map/conv_weights_back/pallas_call | solution.py:234
  102.8 13.4 %all-to-all-done.1.packed_ref = bf16[16,128,384]{2,1,0:T(8,128)(2,1)S(1)} async-done(((bf16[16,128,384]{2,1,0:T(8,128)(2,1)}), bf16[16,128,384]{2,1,0:T(8,128)(2,1)S(1)}, u32[]{:S(2)}, u32[]{:S(2)}) %all-to-all-start.1) | async-done | bytes 1572896 | tf_op jit(solution)/shard_map/all_to_all | solution.py:898
  117.4 26.3 %attend.1 = (bf16[16,128,128]{2,1,0:T(8,128)(2,1)}, f32[4096,64]{1,0:T(8,128)}, f32[4096,1]{1,0:T(8,128)}) custom-call(s32[8]{0:T(128)} %get-tuple-element.107.low_ref, s32[8]{0:T(128)} %get-tuple-element.106.high_ref, bf16[16,128,384]{2,1,0:T(8,128)(2,1)} %copy-done.2, s32[4096,1]{1,0:T(8,128)} %get-tuple-element.105.query_ids_ref, ...), custom_call_target="tpu_custom_call" | custom-call | tf_op jit(solution)/shard_map/attend/pallas_call | solution.py:112
  143.7 18.7 %all_to_all.40.heads_ref = bf16[16,128,128]{2,1,0:T(8,128)(2,1)} all-to-all(bf16[16,128,128]{2,1,0:T(8,128)(2,1)} %get-tuple-element.73), channel_id=1, replica_groups=mesh['rep'=2,'seq'=16] {'seq'}, dimensions={0} | all-to-all | bytes 1048576 | tf_op jit(solution)/shard_map/all_to_all | solution.py:898
  162.4 25.3 %middle.1 = (bf16[256,768]{1,0:T(8,128)(2,1)}, bf16[16,128,128]{2,1,0:T(8,128)(2,1)}, f32[256,768]{1,0:T(8,128)}, bf16[16,96,384]{2,1,0:T(8,128)(2,1)}, f32[8,76...) custom-call(bf16[16,128,128]{2,1,0:T(8,128)(2,1)} %all_to_all.40.heads_ref, ...), custom_call_target="tpu_custom_call" | custom-call | flops 20000000000 | bytes 24727552 | tf_op jit(solution)/shard_map/middle/pallas_call | solution.py:457
  188.7 18.5 %all_to_all.41.grad_ref = bf16[16,128,128]{2,1,0:T(8,128)(2,1)} all-to-all(bf16[16,128,128]{2,1,0:T(8,128)(2,1)S(1)} %copy-done.6), channel_id=1, replica_groups=mesh['rep'=2,'seq'=16] {'seq'}, dimensions={0} | all-to-all | bytes 1048576 | tf_op jit(solution)/shard_map/all_to_all | solution.py:898
  207.2 35.8 %attend_back.1 = bf16[16,128,384]{2,1,0:T(8,128)(2,1)} custom-call(s32[8]{0:T(128)} %get-tuple-element.107.low_ref, s32[8]{0:T(128)} %get-tuple-element.106.high_ref, bf16[16,128,384]{2,1,0:T(8,128)(2,1)} %copy-done.2, bf16[16,128,128]{2,1,0:T(8,128)(2,1)} %all_to_all.41.grad_ref, f32[4096,64]{1,0:T(8,128)} %get-tuple-element.77.wide_ref, ...), custom_call_target="tpu_custom_call" | custom-call | tf_op jit(solution)/shard_map/attend_back/pallas_call | solution.py:199
  242.9 51.6 %all_to_all.42.packed_ref = bf16[16,128,384]{2,1,0:T(8,128)(2,1)} all-to-all(bf16[16,128,384]{2,1,0:T(8,128)(2,1)} %attend_back.1), channel_id=1, replica_groups=mesh['rep'=2,'seq'=16] {'seq'}, dimensions={0} | all-to-all | bytes 3145728 | tf_op jit(solution)/shard_map/all_to_all | solution.py:898
  294.6 9.8 %after_heads.1 = (f32[256,768]{1,0:T(8,128)}, bf16[256,768]{1,0:T(8,128)(2,1)}, bf16[16,32,384]{2,1,0:T(8,128)(2,1)}, bf16[16,384,384]{2,1,0:T(8,128)(2,1)}, f32[8,768]{1,0:T(8,128)}) custom-call(bf16[16,128,384]{2,1,0:T(8,128)(2,1)} %all_to_all.42.packed_ref, f32[256,768]{1,0:T(8,128)} %get-tuple-element.79.grad_second_ref, ...), custom_call_target="tpu_custom_call" | custom-call | flops 6000000000 | bytes 15790080 | tf_op jit(solution)/shard_map/after_heads/pallas_call | solution.py:457
  304.4 5.3 %all-to-all-start.5 = ((bf16[16,32,384]{2,1,0:T(8,128)(2,1)}), bf16[16,32,384]{2,1,0:T(8,128)(2,1)S(1)}, u32[]{:S(2)}, u32[]{:S(2)}) async-start(bf16[16,32,384]{2,1,0:T(8,128)(2,1)} %get-tuple-element.83), calls=%async_computation.5 | async-start | bytes 786432 | tf_op jit(solution)/shard_map/all_to_all | solution.py:898
  316.2 8.2 %collective-permute-done.3 = bf16[64,768]{1,0:T(8,128)(2,1)S(1)} collective-permute-done((bf16[64,768]{1,0:T(8,128)(2,1)S(1)}, bf16[64,768]{1,0:T(8,128)(2,1)S(1)}, u32[]{:S(2)}, u32[]{:S(2)}) %collective-permute-start.3) | collective-permute-done | bytes 98336 | tf_op jit(solution)/shard_map/ppermute | solution.py:874
  324.5 22.0 %conv_back.1.input_ref = f32[256,768]{1,0:T(8,128)S(1)} custom-call(bf16[384,768]{1,0:T(8,128)(2,1)S(1)} %pad_maximum_fusion.1.rows_ref, s32[1,384]{1,0:T(1,128)S(1)} %and_select_fusion.1.ids_ref, bf16[16,384,768]{2,1,0:T(8,128)(2,1)} %conv_weights_back.1.weight_ref), custom_call_target="tpu_custom_call" | custom-call | flops 4831838208 | bytes 9437184 | tf_op jit(solution)/shard_map/conv_back/pallas_call | solution.py:312
  347.4 6.1 %stem_back.1 = (f32[512,512]{1,0:T(8,128)}, f32[1,512]{1,0:T(1,128)}, bf16[16,592,128]{2,1,0:T(8,128)(2,1)}) custom-call(f32[256,768]{1,0:T(8,128)} %copy-done.1, f32[256,768]{1,0:T(8,128)} %get-tuple-element.86.mixed_ref, bf16[256,512]{1,0:T(8,128)(2,1)} %get-tuple-element.87.normed_ref, f32[256,512]{1,0:T(8,128)} %get-tuple-element.88.pre_ref, ...), custom_call_target="tpu_custom_call" | custom-call | flops 6000000000 | bytes 9044992 | tf_op jit(solution)/shard_map/stem_back/pallas_call | solution.py:457
  353.5 27.3 %taps_grad.1 = bf16[16,48,384]{2,1,0:T(8,128)(2,1)} custom-call(bf16[16,32,384]{2,1,0:T(8,128)(2,1)} %copy-done.3, bf16[16,32,384]{2,1,0:T(8,128)(2,1)} %copy-done.4, f32[4096,1]{1,0:T(8,128)} %get-tuple-element.104.input_ids_ref.grad_ids_ref, f32[4096,1]{1,0:T(8,128)} %get-tuple-element.104.input_ids_ref.grad_ids_ref), custom_call_target="tpu_custom_call" | custom-call | tf_op jit(solution)/shard_map/taps_grad/pallas_call | solution.py:405
  385.0 20.4 %reduce-scatter.5.cloned.1.call-done = bf16[1,384,384]{2,1,0:T(8,128)(2,1)} async-done(((bf16[16,384,384]{2,1,0:T(8,128)(2,1)}), bf16[1,384,384]{2,1,0:T(8,128)(2,1)}) %reduce-scatter.5.cloned.1.call-update) | async-done | bytes 294928 | tf_op jit(solution)/shard_map/reduce_scatter | solution.py:972
  408.4 5.5 %all-to-all-start.6 = ((bf16[16,592,128]{2,1,0:T(8,128)(2,1)}), bf16[16,592,128]{2,1,0:T(8,128)(2,1)S(1)}, u32[]{:S(2)}, u32[]{:S(2)}) async-start(bf16[16,592,128]{2,1,0:T(8,128)(2,1)} %get-tuple-element.97), calls=%async_computation.7 | async-start | bytes 4849664 | tf_op jit(solution)/shard_map/all_to_all | solution.py:1108
  419.2 48.9 %collective-permute-done.5 = f32[1,512]{1,0:T(1,128)S(1)} collective-permute-done((f32[1,512]{1,0:T(1,128)S(1)}, f32[1,512]{1,0:T(1,128)S(1)}, u32[]{:S(2)}, u32[]{:S(2)}) %collective-permute-start.5) | collective-permute-done | bytes 2080 | tf_op jit(solution)/shard_map/ppermute | solution.py:874
  480.1 4.8 collective-permute-done.7
  (117 shorter events, 81.3 us)
Async XLA Ops:
  7.2 8.9 %copy-start.8 = (f32[768,9]{0,1:T(8,128)S(1)}, f32[768,9]{0,1:T(8,128)}, u32[]{:S(2)}) copy-start(f32[768,9]{0,1:T(8,128)} %param.25) | copy-start | bytes 82948
  7.9 19.7 %collective-permute-start = (bf16[1,512]{1,0:T(2,128)(2,1)S(1)}, bf16[1,512]{1,0:T(2,128)(2,1)S(1)}, u32[]{:S(2)}, u32[]{:S(2)}) collective-permute-start(bf16[1,512]{1,0:T(2,128)(2,1)S(1)} %slice_bitcast_fusion.2), channel_id=1, source_target_pairs={{1,0},{2,1},{3,2},{4,3},{5,4},{6,5},{7,6},{8,7},{9,8},{10,9},{11,1... | collective-permute-start | bytes 3080 | tf_op jit(solution)/shard_map/ppermute | solution.py:874
  32.9 37.4 %all-to-all-start = ((bf16[16,32,384]{2,1,0:T(8,128)(2,1)}), bf16[16,32,384]{2,1,0:T(8,128)(2,1)S(1)}, u32[]{:S(2)}, u32[]{:S(2)}) async-start(bf16[16,32,384]{2,1,0:T(8,128)(2,1)} %get-tuple-element.67), calls=%async_computation | async-start | bytes 786432 | tf_op jit(solution)/shard_map/all_to_all | solution.py:898
  39.3 11.2 %collective-permute-start.1 = (bf16[64,768]{1,0:T(8,128)(2,1)S(1)}, bf16[64,768]{1,0:T(8,128)(2,1)S(1)}, u32[]{:S(2)}, u32[]{:S(2)}) collective-permute-start(bf16[64,768]{1,0:T(8,128)(2,1)S(1)} %get-tuple-element.115), channel_id=1, source_target_pairs={{0,1},{1,2},{2,3},{3,4},{4,5},{5,6},{6,7},{7,8},{8,9},{9,10},{10,1... | collective-permute-start | bytes 294920 | tf_op jit(solution)/shard_map/ppermute | solution.py:874
  41.3 9.1 %collective-permute-start.2 = (bf16[64,768]{1,0:T(8,128)(2,1)S(1)}, bf16[64,768]{1,0:T(8,128)(2,1)S(1)}, u32[]{:S(2)}, u32[]{:S(2)}) collective-permute-start(bf16[64,768]{1,0:T(8,128)(2,1)S(1)} %get-tuple-element.116), channel_id=1, source_target_pairs={{1,0},{2,1},{3,2},{4,3},{5,4},{6,5},{7,6},{8,7},{9,8},{10,9},{11,1... | collective-permute-start | bytes 294920 | tf_op jit(solution)/shard_map/ppermute | solution.py:874
  70.3 5.3 %copy-start.3 = (bf16[16,32,384]{2,1,0:T(8,128)(2,1)}, bf16[16,32,384]{2,1,0:T(8,128)(2,1)S(1)}, u32[]{:S(2)}) copy-start(bf16[16,32,384]{2,1,0:T(8,128)(2,1)S(1)} %all-to-all-done.input_ref) | copy-start | bytes 1179652
  75.6 40.6 %all-to-all-start.1 = ((bf16[16,128,384]{2,1,0:T(8,128)(2,1)}), bf16[16,128,384]{2,1,0:T(8,128)(2,1)S(1)}, u32[]{:S(2)}, u32[]{:S(2)}) async-start(bf16[16,128,384]{2,1,0:T(8,128)(2,1)} %get-tuple-element.71), calls=%async_computation.1 | async-start | bytes 3145728 | tf_op jit(solution)/shard_map/all_to_all | solution.py:898
  79.8 267.6 %reduce-scatter.3.cloned.1.call-start = ((), (), s32[]{:S(2)}) async-start(), calls=%async_computation.10 | async-start | bytes 10027008 | tf_op jit(solution)/shard_map/reduce_scatter | solution.py:972
  187.7 217.6 %reduce-scatter.5.cloned.1.call-start = ((), (), s32[]{:S(2)}) async-start(), calls=%async_computation.11 | async-start | bytes 5013504 | tf_op jit(solution)/shard_map/reduce_scatter | solution.py:972
  304.3 5.3 %copy-start.5 = (bf16[256,768]{1,0:T(8,128)(2,1)S(1)}, bf16[256,768]{1,0:T(8,128)(2,1)}, u32[]{:S(2)}) copy-start(bf16[256,768]{1,0:T(8,128)(2,1)} %get-tuple-element.81) | copy-start | bytes 1179652
  304.4 43.0 %all-to-all-start.5 = ((bf16[16,32,384]{2,1,0:T(8,128)(2,1)}), bf16[16,32,384]{2,1,0:T(8,128)(2,1)S(1)}, u32[]{:S(2)}, u32[]{:S(2)}) async-start(bf16[16,32,384]{2,1,0:T(8,128)(2,1)} %get-tuple-element.83), calls=%async_computation.5 | async-start | bytes 786432 | tf_op jit(solution)/shard_map/all_to_all | solution.py:898
  309.7 14.7 %collective-permute-start.3 = (bf16[64,768]{1,0:T(8,128)(2,1)S(1)}, bf16[64,768]{1,0:T(8,128)(2,1)S(1)}, u32[]{:S(2)}, u32[]{:S(2)}) collective-permute-start(bf16[64,768]{1,0:T(8,128)(2,1)S(1)} %get-tuple-element.113), channel_id=1, source_target_pairs={{0,1},{1,2},{2,3},{3,4},{4,5},{5,6},{6,7},{7,8},{8,9},{9,10},{10,1... | collective-permute-start | bytes 294920 | tf_op jit(solution)/shard_map/ppermute | solution.py:874
  311.8 12.6 %collective-permute-start.4 = (bf16[64,768]{1,0:T(8,128)(2,1)S(1)}, bf16[64,768]{1,0:T(8,128)(2,1)S(1)}, u32[]{:S(2)}, u32[]{:S(2)}) collective-permute-start(bf16[64,768]{1,0:T(8,128)(2,1)S(1)} %get-tuple-element.114), channel_id=1, source_target_pairs={{1,0},{2,1},{3,2},{4,3},{5,4},{6,5},{7,6},{8,7},{9,8},{10,9},{11,1... | collective-permute-start | bytes 294920 | tf_op jit(solution)/shard_map/ppermute | solution.py:874
  347.4 6.1 %copy-start.4 = (bf16[16,32,384]{2,1,0:T(8,128)(2,1)}, bf16[16,32,384]{2,1,0:T(8,128)(2,1)S(1)}, u32[]{:S(2)}) copy-start(bf16[16,32,384]{2,1,0:T(8,128)(2,1)S(1)} %all-to-all-done.5.grad_ref) | copy-start | bytes 1179652
  380.7 27.7 %all-to-all-start.7 = ((bf16[16,48,384]{2,1,0:T(8,128)(2,1)}), bf16[16,48,384]{2,1,0:T(8,128)(2,1)S(1)}, u32[]{:S(2)}, u32[]{:S(2)}) async-start(bf16[16,48,384]{2,1,0:T(8,128)(2,1)} %taps_grad.1), calls=%async_computation.8 | async-start | bytes 1179648 | tf_op jit(solution)/shard_map/all_to_all | solution.py:898
  405.3 8.6 %copy-start.7 = (bf16[1,384,384]{2,1,0:T(8,128)(2,1)S(1)}, bf16[1,384,384]{2,1,0:T(8,128)(2,1)}, u32[]{:S(2)}) copy-start(bf16[1,384,384]{2,1,0:T(8,128)(2,1)} %reduce-scatter.5.cloned.1.call-done) | copy-start | bytes 884740
  405.3 8.6 %collective-permute-start.8 = (bf16[384,384]{1,0:T(8,128)(2,1)}, bf16[384,384]{1,0:T(8,128)(2,1)}, u32[]{:S(2)}, u32[]{:S(2)}) collective-permute-start(bf16[384,384]{1,0:T(8,128)(2,1)} %bitcast.37), channel_id=1, source_target_pairs={{0,16},{16,0},{1,17},{17,1},{2,18},{18,2},{3,19},{19,3},{4,20},{20... | collective-permute-start | bytes 884744 | tf_op jit(solution)/shard_map/ppermute | solution.py:924
  408.4 70.1 %all-to-all-start.6 = ((bf16[16,592,128]{2,1,0:T(8,128)(2,1)}), bf16[16,592,128]{2,1,0:T(8,128)(2,1)S(1)}, u32[]{:S(2)}, u32[]{:S(2)}) async-start(bf16[16,592,128]{2,1,0:T(8,128)(2,1)} %get-tuple-element.97), calls=%async_computation.7 | async-start | bytes 4849664 | tf_op jit(solution)/shard_map/all_to_all | solution.py:1108
  413.9 2.7 copy-start.11
  415.0 55.2 %collective-permute-start.9 = (bf16[768,384]{1,0:T(8,128)(2,1)}, bf16[768,384]{1,0:T(8,128)(2,1)}, u32[]{:S(2)}, u32[]{:S(2)}) collective-permute-start(bf16[768,384]{1,0:T(8,128)(2,1)} %bitcast.11), channel_id=1, source_target_pairs={{0,16},{16,0},{1,17},{17,1},{2,18},{18,2},{3,19},{19,3},{4,20},{20... | collective-permute-start | bytes 1769480 | tf_op jit(solution)/shard_map/ppermute | solution.py:924
  416.6 2.6 copy-start.9
  416.6 51.5 %collective-permute-start.5 = (f32[1,512]{1,0:T(1,128)S(1)}, f32[1,512]{1,0:T(1,128)S(1)}, u32[]{:S(2)}, u32[]{:S(2)}) collective-permute-start(f32[1,512]{1,0:T(1,128)S(1)} %copy-done.11), channel_id=1, source_target_pairs={{0,1},{1,2},{2,3},{3,4},{4,5},{5,6},{6,7},{7,8},{8,9},{9,10},{10,1... | collective-permute-start | bytes 6152 | tf_op jit(solution)/shard_map/ppermute | solution.py:874
  474.8 10.1 %collective-permute-start.7 = (bf16[16,48,384]{2,1,0:T(8,128)(2,1)S(1)}, bf16[16,48,384]{2,1,0:T(8,128)(2,1)}, u32[]{:S(2)}, u32[]{:S(2)}) collective-permute-start(bf16[16,48,384]{2,1,0:T(8,128)(2,1)S(1)} %all-to-all-done.7), channel_id=1, source_target_pairs={{0,16},{16,0},{1,17},{17,1},{2,18},{18,2},{3,19},{19,3},{4,20},{20... | collective-permute-start | bytes 1769480 | tf_op jit(solution)/shard_map/ppermute | solution.py:924
  478.9 17.7 %collective-permute-start.6 = (bf16[592,128]{1,0:T(8,128)(2,1)S(1)}, bf16[592,128]{1,0:T(8,128)(2,1)S(1)}, u32[]{:S(2)}, u32[]{:S(2)}) collective-permute-start(bf16[592,128]{1,0:T(8,128)(2,1)S(1)} %reduce_sum.49), channel_id=1, source_target_pairs={{0,16},{16,0},{1,17},{17,1},{2,18},{18,2},{3,19},{19,3},{4,20},{20... | collective-permute-start | bytes 454664 | tf_op jit(solution)/shard_map/ppermute | solution.py:924
  (6 other events, 5.3 us)
Sparse Core Ops, SparseCore 0:
  187.8 130.7 reduce-scatter.2
  323.0 82.2 reduce-scatter.4

commit v3 on v2

v3 whole, which is shorter than its diff:
```python
import functools

import jax
import jax.numpy as jnp
from jax import lax
from jax.experimental import pallas as pl
from jax.experimental.pallas import tpu as pltpu
from jax.sharding import PartitionSpec as P

HEADS = 12
KERNEL = 128
GROUPS = 16
MAXLEN = 1536
RING = 16
HEAD_DIM = 64
EPS = 1e-05
BF = jnp.bfloat16
VMEM_WHOLE = pl.BlockSpec(memory_space=pltpu.VMEM)
SMEM_WHOLE = pl.BlockSpec(memory_space=pltpu.SMEM)
TOTAL, BEGIN, SEGMENT, KEYS, ACTIVE, CORE = range(6)


def row_dot(left, right):
    return lax.dot_general(left, right, (((1,), (1,)), ((), ())), preferred_element_type=jnp.float32)


def plain_dot(left, right):
    return lax.dot_general(left, right, (((1,), (0,)), ((), ())), preferred_element_type=jnp.float32)


def over_rows_dot(left, right):
    return lax.dot_general(left, right, (((0,), (0,)), ((), ())), preferred_element_type=jnp.float32)


def pair_slot(shape, share, marks, clips):
    if shape[0] == 1:
        return 0, share
    return (marks[clips + CORE] if share % 2 == 0 else 1 - marks[clips + CORE]), share // 2


def over_clips(clips, step, state):
    if clips <= 8:
        for clip in range(clips):
            state = step(clip, state)
        return state
    return lax.fori_loop(0, clips, step, state)


def clip_bounds(marks, clips, places):
    def step(clip, state):
        first, end = state
        mark = marks[clip]
        return (
            jnp.maximum(first, jnp.where(mark <= places, mark, 0)),
            jnp.minimum(end, jnp.where(mark > places, mark, marks[clips + TOTAL])),
        )

    return over_clips(clips, step, (jnp.zeros_like(places), jnp.zeros_like(places) + marks[clips + TOTAL]))


def like(shape, dtype=jnp.float32):
    return jax.ShapeDtypeStruct(shape, dtype)


def call(kernel, outs, scratch, args, name, flops, grid=None, in_specs=None, out_specs=None, limit=56):
    size = sum(a.size * a.dtype.itemsize for a in args)
    size += sum(o.size * o.dtype.itemsize for o in outs)
    extra = {} if grid is None else {"grid": grid}
    return pl.pallas_call(
        kernel,
        out_shape=tuple(outs),
        in_specs=in_specs or [SMEM_WHOLE if a.dtype == jnp.int32 else VMEM_WHOLE for a in args],
        out_specs=out_specs or (VMEM_WHOLE,) * len(outs),
        scratch_shapes=scratch,
        compiler_params=pltpu.CompilerParams(vmem_limit_bytes=limit << 20),
        cost_estimate=pl.CostEstimate(flops=flops, bytes_accessed=size, transcendentals=0),
        name=name,
        **extra,
    )(*args)


Q_TILE = 512
K_TILE = 512
LOW = -1e30
LOG2E = 1.4426950408889634


def unpack_heads(packed_ref, targets):
    blocks, half, lanes = packed_ref.shape
    share = lanes // 2

    def one(block, carry):
        tile = packed_ref[block]
        turned = tile.T
        for side in range(2):
            row = pl.multiple_of(block * 2 * half + side * half, half)
            for place, (rows, columns) in enumerate(targets):
                begin = side * share + place * HEAD_DIM
                if rows is not None:
                    rows[pl.ds(row, half), :] = tile[:, begin : begin + HEAD_DIM]
                if columns is not None:
                    columns[0:HEAD_DIM, pl.ds(row, half)] = turned[begin : begin + HEAD_DIM]
        return carry

    lax.fori_loop(0, blocks, one, 0)


def tile_spans(marks, clips, index):
    first = marks[clips + SEGMENT] + index * Q_TILE
    begin = marks[clips + KEYS]
    low, low_end = clip_bounds(marks, clips, first)
    high_start, high = clip_bounds(marks, clips, first + Q_TILE - 1)
    low, low_end, high_start, high = (v - begin for v in (low, low_end, high_start, high))
    up = K_TILE - 1
    start = lax.div(low, K_TILE)
    stop = jnp.where(marks[clips + ACTIVE] > 0, lax.div(high + up, K_TILE), start)
    inner = lax.div(high_start + up, K_TILE)
    outer = lax.div(high, K_TILE)
    whole = (low == high_start) & (inner < outer) & (stop > start)
    inner = jnp.where(whole, inner, stop)
    outer = jnp.where(whole, outer, stop)
    places = first + lax.broadcasted_iota(jnp.int32, (1, Q_TILE), 1)
    starts, ends = clip_bounds(marks, clips, places)
    return (start, inner, outer, stop), starts - begin, ends - begin


def allowed(column, starts, ends):
    places = column + lax.broadcasted_iota(jnp.int32, (K_TILE, 1), 0)
    return (places >= starts) & (places < ends)


def over_spans(spans, step, state):
    for at in range(3):
        state = lax.fori_loop(spans[at], spans[at + 1], functools.partial(step, at != 1), state)
    return state


def attend_kernel(clips, halo, marks, packed_ref, out_ref, wide_ref, log_ref, query_t, keys, value_t):
    rows = wide_ref.shape[1]
    half = packed_ref.shape[1]
    block = 2 * half
    more = value_t.shape[0] - HEAD_DIM
    value_t[HEAD_DIM:] = jnp.where(
        lax.broadcasted_iota(jnp.int32, (more, value_t.shape[1]), 0) == 0, 1.0, 0.0
    ).astype(BF)
    unpack_heads(packed_ref, ((None, query_t), (keys, None), (None, value_t)))
    factor = HEAD_DIM ** (-0.5) * LOG2E

    def query_tile(index, carry):
        first = pl.multiple_of(index * Q_TILE, Q_TILE)
        q = query_t[:, pl.ds(halo * block + first, Q_TILE)]
        spans, starts, ends = tile_spans(marks, clips, index)

        def key_tile(masked, at, state):
            top, total = state
            column = pl.multiple_of(at * K_TILE, K_TILE)
            scores = plain_dot(keys[pl.ds(column, K_TILE), :], q) * factor
            if masked:
                scores = jnp.where(allowed(column, starts, ends), scores, LOW)
            new_top = jnp.maximum(top, jnp.max(scores, axis=0, keepdims=True))
            weight = jnp.exp2(scores - new_top).astype(BF)
            total = total * jnp.exp2(top - new_top) + plain_dot(
                value_t[:, pl.ds(column, K_TILE)], weight
            )
            return new_top, total

        top, total = over_spans(
            spans,
            key_tile,
            (
                jnp.full((1, Q_TILE), 0.5 * LOW, jnp.float32),
                jnp.zeros((HEAD_DIM + more, Q_TILE), jnp.float32),
            ),
        )
        mass = jnp.maximum(total[HEAD_DIM : HEAD_DIM + 1], 1e-37)
        attended = total[:HEAD_DIM] / mass
        wide_ref[:, pl.ds(first, Q_TILE)] = attended
        log_ref[:, pl.ds(first, Q_TILE)] = top + jnp.log2(mass)
        narrow = attended.T.astype(BF)
        for inner in range(Q_TILE // block):
            out_ref[index * (Q_TILE // block) + inner] = jnp.concatenate(
                [
                    narrow[inner * block : inner * block + half],
                    narrow[inner * block + half : (inner + 1) * block],
                ],
                axis=1,
            )
        return carry

    lax.fori_loop(0, rows // Q_TILE, query_tile, 0)


def attend(marks, packed, clips, halo):
    blocks, half, _ = packed.shape
    rows = (blocks - 2 * halo) * 2 * half
    key_rows = blocks * 2 * half
    return call(
        functools.partial(attend_kernel, clips, halo),
        [
            like((blocks - 2 * halo, half, 2 * HEAD_DIM), BF),
            like((HEAD_DIM, rows)),
            like((1, rows)),
        ],
        [
            pltpu.VMEM((HEAD_DIM, key_rows), BF),
            pltpu.VMEM((key_rows, HEAD_DIM), BF),
            pltpu.VMEM((HEAD_DIM + 16, key_rows), BF),
        ],
        (marks, packed),
        "attend",
        25 * 10**9,
    )


def attend_back_kernel(
    clips, halo, marks, packed_ref, grad_ref, wide_ref, log_ref, out_ref,
    query, query_t, keys, key_t, values, grads, grad_t, key_grads, value_grads,
):
    unpack_heads(packed_ref, ((query, query_t), (keys, key_t), (values, None)))
    unpack_heads(grad_ref, ((grads, grad_t),))
    blocks, half, _ = packed_ref.shape
    rows = wide_ref.shape[1]
    block = 2 * half
    scale = HEAD_DIM ** (-0.5)
    key_grads[...] = jnp.zeros_like(key_grads)
    value_grads[...] = jnp.zeros_like(value_grads)
    if halo:
        out_ref[...] = jnp.zeros_like(out_ref)

    def query_tile(index, carry):
        first = pl.multiple_of(index * Q_TILE, Q_TILE)
        own = pl.ds(halo * block + first, Q_TILE)
        q, q_t = query[own, :], query_t[:, own]
        g, g_t = grads[pl.ds(first, Q_TILE), :], grad_t[:, pl.ds(first, Q_TILE)]
        log_total = log_ref[:, pl.ds(first, Q_TILE)]
        delta = jnp.sum(
            g_t.astype(jnp.float32) * wide_ref[:, pl.ds(first, Q_TILE)], axis=0, keepdims=True
        )
        spans, starts, ends = tile_spans(marks, clips, index)

        def key_tile(masked, at, running):
            column = pl.multiple_of(at * K_TILE, K_TILE)
            here = pl.ds(column, K_TILE)
            probs = jnp.exp2(plain_dot(keys[here, :], q_t) * (scale * LOG2E) - log_total)
            if masked:
                probs = jnp.where(allowed(column, starts, ends), probs, 0.0)
            prob_grad = plain_dot(values[here, :], g_t)
            score_grad = (probs * (prob_grad - delta)).astype(BF)
            value_grads[here, :] += plain_dot(probs.astype(BF), g)
            key_grads[here, :] += plain_dot(score_grad, q)
            return running + plain_dot(key_t[:, here], score_grad)

        query_grad = over_spans(spans, key_tile, jnp.zeros((HEAD_DIM, Q_TILE), jnp.float32))
        query_grad = (query_grad.T * scale).astype(BF)
        for inner in range(Q_TILE // block):
            spot = halo + index * (Q_TILE // block) + inner
            out_ref[spot, :, 0:HEAD_DIM] = query_grad[inner * block : inner * block + half]
            out_ref[spot, :, 3 * HEAD_DIM : 4 * HEAD_DIM] = query_grad[
                inner * block + half : (inner + 1) * block
            ]
        return carry

    lax.fori_loop(0, rows // Q_TILE, query_tile, 0)

    def finish(spot, carry):
        for side in range(2):
            row = pl.multiple_of(spot * block + side * half, half)
            begin = (3 * side + 1) * HEAD_DIM
            out_ref[spot, :, begin : begin + 2 * HEAD_DIM] = jnp.concatenate(
                [key_grads[pl.ds(row, half), :] * scale, value_grads[pl.ds(row, half), :]], axis=1
            ).astype(BF)
        return carry

    lax.fori_loop(0, blocks, finish, 0)


def attend_back(marks, packed, grad, wide, log_total, clips, halo):
    blocks, half, lanes = packed.shape
    rows = wide.shape[1]
    key_rows = blocks * 2 * half
    return call(
        functools.partial(attend_back_kernel, clips, halo),
        [like((blocks, half, lanes), BF)],
        [
            pltpu.VMEM((key_rows, HEAD_DIM), BF),
            pltpu.VMEM((HEAD_DIM, key_rows), BF),
            pltpu.VMEM((key_rows, HEAD_DIM), BF),
            pltpu.VMEM((HEAD_DIM, key_rows), BF),
            pltpu.VMEM((key_rows, HEAD_DIM), BF),
            pltpu.VMEM((rows, HEAD_DIM), BF),
            pltpu.VMEM((HEAD_DIM, rows), BF),
            pltpu.VMEM((key_rows, HEAD_DIM), jnp.float32),
            pltpu.VMEM((key_rows, HEAD_DIM), jnp.float32),
        ],
        (marks, packed, grad, wide, log_total),
        "attend_back",
        35 * 10**9,
        limit=60,
    )[0]


TAPS = 16
SHOT = 384
TURNS = KERNEL // TAPS


def conv_weights_kernel(back, weight_ref, out_ref):
    group_width = out_ref.shape[1]
    if back:
        for group in range(GROUPS):
            lanes = slice(group_width * group, group_width * (group + 1))
            out_ref[group] = jnp.concatenate(
                [weight_ref[group_width * tap : group_width * (tap + 1), lanes] for tap in range(TAPS)],
                axis=1,
            )
    else:
        turned = weight_ref[...].T
        for group in range(GROUPS):
            out_ref[group] = turned[group_width * group : group_width * (group + 1)]


def conv_weights(back, weight, first, turns):
    width = weight.shape[1]
    group_width = width // GROUPS
    return call(
        functools.partial(conv_weights_kernel, back),
        [like((GROUPS, turns * group_width, TAPS * group_width), weight.dtype)],
        [],
        (weight,),
        "conv_weights_back" if back else "conv_weights",
        0,
        (turns,),
        [pl.BlockSpec((TAPS * group_width, width), lambda turn: (turn + first, 0))],
        (pl.BlockSpec((GROUPS, group_width, TAPS * group_width), lambda turn: (0, turn, 0)),),
    )[0]


def conv_kernel(back, clips, parts, marks, before_ref, rows_ref, after_ref, *refs):
    weight_refs, (out_ref, spaced, total) = refs[:parts], refs[parts:]
    group = pl.program_id(0)
    rows, width = rows_ref.shape
    half = KERNEL // 2
    long = rows + 2 * half
    group_width = width // GROUPS
    room = spaced.shape[1]
    places = marks[clips + BEGIN] - half + lax.broadcasted_iota(jnp.int32, (1, long), 1)
    ids = over_clips(
        clips,
        lambda clip, found: found + jnp.where(places >= marks[clip], 1, 0),
        jnp.zeros((1, long), jnp.int32),
    )
    ids = jnp.where((places >= 0) & (places < marks[clips + TOTAL]), ids, -1)

    def number_of(place):
        step = lambda clip, found: found + jnp.where(place >= marks[clip], 1, 0)
        return over_clips(clips, step, jnp.int32(0))

    first = number_of(marks[clips + BEGIN])
    count = number_of(marks[clips + BEGIN] + rows - 1) - first + 1

    @pl.when(group == 0)
    def _():
        turned = jnp.concatenate(
            [before_ref[...], rows_ref[...], after_ref[...]], axis=0
        ).astype(jnp.float32).T
        rest = jnp.zeros((width, room - long), jnp.float32)

        def of_clip(clip):
            return jnp.concatenate([jnp.where(ids == first + clip, turned, 0.0), rest], axis=1)

        spaced[...] = of_clip(0).astype(BF)

        def place(clip, carry):
            spaced[...] += pltpu.roll(of_clip(clip), clip * half, 1).astype(BF)
            return carry

        lax.fori_loop(1, count, place, 0)

    row = pl.multiple_of(group * group_width, group_width)
    shots = lax.div(rows + half * (count - 1) + SHOT - 1, SHOT)

    def shot(index, carry):
        base = pl.multiple_of(index * SHOT, 128)
        tile = spaced[pl.ds(row, group_width), pl.ds(base, SHOT + 2 * KERNEL)]
        moved = []
        for tap in range(TAPS):
            begin = TAPS - tap if back else tap
            moved.append(tile[:, begin : begin + SHOT + KERNEL])
        moved = jnp.concatenate(moved, axis=0)
        result = None
        turn = 0
        for weight_ref in weight_refs:
            product = plain_dot(weight_ref[0], moved)
            for inner in range(product.shape[0] // group_width):
                begin = (TURNS - 1 - turn if back else turn) * TAPS
                piece = product[inner * group_width : (inner + 1) * group_width, begin : begin + SHOT]
                result = piece if result is None else result + piece
                turn += 1
        total[pl.ds(row, group_width), pl.ds(base, SHOT)] = result
        return carry

    lax.fori_loop(0, shots, shot, 0)

    @pl.when(group == GROUPS - 1)
    def _():
        wide = total.shape[1]
        own = ids[:, half : half + rows]

        def collect(clip, carry):
            moved = pltpu.roll(total[...], lax.rem(wide - clip * half, wide), 1)[:, :rows]
            total[:, :rows] = jnp.where(own == first + clip, moved, total[:, :rows])
            return carry

        lax.fori_loop(1, count, collect, 0)
        out_ref[...] = total[:, :rows].T


def conv_rows(back, marks, before, value, after, weights, clips):
    rows, width = value.shape
    shots = -(-(rows + KERNEL // 2 * (clips - 1)) // SHOT)
    whole = lambda a: pl.BlockSpec(a.shape, lambda group: (0, 0))
    return call(
        functools.partial(conv_kernel, back, clips, len(weights)),
        [like((rows, width))],
        [
            pltpu.VMEM((width, SHOT * shots + 2 * KERNEL), BF),
            pltpu.VMEM((width, SHOT * shots), jnp.float32),
        ],
        (marks, before, value, after) + tuple(weights),
        "conv_back" if back else "conv",
        15 * 10**9,
        (GROUPS,),
        [SMEM_WHOLE, whole(before), whole(value), whole(after)]
        + [pl.BlockSpec((1,) + weight.shape[1:], lambda group: (group, 0, 0)) for weight in weights],
        (pl.BlockSpec((rows, width), lambda group: (0, 0)),),
        limit=48,
    )[0]


def taps_grad_kernel(
    clips, marks, both_ref, out_ref, inputs, spaced, input_cols, grad_cols
):
    half = KERNEL // 2
    group_width = inputs.shape[0]
    long = inputs.shape[1]
    blocks, _, block = both_ref.shape
    halo = (blocks - RING) // 2
    halo_rows = halo * block
    first = over_clips(
        clips,
        lambda clip, found: found + jnp.where(marks[clips + SEGMENT] >= marks[clip], 1, 0),
        jnp.int32(0),
    )
    origin = half + halo_rows
    span = input_cols.shape[1]

    def lay(first_row, begin_block, number, target, reach):
        for at in range(number):
            target[:, at * block : (at + 1) * block] = both_ref[
                begin_block + at, first_row : first_row + group_width
            ].astype(jnp.float32)
        target[:, number * block :] = jnp.zeros((group_width, long - number * block), jnp.float32)
        lanes = lax.broadcasted_iota(jnp.int32, (1, long), 1)
        places = marks[clips + SEGMENT] - reach + lanes
        held = lanes < number * block
        spaced[...] = jnp.zeros_like(spaced)

        def place(clip, carry):
            begin = jnp.where(clip > 0, marks[jnp.maximum(clip - 1, 0)], 0)
            keep = (places >= begin) & (places < marks[clip]) & held
            spaced[...] += pltpu.roll(
                jnp.where(keep, target[...], 0.0), origin - reach + half * (clip - first), 1
            )
            return carry

        lax.fori_loop(first, clips, place, 0)
        return spaced[...]

    laid = lay(0, 0, blocks, inputs, halo_rows)
    for turn in range(TURNS):
        begin = origin - half + turn * TAPS
        input_cols[turn * group_width : (turn + 1) * group_width, :] = laid[
            :, begin : begin + span
        ].astype(BF)
    laid = lay(group_width, halo, RING, inputs, 0)
    for tap in range(TAPS):
        grad_cols[tap * group_width : (tap + 1) * group_width, :] = laid[
            :, origin - tap : origin - tap + span
        ].astype(BF)
    result = row_dot(input_cols[...], grad_cols[...]).astype(BF)
    side_lanes = TAPS * group_width // 2
    for place_at in range(2 * TURNS):
        turn, side = place_at // 2, place_at % 2
        for piece in range(side_lanes // 128):
            begin = side * side_lanes + piece * 128
            row, column = pair_slot(out_ref.shape, place_at, marks, clips)
            out_ref[row, column, piece * group_width : (piece + 1) * group_width] = result[
                turn * group_width : (turn + 1) * group_width, begin : begin + 128
            ]


def taps_grad(marks, both, shape, clips):
    blocks, two, block = both.shape
    group_width = two // 2
    half = KERNEL // 2
    halo_rows = (blocks - RING) // 2 * block
    span = -(-(RING * block + half * clips) // 128) * 128
    long = span + 2 * halo_rows + half + 2 * KERNEL
    long = -(-long // 128) * 128
    more = TAPS * group_width // 2 // 128 * group_width
    return call(
        functools.partial(taps_grad_kernel, clips),
        [like(shape + (more, 128), BF)],
        [
            pltpu.VMEM((group_width, long), jnp.float32),
            pltpu.VMEM((group_width, long), jnp.float32),
            pltpu.VMEM((TURNS * group_width, span), BF),
            pltpu.VMEM((TAPS * group_width, span), BF),
        ],
        (marks, both),
        "taps_grad",
        10**10,
        limit=60,
    )[0]


def weave_taps_kernel(own_ref, other_ref, out_ref):
    group_width = out_ref.shape[1] // GROUPS
    taps = out_ref.shape[0] // group_width
    pieces = own_ref.shape[1] // group_width
    both = []
    for group in range(GROUPS):
        rows = own_ref[group].astype(jnp.float32) + other_ref[group].astype(jnp.float32)
        both.append(
            jnp.concatenate([rows[at * group_width : (at + 1) * group_width] for at in range(pieces)], axis=1)
        )
    for tap in range(taps):
        lanes = slice(tap * group_width, (tap + 1) * group_width)
        out_ref[tap * group_width : (tap + 1) * group_width, :] = jnp.concatenate(
            [value[:, lanes] for value in both], axis=1
        )


def weave_taps(own, other, taps, group_width):
    return call(
        weave_taps_kernel, [like((taps * group_width, GROUPS * group_width))], [], (own, other), "weave_taps", 0
    )[0]


def join_pair_kernel(clips, marks, sums_ref, other_sums_ref, taps_ref, other_taps_ref, out_ref):
    below, rows = sums_ref.shape[2], taps_ref.shape[2]
    out_ref[:, :below] = (
        sums_ref[0].astype(jnp.float32) + other_sums_ref[...].astype(jnp.float32)
    ).astype(BF)
    first = marks[clips + CORE] == 0
    out_ref[:, below : below + rows] = jnp.where(first, taps_ref[0], other_taps_ref[...])
    out_ref[:, below + rows :] = jnp.where(first, other_taps_ref[...], taps_ref[0])


def join_pair(marks, sums, other_sums, taps, other_taps, clips):
    _, chips, below, lanes = sums.shape
    return call(
        functools.partial(join_pair_kernel, clips),
        [like((chips, below + 2 * taps.shape[2], lanes), BF)],
        [],
        (marks, sums, other_sums, taps, other_taps),
        "join_pair",
        0,
    )[0]


SHARE = 384
PIECE = 128


def norm_parts(values):
    center = values - jnp.mean(values, axis=-1, keepdims=True)
    inverse = lax.rsqrt(jnp.mean(center * center, axis=-1, keepdims=True) + EPS)
    return center * inverse, inverse


def norm_back(unit, inverse, scales, grad):
    scaled = grad * scales
    back = inverse * (
        scaled
        - jnp.mean(scaled, axis=-1, keepdims=True)
        - unit * jnp.mean(scaled * unit, axis=-1, keepdims=True)
    )
    return back, row_sum(grad * unit), row_sum(grad)


def row_sum(values):
    return jnp.sum(values, axis=0, keepdims=True)


def gelu_both(values):
    below = 0.5 + 0.5 * lax.erf(values * 0.7071067811865476)
    bell = jnp.exp(-0.5 * values * values) * 0.3989422804014327
    return values * below, below + values * bell


def store_turned(values_b, out_ref, first):
    group_width = values_b.shape[1] // GROUPS
    turned = values_b.T
    for group in range(GROUPS):
        out_ref[group, first : first + group_width] = turned[group * group_width : (group + 1) * group_width]


def same_clip_next(marks, clips, rows):
    following = marks[clips + BEGIN] + 1 + lax.broadcasted_iota(jnp.int32, (rows, 1), 0)
    step = lambda clip, other: jnp.maximum(other, jnp.where(following == marks[clip], 1, 0))
    return over_clips(clips, step, jnp.zeros((rows, 1), jnp.int32)) == 0


def stem_kernel(
    clips, marks, samples_ref, next_ref, weight_ref, gain_ref, bias_ref, proj_ref, gains_ref, biases_ref,
    start_ref, start_b_ref, pre_ref, normed_ref, unfold_ref, table_ref, wide,
):
    rows, chans = pre_ref.shape
    table_ref[0:3] = gains_ref[...]
    table_ref[3:12] = biases_ref[...]
    last = lax.broadcasted_iota(jnp.int32, (rows, 1), 0) == rows - 1
    same = same_clip_next(marks, clips, rows)
    for lane in range(0, chans, PIECE):
        lanes = slice(lane, lane + PIECE)
        wide[...] = samples_ref[:, lanes].astype(jnp.float32)
        even = wide[pl.ds(0, rows, stride=2), :]
        unfold_ref[:, lanes] = even.astype(BF)
        unfold_ref[:, chans + lane : chans + lane + PIECE] = wide[pl.ds(1, rows, stride=2), :].astype(BF)
        moved = jnp.where(last, next_ref[:, lanes].astype(jnp.float32), pltpu.roll(even, rows - 1, 0))
        unfold_ref[:, 2 * chans + lane : 2 * chans + lane + PIECE] = jnp.where(same, moved, 0.0).astype(BF)
    pre = plain_dot(unfold_ref[...], weight_ref[...])
    pre_ref[...] = pre
    unit, _ = norm_parts(gelu_both(pre)[0])
    normed = (unit * gain_ref[...] + bias_ref[...]).astype(BF)
    normed_ref[...] = normed
    start = plain_dot(normed, proj_ref[...]) + table_ref[3:4]
    start_ref[...] = start
    start_b_ref[...] = start.astype(BF)


def stem(marks, samples, next_row, weight, gain, bias, proj, gains, biases, clips):
    rows = samples.shape[0] // 2
    chans, width = proj.shape
    return call(
        functools.partial(stem_kernel, clips),
        [
            like((rows, width)), like((rows, width), BF),
            like((rows, chans)), like((rows, chans), BF), like((rows, 3 * chans), BF), like((12, width)),
        ],
        [pltpu.VMEM((2 * rows, PIECE), jnp.float32)],
        (marks, samples, next_row, weight, gain, bias, proj, gains, biases),
        "stem",
        6 * 10**9,
    )


def project_kernel(conv_ref, start_ref, table_ref, weight_ref, hidden_ref, packed_ref):
    rows, width = start_ref.shape
    half = rows // 2
    mixed = start_ref[...] + gelu_both(conv_ref[...] + table_ref[4:5])[0]
    unit, _ = norm_parts(mixed)
    hidden = unit * table_ref[0:1] + table_ref[5:6]
    hidden_ref[...] = hidden
    hidden_b = hidden.astype(BF)
    shifts = (table_ref[6:7], jnp.zeros((1, width), jnp.float32), table_ref[7:8])
    parts = [
        (plain_dot(hidden_b, weight_ref[:, at * width : (at + 1) * width]) + shift).astype(BF)
        for at, shift in enumerate(shifts)
    ]
    heads = width // HEAD_DIM
    for head in range(heads):
        lanes = slice(head * HEAD_DIM, (head + 1) * HEAD_DIM)
        packed_ref[head] = jnp.concatenate(
            [part[:half, lanes] for part in parts] + [part[half:, lanes] for part in parts], axis=1
        )
    for head in range(heads, RING):
        packed_ref[head] = jnp.zeros_like(packed_ref[head])


def project_heads(conv_sum, start, table, weight):
    rows, width = start.shape
    return call(
        project_kernel,
        [like((rows, width)), like((RING, rows // 2, 6 * HEAD_DIM), BF)],
        [],
        (conv_sum, start, table, weight),
        "project_heads",
        6 * 10**9,
    )


def middle_kernel(
    heads_ref, hidden_ref, table_ref, out_weight_ref, in_ref, in_bias_ref, back_ref, out_grad_ref,
    layer_ref, grad_heads_ref, grad_second_ref, out_part_ref, sums_ref, in_bias_grad_ref, joined_ref,
    attended, before, second, second_b, second_t, inner_b, slope, total, grad_last, grad_last_b,
    joined, sems,
):
    step = pl.program_id(0)
    rows, width = hidden_ref.shape
    half = rows // 2
    chunk = in_ref.shape[1]
    chunks = pl.num_programs(0) // 2
    heads = width // HEAD_DIM
    shares = joined_ref.shape[0]
    in_rows = width // shares
    back_rows = chunk * chunks // shares
    owners = chunk // back_rows

    def in_copy(at):
        place = (slice(None), pl.ds(pl.multiple_of(at * in_rows, 16), in_rows))
        return pltpu.make_async_copy(joined.at[place], joined_ref.at[place], sems.at[0, at])

    def back_copy(at):
        place = (pl.ds(at * owners, owners), pl.ds(in_rows * chunks, joined_ref.shape[1] - in_rows * chunks))
        return pltpu.make_async_copy(joined.at[place], joined_ref.at[place], sems.at[1, at])

    @pl.when(step == 0)
    def _():
        for head in range(heads):
            lanes = slice(head * HEAD_DIM, (head + 1) * HEAD_DIM)
            attended[:half, lanes] = heads_ref[head, :, :HEAD_DIM]
            attended[half:, lanes] = heads_ref[head, :, HEAD_DIM:]
        value = hidden_ref[...] + plain_dot(attended[...], out_weight_ref[...]) + table_ref[8:9]
        before[...] = value
        unit, _ = norm_parts(value)
        value = unit * table_ref[1:2] + table_ref[9:10]
        second[...] = value
        second_b[...] = value.astype(BF)
        second_t[...] = value.T.astype(BF)
        total[...] = jnp.zeros_like(total)

    @pl.when(step < chunks)
    def _():
        at = pl.multiple_of(step * chunk, chunk)
        value, back = gelu_both(plain_dot(second_b[...], in_ref[...]) + in_bias_ref[:, pl.ds(at, chunk)])
        value_b = value.astype(BF)
        inner_b[step] = value_b
        slope[step] = back
        total[...] += plain_dot(value_b, back_ref[...])

    @pl.when(step == chunks - 1)
    def _():
        unit, inverse = norm_parts(second[...] + total[...] + table_ref[10:11])
        layer_ref[...] = (unit * table_ref[2:3] + table_ref[11:12]).astype(BF)
        back, gain, bias = norm_back(unit, inverse, table_ref[2:3], out_grad_ref[...].astype(jnp.float32))
        grad_last[...] = back
        grad_last_b[...] = back.astype(BF)
        total[...] = back
        sums_ref[0:1] = gain
        sums_ref[1:2] = bias
        sums_ref[2:3] = row_sum(back)

    @pl.when(step >= chunks)
    def _():
        turn = step - chunks
        at = pl.multiple_of(turn * chunk, chunk)
        grad = row_dot(grad_last_b[...], back_ref[...]) * slope[turn]
        in_bias_grad_ref[:, pl.ds(at, chunk)] = row_sum(grad)
        grad_b = grad.astype(BF)
        total[...] += row_dot(grad_b, in_ref[...])
        product = plain_dot(second_t[...], grad_b).astype(BF)
        for share in range(shares):
            joined[share, pl.ds(pl.multiple_of(turn * in_rows, 16), in_rows), :] = product[
                share * in_rows : (share + 1) * in_rows
            ]
        in_copy(turn).start()
        product = over_rows_dot(inner_b[turn], grad_last_b[...]).astype(BF)
        for owner in range(owners):
            for place in range(width // SHARE):
                begin = in_rows * chunks + place * back_rows
                joined[turn * owners + owner, begin : begin + back_rows, :] = product[
                    owner * back_rows : (owner + 1) * back_rows, place * SHARE : (place + 1) * SHARE
                ]
        back_copy(turn).start()

    @pl.when(step == 2 * chunks - 1)
    def _():
        unit, inverse = norm_parts(before[...])
        back, gain, bias = norm_back(unit, inverse, table_ref[1:2], total[...])
        grad_second_ref[...] = back
        sums_ref[3:4] = row_sum(back)
        sums_ref[4:5] = gain
        sums_ref[5:6] = bias
        sums_ref[6:8] = jnp.zeros((2, width), jnp.float32)
        back_b = back.astype(BF)
        grads = row_dot(back_b, out_weight_ref[...]).astype(BF)
        for head in range(heads):
            lanes = slice(head * HEAD_DIM, (head + 1) * HEAD_DIM)
            grad_heads_ref[head] = jnp.concatenate([grads[:half, lanes], grads[half:, lanes]], axis=1)
        for head in range(heads, RING):
            grad_heads_ref[head] = jnp.zeros_like(grad_heads_ref[head])
        product = over_rows_dot(attended[...], back_b).astype(BF)
        for share in range(shares):
            for place in range(width // SHARE):
                out_part_ref[share, place * in_rows : (place + 1) * in_rows, :] = product[
                    share * in_rows : (share + 1) * in_rows, place * SHARE : (place + 1) * SHARE
                ]

        def finish(at, carry):
            in_copy(at).wait()
            back_copy(at).wait()
            return carry

        lax.fori_loop(0, chunks, finish, 0)


def middle(heads, hidden, table, out_weight, ffn_in, in_bias, ffn_out, out_grad, count):
    rows, width = hidden.shape
    inner = ffn_in.shape[1]
    chunk = SHARE
    chunks = inner // chunk
    own = lambda shape: pl.BlockSpec(shape, lambda step: (0,) * len(shape))
    outs = [
        like((rows, width), BF),
        like((RING, rows // 2, 2 * HEAD_DIM), BF),
        like((rows, width)),
        like((count, width // count * width // SHARE, SHARE), BF),
        like((8, width)),
        like((1, inner)),
        like((count, 2 * width // count * inner // SHARE, SHARE), BF),
    ]
    args = (heads, hidden, table, out_weight, ffn_in, in_bias, ffn_out, out_grad)
    in_specs = [own(a.shape) for a in args]
    in_specs[4] = pl.BlockSpec((width, chunk), lambda step: (0, step % chunks))
    in_specs[6] = pl.BlockSpec((chunk, width), lambda step: (step % chunks, 0))
    out_specs = [own(o.shape) for o in outs]
    out_specs[6] = pl.BlockSpec(memory_space=pl.ANY)
    scratch = [
        pltpu.VMEM((rows, width), BF),
        pltpu.VMEM((rows, width), jnp.float32),
        pltpu.VMEM((rows, width), jnp.float32),
        pltpu.VMEM((rows, width), BF),
        pltpu.VMEM((width, rows), BF),
        pltpu.VMEM((chunks, rows, chunk), BF),
        pltpu.VMEM((chunks, rows, chunk), jnp.float32),
        pltpu.VMEM((rows, width), jnp.float32),
        pltpu.VMEM((rows, width), jnp.float32),
        pltpu.VMEM((rows, width), BF),
        pltpu.VMEM(outs[6].shape, BF),
        pltpu.SemaphoreType.DMA((2, chunks)),
    ]
    return call(
        middle_kernel, outs, scratch, args, "middle", 2 * 10**10, (2 * chunks,), in_specs, tuple(out_specs)
    )


def after_heads_kernel(
    packed_ref, grad_second_ref, hidden_ref, conv_ref, start_ref, table_ref, weight_ref, out_part_ref,
    mixed_ref, conv_b_ref, groups_ref, joined_ref, sums_ref, grads,
):
    rows, width = hidden_ref.shape
    half = rows // 2
    heads = width // HEAD_DIM
    shares = joined_ref.shape[0]
    own_rows = width // shares
    for head in range(heads):
        tile = packed_ref[head]
        for part in range(3):
            lanes = slice(part * width + head * HEAD_DIM, part * width + (head + 1) * HEAD_DIM)
            grads[:half, lanes] = tile[:, part * HEAD_DIM : (part + 1) * HEAD_DIM]
            grads[half:, lanes] = tile[:, (part + 3) * HEAD_DIM : (part + 4) * HEAD_DIM]
    hidden_t = hidden_ref[...].T.astype(BF)
    blocks = 3 * width // SHARE
    for place in range(blocks):
        lanes = slice(place * SHARE, (place + 1) * SHARE)
        product = plain_dot(hidden_t, grads[:, lanes]).astype(BF)
        for share in range(shares):
            joined_ref[share, place * own_rows : (place + 1) * own_rows, :] = product[
                share * own_rows : (share + 1) * own_rows
            ]
    for share in range(shares):
        joined_ref[share, blocks * own_rows :, :] = out_part_ref[share]
    back = grad_second_ref[...] + row_dot(grads[...], weight_ref[...])
    value, slope = gelu_both(conv_ref[...] + table_ref[4:5])
    unit, inverse = norm_parts(start_ref[...] + value)
    mixed, gain, bias = norm_back(unit, inverse, table_ref[0:1], back)
    mixed_ref[...] = mixed
    conv = mixed * slope
    conv_b = conv.astype(BF)
    conv_b_ref[...] = conv_b
    store_turned(start_ref[...].astype(BF), groups_ref, 0)
    store_turned(conv_b, groups_ref, width // GROUPS)
    sums_ref[0:1] = gain
    sums_ref[1:2] = bias
    sums_ref[2:3] = row_sum(conv)
    sums_ref[3:4] = row_sum(grads[:, :width].astype(jnp.float32))
    sums_ref[4:5] = row_sum(grads[:, 2 * width :].astype(jnp.float32))
    sums_ref[5:8] = jnp.zeros((3, width), jnp.float32)


def after_heads(packed, grad_second, hidden, conv_sum, start, table, weight, out_part):
    rows, width = hidden.shape
    shares = out_part.shape[0]
    return call(
        after_heads_kernel,
        [
            like((rows, width)), like((rows, width), BF),
            like((GROUPS, 2 * width // GROUPS, rows), BF),
            like((shares, out_part.shape[1] + width // shares * 3 * width // SHARE, SHARE), BF),
            like((8, width)),
        ],
        [pltpu.VMEM((rows, 3 * width), BF)],
        (packed, grad_second, hidden, conv_sum, start, table, weight, out_part),
        "after_heads",
        6 * 10**9,
    )


def stem_back_kernel(
    clips, marks, input_ref, mixed_ref, normed_ref, pre_ref, unfold_ref, weight_ref, gain_ref, proj_ref,
    middle_sums_ref, inner_sums_ref, after_sums_ref,
    samples_ref, carried_ref, joined_ref, table, spread, woven,
):
    rows, chans = pre_ref.shape
    width = input_ref.shape[1]
    shares = joined_ref.shape[0] * joined_ref.shape[1]
    start = mixed_ref[...] + input_ref[...]
    start_b = start.astype(BF)

    def share_out(product, begin):
        own, columns = product.shape[0] // shares, product.shape[1]
        for share in range(shares):
            for place in range(columns // PIECE):
                at = begin + place * own
                row, column = pair_slot(joined_ref.shape, share, marks, clips)
                joined_ref[row, column, at : at + own, :] = product[
                    share * own : (share + 1) * own, place * PIECE : (place + 1) * PIECE
                ]
        return begin + own * columns // PIECE

    at = share_out(over_rows_dot(normed_ref[...], start_b).astype(BF), 0)
    value, slope = gelu_both(pre_ref[...])
    unit, inverse = norm_parts(value)
    feature, gain_sum, bias_sum = norm_back(
        unit, inverse, gain_ref[...], row_dot(start_b, proj_ref[...])
    )
    pre_b = (feature * slope).astype(BF)
    taps_t = over_rows_dot(unfold_ref[...], pre_b).astype(BF)
    at = share_out(taps_t, at)
    first = row_dot(pre_b, weight_ref[:chans])
    same = same_clip_next(marks, clips, rows)
    follow = jnp.where(same, row_dot(pre_b, weight_ref[2 * chans :]), 0.0)
    carried_ref[...] = follow[rows - 1 :]
    moved = pltpu.roll(follow, 1, 0)
    top = lax.broadcasted_iota(jnp.int32, (rows, 1), 0) == 0
    even = first + jnp.where(top, 0.0, moved)
    odd = row_dot(pre_b, weight_ref[chans : 2 * chans])
    for lane in range(0, chans, PIECE):
        woven[pl.ds(0, rows, stride=2), :] = even[:, lane : lane + PIECE]
        woven[pl.ds(1, rows, stride=2), :] = odd[:, lane : lane + PIECE]
        samples_ref[:, lane : lane + PIECE] = woven[...]
    table[0:1] = after_sums_ref[0:1]
    table[1:2] = middle_sums_ref[4:5]
    table[2:3] = middle_sums_ref[0:1]
    table[3:4] = row_sum(start)
    table[4:5] = after_sums_ref[2:3]
    table[5:6] = after_sums_ref[1:2]
    table[6:7] = after_sums_ref[3:4]
    table[7:8] = after_sums_ref[4:5]
    table[8:9] = middle_sums_ref[3:4]
    table[9:10] = middle_sums_ref[5:6]
    table[10:11] = middle_sums_ref[2:3]
    table[11:12] = middle_sums_ref[1:2]
    spread[...] = jnp.zeros_like(spread)
    own, own_chans = width // shares, chans // shares
    own_inner = inner_sums_ref.shape[1] // shares
    for share in range(shares):
        spread[share, 0:12, 0:own] = table[:, share * own : (share + 1) * own]
        for place in range(-(-own_inner // PIECE)):
            length = min(PIECE, own_inner - place * PIECE)
            begin = share * own_inner + place * PIECE
            spread[share, 12 + place : 13 + place, 0:length] = inner_sums_ref[:, begin : begin + length]
        lanes = slice(share * own_chans, (share + 1) * own_chans)
        spread[share, 14:15, 0:own_chans] = gain_sum[:, lanes]
        spread[share, 15:16, 0:own_chans] = bias_sum[:, lanes]
        row, column = pair_slot(joined_ref.shape, share, marks, clips)
        joined_ref[row, column, at:, :] = spread[share].astype(BF)


def stem_back(marks, input_grad, mixed, normed, pre, unfold, weight, gain, proj, sums, shares, clips):
    rows, chans = pre.shape
    width = input_grad.shape[1]
    pieces = (chans // RING * width + 3 * chans // RING * chans) // PIECE + 16
    return call(
        functools.partial(stem_back_kernel, clips),
        [like((2 * rows, chans)), like((1, chans)), like(shares + (pieces, PIECE), BF)],
        [pltpu.VMEM((12, width), jnp.float32), pltpu.VMEM((RING, 16, PIECE), jnp.float32),
         pltpu.VMEM((2 * rows, PIECE), jnp.float32)],
        (marks, input_grad, mixed, normed, pre, unfold, weight, gain, proj) + sums,
        "stem_back",
        6 * 10**9,
    )


def from_behind(value, axis, steps):
    count = lax.axis_size(axis)
    initial, last = (max(0, -steps), min(count, count - steps))
    return lax.ppermute(value, axis, [(source, source + steps) for source in range(initial, last)])


def edges(value, width):
    length = value.shape[0]
    return from_behind(value[length - width :], "seq", 1), from_behind(value[:width], "seq", -1)


def near_groups():
    size = lax.axis_size("seq")
    return [[base + i for i in range(RING)] for base in range(0, size, RING)]


def swap(value):
    groups = None if lax.axis_size("seq") == RING else near_groups()
    return lax.all_to_all(value, "seq", 0, 0, axis_index_groups=groups)


def with_far_blocks(value, count):
    if lax.axis_size("seq") == RING or count == 0:
        return value
    before = from_behind(value[value.shape[0] - count :], "seq", RING)
    after = from_behind(value[:count], "seq", -RING)
    return jnp.concatenate([before, value, after], axis=0)


def fold_far_blocks(value, count):
    if lax.axis_size("seq") == RING or count == 0:
        return value
    own = value[count : value.shape[0] - count]
    to_before = from_behind(value[:count], "seq", -RING)
    to_after = from_behind(value[value.shape[0] - count :], "seq", RING)
    wide = own.astype(jnp.float32)
    wide = wide.at[wide.shape[0] - count :].add(to_before.astype(jnp.float32))
    wide = wide.at[:count].add(to_after.astype(jnp.float32))
    return wide.astype(value.dtype)


def other_stream(share):
    return lax.ppermute(share, "rep", [(0, 1), (1, 0)])


def sum_pair(share):
    return share.astype(jnp.float32) + other_stream(share).astype(jnp.float32)


def spread_out(total, sizes, lanes):
    out, at = [], 0
    for rows, columns in sizes:
        parts = []
        for _ in range(columns // lanes):
            parts.append(total[at : at + rows])
            at += rows
        out.append(jnp.concatenate(parts, axis=1))
    return out


def regroup(joined, blocks):
    count = lax.axis_size("seq")
    if count == RING:
        return joined
    parts = count // RING
    lanes = joined.shape[2]
    out, at = [], 0
    for number, rows in blocks:
        piece = joined[:, at : at + number * rows]
        at += number * rows
        piece = piece.reshape(RING, number, parts, rows // parts, lanes).transpose(0, 2, 1, 3, 4)
        out.append(piece.reshape(count, number * rows // parts, lanes))
    return jnp.concatenate(out, axis=1)


def regroup_small(small, widths):
    count = lax.axis_size("seq")
    if count == RING:
        return small
    parts = count // RING
    own, own_inner, own_chans = widths
    lanes = small.shape[2]
    table = small[:, :12, : own * parts].reshape(RING, 12, parts, own).transpose(0, 2, 1, 3)
    table = jnp.pad(table.reshape(count, 12, own), ((0, 0), (0, 0), (0, lanes - own)))
    wide = small[:, 12:14].reshape(RING, 2 * lanes)[:, : own_inner * parts].reshape(count, own_inner)
    wide = jnp.pad(wide, ((0, 0), (0, 2 * lanes - own_inner))).reshape(count, 2, lanes)
    stems = small[:, 14:16, : own_chans * parts].reshape(RING, 2, parts, own_chans).transpose(0, 2, 1, 3)
    stems = jnp.pad(stems.reshape(count, 2, own_chans), ((0, 0), (0, 0), (0, lanes - own_chans)))
    return jnp.concatenate([table, wide, stems], axis=1)


def over_seq(joined):
    return lax.psum_scatter(joined, "seq", scatter_dimension=0, tiled=False).astype(jnp.bfloat16)


def local(
    samples,
    clip_lengths,
    stem_weight,
    stem_gain,
    stem_bias,
    proj_weight,
    pos_weight,
    norm_gains,
    biases,
    attn_in,
    attn_out,
    ffn_in,
    ffn_in_bias,
    ffn_out,
    out_grad,
):
    rows_dev = out_grad.shape[1]
    width = attn_out.shape[0]
    chans = stem_weight.shape[1]
    inner = ffn_in.shape[1]
    group_width = width // GROUPS
    count = lax.axis_size("seq")
    place = lax.axis_index("seq")
    total = rows_dev * count
    begin = place * rows_dev
    ends = jnp.cumsum(clip_lengths[0])
    clips = ends.shape[0]
    half = KERNEL // 2
    far = 0 if count == RING else -(-MAXLEN // rows_dev)
    segment_begin = (place // RING) * RING * rows_dev
    active = jnp.where(place % RING < HEADS, 1, 0)
    marks = jnp.concatenate(
        [ends, jnp.stack([jnp.int32(total), begin, segment_begin, segment_begin - far * rows_dev, active, place % 2])]
    ).astype(jnp.int32)
    next_row = from_behind(samples[0, :1], "seq", -1)
    one_weights = conv_weights(False, pos_weight, 0, TURNS // 2)
    next_row, one_weights = lax.optimization_barrier((next_row, one_weights))
    start_x, start_b, stem_pre, normed_b, unfold, table = stem(
        marks, samples[0], next_row, stem_weight, stem_gain[None], stem_bias[None], proj_weight,
        norm_gains.T, biases.T, clips,
    )
    before, after = edges(start_b, half)
    rest_source, _ = lax.optimization_barrier((pos_weight, table))
    rest_weights = conv_weights(False, rest_source, TURNS // 2, TURNS // 2)
    before, after, rest_weights = lax.optimization_barrier((before, after, rest_weights))
    conv_sum = conv_rows(False, marks, before, start_b, after, (one_weights, rest_weights), clips)
    hidden, packed = project_heads(conv_sum, start_x, table, attn_in)
    back_source, _ = lax.optimization_barrier((pos_weight, hidden))
    packed = with_far_blocks(swap(packed), far)
    back_weights = conv_weights(True, back_source, 0, TURNS)
    packed, back_weights = lax.optimization_barrier((packed, back_weights))
    attended_heads, wide, log_total = attend(marks, packed, clips, far)
    layer_out, grad_heads, grad_pre_second, out_part, middle_sums, inner_sums, ffn_joined = middle(
        swap(attended_heads), hidden, table, attn_out, ffn_in, ffn_in_bias[None], ffn_out, out_grad[0],
        RING,
    )
    near_rows, near_chans, near_inner = width // RING, chans // RING, inner // RING
    grad_heads = swap(grad_heads)
    ffn_share = over_seq(
        regroup(ffn_joined, [(inner // SHARE, near_rows), (width // SHARE, near_inner)])
    )
    packed_grad = attend_back(marks, packed, grad_heads, wide, log_total, clips, far)
    grad_mixed, grad_conv_b, grad_packed, attn_joined, after_sums = after_heads(
        swap(fold_far_blocks(packed_grad, far)), grad_pre_second, hidden, conv_sum, start_x, table,
        attn_in, out_part,
    )
    before, after = edges(grad_conv_b, half)
    before, after, grad_packed = lax.optimization_barrier((before, after, grad_packed))
    grad_groups = swap(grad_packed)
    input_grad = conv_rows(True, marks, before, grad_conv_b, after, (back_weights,), clips)
    input_grad, grad_groups, ffn_share = lax.optimization_barrier((input_grad, grad_groups, ffn_share))
    attn_share = over_seq(regroup(attn_joined, [(4 * width // SHARE, near_rows)]))
    shape = (2, RING // 2) if count == RING else (1, RING)
    sample_grad, carried, stem_joined = stem_back(
        marks, input_grad, grad_mixed, normed_b, stem_pre, unfold, stem_weight, stem_gain[None],
        proj_weight, (middle_sums, inner_sums, after_sums), shape, clips,
    )
    carried = from_behind(carried, "seq", 1)
    own = width // count
    own_chans = chans // count
    own_taps = KERNEL // count
    below = stem_joined.shape[2]
    grad_ffn = spread_out(sum_pair(ffn_share), [(own, inner), (inner // count, width)], SHARE)
    stem_joined, grad_ffn, grad_groups = lax.optimization_barrier((stem_joined, grad_ffn, grad_groups))
    taps = taps_grad(marks, with_far_blocks(grad_groups, 0 if count == RING else 1), shape, clips)
    if count == RING:
        pairs = [(i, i ^ 1) for i in range(count)]
        joined = join_pair(
            marks,
            stem_joined,
            lax.ppermute(stem_joined[1], "seq", pairs),
            taps,
            lax.ppermute(taps[1], "seq", pairs),
            clips,
        )
        alike = [list(range(core, count, 2)) for core in range(2)]
        received = lax.all_to_all(joined, "seq", 0, 0, axis_index_groups=alike)
        pos_pieces = received[:, below:].reshape(GROUPS, -1, PIECE)
    else:
        stem_joined = stem_joined[0]
        stem_joined = jnp.concatenate(
            [
                regroup(
                    stem_joined[:, :-16],
                    [(width // PIECE, near_chans), (chans // PIECE, 3 * near_chans)],
                ),
                regroup_small(stem_joined[:, -16:], (own, inner // count, own_chans)),
            ],
            axis=1,
        )
        received = lax.all_to_all(stem_joined, "seq", 0, 0)
        below = stem_joined.shape[1]
        segments = count // RING
        by_tap = taps.reshape(2 * TURNS, 3, group_width, PIECE).transpose(0, 2, 1, 3)
        by_tap = by_tap.reshape(2 * TURNS, group_width, TAPS // 2, group_width)
        by_tap = by_tap.transpose(0, 2, 1, 3).reshape(segments, -1, 2 * PIECE)
        across = [[low_at + RING * j for j in range(segments)] for low_at in range(RING)]
        by_tap = lax.all_to_all(by_tap, "seq", 0, 0, axis_index_groups=across)
        by_tap = jnp.sum(by_tap.astype(jnp.float32), axis=0).astype(jnp.bfloat16)
        by_tap = by_tap.reshape(RING, own_taps, group_width, group_width).transpose(0, 2, 1, 3)
        pos_pieces = swap(by_tap.reshape(RING, group_width, own_taps * group_width))
    pos_grad = weave_taps(pos_pieces, other_stream(pos_pieces), own_taps, group_width)
    stem_total = sum_pair(jnp.sum(received[:, :below].astype(jnp.float32), axis=0).astype(jnp.bfloat16))
    grad_proj, grad_stem = spread_out(
        stem_total[:-16], [(own_chans, width), (3 * own_chans, chans)], PIECE
    )
    small = stem_total[-16:]
    grad_ffn_in, grad_ffn_out = grad_ffn
    grad_attn_in, grad_attn_out = spread_out(
        sum_pair(attn_share), [(own, 3 * width), (own, width)], SHARE
    )
    sample_grad = sample_grad.at[:1].add(carried)
    return (
        layer_out[None],
        sample_grad[None],
        grad_stem,
        small[14, :own_chans],
        small[15, :own_chans],
        grad_proj,
        pos_grad,
        small[:3, :own].T,
        small[3:12, :own].T,
        grad_attn_in,
        grad_attn_out,
        grad_ffn_in,
        small[12:14].reshape(-1)[: inner // count],
        grad_ffn_out,
    )


def solution(mesh):
    streams = P("rep", "seq", None)
    rows = P("seq", None)
    return jax.shard_map(
        local,
        mesh=mesh,
        in_specs=(streams, P("rep", None)) + (P(),) * 12 + (streams,),
        out_specs=(streams, streams, rows, P("seq"), P("seq"))
        + (rows,) * 7
        + (P("seq"), rows),
        check_vma=False,
    )
```

time: 515 us -> 452 us (0.88)
  Pallas kernels: 203 us -> 186 us
  local copies, waits for them, and re-layouts: 32.9 us -> 16.8 us
  other arithmetic: 15.5 us -> 5.15 us
  waiting for transfers between devices: 102 us -> 93.4 us
  starting transfers between devices: 47.5 us -> 41.5 us
    ppermute x6, waiting for transfers between devices: 61.9 us -> 9.78 us  [from_behind(): lax.ppermute(value, axis, [(source, source + steps) for source in range(i...]
    ppermute x4 -> x6, waiting for transfers between devices: 4.8 us -> 22.6 us  [the longest x4 21.3 us: other_stream(): return lax.ppermute(share, 'rep', [(0, 1), (1, 0)])]
    pallas_call x12 -> x15, Pallas kernels: 203 us -> 186 us  [call(): pl.pallas_call(kernel, out_shape=tuple(outs), in_specs=in_specs or [SMEM_...]
    all_to_all x1, waiting for transfers between devices: 0.01 us -> 10.6 us  [local(): received = lax.all_to_all(joined, 'seq', 0, 0, axis_index_groups=alike)]
    all_to_all x4 -> x2, waiting for transfers between devices: 15 us -> 23.8 us  [swap(): return lax.all_to_all(value, 'seq', 0, 0, axis_index_groups=groups)]
    all_to_all x4 -> x2, starting transfers between devices: 19.2 us -> 11 us  [swap(): return lax.all_to_all(value, 'seq', 0, 0, axis_index_groups=groups)]
    reshape x2 -> x0, local copies, waits for them, and re-layouts: 6.09 us -> none  [the longest x1 3.6 us: local(): pos_total.transpose(2, 1, 0, 3).reshape(own_taps * group_width, width)]
    reduce_scatter x2, waiting for transfers between devices: 20.4 us -> 26.2 us  [over_seq(): lax.psum_scatter(joined, 'seq', scatter_dimension=0, tiled=False)]
  transfers between devices with their start and end apart: 17 -> 17, of which waited for: 7 -> 10; matrix products, arithmetic and copies ran while one was open for 8% -> 3% of each run, Pallas kernels for 28% -> 24%
where the time goes in v3:
time: 452 us; the launch traced here: 445 us
  Pallas kernels  186 us (41%)
  waiting for transfers between devices  93.4 us (21%)
  blocking collectives  87.4 us (19%)
  starting transfers between devices  41.5 us (9%)
  local copies, waits for them, and re-layouts  16.8 us (4%)
  between operations  14.5 us (3%)
  other arithmetic  5.15 us (1%)
    pallas_call x15, Pallas kernels, call(): pl.pallas_call(kernel, out_shape=tuple(outs), in_specs=in_specs or [SMEM_...  186 us
    all_to_all x3, blocking collectives, swap(): return lax.all_to_all(value, 'seq', 0, 0, axis_index_groups=groups)  87.4 us
    reduce_scatter x2, waiting for transfers between devices, over_seq(): lax.psum_scatter(joined, 'seq', scatter_dimension=0, tiled=False)  26.2 us
    all_to_all x2, waiting for transfers between devices, swap(): return lax.all_to_all(value, 'seq', 0, 0, axis_index_groups=groups)  23.8 us
    ppermute x4, waiting for transfers between devices, other_stream(): return lax.ppermute(share, 'rep', [(0, 1), (1, 0)])  21.3 us
    ppermute x6, starting transfers between devices, from_behind(): lax.ppermute(value, axis, [(source, source + steps) for source in range(i...  14.1 us
    all_to_all x2, starting transfers between devices, swap(): return lax.all_to_all(value, 'seq', 0, 0, axis_index_groups=groups)  11 us
    all_to_all x1, waiting for transfers between devices, local(): received = lax.all_to_all(joined, 'seq', 0, 0, axis_index_groups=alike)  10.6 us
  transfers between devices with their start and end apart: 17, of which 10 were waited for; matrix products, arithmetic and copies ran while one was open for 3% of the time, Pallas kernels for 24%

profile of v3, /device:TPU:16, one launch (start us, length us, event | category | flops | bytes accessed | tf_op | source)
XLA Modules:
  0.0 445.1 jit_solution(17824814494799231920)
XLA Ops:
  11.5 5.6 %conv_weights.2.refs_0_ = bf16[16,192,768]{2,1,0:T(8,128)(2,1)} custom-call(bf16[6144,768]{1,0:T(8,128)(2,1)} %weight_ref.9), custom_call_target="tpu_custom_call" | custom-call | bytes 14155776 | tf_op jit(solution)/shard_map/conv_weights/pallas_call | solution.py:69
  28.5 5.7 %conv_weights.3.refs_1_ = bf16[16,192,768]{2,1,0:T(8,128)(2,1)} custom-call(bf16[6144,768]{1,0:T(8,128)(2,1)} %weight_ref.9), custom_call_target="tpu_custom_call" | custom-call | bytes 14155776 | tf_op jit(solution)/shard_map/conv_weights/pallas_call | solution.py:69
  34.2 16.1 %conv.1.conv_ref = f32[256,768]{1,0:T(8,128)S(1)} custom-call(s32[10]{0:T(128)S(1)} %copy-done.2, bf16[64,768]{1,0:T(8,128)(2,1)S(1)} %collective-permute-done.1.before_ref, bf16[256,768]{1,0:T(8,128)(2,1)S(1)} %copy-done.1, bf16[64,768]{1,0:T(8,128)(2,1)S(1)} %collective-permute-done.2.after_ref, bf16[16,192,768]{2,1,0:T(8,128)(2,1)S(1)} %bitcast.39, ...), custom_call_target="tpu_custom_call" | custom-call | flops 15000000512 | bytes 10813480 | tf_op jit(solution)/shard_map/conv/pallas_call | solution.py:69
  51.1 5.2 %project_heads.1 = (f32[256,768]{1,0:T(8,128)}, bf16[16,128,384]{2,1,0:T(8,128)(2,1)}) custom-call(f32[256,768]{1,0:T(8,128)} %copy-done.4, f32[256,768]{1,0:T(8,128)} %get-tuple-element.79.start_ref, f32[12,768]{1,0:T(8,128)} %get-tuple-element.73.table_ref, bf16[768,2304]{1,0:T(8,128)(2,1)} %weight_ref.10), custom_call_target="tpu_custom_call" | custom-call | flops 6000000000 | bytes 7507968 | tf_op jit(solution)/shard_map/project_heads/pallas_call | solution.py:69
  56.3 6.8 %all-to-all-start = ((bf16[16,128,384]{2,1,0:T(8,128)(2,1)}), bf16[16,128,384]{2,1,0:T(8,128)(2,1)S(1)}, u32[]{:S(2)}, u32[]{:S(2)}) async-start(bf16[16,128,384]{2,1,0:T(8,128)(2,1)} %get-tuple-element.80), calls=%async_computation | async-start | bytes 3145728 | tf_op jit(solution)/shard_map/all_to_all | solution.py:1014
  63.1 12.5 %conv_weights_back.1.refs_0_ = bf16[16,384,768]{2,1,0:T(8,128)(2,1)} custom-call(bf16[6144,768]{1,0:T(8,128)(2,1)} %weight_ref.9), custom_call_target="tpu_custom_call" | custom-call | bytes 18874368 | tf_op jit(solution)/shard_map/conv_weights_back/pallas_call | solution.py:69
  75.6 23.8 %all-to-all-done.packed_ref = bf16[16,128,384]{2,1,0:T(8,128)(2,1)S(1)} async-done(((bf16[16,128,384]{2,1,0:T(8,128)(2,1)}), bf16[16,128,384]{2,1,0:T(8,128)(2,1)S(1)}, u32[]{:S(2)}, u32[]{:S(2)}) %all-to-all-start) | async-done | bytes 1572896 | tf_op jit(solution)/shard_map/all_to_all | solution.py:1014
  100.7 24.1 %attend.1 = (bf16[16,128,128]{2,1,0:T(8,128)(2,1)}, f32[64,4096]{1,0:T(8,128)}, f32[1,4096]{1,0:T(1,128)}) custom-call(s32[10]{0:T(128)} %concatenate.23.marks, bf16[16,128,384]{2,1,0:T(8,128)(2,1)} %copy-done.8), custom_call_target="tpu_custom_call" | custom-call | flops 24999999488 | bytes 3162152 | tf_op jit(solution)/shard_map/attend/pallas_call | solution.py:69
  124.8 18.2 %all_to_all.30.heads_ref = bf16[16,128,128]{2,1,0:T(8,128)(2,1)} all-to-all(bf16[16,128,128]{2,1,0:T(8,128)(2,1)} %get-tuple-element.84), channel_id=1, replica_groups=mesh['rep'=2,'seq'=16] {'seq'}, dimensions={0} | all-to-all | bytes 1048576 | tf_op jit(solution)/shard_map/all_to_all | solution.py:1014
  143.0 25.3 %middle.1 = (bf16[256,768]{1,0:T(8,128)(2,1)}, bf16[16,128,128]{2,1,0:T(8,128)(2,1)}, f32[256,768]{1,0:T(8,128)}, bf16[16,96,384]{2,1,0:T(8,128)(2,1)}, f32[8,76...) custom-call(bf16[16,128,128]{2,1,0:T(8,128)(2,1)} %all_to_all.30.heads_ref, ...), custom_call_target="tpu_custom_call" | custom-call | flops 20000000000 | bytes 24727552 | tf_op jit(solution)/shard_map/middle/pallas_call | solution.py:69
  169.3 18.5 %all_to_all.31.grad_ref = bf16[16,128,128]{2,1,0:T(8,128)(2,1)} all-to-all(bf16[16,128,128]{2,1,0:T(8,128)(2,1)S(1)} %copy-done.13), channel_id=1, replica_groups=mesh['rep'=2,'seq'=16] {'seq'}, dimensions={0} | all-to-all | bytes 1048576 | tf_op jit(solution)/shard_map/all_to_all | solution.py:1014
  187.8 35.0 %attend_back.1 = bf16[16,128,384]{2,1,0:T(8,128)(2,1)} custom-call(s32[10]{0:T(128)} %concatenate.23.marks, bf16[16,128,384]{2,1,0:T(8,128)(2,1)} %copy-done.8, bf16[16,128,128]{2,1,0:T(8,128)(2,1)} %all_to_all.31.grad_ref, f32[64,4096]{1,0:T(8,128)} %get-tuple-element.87.wide_ref, f32[1,4096]{1,0:T(1,128)} %get-tuple-element.88.log_ref), custom_call_target="tpu_custom_call" | custom-call | flops 35000000512 | bytes 4735016 | tf_op jit(solution)/shard_map/attend_back/pallas_call | solution.py:69
  222.7 50.8 %all_to_all.32.packed_ref = bf16[16,128,384]{2,1,0:T(8,128)(2,1)} all-to-all(bf16[16,128,384]{2,1,0:T(8,128)(2,1)} %attend_back.1), channel_id=1, replica_groups=mesh['rep'=2,'seq'=16] {'seq'}, dimensions={0} | all-to-all | bytes 3145728 | tf_op jit(solution)/shard_map/all_to_all | solution.py:1014
  273.5 9.8 %after_heads.1 = (f32[256,768]{1,0:T(8,128)}, bf16[256,768]{1,0:T(8,128)(2,1)}, bf16[16,96,256]{2,1,0:T(8,128)(2,1)}, bf16[16,384,384]{2,1,0:T(8,128)(2,1)}, f32[8,768]{1,0:T(8,128)}) custom-call(bf16[16,128,384]{2,1,0:T(8,128)(2,1)} %all_to_all.32.packed_ref, f32[256,768]{1,0:T(8,128)} %get-tuple-element.89.grad_second_ref, ...), custom_call_target="tpu_custom_call" | custom-call | flops 6000000000 | bytes 16183296 | tf_op jit(solution)/shard_map/after_heads/pallas_call | solution.py:69
  293.5 5.4 %collective-permute-done.3.before_ref = bf16[64,768]{1,0:T(8,128)(2,1)S(1)} collective-permute-done((bf16[64,768]{1,0:T(8,128)(2,1)S(1)}, bf16[64,768]{1,0:T(8,128)(2,1)S(1)}, u32[]{:S(2)}, u32[]{:S(2)}) %collective-permute-start.3) | collective-permute-done | bytes 98336 | tf_op jit(solution)/shard_map/ppermute | solution.py:999
  304.4 19.2 %conv_back.1.input_ref = f32[256,768]{1,0:T(8,128)S(1)} custom-call(s32[10]{0:T(128)S(1)} %copy-done.3, bf16[64,768]{1,0:T(8,128)(2,1)S(1)} %collective-permute-done.3.before_ref, bf16[256,768]{1,0:T(8,128)(2,1)S(1)} %copy-done, bf16[64,768]{1,0:T(8,128)(2,1)S(1)} %collective-permute-done.4.after_ref, bf16[16,384,768]{2,1,0:T(8,128)(2,1)} %conv_weights_back.1.refs_0_), custom_call_target="tpu_custom_call" | custom-call | flops 15000000512 | bytes 10813480 | tf_op jit(solution)/shard_map/conv_back/pallas_call | solution.py:69
  328.4 6.2 %stem_back.1 = (f32[512,512]{1,0:T(8,128)}, f32[1,512]{1,0:T(1,128)}, bf16[2,8,592,128]{3,2,1,0:T(8,128)(2,1)}) custom-call(s32[10]{0:T(128)} %concatenate.23.marks, f32[256,768]{1,0:T(8,128)} %copy-done.5, f32[256,768]{1,0:T(8,128)} %get-tuple-element.99.mixed_ref, bf16[256,512]{1,0:T(8,128)(2,1)} %get-tuple-element.100.normed_ref, ...), custom_call_target="tpu_custom_call" | custom-call | flops 6000000000 | bytes 9044008 | tf_op jit(solution)/shard_map/stem_back/pallas_call | solution.py:69
  334.6 5.5 %collective-permute-done.6 = bf16[768,384]{1,0:T(8,128)(2,1)S(1)} collective-permute-done((bf16[768,384]{1,0:T(8,128)(2,1)}, bf16[768,384]{1,0:T(8,128)(2,1)S(1)}, u32[]{:S(2)}, u32[]{:S(2)}) %collective-permute-start.6) | collective-permute-done | bytes 589856 | tf_op jit(solution)/shard_map/ppermute | solution.py:1038
  342.3 10.0 %taps_grad.1.taps_ref = bf16[2,8,144,128]{3,2,1,0:T(8,128)(2,1)} custom-call(s32[10]{0:T(128)} %concatenate.23.marks, bf16[16,96,256]{2,1,0:T(8,128)(2,1)} %copy-done.10), custom_call_target="tpu_custom_call" | custom-call | flops 10000000000 | bytes 1376296 | tf_op jit(solution)/shard_map/taps_grad/pallas_call | solution.py:69
  360.7 6.1 %all-to-all-start.5 = ((bf16[8,880,128]{2,1,0:T(8,128)(2,1)}), bf16[8,880,128]{2,1,0:T(8,128)(2,1)S(1)}, u32[]{:S(2)}, u32[]{:S(2)}) async-start(bf16[8,880,128]{2,1,0:T(8,128)(2,1)} %join_pair.1), calls=%async_computation.6 | async-start | bytes 3604480 | tf_op jit(solution)/shard_map/all_to_all | solution.py:1188
  366.8 26.2 %reduce-scatter.5.cloned.1.call-done = bf16[1,384,384]{2,1,0:T(8,128)(2,1)} async-done(((bf16[16,384,384]{2,1,0:T(8,128)(2,1)}), bf16[1,384,384]{2,1,0:T(8,128)(2,1)}) %reduce-scatter.5.cloned.1.call-update) | async-done | bytes 294928 | tf_op jit(solution)/shard_map/reduce_scatter | solution.py:1088
  395.6 5.5 %collective-permute-done.11 = bf16[384,384]{1,0:T(8,128)(2,1)S(1)} collective-permute-done((bf16[384,384]{1,0:T(8,128)(2,1)}, bf16[384,384]{1,0:T(8,128)(2,1)S(1)}, u32[]{:S(2)}, u32[]{:S(2)}) %collective-permute-start.11) | collective-permute-done | bytes 294944 | tf_op jit(solution)/shard_map/ppermute | solution.py:1038
  404.9 10.6 %all-to-all-done.5 = bf16[8,880,128]{2,1,0:T(8,128)(2,1)S(1)} async-done(((bf16[8,880,128]{2,1,0:T(8,128)(2,1)}), bf16[8,880,128]{2,1,0:T(8,128)(2,1)S(1)}, u32[]{:S(2)}, u32[]{:S(2)}) %all-to-all-start.5) | async-done | bytes 1802272 | tf_op jit(solution)/shard_map/all_to_all | solution.py:1188
  424.5 9.7 %collective-permute-done.10.other_ref = bf16[16,144,128]{2,1,0:T(8,128)(2,1)S(1)} collective-permute-done((bf16[16,144,128]{2,1,0:T(8,128)(2,1)S(1)}, bf16[16,144,128]{2,1,0:T(8,128)(2,1)S(1)}, u32[]{:S(2)}, u32[]{:S(2)}) %collective-permute-start.10) | collective-permute-done | bytes 589856 | tf_op jit(solution)/shard_map/ppermute | solution.py:1038
  (118 shorter events, 68.9 us)
Async XLA Ops:
  7.9 9.8 %collective-permute-start = (bf16[1,512]{1,0:T(2,128)(2,1)S(1)}, bf16[1,512]{1,0:T(2,128)(2,1)S(1)}, u32[]{:S(2)}, u32[]{:S(2)}) collective-permute-start(bf16[1,512]{1,0:T(2,128)(2,1)S(1)} %slice_bitcast_fusion.4), channel_id=1, source_target_pairs={{1,0},{2,1},{3,2},{4,3},{5,4},{6,5},{7,6},{8,7},{9,8},{10,9},{11,1... | collective-permute-start | bytes 3080 | tf_op jit(solution)/shard_map/ppermute | solution.py:999
  22.7 11.5 %slice-start = ((s8[4718592]{0:T(1024)(128)(4,1)}), s8[4194304]{0:T(1024)(128)(4,1)S(1)}, s32[]{:S(2)}) async-start(s8[4718592]{0:T(1024)(128)(4,1)} %bitcast.38), calls=%async_computation.10 | async-start | bytes 8388608
  23.8 10.4 %collective-permute-start.2 = (bf16[64,768]{1,0:T(8,128)(2,1)S(1)}, bf16[64,768]{1,0:T(8,128)(2,1)S(1)}, u32[]{:S(2)}, u32[]{:S(2)}) collective-permute-start(bf16[64,768]{1,0:T(8,128)(2,1)S(1)} %get-tuple-element.123), channel_id=1, source_target_pairs={{1,0},{2,1},{3,2},{4,3},{5,4},{6,5},{7,6},{8,7},{9,8},{10,9},{11,1... | collective-permute-start | bytes 294920 | tf_op jit(solution)/shard_map/ppermute | solution.py:999
  26.5 7.6 %collective-permute-start.1 = (bf16[64,768]{1,0:T(8,128)(2,1)S(1)}, bf16[64,768]{1,0:T(8,128)(2,1)S(1)}, u32[]{:S(2)}, u32[]{:S(2)}) collective-permute-start(bf16[64,768]{1,0:T(8,128)(2,1)S(1)} %get-tuple-element.124), channel_id=1, source_target_pairs={{0,1},{1,2},{2,3},{3,4},{4,5},{5,6},{6,7},{7,8},{8,9},{9,10},{10,1... | collective-permute-start | bytes 294920 | tf_op jit(solution)/shard_map/ppermute | solution.py:999
  56.3 43.2 %all-to-all-start = ((bf16[16,128,384]{2,1,0:T(8,128)(2,1)}), bf16[16,128,384]{2,1,0:T(8,128)(2,1)S(1)}, u32[]{:S(2)}, u32[]{:S(2)}) async-start(bf16[16,128,384]{2,1,0:T(8,128)(2,1)} %get-tuple-element.80), calls=%async_computation | async-start | bytes 3145728 | tf_op jit(solution)/shard_map/all_to_all | solution.py:1014
  63.1 261.4 %reduce-scatter.3.cloned.1.call-start = ((), (), s32[]{:S(2)}) async-start(), calls=%async_computation.8 | async-start | bytes 10027008 | tf_op jit(solution)/shard_map/reduce_scatter | solution.py:1088
  284.3 9.2 %collective-permute-start.4 = (bf16[64,768]{1,0:T(8,128)(2,1)S(1)}, bf16[64,768]{1,0:T(8,128)(2,1)S(1)}, u32[]{:S(2)}, u32[]{:S(2)}) collective-permute-start(bf16[64,768]{1,0:T(8,128)(2,1)S(1)} %get-tuple-element.121), channel_id=1, source_target_pairs={{1,0},{2,1},{3,2},{4,3},{5,4},{6,5},{7,6},{8,7},{9,8},{10,9},{11,1... | collective-permute-start | bytes 294920 | tf_op jit(solution)/shard_map/ppermute | solution.py:999
  287.2 11.7 %collective-permute-start.3 = (bf16[64,768]{1,0:T(8,128)(2,1)S(1)}, bf16[64,768]{1,0:T(8,128)(2,1)S(1)}, u32[]{:S(2)}, u32[]{:S(2)}) collective-permute-start(bf16[64,768]{1,0:T(8,128)(2,1)S(1)} %get-tuple-element.122), channel_id=1, source_target_pairs={{0,1},{1,2},{2,3},{3,4},{4,5},{5,6},{6,7},{7,8},{8,9},{9,10},{10,1... | collective-permute-start | bytes 294920 | tf_op jit(solution)/shard_map/ppermute | solution.py:999
  298.9 25.6 %all-to-all-start.4 = ((bf16[16,96,256]{2,1,0:T(8,128)(2,1)}), bf16[16,96,256]{2,1,0:T(8,128)(2,1)S(1)}, u32[]{:S(2)}, u32[]{:S(2)}) async-start(bf16[16,96,256]{2,1,0:T(8,128)(2,1)} %get-tuple-element.96), calls=%async_computation.4 | async-start | bytes 1572864 | tf_op jit(solution)/shard_map/all_to_all | solution.py:1014
  303.1 89.9 %reduce-scatter.5.cloned.1.call-start = ((), (), s32[]{:S(2)}) async-start(), calls=%async_computation.9 | async-start | bytes 5013504 | tf_op jit(solution)/shard_map/reduce_scatter | solution.py:1088
  324.5 10.1 %copy-start.10 = (bf16[16,96,256]{2,1,0:T(8,128)(2,1)}, bf16[16,96,256]{2,1,0:T(8,128)(2,1)S(1)}, u32[]{:S(2)}) copy-start(bf16[16,96,256]{2,1,0:T(8,128)(2,1)S(1)} %all-to-all-done.4.both_ref) | copy-start | bytes 2359300
  324.5 15.6 %collective-permute-start.6 = (bf16[768,384]{1,0:T(8,128)(2,1)}, bf16[768,384]{1,0:T(8,128)(2,1)S(1)}, u32[]{:S(2)}, u32[]{:S(2)}) collective-permute-start(bf16[768,384]{1,0:T(8,128)(2,1)} %bitcast.42), channel_id=1, source_target_pairs={{0,16},{16,0},{1,17},{17,1},{2,18},{18,2},{3,19},{19,3},{4,20},{20... | collective-permute-start | bytes 1769480 | tf_op jit(solution)/shard_map/ppermute | solution.py:1038
  328.4 11.7 %copy-start.11 = (bf16[1,768,384]{2,1,0:T(8,128)(2,1)S(1)}, bf16[1,768,384]{2,1,0:T(8,128)(2,1)}, u32[]{:S(2)}) copy-start(bf16[1,768,384]{2,1,0:T(8,128)(2,1)} %reduce-scatter.3.cloned.1.call-done) | copy-start | bytes 1769476
  342.2 12.9 %collective-permute-start.7 = (bf16[8,592,128]{2,1,0:T(8,128)(2,1)S(1)}, bf16[8,592,128]{2,1,0:T(8,128)(2,1)S(1)}, u32[]{:S(2)}, u32[]{:S(2)}) collective-permute-start(bf16[8,592,128]{2,1,0:T(8,128)(2,1)S(1)} %slice_bitcast_fusion), channel_id=1, source_target_pairs={{0,1},{1,0},{2,3},{3,2},{4,5},{5,4},{6,7},{7,6},{8,9},{9,8},{10,11... | collective-permute-start | bytes 3637256 | tf_op jit(solution)/shard_map/ppermute | solution.py:1182
  353.3 1.8 collective-permute-start.8
  360.7 54.7 %all-to-all-start.5 = ((bf16[8,880,128]{2,1,0:T(8,128)(2,1)}), bf16[8,880,128]{2,1,0:T(8,128)(2,1)S(1)}, u32[]{:S(2)}, u32[]{:S(2)}) async-start(bf16[8,880,128]{2,1,0:T(8,128)(2,1)} %join_pair.1), calls=%async_computation.6 | async-start | bytes 3604480 | tf_op jit(solution)/shard_map/all_to_all | solution.py:1188
  393.0 9.9 %copy-start.18 = (f32[1,512]{1,0:T(1,128)S(1)}, f32[1,512]{1,0:T(1,128)}, u32[]{:S(2)}) copy-start(f32[1,512]{1,0:T(1,128)} %get-tuple-element.107) | copy-start | bytes 6148
  393.0 8.1 %collective-permute-start.11 = (bf16[384,384]{1,0:T(8,128)(2,1)}, bf16[384,384]{1,0:T(8,128)(2,1)S(1)}, u32[]{:S(2)}, u32[]{:S(2)}) collective-permute-start(bf16[384,384]{1,0:T(8,128)(2,1)} %bitcast.44), channel_id=1, source_target_pairs={{0,16},{16,0},{1,17},{17,1},{2,18},{18,2},{3,19},{19,3},{4,20},{20... | collective-permute-start | bytes 884744 | tf_op jit(solution)/shard_map/ppermute | solution.py:1038
  402.2 17.0 %copy-start.15 = (f32[48,2304]{1,0:T(8,128)}, f32[48,2304]{1,0:T(8,128)S(1)}, u32[]{:S(2)}) copy-start(f32[48,2304]{1,0:T(8,128)S(1)} %get-tuple-element.120) | copy-start | bytes 1327108
  403.0 14.2 %collective-permute-start.5 = (f32[1,512]{1,0:T(1,128)S(1)}, f32[1,512]{1,0:T(1,128)S(1)}, u32[]{:S(2)}, u32[]{:S(2)}) collective-permute-start(f32[1,512]{1,0:T(1,128)S(1)} %copy-done.18), channel_id=1, source_target_pairs={{0,1},{1,2},{2,3},{3,4},{4,5},{5,6},{6,7},{7,8},{8,9},{9,10},{10,1... | collective-permute-start | bytes 6152 | tf_op jit(solution)/shard_map/ppermute | solution.py:999
  415.6 5.8 %collective-permute-start.9 = (bf16[592,128]{1,0:T(8,128)(2,1)S(1)}, bf16[592,128]{1,0:T(8,128)(2,1)S(1)}, u32[]{:S(2)}, u32[]{:S(2)}) collective-permute-start(bf16[592,128]{1,0:T(8,128)(2,1)S(1)} %slice_reduce_fusion), channel_id=1, source_target_pairs={{0,16},{16,0},{1,17},{17,1},{2,18},{18,2},{3,19},{19,3},{4,20},{20... | collective-permute-start | bytes 454664 | tf_op jit(solution)/shard_map/ppermute | solution.py:1038
  419.3 14.9 %copy-start.7 = (bf16[8,288,128]{2,1,0:T(8,128)(2,1)}, bf16[8,288,128]{2,1,0:T(8,128)(2,1)S(1)}, u32[]{:S(2)}) copy-start(bf16[8,288,128]{2,1,0:T(8,128)(2,1)S(1)} %slice.233) | copy-start | bytes 1769476
  419.3 14.9 %collective-permute-start.10 = (bf16[16,144,128]{2,1,0:T(8,128)(2,1)S(1)}, bf16[16,144,128]{2,1,0:T(8,128)(2,1)S(1)}, u32[]{:S(2)}, u32[]{:S(2)}) collective-permute-start(bf16[16,144,128]{2,1,0:T(8,128)(2,1)S(1)} %bitcast.40), channel_id=1, source_target_pairs={{0,16},{16,0},{1,17},{17,1},{2,18},{18,2},{3,19},{19,3},{4,20},{20... | collective-permute-start | bytes 1769480 | tf_op jit(solution)/shard_map/ppermute | solution.py:1038
  424.5 13.7 %copy-start.17 = (f32[32,768]{1,0:T(8,128)}, f32[32,768]{1,0:T(8,128)S(1)}, u32[]{:S(2)}) copy-start(f32[32,768]{1,0:T(8,128)S(1)} %constant_dynamic-update-slice_fusion) | copy-start | bytes 294916
  (15 other events, 29.2 us)
Sparse Core Ops, SparseCore 0:
  168.4 135.7 reduce-scatter.2
  308.5 84.4 reduce-scatter.4

commit v4 on v3

--- a/solution.py
+++ b/solution.py
@@ -32,10 +32,16 @@
     return lax.dot_general(left, right, (((0,), (0,)), ((), ())), preferred_element_type=jnp.float32)
 
 
-def pair_slot(shape, share, marks, clips):
-    if shape[0] == 1:
-        return 0, share
-    return (marks[clips + CORE] if share % 2 == 0 else 1 - marks[clips + CORE]), share // 2
+def store_pairs(refs, even, rows, values):
+    if len(refs) == 1:
+        for share, value in enumerate(values):
+            refs[0][share, rows, :] = value
+        return
+    kept, sent = refs
+    for at in range(len(values) // 2):
+        first, second = values[2 * at], values[2 * at + 1]
+        kept[at, rows, :] = jnp.where(even, first, second)
+        sent[at, rows, :] = jnp.where(even, second, first)
 
 
 def over_clips(clips, step, state):
@@ -438,9 +444,10 @@
 
 
 def taps_grad_kernel(
-    clips, marks, both_ref, out_ref, inputs, spaced, input_cols, grad_cols
+    clips, marks, both_ref, *refs
 ):
     half = KERNEL // 2
+    out_refs, (inputs, spaced, input_cols, grad_cols) = refs[:-4], refs[-4:]
     group_width = inputs.shape[0]
     long = inputs.shape[1]
     blocks, _, block = both_ref.shape
@@ -489,14 +496,13 @@
         ].astype(BF)
     result = row_dot(input_cols[...], grad_cols[...]).astype(BF)
     side_lanes = TAPS * group_width // 2
-    for place_at in range(2 * TURNS):
-        turn, side = place_at // 2, place_at % 2
-        for piece in range(side_lanes // 128):
-            begin = side * side_lanes + piece * 128
-            row, column = pair_slot(out_ref.shape, place_at, marks, clips)
-            out_ref[row, column, piece * group_width : (piece + 1) * group_width] = result[
-                turn * group_width : (turn + 1) * group_width, begin : begin + 128
-            ]
+    even_core = marks[clips + CORE] == 0
+    for piece in range(side_lanes // 128):
+        values = []
+        for place_at in range(2 * TURNS):
+            turn, begin = place_at // 2, place_at % 2 * side_lanes + piece * 128
+            values.append(result[turn * group_width : (turn + 1) * group_width, begin : begin + 128])
+        store_pairs(out_refs, even_core, slice(piece * group_width, (piece + 1) * group_width), values)
 
 
 def taps_grad(marks, both, shape, clips):
@@ -510,7 +516,7 @@
     more = TAPS * group_width // 2 // 128 * group_width
     return call(
         functools.partial(taps_grad_kernel, clips),
-        [like(shape + (more, 128), BF)],
+        [like((n, more, 128), BF) for n in shape],
         [
             pltpu.VMEM((group_width, long), jnp.float32),
             pltpu.VMEM((group_width, long), jnp.float32),
@@ -521,16 +527,16 @@
         "taps_grad",
         10**10,
         limit=60,
-    )[0]
-
-
-def weave_taps_kernel(own_ref, other_ref, out_ref):
+    )
+
+
+def weave_taps_kernel(own_ref, out_ref):
     group_width = out_ref.shape[1] // GROUPS
     taps = out_ref.shape[0] // group_width
     pieces = own_ref.shape[1] // group_width
     both = []
     for group in range(GROUPS):
-        rows = own_ref[group].astype(jnp.float32) + other_ref[group].astype(jnp.float32)
+        rows = own_ref[group].astype(jnp.float32)
         both.append(
             jnp.concatenate([rows[at * group_width : (at + 1) * group_width] for at in range(pieces)], axis=1)
         )
@@ -541,29 +547,34 @@
         )
 
 
-def weave_taps(own, other, taps, group_width):
+def weave_taps(own, taps, group_width):
     return call(
-        weave_taps_kernel, [like((taps * group_width, GROUPS * group_width))], [], (own, other), "weave_taps", 0
+        weave_taps_kernel, [like((taps * group_width, GROUPS * group_width))], [], (own,), "weave_taps", 0
     )[0]
 
 
-def join_pair_kernel(clips, marks, sums_ref, other_sums_ref, taps_ref, other_taps_ref, out_ref):
-    below, rows = sums_ref.shape[2], taps_ref.shape[2]
-    out_ref[:, :below] = (
-        sums_ref[0].astype(jnp.float32) + other_sums_ref[...].astype(jnp.float32)
-    ).astype(BF)
+def add_shares_kernel(own_ref, other_ref, out_ref):
+    out_ref[...] = (own_ref[...].astype(jnp.float32) + other_ref[...].astype(jnp.float32)).astype(BF)
+
+
+def add_shares(own, other):
+    return call(add_shares_kernel, [like(other.shape, BF)], [], (own, other), "add_shares", 0)[0]
+
+
+def join_pair_kernel(clips, marks, taps_ref, other_ref, out_ref):
+    rows = taps_ref.shape[1]
     first = marks[clips + CORE] == 0
-    out_ref[:, below : below + rows] = jnp.where(first, taps_ref[0], other_taps_ref[...])
-    out_ref[:, below + rows :] = jnp.where(first, other_taps_ref[...], taps_ref[0])
-
-
-def join_pair(marks, sums, other_sums, taps, other_taps, clips):
-    _, chips, below, lanes = sums.shape
+    out_ref[:, :rows] = jnp.where(first, taps_ref[...], other_ref[...])
+    out_ref[:, rows:] = jnp.where(first, other_ref[...], taps_ref[...])
+
+
+def join_pair(marks, taps, other, clips):
+    chips, rows, lanes = taps.shape
     return call(
         functools.partial(join_pair_kernel, clips),
-        [like((chips, below + 2 * taps.shape[2], lanes), BF)],
+        [like((chips, 2 * rows, lanes), BF)],
         [],
-        (marks, sums, other_sums, taps, other_taps),
+        (marks, taps, other),
         "join_pair",
         0,
     )[0]
@@ -910,23 +921,29 @@
 def stem_back_kernel(
     clips, marks, input_ref, mixed_ref, normed_ref, pre_ref, unfold_ref, weight_ref, gain_ref, proj_ref,
     middle_sums_ref, inner_sums_ref, after_sums_ref,
-    samples_ref, carried_ref, joined_ref, table, spread, woven,
+    samples_ref, carried_ref, *refs,
 ):
     rows, chans = pre_ref.shape
     width = input_ref.shape[1]
-    shares = joined_ref.shape[0] * joined_ref.shape[1]
+    joined_refs, (table, spread, woven) = refs[:-3], refs[-3:]
+    shares = RING
+    even_core = marks[clips + CORE] == 0
     start = mixed_ref[...] + input_ref[...]
     start_b = start.astype(BF)
 
     def share_out(product, begin):
         own, columns = product.shape[0] // shares, product.shape[1]
-        for share in range(shares):
-            for place in range(columns // PIECE):
-                at = begin + place * own
-                row, column = pair_slot(joined_ref.shape, share, marks, clips)
-                joined_ref[row, column, at : at + own, :] = product[
-                    share * own : (share + 1) * own, place * PIECE : (place + 1) * PIECE
-                ]
+        for place in range(columns // PIECE):
+            at = begin + place * own
+            store_pairs(
+                joined_refs,
+                even_core,
+                slice(at, at + own),
+                [
+                    product[share * own : (share + 1) * own, place * PIECE : (place + 1) * PIECE]
+                    for share in range(shares)
+                ],
+            )
         return begin + own * columns // PIECE
 
     at = share_out(over_rows_dot(normed_ref[...], start_b).astype(BF), 0)
@@ -974,8 +991,9 @@
         lanes = slice(share * own_chans, (share + 1) * own_chans)
         spread[share, 14:15, 0:own_chans] = gain_sum[:, lanes]
         spread[share, 15:16, 0:own_chans] = bias_sum[:, lanes]
-        row, column = pair_slot(joined_ref.shape, share, marks, clips)
-        joined_ref[row, column, at:, :] = spread[share].astype(BF)
+    store_pairs(
+        joined_refs, even_core, slice(at, at + 16), [spread[share].astype(BF) for share in range(shares)]
+    )
 
 
 def stem_back(marks, input_grad, mixed, normed, pre, unfold, weight, gain, proj, sums, shares, clips):
@@ -984,7 +1002,7 @@
     pieces = (chans // RING * width + 3 * chans // RING * chans) // PIECE + 16
     return call(
         functools.partial(stem_back_kernel, clips),
-        [like((2 * rows, chans)), like((1, chans)), like(shares + (pieces, PIECE), BF)],
+        [like((2 * rows, chans)), like((1, chans))] + [like((n, pieces, PIECE), BF) for n in shares],
         [pltpu.VMEM((12, width), jnp.float32), pltpu.VMEM((RING, 16, PIECE), jnp.float32),
          pltpu.VMEM((2 * rows, PIECE), jnp.float32)],
         (marks, input_grad, mixed, normed, pre, unfold, weight, gain, proj) + sums,
@@ -1161,8 +1179,8 @@
     input_grad = conv_rows(True, marks, before, grad_conv_b, after, (back_weights,), clips)
     input_grad, grad_groups, ffn_share = lax.optimization_barrier((input_grad, grad_groups, ffn_share))
     attn_share = over_seq(regroup(attn_joined, [(4 * width // SHARE, near_rows)]))
-    shape = (2, RING // 2) if count == RING else (1, RING)
-    sample_grad, carried, stem_joined = stem_back(
+    shape = (RING // 2,) * 2 if count == RING else (RING,)
+    sample_grad, carried, *stem_shares = stem_back(
         marks, input_grad, grad_mixed, normed_b, stem_pre, unfold, stem_weight, stem_gain[None],
         proj_weight, (middle_sums, inner_sums, after_sums), shape, clips,
     )
@@ -1170,25 +1188,23 @@
     own = width // count
     own_chans = chans // count
     own_taps = KERNEL // count
-    below = stem_joined.shape[2]
     grad_ffn = spread_out(sum_pair(ffn_share), [(own, inner), (inner // count, width)], SHARE)
-    stem_joined, grad_ffn, grad_groups = lax.optimization_barrier((stem_joined, grad_ffn, grad_groups))
-    taps = taps_grad(marks, with_far_blocks(grad_groups, 0 if count == RING else 1), shape, clips)
     if count == RING:
         pairs = [(i, i ^ 1) for i in range(count)]
-        joined = join_pair(
-            marks,
-            stem_joined,
-            lax.ppermute(stem_joined[1], "seq", pairs),
-            taps,
-            lax.ppermute(taps[1], "seq", pairs),
-            clips,
-        )
         alike = [list(range(core, count, 2)) for core in range(2)]
-        received = lax.all_to_all(joined, "seq", 0, 0, axis_index_groups=alike)
-        pos_pieces = received[:, below:].reshape(GROUPS, -1, PIECE)
+        stem_joined = add_shares(stem_shares[0], lax.ppermute(stem_shares[1], "seq", pairs))
+        stem_joined, grad_groups = lax.optimization_barrier((stem_joined, grad_groups))
+        received = lax.all_to_all(stem_joined, "seq", 0, 0, axis_index_groups=alike)
+        taps, sent_taps = taps_grad(marks, grad_groups, shape, clips)
+        taps = join_pair(marks, taps, lax.ppermute(sent_taps, "seq", pairs), clips)
+        taps = add_shares(taps, other_stream(taps))
+        taps, received, grad_ffn = lax.optimization_barrier((taps, received, grad_ffn))
+        pos_pieces = lax.all_to_all(taps, "seq", 0, 0, axis_index_groups=alike)
+        pos_pieces = pos_pieces.reshape(GROUPS, -1, PIECE)
     else:
-        stem_joined = stem_joined[0]
+        (taps,) = taps_grad(marks, with_far_blocks(grad_groups, 1), shape, clips)
+        taps = add_shares(taps, other_stream(taps))
+        stem_joined = stem_shares[0]
         stem_joined = jnp.concatenate(
             [
                 regroup(
@@ -1200,7 +1216,6 @@
             axis=1,
         )
         received = lax.all_to_all(stem_joined, "seq", 0, 0)
-        below = stem_joined.shape[1]
         segments = count // RING
         by_tap = taps.reshape(2 * TURNS, 3, group_width, PIECE).transpose(0, 2, 1, 3)
         by_tap = by_tap.reshape(2 * TURNS, group_width, TAPS // 2, group_width)
@@ -1210,8 +1225,9 @@
         by_tap = jnp.sum(by_tap.astype(jnp.float32), axis=0).astype(jnp.bfloat16)
         by_tap = by_tap.reshape(RING, own_taps, group_width, group_width).transpose(0, 2, 1, 3)
         pos_pieces = swap(by_tap.reshape(RING, group_width, own_taps * group_width))
-    pos_grad = weave_taps(pos_pieces, other_stream(pos_pieces), own_taps, group_width)
-    stem_total = sum_pair(jnp.sum(received[:, :below].astype(jnp.float32), axis=0).astype(jnp.bfloat16))
+    pos_pieces, attn_share = lax.optimization_barrier((pos_pieces, attn_share))
+    pos_grad = weave_taps(pos_pieces, own_taps, group_width)
+    stem_total = sum_pair(jnp.sum(received.astype(jnp.float32), axis=0).astype(jnp.bfloat16))
     grad_proj, grad_stem = spread_out(
         stem_total[:-16], [(own_chans, width), (3 * own_chans, chans)], PIECE
     )

time: 452 us -> 440 us (0.973)
  waiting for transfers between devices: 93.4 us -> 77 us
  blocking collectives: 87.4 us -> 101 us
  Pallas kernels: 186 us -> 180 us
    reduce_scatter x2, waiting for transfers between devices: 26.2 us -> 9.69 us  [over_seq(): lax.psum_scatter(joined, 'seq', scatter_dimension=0, tiled=False)]
    all_to_all x3, blocking collectives: 87.4 us -> 101 us  [swap(): return lax.all_to_all(value, 'seq', 0, 0, axis_index_groups=groups)]
    all_to_all x1 -> x2, starting transfers between devices: 6.05 us -> 12.7 us  [the longest x1 6.74 us: local(): pos_pieces = lax.all_to_all(taps, 'seq', 0, 0, axis_index_groups=alike)]
    pallas_call x15 -> x17, Pallas kernels: 186 us -> 180 us  [call(): pl.pallas_call(kernel, out_shape=tuple(outs), in_specs=in_specs or [SMEM_...]
    all_to_all x1 -> x2, waiting for transfers between devices: 10.6 us -> 8.54 us  [the longest x1 5.43 us: local(): pos_pieces = lax.all_to_all(taps, 'seq', 0, 0, axis_index_groups=alike)]
  transfers between devices with their start and end apart: 17 -> 18, of which waited for: 10 -> 10; matrix products, arithmetic and copies ran while one was open for 3% -> 2% of each run, Pallas kernels for 24% -> 25%
where the time goes in v4:
time: 440 us; the launch traced here: 435 us
  Pallas kernels  180 us (41%)
  blocking collectives  101 us (23%)
  waiting for transfers between devices  77 us (18%)
  starting transfers between devices  43.9 us (10%)
  local copies, waits for them, and re-layouts  14.9 us (3%)
  between operations  14.5 us (3%)
    pallas_call x17, Pallas kernels, call(): pl.pallas_call(kernel, out_shape=tuple(outs), in_specs=in_specs or [SMEM_...  180 us
    all_to_all x3, blocking collectives, swap(): return lax.all_to_all(value, 'seq', 0, 0, axis_index_groups=groups)  101 us
    all_to_all x2, waiting for transfers between devices, swap(): return lax.all_to_all(value, 'seq', 0, 0, axis_index_groups=groups)  23.8 us
    ppermute x4, waiting for transfers between devices, other_stream(): return lax.ppermute(share, 'rep', [(0, 1), (1, 0)])  22.7 us
    ppermute x6, starting transfers between devices, from_behind(): lax.ppermute(value, axis, [(source, source + steps) for source in range(i...  14.5 us
    all_to_all x2, starting transfers between devices, swap(): return lax.all_to_all(value, 'seq', 0, 0, axis_index_groups=groups)  10.6 us
    ppermute x6, waiting for transfers between devices, from_behind(): lax.ppermute(value, axis, [(source, source + steps) for source in range(i...  9.97 us
    reduce_scatter x2, waiting for transfers between devices, over_seq(): lax.psum_scatter(joined, 'seq', scatter_dimension=0, tiled=False)  9.69 us
  transfers between devices with their start and end apart: 18, of which 10 were waited for; matrix products, arithmetic and copies ran while one was open for 2% of the time, Pallas kernels for 25%

profile of v4, /device:TPU:16, one launch (start us, length us, event | category | flops | bytes accessed | tf_op | source)
XLA Modules:
  0.0 435.1 jit_solution(1642751851452743200)
XLA Ops:
  11.5 5.5 %conv_weights.2.refs_0_ = bf16[16,192,768]{2,1,0:T(8,128)(2,1)} custom-call(bf16[6144,768]{1,0:T(8,128)(2,1)} %weight_ref.9), custom_call_target="tpu_custom_call" | custom-call | bytes 14155776 | tf_op jit(solution)/shard_map/conv_weights/pallas_call | solution.py:75
  28.4 5.7 %conv_weights.3.refs_1_ = bf16[16,192,768]{2,1,0:T(8,128)(2,1)} custom-call(bf16[6144,768]{1,0:T(8,128)(2,1)} %weight_ref.9), custom_call_target="tpu_custom_call" | custom-call | bytes 14155776 | tf_op jit(solution)/shard_map/conv_weights/pallas_call | solution.py:75
  34.1 16.1 %conv.1.conv_ref = f32[256,768]{1,0:T(8,128)S(1)} custom-call(s32[10]{0:T(128)S(1)} %copy-done.2, bf16[64,768]{1,0:T(8,128)(2,1)S(1)} %collective-permute-done.1.before_ref, bf16[256,768]{1,0:T(8,128)(2,1)S(1)} %copy-done.1, bf16[64,768]{1,0:T(8,128)(2,1)S(1)} %collective-permute-done.2.after_ref, bf16[16,192,768]{2,1,0:T(8,128)(2,1)S(1)} %bitcast.34, ...), custom_call_target="tpu_custom_call" | custom-call | flops 15000000512 | bytes 10813480 | tf_op jit(solution)/shard_map/conv/pallas_call | solution.py:75
  51.1 5.2 %project_heads.1 = (f32[256,768]{1,0:T(8,128)}, bf16[16,128,384]{2,1,0:T(8,128)(2,1)}) custom-call(f32[256,768]{1,0:T(8,128)} %copy-done.4, f32[256,768]{1,0:T(8,128)} %get-tuple-element.86.start_ref, f32[12,768]{1,0:T(8,128)} %get-tuple-element.80.table_ref, bf16[768,2304]{1,0:T(8,128)(2,1)} %weight_ref.10), custom_call_target="tpu_custom_call" | custom-call | flops 6000000000 | bytes 7507968 | tf_op jit(solution)/shard_map/project_heads/pallas_call | solution.py:75
  56.3 6.4 %all-to-all-start = ((bf16[16,128,384]{2,1,0:T(8,128)(2,1)}), bf16[16,128,384]{2,1,0:T(8,128)(2,1)S(1)}, u32[]{:S(2)}, u32[]{:S(2)}) async-start(bf16[16,128,384]{2,1,0:T(8,128)(2,1)} %get-tuple-element.87), calls=%async_computation | async-start | bytes 3145728 | tf_op jit(solution)/shard_map/all_to_all | solution.py:1032
  62.7 12.6 %conv_weights_back.1.refs_0_ = bf16[16,384,768]{2,1,0:T(8,128)(2,1)} custom-call(bf16[6144,768]{1,0:T(8,128)(2,1)} %weight_ref.9), custom_call_target="tpu_custom_call" | custom-call | bytes 18874368 | tf_op jit(solution)/shard_map/conv_weights_back/pallas_call | solution.py:75
  75.3 23.8 %all-to-all-done.packed_ref = bf16[16,128,384]{2,1,0:T(8,128)(2,1)S(1)} async-done(((bf16[16,128,384]{2,1,0:T(8,128)(2,1)}), bf16[16,128,384]{2,1,0:T(8,128)(2,1)S(1)}, u32[]{:S(2)}, u32[]{:S(2)}) %all-to-all-start) | async-done | bytes 1572896 | tf_op jit(solution)/shard_map/all_to_all | solution.py:1032
  100.2 19.9 %attend.1 = (bf16[16,128,128]{2,1,0:T(8,128)(2,1)}, f32[64,4096]{1,0:T(8,128)}, f32[1,4096]{1,0:T(1,128)}) custom-call(s32[10]{0:T(128)} %concatenate.23.marks, bf16[16,128,384]{2,1,0:T(8,128)(2,1)} %copy-done.7), custom_call_target="tpu_custom_call" | custom-call | flops 24999999488 | bytes 3162152 | tf_op jit(solution)/shard_map/attend/pallas_call | solution.py:75
  120.1 18.2 %all_to_all.35.heads_ref = bf16[16,128,128]{2,1,0:T(8,128)(2,1)} all-to-all(bf16[16,128,128]{2,1,0:T(8,128)(2,1)} %get-tuple-element.91), channel_id=1, replica_groups=mesh['rep'=2,'seq'=16] {'seq'}, dimensions={0} | all-to-all | bytes 1048576 | tf_op jit(solution)/shard_map/all_to_all | solution.py:1032
  138.3 25.3 %middle.1 = (bf16[256,768]{1,0:T(8,128)(2,1)}, bf16[16,128,128]{2,1,0:T(8,128)(2,1)}, f32[256,768]{1,0:T(8,128)}, bf16[16,96,384]{2,1,0:T(8,128)(2,1)}, f32[8,76...) custom-call(bf16[16,128,128]{2,1,0:T(8,128)(2,1)} %all_to_all.35.heads_ref, ...), custom_call_target="tpu_custom_call" | custom-call | flops 20000000000 | bytes 24727552 | tf_op jit(solution)/shard_map/middle/pallas_call | solution.py:75
  164.6 18.5 %all_to_all.36.grad_ref = bf16[16,128,128]{2,1,0:T(8,128)(2,1)} all-to-all(bf16[16,128,128]{2,1,0:T(8,128)(2,1)S(1)} %copy-done.12), channel_id=1, replica_groups=mesh['rep'=2,'seq'=16] {'seq'}, dimensions={0} | all-to-all | bytes 1048576 | tf_op jit(solution)/shard_map/all_to_all | solution.py:1032
  183.1 29.5 %attend_back.1 = bf16[16,128,384]{2,1,0:T(8,128)(2,1)} custom-call(s32[10]{0:T(128)} %concatenate.23.marks, bf16[16,128,384]{2,1,0:T(8,128)(2,1)} %copy-done.7, bf16[16,128,128]{2,1,0:T(8,128)(2,1)} %all_to_all.36.grad_ref, f32[64,4096]{1,0:T(8,128)} %get-tuple-element.94.wide_ref, f32[1,4096]{1,0:T(1,128)} %get-tuple-element.95.log_ref), custom_call_target="tpu_custom_call" | custom-call | flops 35000000512 | bytes 4735016 | tf_op jit(solution)/shard_map/attend_back/pallas_call | solution.py:75
  212.5 64.0 %all_to_all.37.packed_ref = bf16[16,128,384]{2,1,0:T(8,128)(2,1)} all-to-all(bf16[16,128,384]{2,1,0:T(8,128)(2,1)} %attend_back.1), channel_id=1, replica_groups=mesh['rep'=2,'seq'=16] {'seq'}, dimensions={0} | all-to-all | bytes 3145728 | tf_op jit(solution)/shard_map/all_to_all | solution.py:1032
  276.5 10.1 %after_heads.1 = (f32[256,768]{1,0:T(8,128)}, bf16[256,768]{1,0:T(8,128)(2,1)}, bf16[16,96,256]{2,1,0:T(8,128)(2,1)}, bf16[16,384,384]{2,1,0:T(8,128)(2,1)}, f32[8,768]{1,0:T(8,128)}) custom-call(bf16[16,128,384]{2,1,0:T(8,128)(2,1)} %all_to_all.37.packed_ref, f32[256,768]{1,0:T(8,128)} %get-tuple-element.96.grad_second_ref, ...), custom_call_target="tpu_custom_call" | custom-call | flops 6000000000 | bytes 16183296 | tf_op jit(solution)/shard_map/after_heads/pallas_call | solution.py:75
  295.8 6.4 %collective-permute-done.3.before_ref = bf16[64,768]{1,0:T(8,128)(2,1)S(1)} collective-permute-done((bf16[64,768]{1,0:T(8,128)(2,1)S(1)}, bf16[64,768]{1,0:T(8,128)(2,1)S(1)}, u32[]{:S(2)}, u32[]{:S(2)}) %collective-permute-start.3) | collective-permute-done | bytes 98336 | tf_op jit(solution)/shard_map/ppermute | solution.py:1017
  307.7 19.2 %conv_back.1.input_ref = f32[256,768]{1,0:T(8,128)S(1)} custom-call(s32[10]{0:T(128)S(1)} %copy-done.3, bf16[64,768]{1,0:T(8,128)(2,1)S(1)} %collective-permute-done.3.before_ref, bf16[256,768]{1,0:T(8,128)(2,1)S(1)} %copy-done, bf16[64,768]{1,0:T(8,128)(2,1)S(1)} %collective-permute-done.4.after_ref, bf16[16,384,768]{2,1,0:T(8,128)(2,1)} %conv_weights_back.1.refs_0_), custom_call_target="tpu_custom_call" | custom-call | flops 15000000512 | bytes 10813480 | tf_op jit(solution)/shard_map/conv_back/pallas_call | solution.py:75
  329.2 6.2 %stem_back.1 = (f32[512,512]{1,0:T(8,128)}, f32[1,512]{1,0:T(1,128)}, bf16[8,592,128]{2,1,0:T(8,128)(2,1)}, bf16[8,592,128]{2,1,0:T(8,128)(2,1)}) custom-call(s32[10]{0:T(128)} %concatenate.23.marks, f32[256,768]{1,0:T(8,128)} %copy-done.5, f32[256,768]{1,0:T(8,128)} %get-tuple-element.106.mixed_ref, bf16[256,512]{1,0:T(8,128)(2,1)} %get-tuple-element.107.normed_ref, ...), custom_call_target="tpu_custom_call" | custom-call | flops 6000000000 | bytes 9044008 | tf_op jit(solution)/shard_map/stem_back/pallas_call | solution.py:75
  338.0 5.5 %collective-permute-done.9 = bf16[768,384]{1,0:T(8,128)(2,1)S(1)} collective-permute-done((bf16[768,384]{1,0:T(8,128)(2,1)}, bf16[768,384]{1,0:T(8,128)(2,1)S(1)}, u32[]{:S(2)}, u32[]{:S(2)}) %collective-permute-start.9) | collective-permute-done | bytes 589856 | tf_op jit(solution)/shard_map/ppermute | solution.py:1056
  347.9 6.0 %all-to-all-start.5 = ((bf16[8,592,128]{2,1,0:T(8,128)(2,1)}), bf16[8,592,128]{2,1,0:T(8,128)(2,1)S(1)}, u32[]{:S(2)}, u32[]{:S(2)}) async-start(bf16[8,592,128]{2,1,0:T(8,128)(2,1)} %add_shares.2), calls=%async_computation.6 | async-start | bytes 2424832 | tf_op jit(solution)/shard_map/all_to_all | solution.py:1197
  353.9 10.3 %taps_grad.1 = (bf16[8,144,128]{2,1,0:T(8,128)(2,1)}, bf16[8,144,128]{2,1,0:T(8,128)(2,1)}) custom-call(s32[10]{0:T(128)} %concatenate.23.marks, bf16[16,96,256]{2,1,0:T(8,128)(2,1)} %copy-done.9), custom_call_target="tpu_custom_call" | custom-call | flops 10000000000 | bytes 1376296 | tf_op jit(solution)/shard_map/taps_grad/pallas_call | solution.py:75
  371.2 13.1 %collective-permute-done.8.other_ref = bf16[8,288,128]{2,1,0:T(8,128)(2,1)S(1)} collective-permute-done((bf16[8,288,128]{2,1,0:T(8,128)(2,1)}, bf16[8,288,128]{2,1,0:T(8,128)(2,1)S(1)}, u32[]{:S(2)}, u32[]{:S(2)}) %collective-permute-start.8) | collective-permute-done | bytes 589856 | tf_op jit(solution)/shard_map/ppermute | solution.py:1056
  394.4 6.7 %all-to-all-start.6 = ((bf16[8,288,128]{2,1,0:T(8,128)(2,1)}), bf16[8,288,128]{2,1,0:T(8,128)(2,1)S(1)}, u32[]{:S(2)}, u32[]{:S(2)}) async-start(bf16[8,288,128]{2,1,0:T(8,128)(2,1)} %add_shares.3), calls=%async_computation.7 | async-start | bytes 1179648 | tf_op jit(solution)/shard_map/all_to_all | solution.py:1202
  403.5 9.7 %reduce-scatter.5.cloned.1.call-done = bf16[1,384,384]{2,1,0:T(8,128)(2,1)} async-done(((bf16[16,384,384]{2,1,0:T(8,128)(2,1)}), bf16[1,384,384]{2,1,0:T(8,128)(2,1)}) %reduce-scatter.5.cloned.1.call-update) | async-done | bytes 294928 | tf_op jit(solution)/shard_map/reduce_scatter | solution.py:1106
  413.1 5.4 %all-to-all-done.6 = bf16[8,288,128]{2,1,0:T(8,128)(2,1)S(1)} async-done(((bf16[8,288,128]{2,1,0:T(8,128)(2,1)}), bf16[8,288,128]{2,1,0:T(8,128)(2,1)S(1)}, u32[]{:S(2)}, u32[]{:S(2)}) %all-to-all-start.6) | async-done | bytes 589856 | tf_op jit(solution)/shard_map/all_to_all | solution.py:1202
  (117 shorter events, 71.6 us)
Async XLA Ops:
  7.9 9.7 %collective-permute-start = (bf16[1,512]{1,0:T(2,128)(2,1)S(1)}, bf16[1,512]{1,0:T(2,128)(2,1)S(1)}, u32[]{:S(2)}, u32[]{:S(2)}) collective-permute-start(bf16[1,512]{1,0:T(2,128)(2,1)S(1)} %slice_bitcast_fusion.2), channel_id=1, source_target_pairs={{1,0},{2,1},{3,2},{4,3},{5,4},{6,5},{7,6},{8,7},{9,8},{10,9},{11,1... | collective-permute-start | bytes 3080 | tf_op jit(solution)/shard_map/ppermute | solution.py:1017
  22.6 11.5 %slice-start = ((s8[4718592]{0:T(1024)(128)(4,1)}), s8[4194304]{0:T(1024)(128)(4,1)S(1)}, s32[]{:S(2)}) async-start(s8[4718592]{0:T(1024)(128)(4,1)} %bitcast.33), calls=%async_computation.11 | async-start | bytes 8388608
  23.7 10.4 %collective-permute-start.2 = (bf16[64,768]{1,0:T(8,128)(2,1)S(1)}, bf16[64,768]{1,0:T(8,128)(2,1)S(1)}, u32[]{:S(2)}, u32[]{:S(2)}) collective-permute-start(bf16[64,768]{1,0:T(8,128)(2,1)S(1)} %get-tuple-element.137), channel_id=1, source_target_pairs={{1,0},{2,1},{3,2},{4,3},{5,4},{6,5},{7,6},{8,7},{9,8},{10,9},{11,1... | collective-permute-start | bytes 294920 | tf_op jit(solution)/shard_map/ppermute | solution.py:1017
  26.4 7.7 %collective-permute-start.1 = (bf16[64,768]{1,0:T(8,128)(2,1)S(1)}, bf16[64,768]{1,0:T(8,128)(2,1)S(1)}, u32[]{:S(2)}, u32[]{:S(2)}) collective-permute-start(bf16[64,768]{1,0:T(8,128)(2,1)S(1)} %get-tuple-element.138), channel_id=1, source_target_pairs={{0,1},{1,2},{2,3},{3,4},{4,5},{5,6},{6,7},{7,8},{8,9},{9,10},{10,1... | collective-permute-start | bytes 294920 | tf_op jit(solution)/shard_map/ppermute | solution.py:1017
  56.3 42.8 %all-to-all-start = ((bf16[16,128,384]{2,1,0:T(8,128)(2,1)}), bf16[16,128,384]{2,1,0:T(8,128)(2,1)S(1)}, u32[]{:S(2)}, u32[]{:S(2)}) async-start(bf16[16,128,384]{2,1,0:T(8,128)(2,1)} %get-tuple-element.87), calls=%async_computation | async-start | bytes 3145728 | tf_op jit(solution)/shard_map/all_to_all | solution.py:1032
  62.7 265.2 %reduce-scatter.3.cloned.1.call-start = ((), (), s32[]{:S(2)}) async-start(), calls=%async_computation.9 | async-start | bytes 10027008 | tf_op jit(solution)/shard_map/reduce_scatter | solution.py:1106
  287.5 8.3 %collective-permute-start.4 = (bf16[64,768]{1,0:T(8,128)(2,1)S(1)}, bf16[64,768]{1,0:T(8,128)(2,1)S(1)}, u32[]{:S(2)}, u32[]{:S(2)}) collective-permute-start(bf16[64,768]{1,0:T(8,128)(2,1)S(1)} %get-tuple-element.135), channel_id=1, source_target_pairs={{1,0},{2,1},{3,2},{4,3},{5,4},{6,5},{7,6},{8,7},{9,8},{10,9},{11,1... | collective-permute-start | bytes 294920 | tf_op jit(solution)/shard_map/ppermute | solution.py:1017
  290.4 11.9 %collective-permute-start.3 = (bf16[64,768]{1,0:T(8,128)(2,1)S(1)}, bf16[64,768]{1,0:T(8,128)(2,1)S(1)}, u32[]{:S(2)}, u32[]{:S(2)}) collective-permute-start(bf16[64,768]{1,0:T(8,128)(2,1)S(1)} %get-tuple-element.136), channel_id=1, source_target_pairs={{0,1},{1,2},{2,3},{3,4},{4,5},{5,6},{6,7},{7,8},{8,9},{9,10},{10,1... | collective-permute-start | bytes 294920 | tf_op jit(solution)/shard_map/ppermute | solution.py:1017
  302.3 25.6 %all-to-all-start.4 = ((bf16[16,96,256]{2,1,0:T(8,128)(2,1)}), bf16[16,96,256]{2,1,0:T(8,128)(2,1)S(1)}, u32[]{:S(2)}, u32[]{:S(2)}) async-start(bf16[16,96,256]{2,1,0:T(8,128)(2,1)} %get-tuple-element.103), calls=%async_computation.4 | async-start | bytes 1572864 | tf_op jit(solution)/shard_map/all_to_all | solution.py:1032
  306.5 106.7 %reduce-scatter.5.cloned.1.call-start = ((), (), s32[]{:S(2)}) async-start(), calls=%async_computation.10 | async-start | bytes 5013504 | tf_op jit(solution)/shard_map/reduce_scatter | solution.py:1106
  327.8 7.6 %copy-start.9 = (bf16[16,96,256]{2,1,0:T(8,128)(2,1)}, bf16[16,96,256]{2,1,0:T(8,128)(2,1)S(1)}, u32[]{:S(2)}) copy-start(bf16[16,96,256]{2,1,0:T(8,128)(2,1)S(1)} %all-to-all-done.4.both_ref) | copy-start | bytes 2359300
  327.8 15.6 %collective-permute-start.9 = (bf16[768,384]{1,0:T(8,128)(2,1)}, bf16[768,384]{1,0:T(8,128)(2,1)S(1)}, u32[]{:S(2)}, u32[]{:S(2)}) collective-permute-start(bf16[768,384]{1,0:T(8,128)(2,1)} %bitcast.36), channel_id=1, source_target_pairs={{0,16},{16,0},{1,17},{17,1},{2,18},{18,2},{3,19},{19,3},{4,20},{20... | collective-permute-start | bytes 1769480 | tf_op jit(solution)/shard_map/ppermute | solution.py:1056
  329.2 14.2 %copy-start.11 = (bf16[1,768,384]{2,1,0:T(8,128)(2,1)S(1)}, bf16[1,768,384]{2,1,0:T(8,128)(2,1)}, u32[]{:S(2)}) copy-start(bf16[1,768,384]{2,1,0:T(8,128)(2,1)} %reduce-scatter.3.cloned.1.call-done) | copy-start | bytes 1769476
  335.5 8.1 %collective-permute-start.6 = (bf16[8,592,128]{2,1,0:T(8,128)(2,1)}, bf16[8,592,128]{2,1,0:T(8,128)(2,1)S(1)}, u32[]{:S(2)}, u32[]{:S(2)}) collective-permute-start(bf16[8,592,128]{2,1,0:T(8,128)(2,1)} %get-tuple-element.116), channel_id=1, source_target_pairs={{0,1},{1,0},{2,3},{3,2},{4,5},{5,4},{6,7},{7,6},{8,9},{9,8},{10,11... | collective-permute-start | bytes 3637256 | tf_op jit(solution)/shard_map/ppermute | solution.py:1195
  335.6 56.8 %collective-permute-start.5 = (f32[1,512]{1,0:T(1,128)}, f32[1,512]{1,0:T(1,128)S(1)}, u32[]{:S(2)}, u32[]{:S(2)}) collective-permute-start(f32[1,512]{1,0:T(1,128)} %get-tuple-element.114), channel_id=1, source_target_pairs={{0,1},{1,2},{2,3},{3,4},{4,5},{5,6},{6,7},{7,8},{8,9},{9,10},{10,1... | collective-permute-start | bytes 6152 | tf_op jit(solution)/shard_map/ppermute | solution.py:1017
  347.9 42.6 %all-to-all-start.5 = ((bf16[8,592,128]{2,1,0:T(8,128)(2,1)}), bf16[8,592,128]{2,1,0:T(8,128)(2,1)S(1)}, u32[]{:S(2)}, u32[]{:S(2)}) async-start(bf16[8,592,128]{2,1,0:T(8,128)(2,1)} %add_shares.2), calls=%async_computation.6 | async-start | bytes 2424832 | tf_op jit(solution)/shard_map/all_to_all | solution.py:1197
  364.2 1.8 collective-permute-start.7
  368.7 15.6 %collective-permute-start.8 = (bf16[8,288,128]{2,1,0:T(8,128)(2,1)}, bf16[8,288,128]{2,1,0:T(8,128)(2,1)S(1)}, u32[]{:S(2)}, u32[]{:S(2)}) collective-permute-start(bf16[8,288,128]{2,1,0:T(8,128)(2,1)} %join_pair.1.own_ref), channel_id=1, source_target_pairs={{0,16},{16,0},{1,17},{17,1},{2,18},{18,2},{3,19},{19,3},{4,20},{20... | collective-permute-start | bytes 1769480 | tf_op jit(solution)/shard_map/ppermute | solution.py:1056
  370.2 17.2 %copy-start.16 = (f32[48,3072]{1,0:T(8,128)}, f32[48,3072]{1,0:T(8,128)S(1)}, u32[]{:S(2)}) copy-start(f32[48,3072]{1,0:T(8,128)S(1)} %slice_dynamic-update-slice_fusion.6) | copy-start | bytes 1769476
  390.7 10.4 %collective-permute-start.10 = (bf16[592,128]{1,0:T(8,128)(2,1)S(1)}, bf16[592,128]{1,0:T(8,128)(2,1)S(1)}, u32[]{:S(2)}, u32[]{:S(2)}) collective-permute-start(bf16[592,128]{1,0:T(8,128)(2,1)S(1)} %reduce_sum.12), channel_id=1, source_target_pairs={{0,16},{16,0},{1,17},{17,1},{2,18},{18,2},{3,19},{19,3},{4,20},{20... | collective-permute-start | bytes 454664 | tf_op jit(solution)/shard_map/ppermute | solution.py:1056
  394.4 24.2 %all-to-all-start.6 = ((bf16[8,288,128]{2,1,0:T(8,128)(2,1)}), bf16[8,288,128]{2,1,0:T(8,128)(2,1)S(1)}, u32[]{:S(2)}, u32[]{:S(2)}) async-start(bf16[8,288,128]{2,1,0:T(8,128)(2,1)} %add_shares.3), calls=%async_computation.7 | async-start | bytes 1179648 | tf_op jit(solution)/shard_map/all_to_all | solution.py:1202
  413.1 14.2 %copy-start.13 = (bf16[1,384,384]{2,1,0:T(8,128)(2,1)S(1)}, bf16[1,384,384]{2,1,0:T(8,128)(2,1)}, u32[]{:S(2)}) copy-start(bf16[1,384,384]{2,1,0:T(8,128)(2,1)} %reduce-scatter.5.cloned.1.call-done) | copy-start | bytes 884740
  418.6 8.7 %collective-permute-start.11 = (bf16[384,384]{1,0:T(8,128)(2,1)}, bf16[384,384]{1,0:T(8,128)(2,1)S(1)}, u32[]{:S(2)}, u32[]{:S(2)}) collective-permute-start(bf16[384,384]{1,0:T(8,128)(2,1)} %bitcast.38), channel_id=1, source_target_pairs={{0,16},{16,0},{1,17},{17,1},{2,18},{18,2},{3,19},{19,3},{4,20},{20... | collective-permute-start | bytes 884744 | tf_op jit(solution)/shard_map/ppermute | solution.py:1056
  420.5 6.9 %copy-start.17 = (f32[32,768]{1,0:T(8,128)}, f32[32,768]{1,0:T(8,128)S(1)}, u32[]{:S(2)}) copy-start(f32[32,768]{1,0:T(8,128)S(1)} %constant_dynamic-update-slice_fusion) | copy-start | bytes 294916
  (15 other events, 29.1 us)
Sparse Core Ops, SparseCore 0:
  163.7 146.9 reduce-scatter.2
  315.1 98.0 reduce-scatter.4

commit v5 on v4

--- a/solution.py
+++ b/solution.py
@@ -17,7 +17,7 @@
 BF = jnp.bfloat16
 VMEM_WHOLE = pl.BlockSpec(memory_space=pltpu.VMEM)
 SMEM_WHOLE = pl.BlockSpec(memory_space=pltpu.SMEM)
-TOTAL, BEGIN, SEGMENT, KEYS, ACTIVE, CORE = range(6)
+TOTAL, BEGIN, SEGMENT, KEYS, ACTIVE, CORE, REP = range(7)
 
 
 def row_dot(left, right):
@@ -68,7 +68,9 @@
     return jax.ShapeDtypeStruct(shape, dtype)
 
 
-def call(kernel, outs, scratch, args, name, flops, grid=None, in_specs=None, out_specs=None, limit=56):
+def call(
+    kernel, outs, scratch, args, name, flops, grid=None, in_specs=None, out_specs=None, limit=56, aliases=None
+):
     size = sum(a.size * a.dtype.itemsize for a in args)
     size += sum(o.size * o.dtype.itemsize for o in outs)
     extra = {} if grid is None else {"grid": grid}
@@ -81,6 +83,7 @@
         compiler_params=pltpu.CompilerParams(vmem_limit_bytes=limit << 20),
         cost_estimate=pl.CostEstimate(flops=flops, bytes_accessed=size, transcendentals=0),
         name=name,
+        input_output_aliases=aliases or {},
         **extra,
     )(*args)
 
@@ -92,20 +95,16 @@
 
 
 def unpack_heads(packed_ref, targets):
-    blocks, half, lanes = packed_ref.shape
-    share = lanes // 2
-
-    def one(block, carry):
-        tile = packed_ref[block]
-        turned = tile.T
-        for side in range(2):
-            row = pl.multiple_of(block * 2 * half + side * half, half)
-            for place, (rows, columns) in enumerate(targets):
-                begin = side * share + place * HEAD_DIM
-                if rows is not None:
-                    rows[pl.ds(row, half), :] = tile[:, begin : begin + HEAD_DIM]
-                if columns is not None:
-                    columns[0:HEAD_DIM, pl.ds(row, half)] = turned[begin : begin + HEAD_DIM]
+    blocks, _, block = packed_ref.shape
+
+    def one(at, carry):
+        here = pl.ds(pl.multiple_of(at * block, block), block)
+        for place, (rows, columns) in enumerate(targets):
+            piece = packed_ref[at, place * HEAD_DIM : (place + 1) * HEAD_DIM]
+            if rows is not None:
+                rows[here, :] = piece.T
+            if columns is not None:
+                columns[0:HEAD_DIM, here] = piece
         return carry
 
     lax.fori_loop(0, blocks, one, 0)
@@ -143,8 +142,7 @@
 
 def attend_kernel(clips, halo, marks, packed_ref, out_ref, wide_ref, log_ref, query_t, keys, value_t):
     rows = wide_ref.shape[1]
-    half = packed_ref.shape[1]
-    block = 2 * half
+    block = packed_ref.shape[2]
     more = value_t.shape[0] - HEAD_DIM
     value_t[HEAD_DIM:] = jnp.where(
         lax.broadcasted_iota(jnp.int32, (more, value_t.shape[1]), 0) == 0, 1.0, 0.0
@@ -182,28 +180,22 @@
         attended = total[:HEAD_DIM] / mass
         wide_ref[:, pl.ds(first, Q_TILE)] = attended
         log_ref[:, pl.ds(first, Q_TILE)] = top + jnp.log2(mass)
-        narrow = attended.T.astype(BF)
+        narrow = attended.astype(BF)
         for inner in range(Q_TILE // block):
-            out_ref[index * (Q_TILE // block) + inner] = jnp.concatenate(
-                [
-                    narrow[inner * block : inner * block + half],
-                    narrow[inner * block + half : (inner + 1) * block],
-                ],
-                axis=1,
-            )
+            out_ref[index * (Q_TILE // block) + inner] = narrow[:, inner * block : (inner + 1) * block]
         return carry
 
     lax.fori_loop(0, rows // Q_TILE, query_tile, 0)
 
 
 def attend(marks, packed, clips, halo):
-    blocks, half, _ = packed.shape
-    rows = (blocks - 2 * halo) * 2 * half
-    key_rows = blocks * 2 * half
+    blocks, _, block = packed.shape
+    rows = (blocks - 2 * halo) * block
+    key_rows = blocks * block
     return call(
         functools.partial(attend_kernel, clips, halo),
         [
-            like((blocks - 2 * halo, half, 2 * HEAD_DIM), BF),
+            like((blocks - 2 * halo, HEAD_DIM, block), BF),
             like((HEAD_DIM, rows)),
             like((1, rows)),
         ],
@@ -220,13 +212,12 @@
 
 def attend_back_kernel(
     clips, halo, marks, packed_ref, grad_ref, wide_ref, log_ref, out_ref,
-    query, query_t, keys, key_t, values, grads, grad_t, key_grads, value_grads,
+    query_t, keys, key_t, values, grad_t, key_grads, value_grads,
 ):
-    unpack_heads(packed_ref, ((query, query_t), (keys, key_t), (values, None)))
-    unpack_heads(grad_ref, ((grads, grad_t),))
-    blocks, half, _ = packed_ref.shape
+    unpack_heads(packed_ref, ((None, query_t), (keys, key_t), (values, None)))
+    unpack_heads(grad_ref, ((None, grad_t),))
+    blocks, _, block = packed_ref.shape
     rows = wide_ref.shape[1]
-    block = 2 * half
     scale = HEAD_DIM ** (-0.5)
     key_grads[...] = jnp.zeros_like(key_grads)
     value_grads[...] = jnp.zeros_like(value_grads)
@@ -236,8 +227,7 @@
     def query_tile(index, carry):
         first = pl.multiple_of(index * Q_TILE, Q_TILE)
         own = pl.ds(halo * block + first, Q_TILE)
-        q, q_t = query[own, :], query_t[:, own]
-        g, g_t = grads[pl.ds(first, Q_TILE), :], grad_t[:, pl.ds(first, Q_TILE)]
+        q_t, g_t = query_t[:, own], grad_t[:, pl.ds(first, Q_TILE)]
         log_total = log_ref[:, pl.ds(first, Q_TILE)]
         delta = jnp.sum(
             g_t.astype(jnp.float32) * wide_ref[:, pl.ds(first, Q_TILE)], axis=0, keepdims=True
@@ -252,51 +242,43 @@
                 probs = jnp.where(allowed(column, starts, ends), probs, 0.0)
             prob_grad = plain_dot(values[here, :], g_t)
             score_grad = (probs * (prob_grad - delta)).astype(BF)
-            value_grads[here, :] += plain_dot(probs.astype(BF), g)
-            key_grads[here, :] += plain_dot(score_grad, q)
+            value_grads[:, here] += row_dot(g_t, probs.astype(BF))
+            key_grads[:, here] += row_dot(q_t, score_grad)
             return running + plain_dot(key_t[:, here], score_grad)
 
         query_grad = over_spans(spans, key_tile, jnp.zeros((HEAD_DIM, Q_TILE), jnp.float32))
-        query_grad = (query_grad.T * scale).astype(BF)
+        query_grad = (query_grad * scale).astype(BF)
         for inner in range(Q_TILE // block):
             spot = halo + index * (Q_TILE // block) + inner
-            out_ref[spot, :, 0:HEAD_DIM] = query_grad[inner * block : inner * block + half]
-            out_ref[spot, :, 3 * HEAD_DIM : 4 * HEAD_DIM] = query_grad[
-                inner * block + half : (inner + 1) * block
-            ]
+            out_ref[spot, 0:HEAD_DIM] = query_grad[:, inner * block : (inner + 1) * block]
         return carry
 
     lax.fori_loop(0, rows // Q_TILE, query_tile, 0)
 
     def finish(spot, carry):
-        for side in range(2):
-            row = pl.multiple_of(spot * block + side * half, half)
-            begin = (3 * side + 1) * HEAD_DIM
-            out_ref[spot, :, begin : begin + 2 * HEAD_DIM] = jnp.concatenate(
-                [key_grads[pl.ds(row, half), :] * scale, value_grads[pl.ds(row, half), :]], axis=1
-            ).astype(BF)
+        here = pl.ds(pl.multiple_of(spot * block, block), block)
+        out_ref[spot, HEAD_DIM : 2 * HEAD_DIM] = (key_grads[:, here] * scale).astype(BF)
+        out_ref[spot, 2 * HEAD_DIM :] = value_grads[:, here].astype(BF)
         return carry
 
     lax.fori_loop(0, blocks, finish, 0)
 
 
 def attend_back(marks, packed, grad, wide, log_total, clips, halo):
-    blocks, half, lanes = packed.shape
+    blocks, lanes, block = packed.shape
     rows = wide.shape[1]
-    key_rows = blocks * 2 * half
+    key_rows = blocks * block
     return call(
         functools.partial(attend_back_kernel, clips, halo),
-        [like((blocks, half, lanes), BF)],
+        [like((blocks, lanes, block), BF)],
         [
-            pltpu.VMEM((key_rows, HEAD_DIM), BF),
             pltpu.VMEM((HEAD_DIM, key_rows), BF),
             pltpu.VMEM((key_rows, HEAD_DIM), BF),
             pltpu.VMEM((HEAD_DIM, key_rows), BF),
             pltpu.VMEM((key_rows, HEAD_DIM), BF),
-            pltpu.VMEM((rows, HEAD_DIM), BF),
             pltpu.VMEM((HEAD_DIM, rows), BF),
-            pltpu.VMEM((key_rows, HEAD_DIM), jnp.float32),
-            pltpu.VMEM((key_rows, HEAD_DIM), jnp.float32),
+            pltpu.VMEM((HEAD_DIM, key_rows), jnp.float32),
+            pltpu.VMEM((HEAD_DIM, key_rows), jnp.float32),
         ],
         (marks, packed, grad, wide, log_total),
         "attend_back",
@@ -505,9 +487,9 @@
         store_pairs(out_refs, even_core, slice(piece * group_width, (piece + 1) * group_width), values)
 
 
-def taps_grad(marks, both, shape, clips):
-    blocks, two, block = both.shape
-    group_width = two // 2
+def taps_grad(marks, both, shape, clips, width):
+    blocks, _, block = both.shape
+    group_width = width // GROUPS
     half = KERNEL // 2
     halo_rows = (blocks - RING) // 2 * block
     span = -(-(RING * block + half * clips) // 128) * 128
@@ -558,7 +540,58 @@
 
 
 def add_shares(own, other):
-    return call(add_shares_kernel, [like(other.shape, BF)], [], (own, other), "add_shares", 0)[0]
+    block = pl.BlockSpec((2,) + other.shape[1:], lambda at: (at, 0, 0))
+    return call(
+        add_shares_kernel,
+        [like(other.shape, BF)],
+        [],
+        (own, other),
+        "add_shares",
+        0,
+        (other.shape[0] // 2,),
+        [block] * 2,
+        (block,),
+    )[0]
+
+
+def split_shares_kernel(clips, marks, own_ref, other_ref, kept_ref, sent_ref):
+    total = (own_ref[...].astype(jnp.float32) + other_ref[...].astype(jnp.float32)).astype(BF)
+    rows = kept_ref.shape[1]
+    lower = marks[clips + REP] == 0
+    kept_ref[...] = jnp.where(lower, total[:, :rows], total[:, rows:])
+    sent_ref[...] = jnp.where(lower, total[:, rows:], total[:, :rows])
+
+
+def split_shares(marks, own, other, clips):
+    shares, rows, lanes = own.shape
+    return call(
+        functools.partial(split_shares_kernel, clips),
+        [like((shares, rows // 2, lanes), BF)] * 2,
+        [],
+        (marks, own, other),
+        "split_shares",
+        0,
+    )
+
+
+def add_below_kernel(own_ref, other_ref, _, out_ref):
+    add_shares_kernel(own_ref, other_ref, out_ref)
+
+
+def add_below(own, other, straight):
+    block = pl.BlockSpec((2,) + own.shape[1:], lambda at: (at, 0, 0))
+    return call(
+        add_below_kernel,
+        [like(straight.shape, BF)],
+        [],
+        (own, other, straight),
+        "add_below",
+        0,
+        (own.shape[0] // 2,),
+        [block, block, pl.BlockSpec(memory_space=pl.ANY)],
+        (pl.BlockSpec((2,) + own.shape[1:], lambda at: (at, 1, 0)),),
+        aliases={2: 0},
+    )[0]
 
 
 def join_pair_kernel(clips, marks, taps_ref, other_ref, out_ref):
@@ -666,25 +699,23 @@
     )
 
 
-def project_kernel(conv_ref, start_ref, table_ref, weight_ref, hidden_ref, packed_ref):
+def project_kernel(conv_ref, start_ref, table_ref, weight_ref, hidden_ref, hidden_b_ref, packed_ref):
     rows, width = start_ref.shape
-    half = rows // 2
     mixed = start_ref[...] + gelu_both(conv_ref[...] + table_ref[4:5])[0]
     unit, _ = norm_parts(mixed)
     hidden = unit * table_ref[0:1] + table_ref[5:6]
     hidden_ref[...] = hidden
     hidden_b = hidden.astype(BF)
+    hidden_b_ref[...] = hidden_b
     shifts = (table_ref[6:7], jnp.zeros((1, width), jnp.float32), table_ref[7:8])
-    parts = [
-        (plain_dot(hidden_b, weight_ref[:, at * width : (at + 1) * width]) + shift).astype(BF)
-        for at, shift in enumerate(shifts)
-    ]
     heads = width // HEAD_DIM
-    for head in range(heads):
-        lanes = slice(head * HEAD_DIM, (head + 1) * HEAD_DIM)
-        packed_ref[head] = jnp.concatenate(
-            [part[:half, lanes] for part in parts] + [part[half:, lanes] for part in parts], axis=1
-        )
+    for at, shift in enumerate(shifts):
+        part = plain_dot(hidden_b, weight_ref[:, at * width : (at + 1) * width]) + shift
+        turned = part.astype(BF).T
+        for head in range(heads):
+            packed_ref[head, at * HEAD_DIM : (at + 1) * HEAD_DIM] = turned[
+                head * HEAD_DIM : (head + 1) * HEAD_DIM
+            ]
     for head in range(heads, RING):
         packed_ref[head] = jnp.zeros_like(packed_ref[head])
 
@@ -693,7 +724,7 @@
     rows, width = start.shape
     return call(
         project_kernel,
-        [like((rows, width)), like((RING, rows // 2, 6 * HEAD_DIM), BF)],
+        [like((rows, width)), like((rows, width), BF), like((RING, 3 * HEAD_DIM, rows), BF)],
         [],
         (conv_sum, start, table, weight),
         "project_heads",
@@ -702,37 +733,62 @@
 
 
 def middle_kernel(
-    heads_ref, hidden_ref, table_ref, out_weight_ref, in_ref, in_bias_ref, back_ref, out_grad_ref,
-    layer_ref, grad_heads_ref, grad_second_ref, out_part_ref, sums_ref, in_bias_grad_ref, joined_ref,
+    clips, marks, heads_ref, hidden_ref, table_ref, out_weight_ref, in_ref, in_bias_ref, back_ref, out_grad_ref,
+    layer_ref, grad_heads_ref, grad_second_ref, sums_ref, in_bias_grad_ref, kept_ref, sent_ref, straight_ref,
     attended, before, second, second_b, second_t, inner_b, slope, total, grad_last, grad_last_b,
     joined, sems,
 ):
     step = pl.program_id(0)
     rows, width = hidden_ref.shape
-    half = rows // 2
     chunk = in_ref.shape[1]
     chunks = pl.num_programs(0) // 2
     heads = width // HEAD_DIM
-    shares = joined_ref.shape[0]
+    shares = kept_ref.shape[0]
+    lower = marks[clips + REP] == 0
     in_rows = width // shares
     back_rows = chunk * chunks // shares
     owners = chunk // back_rows
 
-    def in_copy(at):
-        place = (slice(None), pl.ds(pl.multiple_of(at * in_rows, 16), in_rows))
-        return pltpu.make_async_copy(joined.at[place], joined_ref.at[place], sems.at[0, at])
-
-    def back_copy(at):
-        place = (pl.ds(at * owners, owners), pl.ds(in_rows * chunks, joined_ref.shape[1] - in_rows * chunks))
-        return pltpu.make_async_copy(joined.at[place], joined_ref.at[place], sems.at[1, at])
+    first_blocks = 3 * chunks // 4
+
+    def moves(half, place, sem, act):
+        for keeps, target in ((lower, (kept_ref, sent_ref)[half]), (~lower, (sent_ref, kept_ref)[half])):
+
+            @pl.when(keeps)
+            def _():
+                act(pltpu.make_async_copy(joined.at[half].at[place], target.at[place], sem))
+
+    def in_moves(at, act):
+        @pl.when(at < first_blocks)
+        def _():
+            place = (slice(None), pl.ds(pl.multiple_of(at * in_rows, 16), in_rows))
+            moves(0, place, sems.at[0, at], act)
+
+        @pl.when(at >= first_blocks)
+        def _():
+            place = (slice(None), pl.ds(pl.multiple_of((at - first_blocks) * in_rows, 16), in_rows))
+            act(pltpu.make_async_copy(joined.at[2].at[place], straight_ref.at[place], sems.at[0, at]))
+
+    def back_moves(at, act):
+        mine = pl.ds(at * owners, owners)
+        moves(1, (mine, pl.ds(0, back_rows)), sems.at[1, at], act)
+        place = (mine, pl.ds((chunks - first_blocks) * in_rows, back_rows))
+        act(pltpu.make_async_copy(joined.at[2].at[place], straight_ref.at[place], sems.at[2, at]))
+
+    def out_moves(act):
+        moves(1, (slice(None), pl.ds(back_rows, 2 * in_rows)), sems.at[3, 0], act)
+
+    def go(copy):
+        copy.start()
+
+    def wait(copy):
+        copy.wait()
 
     @pl.when(step == 0)
     def _():
         for head in range(heads):
-            lanes = slice(head * HEAD_DIM, (head + 1) * HEAD_DIM)
-            attended[:half, lanes] = heads_ref[head, :, :HEAD_DIM]
-            attended[half:, lanes] = heads_ref[head, :, HEAD_DIM:]
-        value = hidden_ref[...] + plain_dot(attended[...], out_weight_ref[...]) + table_ref[8:9]
+            attended[head * HEAD_DIM : (head + 1) * HEAD_DIM] = heads_ref[head]
+        value = hidden_ref[...] + over_rows_dot(attended[...], out_weight_ref[...]) + table_ref[8:9]
         before[...] = value
         unit, _ = norm_parts(value)
         value = unit * table_ref[1:2] + table_ref[9:10]
@@ -771,19 +827,21 @@
         grad_b = grad.astype(BF)
         total[...] += row_dot(grad_b, in_ref[...])
         product = plain_dot(second_t[...], grad_b).astype(BF)
+        straight = turn >= first_blocks
+        row = pl.multiple_of(jnp.where(straight, turn - first_blocks, turn) * in_rows, 16)
         for share in range(shares):
-            joined[share, pl.ds(pl.multiple_of(turn * in_rows, 16), in_rows), :] = product[
+            joined[jnp.where(straight, 2, 0), share, pl.ds(row, in_rows), :] = product[
                 share * in_rows : (share + 1) * in_rows
             ]
-        in_copy(turn).start()
+        in_moves(turn, go)
         product = over_rows_dot(inner_b[turn], grad_last_b[...]).astype(BF)
         for owner in range(owners):
             for place in range(width // SHARE):
-                begin = in_rows * chunks + place * back_rows
-                joined[turn * owners + owner, begin : begin + back_rows, :] = product[
+                begin = (chunks - first_blocks) * in_rows if place else 0
+                joined[1 + place, turn * owners + owner, begin : begin + back_rows, :] = product[
                     owner * back_rows : (owner + 1) * back_rows, place * SHARE : (place + 1) * SHARE
                 ]
-        back_copy(turn).start()
+        back_moves(turn, go)
 
     @pl.when(step == 2 * chunks - 1)
     def _():
@@ -795,50 +853,54 @@
         sums_ref[5:6] = bias
         sums_ref[6:8] = jnp.zeros((2, width), jnp.float32)
         back_b = back.astype(BF)
-        grads = row_dot(back_b, out_weight_ref[...]).astype(BF)
+        grads = row_dot(out_weight_ref[...], back_b).astype(BF)
         for head in range(heads):
-            lanes = slice(head * HEAD_DIM, (head + 1) * HEAD_DIM)
-            grad_heads_ref[head] = jnp.concatenate([grads[:half, lanes], grads[half:, lanes]], axis=1)
+            grad_heads_ref[head] = grads[head * HEAD_DIM : (head + 1) * HEAD_DIM]
         for head in range(heads, RING):
             grad_heads_ref[head] = jnp.zeros_like(grad_heads_ref[head])
-        product = over_rows_dot(attended[...], back_b).astype(BF)
+        product = plain_dot(attended[...], back_b).astype(BF)
         for share in range(shares):
             for place in range(width // SHARE):
-                out_part_ref[share, place * in_rows : (place + 1) * in_rows, :] = product[
+                begin = back_rows + place * in_rows
+                joined[1, share, begin : begin + in_rows, :] = product[
                     share * in_rows : (share + 1) * in_rows, place * SHARE : (place + 1) * SHARE
                 ]
+        out_moves(go)
 
         def finish(at, carry):
-            in_copy(at).wait()
-            back_copy(at).wait()
+            in_moves(at, wait)
+            back_moves(at, wait)
             return carry
 
         lax.fori_loop(0, chunks, finish, 0)
-
-
-def middle(heads, hidden, table, out_weight, ffn_in, in_bias, ffn_out, out_grad, count):
+        out_moves(wait)
+
+
+def middle(marks, clips, heads, hidden, table, out_weight, ffn_in, in_bias, ffn_out, out_grad, count):
     rows, width = hidden.shape
     inner = ffn_in.shape[1]
     chunk = SHARE
     chunks = inner // chunk
     own = lambda shape: pl.BlockSpec(shape, lambda step: (0,) * len(shape))
+    third = (2 * inner + width) * (width // count) // SHARE // 3
     outs = [
         like((rows, width), BF),
-        like((RING, rows // 2, 2 * HEAD_DIM), BF),
+        like((RING, HEAD_DIM, rows), BF),
         like((rows, width)),
-        like((count, width // count * width // SHARE, SHARE), BF),
         like((8, width)),
         like((1, inner)),
-        like((count, 2 * width // count * inner // SHARE, SHARE), BF),
+        like((count, third, SHARE), BF),
+        like((count, third, SHARE), BF),
+        like((count, 2 * third, SHARE), BF),
     ]
-    args = (heads, hidden, table, out_weight, ffn_in, in_bias, ffn_out, out_grad)
-    in_specs = [own(a.shape) for a in args]
-    in_specs[4] = pl.BlockSpec((width, chunk), lambda step: (0, step % chunks))
-    in_specs[6] = pl.BlockSpec((chunk, width), lambda step: (step % chunks, 0))
+    args = (marks, heads, hidden, table, out_weight, ffn_in, in_bias, ffn_out, out_grad)
+    in_specs = [SMEM_WHOLE] + [own(a.shape) for a in args[1:]]
+    in_specs[5] = pl.BlockSpec((width, chunk), lambda step: (0, step % chunks))
+    in_specs[7] = pl.BlockSpec((chunk, width), lambda step: (step % chunks, 0))
     out_specs = [own(o.shape) for o in outs]
-    out_specs[6] = pl.BlockSpec(memory_space=pl.ANY)
+    out_specs[5] = out_specs[6] = out_specs[7] = pl.BlockSpec(memory_space=pl.ANY)
     scratch = [
-        pltpu.VMEM((rows, width), BF),
+        pltpu.VMEM((width, rows), BF),
         pltpu.VMEM((rows, width), jnp.float32),
         pltpu.VMEM((rows, width), jnp.float32),
         pltpu.VMEM((rows, width), BF),
@@ -848,41 +910,44 @@
         pltpu.VMEM((rows, width), jnp.float32),
         pltpu.VMEM((rows, width), jnp.float32),
         pltpu.VMEM((rows, width), BF),
-        pltpu.VMEM(outs[6].shape, BF),
-        pltpu.SemaphoreType.DMA((2, chunks)),
+        pltpu.VMEM((3,) + outs[5].shape, BF),
+        pltpu.SemaphoreType.DMA((4, chunks)),
     ]
     return call(
-        middle_kernel, outs, scratch, args, "middle", 2 * 10**10, (2 * chunks,), in_specs, tuple(out_specs)
+        functools.partial(middle_kernel, clips), outs, scratch, args, "middle", 2 * 10**10, (2 * chunks,), in_specs, tuple(out_specs)
     )
 
 
 def after_heads_kernel(
-    packed_ref, grad_second_ref, hidden_ref, conv_ref, start_ref, table_ref, weight_ref, out_part_ref,
-    mixed_ref, conv_b_ref, groups_ref, joined_ref, sums_ref, grads,
+    whole, packed_ref, grad_second_ref, hidden_ref, conv_ref, start_ref, table_ref, weight_ref, *refs
 ):
     rows, width = hidden_ref.shape
-    half = rows // 2
     heads = width // HEAD_DIM
-    shares = joined_ref.shape[0]
-    own_rows = width // shares
+    if whole:
+        heads_ref, mixed_ref, conv_b_ref, groups_ref, sums_ref, grads = refs
+        groups_ref[:, 2 * width // GROUPS :] = heads_ref[...]
+    else:
+        mixed_ref, conv_b_ref, groups_ref, sums_ref, joined_ref, grads, hidden_t = refs
     for head in range(heads):
-        tile = packed_ref[head]
         for part in range(3):
-            lanes = slice(part * width + head * HEAD_DIM, part * width + (head + 1) * HEAD_DIM)
-            grads[:half, lanes] = tile[:, part * HEAD_DIM : (part + 1) * HEAD_DIM]
-            grads[half:, lanes] = tile[:, (part + 3) * HEAD_DIM : (part + 4) * HEAD_DIM]
-    hidden_t = hidden_ref[...].T.astype(BF)
-    blocks = 3 * width // SHARE
-    for place in range(blocks):
-        lanes = slice(place * SHARE, (place + 1) * SHARE)
-        product = plain_dot(hidden_t, grads[:, lanes]).astype(BF)
-        for share in range(shares):
-            joined_ref[share, place * own_rows : (place + 1) * own_rows, :] = product[
-                share * own_rows : (share + 1) * own_rows
-            ]
-    for share in range(shares):
-        joined_ref[share, blocks * own_rows :, :] = out_part_ref[share]
-    back = grad_second_ref[...] + row_dot(grads[...], weight_ref[...])
+            row = part * width + head * HEAD_DIM
+            grads[row : row + HEAD_DIM] = packed_ref[head, part * HEAD_DIM : (part + 1) * HEAD_DIM]
+    if not whole:
+        shares = joined_ref.shape[0]
+        own_rows = width // shares
+        hidden_t[...] = hidden_ref[...].T.astype(BF)
+
+        def weight_block(place, carry):
+            row = pl.multiple_of(place * SHARE, SHARE)
+            product = row_dot(hidden_t[...], grads[pl.ds(row, SHARE), :]).astype(BF)
+            for share in range(shares):
+                joined_ref[share, pl.ds(pl.multiple_of(place * own_rows, 16), own_rows), :] = product[
+                    share * own_rows : (share + 1) * own_rows
+                ]
+            return carry
+
+        lax.fori_loop(0, 3 * width // SHARE, weight_block, 0)
+    back = grad_second_ref[...] + plain_dot(weight_ref[...], grads[...]).T
     value, slope = gelu_both(conv_ref[...] + table_ref[4:5])
     unit, inverse = norm_parts(start_ref[...] + value)
     mixed, gain, bias = norm_back(unit, inverse, table_ref[0:1], back)
@@ -895,27 +960,76 @@
     sums_ref[0:1] = gain
     sums_ref[1:2] = bias
     sums_ref[2:3] = row_sum(conv)
-    sums_ref[3:4] = row_sum(grads[:, :width].astype(jnp.float32))
-    sums_ref[4:5] = row_sum(grads[:, 2 * width :].astype(jnp.float32))
+    ones = jnp.ones((8, rows), BF)
+    sums_ref[3:4] = row_dot(ones, grads[:width])[0:1]
+    sums_ref[4:5] = row_dot(ones, grads[2 * width :])[0:1]
     sums_ref[5:8] = jnp.zeros((3, width), jnp.float32)
 
 
-def after_heads(packed, grad_second, hidden, conv_sum, start, table, weight, out_part):
+def after_heads(packed, grad_second, hidden, conv_sum, start, table, weight, head_grads):
     rows, width = hidden.shape
-    shares = out_part.shape[0]
-    return call(
-        after_heads_kernel,
-        [
-            like((rows, width)), like((rows, width), BF),
-            like((GROUPS, 2 * width // GROUPS, rows), BF),
-            like((shares, out_part.shape[1] + width // shares * 3 * width // SHARE, SHARE), BF),
-            like((8, width)),
-        ],
-        [pltpu.VMEM((rows, 3 * width), BF)],
-        (packed, grad_second, hidden, conv_sum, start, table, weight, out_part),
-        "after_heads",
-        6 * 10**9,
-    )
+    whole = head_grads is not None
+    lines = 2 * width // GROUPS + (width // RING if whole else 0)
+    outs = [like((rows, width)), like((rows, width), BF), like((GROUPS, lines, rows), BF), like((8, width))]
+    scratch = [pltpu.VMEM((3 * width, rows), BF)]
+    args = (packed, grad_second, hidden, conv_sum, start, table, weight)
+    if whole:
+        args += (head_grads,)
+    else:
+        outs.append(like((RING, width // RING * 3 * width // SHARE, SHARE), BF))
+        scratch.append(pltpu.VMEM((width, rows), BF))
+    return call(
+        functools.partial(after_heads_kernel, whole), outs, scratch, args, "after_heads", 5 * 10**9
+    )
+
+
+def head_grads_kernel(clips, marks, packed_ref, hidden_ref, other_ref, out_ref, turned):
+    blocks, lines, block = packed_ref.shape
+    core = marks[clips + CORE]
+    width = hidden_ref.shape[2]
+
+    def one(at, total):
+        total = total + plain_dot(packed_ref[2 * at + core], hidden_ref[at])
+        return total + plain_dot(packed_ref[2 * at + 1 - core], other_ref[at])
+
+    total = lax.fori_loop(0, blocks // 2, one, jnp.zeros((lines, width), jnp.float32))
+    turned[...] = jnp.concatenate([total, jnp.zeros((block - lines, width), jnp.float32)], axis=0).T.astype(BF)
+    own = width // RING
+    for share in range(RING):
+        out_ref[share] = turned[share * own : (share + 1) * own]
+
+
+def head_grads(marks, packed, hidden, other, clips):
+    block = packed.shape[2]
+    width = hidden.shape[2]
+    return call(
+        functools.partial(head_grads_kernel, clips),
+        [like((RING, width // RING, block), BF)],
+        [pltpu.VMEM((width, block), BF)],
+        (marks, packed, hidden, other),
+        "head_grads",
+        3 * 10**9,
+    )[0]
+
+
+def weave_heads_kernel(own_ref, other_ref, out_ref):
+    heads = own_ref.shape[0]
+    for part in range(3):
+        lanes = slice(part * HEAD_DIM, (part + 1) * HEAD_DIM)
+        out_ref[:, part * heads * HEAD_DIM : (part + 1) * heads * HEAD_DIM] = jnp.concatenate(
+            [
+                own_ref[head, :, lanes].astype(jnp.float32) + other_ref[head, :, lanes].astype(jnp.float32)
+                for head in range(heads)
+            ],
+            axis=1,
+        )
+
+
+def weave_heads(own, other):
+    heads, rows, _ = own.shape
+    return call(
+        weave_heads_kernel, [like((rows, 3 * heads * HEAD_DIM))], [], (own, other), "weave_heads", 0
+    )[0]
 
 
 def stem_back_kernel(
@@ -992,18 +1106,18 @@
         spread[share, 14:15, 0:own_chans] = gain_sum[:, lanes]
         spread[share, 15:16, 0:own_chans] = bias_sum[:, lanes]
     store_pairs(
-        joined_refs, even_core, slice(at, at + 16), [spread[share].astype(BF) for share in range(shares)]
+        joined_refs, even_core, slice(at, at + 32), [spread[share].astype(BF) for share in range(shares)]
     )
 
 
 def stem_back(marks, input_grad, mixed, normed, pre, unfold, weight, gain, proj, sums, shares, clips):
     rows, chans = pre.shape
     width = input_grad.shape[1]
-    pieces = (chans // RING * width + 3 * chans // RING * chans) // PIECE + 16
+    pieces = (chans // RING * width + 3 * chans // RING * chans) // PIECE + 32
     return call(
         functools.partial(stem_back_kernel, clips),
         [like((2 * rows, chans)), like((1, chans))] + [like((n, pieces, PIECE), BF) for n in shares],
-        [pltpu.VMEM((12, width), jnp.float32), pltpu.VMEM((RING, 16, PIECE), jnp.float32),
+        [pltpu.VMEM((12, width), jnp.float32), pltpu.VMEM((RING, 32, PIECE), jnp.float32),
          pltpu.VMEM((2 * rows, PIECE), jnp.float32)],
         (marks, input_grad, mixed, normed, pre, unfold, weight, gain, proj) + sums,
         "stem_back",
@@ -1139,7 +1253,7 @@
     segment_begin = (place // RING) * RING * rows_dev
     active = jnp.where(place % RING < HEADS, 1, 0)
     marks = jnp.concatenate(
-        [ends, jnp.stack([jnp.int32(total), begin, segment_begin, segment_begin - far * rows_dev, active, place % 2])]
+        [ends, jnp.stack([jnp.int32(total), begin, segment_begin, segment_begin - far * rows_dev, active, place % 2, lax.axis_index("rep") if count == RING else 0])]
     ).astype(jnp.int32)
     next_row = from_behind(samples[0, :1], "seq", -1)
     one_weights = conv_weights(False, pos_weight, 0, TURNS // 2)
@@ -1153,32 +1267,56 @@
     rest_weights = conv_weights(False, rest_source, TURNS // 2, TURNS // 2)
     before, after, rest_weights = lax.optimization_barrier((before, after, rest_weights))
     conv_sum = conv_rows(False, marks, before, start_b, after, (one_weights, rest_weights), clips)
-    hidden, packed = project_heads(conv_sum, start_x, table, attn_in)
+    hidden, hidden_b, packed = project_heads(conv_sum, start_x, table, attn_in)
+    pairs = [(i, i ^ 1) for i in range(count)]
+    alike = [list(range(core, count, 2)) for core in range(2)]
     back_source, _ = lax.optimization_barrier((pos_weight, hidden))
     packed = with_far_blocks(swap(packed), far)
     back_weights = conv_weights(True, back_source, 0, TURNS)
-    packed, back_weights = lax.optimization_barrier((packed, back_weights))
+    packed, back_weights, hidden_b = lax.optimization_barrier((packed, back_weights, hidden_b))
+    if count == RING:
+        gathered = lax.all_gather(hidden_b, "seq", axis=0, tiled=False, axis_index_groups=alike)
     attended_heads, wide, log_total = attend(marks, packed, clips, far)
-    layer_out, grad_heads, grad_pre_second, out_part, middle_sums, inner_sums, ffn_joined = middle(
-        swap(attended_heads), hidden, table, attn_out, ffn_in, ffn_in_bias[None], ffn_out, out_grad[0],
+    layer_out, grad_heads, grad_pre_second, middle_sums, inner_sums, ffn_kept, ffn_sent, straight = middle(
+        marks, clips, swap(attended_heads), hidden, table, attn_out, ffn_in, ffn_in_bias[None], ffn_out, out_grad[0],
         RING,
     )
     near_rows, near_chans, near_inner = width // RING, chans // RING, inner // RING
+    if count == RING:
+        grad_heads, gathered = lax.optimization_barrier((grad_heads, gathered))
+        other_gathered = lax.ppermute(gathered, "seq", pairs)
+        ffn_other = other_stream(ffn_sent)
     grad_heads = swap(grad_heads)
-    ffn_share = over_seq(
-        regroup(ffn_joined, [(inner // SHARE, near_rows), (width // SHARE, near_inner)])
-    )
     packed_grad = attend_back(marks, packed, grad_heads, wide, log_total, clips, far)
-    grad_mixed, grad_conv_b, grad_packed, attn_joined, after_sums = after_heads(
-        swap(fold_far_blocks(packed_grad, far)), grad_pre_second, hidden, conv_sum, start_x, table,
-        attn_in, out_part,
-    )
+    own_heads = None
+    if count == RING:
+        own_heads = head_grads(marks, packed_grad, gathered, other_gathered, clips)
+    swapped = swap(fold_far_blocks(packed_grad, far))
+    if count == RING:
+        ffn_other, own_heads = lax.optimization_barrier((ffn_other, own_heads))
+        ffn_joined = add_below(ffn_kept, ffn_other, straight)
+        swapped, own_heads, ffn_joined = lax.optimization_barrier((swapped, own_heads, ffn_joined))
+    grad_mixed, grad_conv_b, grad_packed, after_sums, *attn_joined = after_heads(
+        swapped, grad_pre_second, hidden, conv_sum, start_x, table, attn_in, own_heads
+    )
+    if count != RING:
+        ffn_joined = jnp.concatenate([straight[:, : ffn_kept.shape[1]], ffn_kept, ffn_sent], axis=1)
+        first_blocks = 3 * inner // SHARE // 4
+        ffn_joined = regroup(
+            ffn_joined,
+            [
+                (inner // SHARE - first_blocks, near_rows),
+                (1, near_inner),
+                (first_blocks, near_rows),
+                (1, near_inner),
+                (2, near_rows),
+            ],
+        )
+    ffn_share = over_seq(ffn_joined)
     before, after = edges(grad_conv_b, half)
     before, after, grad_packed = lax.optimization_barrier((before, after, grad_packed))
     grad_groups = swap(grad_packed)
     input_grad = conv_rows(True, marks, before, grad_conv_b, after, (back_weights,), clips)
-    input_grad, grad_groups, ffn_share = lax.optimization_barrier((input_grad, grad_groups, ffn_share))
-    attn_share = over_seq(regroup(attn_joined, [(4 * width // SHARE, near_rows)]))
     shape = (RING // 2,) * 2 if count == RING else (RING,)
     sample_grad, carried, *stem_shares = stem_back(
         marks, input_grad, grad_mixed, normed_b, stem_pre, unfold, stem_weight, stem_gain[None],
@@ -1188,30 +1326,57 @@
     own = width // count
     own_chans = chans // count
     own_taps = KERNEL // count
-    grad_ffn = spread_out(sum_pair(ffn_share), [(own, inner), (inner // count, width)], SHARE)
+
+    def ffn_parts(share):
+        other = other_stream(share)
+        if count == RING:
+            at = share.shape[0] // 2
+            lower = lax.axis_index("rep") == 0
+            share = jnp.concatenate(
+                [
+                    share[:at].astype(jnp.float32) + other[:at].astype(jnp.float32),
+                    jnp.where(lower, share[at:], other[at:]).astype(jnp.float32),
+                    jnp.where(lower, other[at:], share[at:]).astype(jnp.float32),
+                ],
+                axis=0,
+            )
+        else:
+            share = share.astype(jnp.float32) + other.astype(jnp.float32)
+        most = 3 * inner // 4
+        sizes = [(own, inner - most), (inner // count, SHARE), (own, most), (inner // count, SHARE), (own, width)]
+        in_end, back_end, in_start, back_start, out = spread_out(share, sizes, SHARE)
+        return (
+            jnp.concatenate([in_start, in_end], axis=1),
+            jnp.concatenate([back_start, back_end], axis=1),
+            out,
+        )
+
     if count == RING:
-        pairs = [(i, i ^ 1) for i in range(count)]
-        alike = [list(range(core, count, 2)) for core in range(2)]
-        stem_joined = add_shares(stem_shares[0], lax.ppermute(stem_shares[1], "seq", pairs))
-        stem_joined, grad_groups = lax.optimization_barrier((stem_joined, grad_groups))
-        received = lax.all_to_all(stem_joined, "seq", 0, 0, axis_index_groups=alike)
-        taps, sent_taps = taps_grad(marks, grad_groups, shape, clips)
+        kept, sent = split_shares(marks, stem_shares[0], lax.ppermute(stem_shares[1], "seq", pairs), clips)
+        other_sent = other_stream(sent)
+        taps, sent_taps = taps_grad(marks, grad_groups, shape, clips, width)
+        other_sent, taps, sent_taps = lax.optimization_barrier((other_sent, taps, sent_taps))
+        received = lax.all_to_all(add_shares(kept, other_sent), "seq", 0, 0, axis_index_groups=alike)
         taps = join_pair(marks, taps, lax.ppermute(sent_taps, "seq", pairs), clips)
         taps = add_shares(taps, other_stream(taps))
-        taps, received, grad_ffn = lax.optimization_barrier((taps, received, grad_ffn))
+        taps, received, grad_groups = lax.optimization_barrier((taps, received, grad_groups))
+        by_head = grad_groups[:HEADS, 2 * group_width :]
+        grad_attn_in = weave_heads(by_head, other_stream(by_head))
         pos_pieces = lax.all_to_all(taps, "seq", 0, 0, axis_index_groups=alike)
         pos_pieces = pos_pieces.reshape(GROUPS, -1, PIECE)
     else:
-        (taps,) = taps_grad(marks, with_far_blocks(grad_groups, 1), shape, clips)
+        attn_share = over_seq(regroup(attn_joined[0], [(3 * width // SHARE, near_rows)]))
+        (grad_attn_in,) = spread_out(sum_pair(attn_share), [(own, 3 * width)], SHARE)
+        (taps,) = taps_grad(marks, with_far_blocks(grad_groups, 1), shape, clips, width)
         taps = add_shares(taps, other_stream(taps))
         stem_joined = stem_shares[0]
         stem_joined = jnp.concatenate(
             [
                 regroup(
-                    stem_joined[:, :-16],
+                    stem_joined[:, :-32],
                     [(width // PIECE, near_chans), (chans // PIECE, 3 * near_chans)],
                 ),
-                regroup_small(stem_joined[:, -16:], (own, inner // count, own_chans)),
+                regroup_small(stem_joined[:, -32:-16], (own, inner // count, own_chans)),
             ],
             axis=1,
         )
@@ -1225,17 +1390,21 @@
         by_tap = jnp.sum(by_tap.astype(jnp.float32), axis=0).astype(jnp.bfloat16)
         by_tap = by_tap.reshape(RING, own_taps, group_width, group_width).transpose(0, 2, 1, 3)
         pos_pieces = swap(by_tap.reshape(RING, group_width, own_taps * group_width))
-    pos_pieces, attn_share = lax.optimization_barrier((pos_pieces, attn_share))
     pos_grad = weave_taps(pos_pieces, own_taps, group_width)
-    stem_total = sum_pair(jnp.sum(received.astype(jnp.float32), axis=0).astype(jnp.bfloat16))
+    stem_total = jnp.sum(received.astype(jnp.float32), axis=0).astype(jnp.bfloat16)
+    if count == RING:
+        other = other_stream(stem_total)
+        lower = lax.axis_index("rep") == 0
+        stem_total = jnp.concatenate(
+            [jnp.where(lower, stem_total, other), jnp.where(lower, other, stem_total)], axis=0
+        )[:-16].astype(jnp.float32)
+    else:
+        stem_total = sum_pair(stem_total)
     grad_proj, grad_stem = spread_out(
         stem_total[:-16], [(own_chans, width), (3 * own_chans, chans)], PIECE
     )
     small = stem_total[-16:]
-    grad_ffn_in, grad_ffn_out = grad_ffn
-    grad_attn_in, grad_attn_out = spread_out(
-        sum_pair(attn_share), [(own, 3 * width), (own, width)], SHARE
-    )
+    grad_ffn_in, grad_ffn_out, grad_attn_out = ffn_parts(ffn_share)
     sample_grad = sample_grad.at[:1].add(carried)
     return (
         layer_out[None],

time: 440 us -> 429 us (0.975)
  blocking collectives: 101 us -> 29.7 us
  waiting for transfers between devices: 77 us -> 107 us
  Pallas kernels: 180 us -> 193 us
  starting transfers between devices: 43.9 us -> 51.9 us
    all_to_all x3 -> x1, blocking collectives: 101 us -> 29.7 us  [swap(): return lax.all_to_all(value, 'seq', 0, 0, axis_index_groups=groups)]
    all_to_all x2 -> x4, waiting for transfers between devices: 23.8 us -> 50.7 us  [swap(): return lax.all_to_all(value, 'seq', 0, 0, axis_index_groups=groups)]
    ppermute x4 -> x6, waiting for transfers between devices: 22.7 us -> 47.1 us  [other_stream(): return lax.ppermute(share, 'rep', [(0, 1), (1, 0)])]
    pallas_call x17 -> x21, Pallas kernels: 180 us -> 193 us  [call(): pl.pallas_call(kernel, out_shape=tuple(outs), in_specs=in_specs or [SMEM_...]
    all_to_all x2 -> x4, starting transfers between devices: 10.6 us -> 21 us  [swap(): return lax.all_to_all(value, 'seq', 0, 0, axis_index_groups=groups)]
    reduce_scatter x2 -> x1, waiting for transfers between devices: 9.69 us -> 0.02 us  [over_seq(): lax.psum_scatter(joined, 'seq', scatter_dimension=0, tiled=False)]
    all_to_all x1, waiting for transfers between devices: 5.43 us -> 0.01 us  [local(): pos_pieces = lax.all_to_all(taps, 'seq', 0, 0, axis_index_groups=alike)]
    ppermute x6, waiting for transfers between devices: 9.97 us -> 4.84 us  [from_behind(): lax.ppermute(value, axis, [(source, source + steps) for source in range(i...]
  transfers between devices with their start and end apart: 18 -> 23, of which waited for: 10 -> 11; matrix products, arithmetic and copies ran while one was open for 2% -> 2% of each run, Pallas kernels for 25% -> 40%
where the time goes in v5:
time: 429 us; the launch traced here: 421 us
  Pallas kernels  193 us (45%)
  waiting for transfers between devices  107 us (25%)
  starting transfers between devices  51.9 us (12%)
  blocking collectives  29.7 us (7%)
  local copies, waits for them, and re-layouts  18.2 us (4%)
  between operations  14.5 us (3%)
  other arithmetic  6.36 us (1%)
    pallas_call x21, Pallas kernels, call(): pl.pallas_call(kernel, out_shape=tuple(outs), in_specs=in_specs or [SMEM_...  193 us
    all_to_all x4, waiting for transfers between devices, swap(): return lax.all_to_all(value, 'seq', 0, 0, axis_index_groups=groups)  50.7 us
    ppermute x6, waiting for transfers between devices, other_stream(): return lax.ppermute(share, 'rep', [(0, 1), (1, 0)])  47.1 us
    all_to_all x1, blocking collectives, swap(): return lax.all_to_all(value, 'seq', 0, 0, axis_index_groups=groups)  29.7 us
    all_to_all x4, starting transfers between devices, swap(): return lax.all_to_all(value, 'seq', 0, 0, axis_index_groups=groups)  21 us
    ppermute x6, starting transfers between devices, from_behind(): lax.ppermute(value, axis, [(source, source + steps) for source in range(i...  13.6 us
    unnamed x52, local copies, waits for them, and re-layouts  12.3 us
  transfers between devices with their start and end apart: 23, of which 11 were waited for; matrix products, arithmetic and copies ran while one was open for 2% of the time, Pallas kernels for 40%

profile of v5, /device:TPU:16, one launch (start us, length us, event | category | flops | bytes accessed | tf_op | source)
XLA Modules:
  0.0 421.0 jit_solution(18066781634100493418)
XLA Ops:
  11.5 5.6 %conv_weights.2.refs_0_ = bf16[16,192,768]{2,1,0:T(8,128)(2,1)} custom-call(bf16[6144,768]{1,0:T(8,128)(2,1)} %weight_ref.9), custom_call_target="tpu_custom_call" | custom-call | bytes 14155776 | tf_op jit(solution)/shard_map/conv_weights/pallas_call | solution.py:77
  28.5 5.7 %conv_weights.3.refs_1_ = bf16[16,192,768]{2,1,0:T(8,128)(2,1)} custom-call(bf16[6144,768]{1,0:T(8,128)(2,1)} %weight_ref.9), custom_call_target="tpu_custom_call" | custom-call | bytes 14155776 | tf_op jit(solution)/shard_map/conv_weights/pallas_call | solution.py:77
  34.3 16.1 %conv.1.conv_ref = f32[256,768]{1,0:T(8,128)S(1)} custom-call(s32[11]{0:T(128)S(1)} %copy-done.2, bf16[64,768]{1,0:T(8,128)(2,1)S(1)} %collective-permute-done.1.before_ref, bf16[256,768]{1,0:T(8,128)(2,1)S(1)} %copy-done.1, bf16[64,768]{1,0:T(8,128)(2,1)S(1)} %collective-permute-done.2.after_ref, bf16[16,192,768]{2,1,0:T(8,128)(2,1)S(1)} %bitcast.46, ...), custom_call_target="tpu_custom_call" | custom-call | flops 15000000512 | bytes 10813484 | tf_op jit(solution)/shard_map/conv/pallas_call | solution.py:77
  51.3 5.2 %project_heads.1 = (f32[256,768]{1,0:T(8,128)}, bf16[256,768]{1,0:T(8,128)(2,1)}, bf16[16,192,256]{2,1,0:T(8,128)(2,1)}) custom-call(f32[256,768]{1,0:T(8,128)} %copy-done.4, f32[256,768]{1,0:T(8,128)} %get-tuple-element.92.start_ref, f32[12,768]{1,0:T(8,128)} %get-tuple-element.86.table_ref, bf16[768,2304]{1,0:T(8,128)(2,1)} %weight_ref.10), custom_call_target="tpu_custom_call" | custom-call | flops 6000000000 | bytes 7901184 | tf_op jit(solution)/shard_map/project_heads/pallas_call | solution.py:77
  56.4 6.4 %all-to-all-start = ((bf16[16,192,256]{2,1,0:T(8,128)(2,1)}), bf16[16,192,256]{2,1,0:T(8,128)(2,1)S(1)}, u32[]{:S(2)}, u32[]{:S(2)}) async-start(bf16[16,192,256]{2,1,0:T(8,128)(2,1)} %get-tuple-element.93), calls=%async_computation | async-start | bytes 3145728 | tf_op jit(solution)/shard_map/all_to_all | solution.py:1146
  62.9 12.6 %conv_weights_back.1.refs_0_ = bf16[16,384,768]{2,1,0:T(8,128)(2,1)} custom-call(bf16[6144,768]{1,0:T(8,128)(2,1)} %weight_ref.9), custom_call_target="tpu_custom_call" | custom-call | bytes 18874368 | tf_op jit(solution)/shard_map/conv_weights_back/pallas_call | solution.py:77
  75.4 23.8 %all-to-all-done.packed_ref = bf16[16,192,256]{2,1,0:T(8,128)(2,1)S(1)} async-done(((bf16[16,192,256]{2,1,0:T(8,128)(2,1)}), bf16[16,192,256]{2,1,0:T(8,128)(2,1)S(1)}, u32[]{:S(2)}, u32[]{:S(2)}) %all-to-all-start) | async-done | bytes 1572896 | tf_op jit(solution)/shard_map/all_to_all | solution.py:1146
  100.4 19.4 %attend.1 = (bf16[16,64,256]{2,1,0:T(8,128)(2,1)}, f32[64,4096]{1,0:T(8,128)}, f32[1,4096]{1,0:T(1,128)}) custom-call(s32[11]{0:T(128)} %concatenate.23.marks, bf16[16,192,256]{2,1,0:T(8,128)(2,1)} %copy-done.9), custom_call_target="tpu_custom_call" | custom-call | flops 24999999488 | bytes 3162156 | tf_op jit(solution)/shard_map/attend/pallas_call | solution.py:77
  119.7 29.7 %all_to_all.35.heads_ref = bf16[16,64,256]{2,1,0:T(8,128)(2,1)} all-to-all(bf16[16,64,256]{2,1,0:T(8,128)(2,1)} %get-tuple-element.98), channel_id=1, replica_groups=mesh['rep'=2,'seq'=16] {'seq'}, dimensions={0} | all-to-all | bytes 1048576 | tf_op jit(solution)/shard_map/all_to_all | solution.py:1146
  149.5 25.9 %middle.1 = (bf16[256,768]{1,0:T(8,128)(2,1)}, bf16[16,64,256]{2,1,0:T(8,128)(2,1)}, f32[256,768]{1,0:T(8,128)}, f32[8,768]{1,0:T(8,128)}, f32[1,3072]{1,0:T(1,1...) custom-call(s32[11]{0:T(128)} %concatenate.23.marks, ...), custom_call_target="tpu_custom_call" | custom-call | flops 20000000000 | bytes 28266540 | tf_op jit(solution)/shard_map/middle/pallas_call | solution.py:77
  180.4 13.8 %all-to-all-done.2.grad_ref = bf16[16,64,256]{2,1,0:T(8,128)(2,1)} async-done(((bf16[16,64,256]{2,1,0:T(8,128)(2,1)}), bf16[16,64,256]{2,1,0:T(8,128)(2,1)}, u32[]{:S(2)}, u32[]{:S(2)}) %all-to-all-start.2) | async-done | bytes 524320 | tf_op jit(solution)/shard_map/all_to_all | solution.py:1146
  194.2 24.7 %attend_back.1.packed_ref = bf16[16,192,256]{2,1,0:T(8,128)(2,1)} custom-call(s32[11]{0:T(128)} %concatenate.23.marks, bf16[16,192,256]{2,1,0:T(8,128)(2,1)} %copy-done.9, bf16[16,64,256]{2,1,0:T(8,128)(2,1)} %all-to-all-done.2.grad_ref, f32[64,4096]{1,0:T(8,128)} %get-tuple-element.103.wide_ref, f32[1,4096]{1,0:T(1,128)} %get-tuple-element.104.log_ref), custom_call_target="tpu_custom_call" | custom-call | flops 35000000512 | bytes 4735020 | tf_op jit(solution)/shard_map/attend_back/pallas_call | solution.py:77
  218.9 4.9 %all-to-all-start.3 = ((bf16[16,192,256]{2,1,0:T(8,128)(2,1)}), bf16[16,192,256]{2,1,0:T(8,128)(2,1)}, u32[]{:S(2)}, u32[]{:S(2)}) async-start(bf16[16,192,256]{2,1,0:T(8,128)(2,1)} %attend_back.1.packed_ref), calls=%async_computation.3 | async-start | bytes 3145728 | tf_op jit(solution)/shard_map/all_to_all | solution.py:1146
  223.8 7.3 %head_grads.1.refs_0_ = bf16[16,48,256]{2,1,0:T(8,128)(2,1)} custom-call(s32[11]{0:T(128)} %concatenate.23.marks, bf16[16,192,256]{2,1,0:T(8,128)(2,1)} %attend_back.1.packed_ref, bf16[8,256,768]{2,1,0:T(8,128)(2,1)} %bitcast.54, bf16[8,256,768]{2,1,0:T(8,128)(2,1)} %collective-permute-done.4.other_ref), custom_call_target="tpu_custom_call" | custom-call | flops 3000000000 | bytes 8257580 | tf_op jit(solution)/shard_map/head_grads/pallas_call | solution.py:77
  231.2 27.8 %collective-permute-done.3.other_ref = bf16[16,288,384]{2,1,0:T(8,128)(2,1)S(1)} collective-permute-done((bf16[16,288,384]{2,1,0:T(8,128)(2,1)}, bf16[16,288,384]{2,1,0:T(8,128)(2,1)S(1)}, u32[]{:S(2)}, u32[]{:S(2)}) %collective-permute-start.3) | collective-permute-done | bytes 3538976 | tf_op jit(solution)/shard_map/ppermute | solution.py:1170
  260.8 7.3 %add_below.1 = bf16[16,576,384]{2,1,0:T(8,128)(2,1)} custom-call(bf16[16,288,384]{2,1,0:T(8,128)(2,1)} %get-tuple-element.108.own_ref, bf16[16,288,384]{2,1,0:T(8,128)(2,1)} %copy-done.6, bf16[16,576,384]{2,1,0:T(8,128)(2,1)} %get-tuple-element.110._), custom_call_target="tpu_custom_call", output_to_operand_aliasing={{}: (2, {})} | custom-call | bytes 21233664 | tf_op jit(solution)/shard_map/add_below/pallas_call | solution.py:77
  268.1 6.8 %after_heads.1 = (f32[256,768]{1,0:T(8,128)}, bf16[256,768]{1,0:T(8,128)(2,1)}, bf16[16,144,256]{2,1,0:T(8,128)(2,1)}, f32[8,768]{1,0:T(8,128)}) custom-call(bf16[16,192,256]{2,1,0:T(8,128)(2,1)} %all-to-all-done.3.packed_ref, f32[256,768]{1,0:T(8,128)} %get-tuple-element.112.grad_second_ref, f32[256,768]{1,0:T(8,128)} %get-tuple-element.94.hidden_ref, ...), custom_call_target="tpu_custom_call" | custom-call | flops 5000000000 | bytes 11071488 | tf_op jit(solution)/shard_map/after_heads/pallas_call | solution.py:77
  285.0 5.0 %all-to-all-start.4 = ((bf16[16,144,256]{2,1,0:T(8,128)(2,1)}), bf16[16,144,256]{2,1,0:T(8,128)(2,1)S(1)}, u32[]{:S(2)}, u32[]{:S(2)}) async-start(bf16[16,144,256]{2,1,0:T(8,128)(2,1)} %get-tuple-element.131), calls=%async_computation.4 | async-start | bytes 2359296 | tf_op jit(solution)/shard_map/all_to_all | solution.py:1146
  291.1 19.3 %conv_back.1.input_ref = f32[256,768]{1,0:T(8,128)S(1)} custom-call(s32[11]{0:T(128)S(1)} %copy-done.3, bf16[64,768]{1,0:T(8,128)(2,1)S(1)} %collective-permute-done.5.before_ref, bf16[256,768]{1,0:T(8,128)(2,1)S(1)} %copy-done, bf16[64,768]{1,0:T(8,128)(2,1)S(1)} %collective-permute-done.6.after_ref, bf16[16,384,768]{2,1,0:T(8,128)(2,1)} %conv_weights_back.1.refs_0_), custom_call_target="tpu_custom_call" | custom-call | flops 15000000512 | bytes 10813484 | tf_op jit(solution)/shard_map/conv_back/pallas_call | solution.py:77
  311.3 6.3 %stem_back.1 = (f32[512,512]{1,0:T(8,128)}, f32[1,512]{1,0:T(1,128)}, bf16[8,608,128]{2,1,0:T(8,128)(2,1)}, bf16[8,608,128]{2,1,0:T(8,128)(2,1)}) custom-call(s32[11]{0:T(128)} %concatenate.23.marks, f32[256,768]{1,0:T(8,128)} %copy-done.5, f32[256,768]{1,0:T(8,128)} %get-tuple-element.119.mixed_ref, bf16[256,512]{1,0:T(8,128)(2,1)} %get-tuple-element.120.normed_ref, ...), custom_call_target="tpu_custom_call" | custom-call | flops 6000000000 | bytes 9109548 | tf_op jit(solution)/shard_map/stem_back/pallas_call | solution.py:77
  327.9 13.1 %all-to-all-done.4.both_ref = bf16[16,144,256]{2,1,0:T(8,128)(2,1)S(1)} async-done(((bf16[16,144,256]{2,1,0:T(8,128)(2,1)}), bf16[16,144,256]{2,1,0:T(8,128)(2,1)S(1)}, u32[]{:S(2)}, u32[]{:S(2)}) %all-to-all-start.4) | async-done | bytes 1179680 | tf_op jit(solution)/shard_map/all_to_all | solution.py:1146
  341.9 10.2 %taps_grad.1 = (bf16[8,144,128]{2,1,0:T(8,128)(2,1)}, bf16[8,144,128]{2,1,0:T(8,128)(2,1)}) custom-call(s32[11]{0:T(128)} %concatenate.23.marks, bf16[16,144,256]{2,1,0:T(8,128)(2,1)} %copy-done.8), custom_call_target="tpu_custom_call" | custom-call | flops 10000000000 | bytes 1769516 | tf_op jit(solution)/shard_map/taps_grad/pallas_call | solution.py:77
  367.8 13.5 %collective-permute-done.11.other_ref = bf16[8,288,128]{2,1,0:T(8,128)(2,1)S(1)} collective-permute-done((bf16[8,288,128]{2,1,0:T(8,128)(2,1)}, bf16[8,288,128]{2,1,0:T(8,128)(2,1)S(1)}, u32[]{:S(2)}, u32[]{:S(2)}) %collective-permute-start.11) | collective-permute-done | bytes 589856 | tf_op jit(solution)/shard_map/ppermute | solution.py:1170
  388.0 6.0 %all-to-all-start.6 = ((bf16[8,288,128]{2,1,0:T(8,128)(2,1)}), bf16[8,288,128]{2,1,0:T(8,128)(2,1)S(1)}, u32[]{:S(2)}, u32[]{:S(2)}) async-start(bf16[8,288,128]{2,1,0:T(8,128)(2,1)} %add_shares.2), calls=%async_computation.6 | async-start | bytes 1179648 | tf_op jit(solution)/shard_map/all_to_all | solution.py:1365
  (130 shorter events, 90.2 us)
Async XLA Ops:
  7.9 9.9 %collective-permute-start = (bf16[1,512]{1,0:T(2,128)(2,1)S(1)}, bf16[1,512]{1,0:T(2,128)(2,1)S(1)}, u32[]{:S(2)}, u32[]{:S(2)}) collective-permute-start(bf16[1,512]{1,0:T(2,128)(2,1)S(1)} %slice_bitcast_fusion.2), channel_id=1, source_target_pairs={{1,0},{2,1},{3,2},{4,3},{5,4},{6,5},{7,6},{8,7},{9,8},{10,9},{11,1... | collective-permute-start | bytes 3080 | tf_op jit(solution)/shard_map/ppermute | solution.py:1131
  23.8 10.4 %collective-permute-start.2 = (bf16[64,768]{1,0:T(8,128)(2,1)S(1)}, bf16[64,768]{1,0:T(8,128)(2,1)S(1)}, u32[]{:S(2)}, u32[]{:S(2)}) collective-permute-start(bf16[64,768]{1,0:T(8,128)(2,1)S(1)} %get-tuple-element.148), channel_id=1, source_target_pairs={{1,0},{2,1},{3,2},{4,3},{5,4},{6,5},{7,6},{8,7},{9,8},{10,9},{11,1... | collective-permute-start | bytes 294920 | tf_op jit(solution)/shard_map/ppermute | solution.py:1131
  26.6 7.7 %collective-permute-start.1 = (bf16[64,768]{1,0:T(8,128)(2,1)S(1)}, bf16[64,768]{1,0:T(8,128)(2,1)S(1)}, u32[]{:S(2)}, u32[]{:S(2)}) collective-permute-start(bf16[64,768]{1,0:T(8,128)(2,1)S(1)} %get-tuple-element.149), channel_id=1, source_target_pairs={{0,1},{1,2},{2,3},{3,4},{4,5},{5,6},{6,7},{7,8},{8,9},{9,10},{10,1... | collective-permute-start | bytes 294920 | tf_op jit(solution)/shard_map/ppermute | solution.py:1131
  56.4 42.8 %all-to-all-start = ((bf16[16,192,256]{2,1,0:T(8,128)(2,1)}), bf16[16,192,256]{2,1,0:T(8,128)(2,1)S(1)}, u32[]{:S(2)}, u32[]{:S(2)}) async-start(bf16[16,192,256]{2,1,0:T(8,128)(2,1)} %get-tuple-element.93), calls=%async_computation | async-start | bytes 3145728 | tf_op jit(solution)/shard_map/all_to_all | solution.py:1146
  62.8 112.6 %all-gather.3.cloned.1.call-start = ((), (), s32[]{:S(2)}) async-start(), calls=%async_computation.9 | async-start | bytes 3538944 | tf_op jit(solution)/shard_map/all_gather | solution.py:1278
  175.4 18.8 %all-to-all-start.2 = ((bf16[16,64,256]{2,1,0:T(8,128)(2,1)}), bf16[16,64,256]{2,1,0:T(8,128)(2,1)}, u32[]{:S(2)}, u32[]{:S(2)}) async-start(bf16[16,64,256]{2,1,0:T(8,128)(2,1)} %get-tuple-element.102), calls=%async_computation.2 | async-start | bytes 1048576 | tf_op jit(solution)/shard_map/all_to_all | solution.py:1146
  180.2 78.8 %collective-permute-start.3 = (bf16[16,288,384]{2,1,0:T(8,128)(2,1)}, bf16[16,288,384]{2,1,0:T(8,128)(2,1)S(1)}, u32[]{:S(2)}, u32[]{:S(2)}) collective-permute-start(bf16[16,288,384]{2,1,0:T(8,128)(2,1)} %get-tuple-element.105), channel_id=1, source_target_pairs={{0,16},{16,0},{1,17},{17,1},{2,18},{18,2},{3,19},{19,3},{4,20},{20... | collective-permute-start | bytes 10616840 | tf_op jit(solution)/shard_map/ppermute | solution.py:1170
  180.2 43.6 %collective-permute-start.4 = (bf16[8,256,768]{2,1,0:T(8,128)(2,1)}, bf16[8,256,768]{2,1,0:T(8,128)(2,1)}, u32[]{:S(2)}, u32[]{:S(2)}) collective-permute-start(bf16[8,256,768]{2,1,0:T(8,128)(2,1)} %bitcast.53), channel_id=1, source_target_pairs={{0,1},{1,0},{2,3},{3,2},{4,5},{5,4},{6,7},{7,6},{8,9},{9,8},{10,11... | collective-permute-start | bytes 9437192 | tf_op jit(solution)/shard_map/ppermute | solution.py:1287
  218.9 49.1 %all-to-all-start.3 = ((bf16[16,192,256]{2,1,0:T(8,128)(2,1)}), bf16[16,192,256]{2,1,0:T(8,128)(2,1)}, u32[]{:S(2)}, u32[]{:S(2)}) async-start(bf16[16,192,256]{2,1,0:T(8,128)(2,1)} %attend_back.1.packed_ref), calls=%async_computation.3 | async-start | bytes 3145728 | tf_op jit(solution)/shard_map/all_to_all | solution.py:1146
  223.8 174.9 %reduce-scatter.2.cloned.1.call-start = ((), (), s32[]{:S(2)}) async-start(), calls=%async_computation.8 | async-start | bytes 7520256 | tf_op jit(solution)/shard_map/reduce_scatter | solution.py:1220
  268.1 22.0 %copy-start.3 = (s32[11]{0:T(128)S(1)}, s32[11]{0:T(128)}, u32[]{:S(2)}) copy-start(s32[11]{0:T(128)} %concatenate.23.marks) | copy-start | bytes 136
  275.9 4.5 %collective-permute-start.6 = (bf16[64,768]{1,0:T(8,128)(2,1)S(1)}, bf16[64,768]{1,0:T(8,128)(2,1)S(1)}, u32[]{:S(2)}, u32[]{:S(2)}) collective-permute-start(bf16[64,768]{1,0:T(8,128)(2,1)S(1)} %get-tuple-element.146), channel_id=1, source_target_pairs={{1,0},{2,1},{3,2},{4,3},{5,4},{6,5},{7,6},{8,7},{9,8},{10,9},{11,1... | collective-permute-start | bytes 294920 | tf_op jit(solution)/shard_map/ppermute | solution.py:1131
  278.2 6.8 %collective-permute-start.5 = (bf16[64,768]{1,0:T(8,128)(2,1)S(1)}, bf16[64,768]{1,0:T(8,128)(2,1)S(1)}, u32[]{:S(2)}, u32[]{:S(2)}) collective-permute-start(bf16[64,768]{1,0:T(8,128)(2,1)S(1)} %get-tuple-element.147), channel_id=1, source_target_pairs={{0,1},{1,2},{2,3},{3,4},{4,5},{5,6},{6,7},{7,8},{8,9},{9,10},{10,1... | collective-permute-start | bytes 294920 | tf_op jit(solution)/shard_map/ppermute | solution.py:1131
  285.0 55.9 %all-to-all-start.4 = ((bf16[16,144,256]{2,1,0:T(8,128)(2,1)}), bf16[16,144,256]{2,1,0:T(8,128)(2,1)S(1)}, u32[]{:S(2)}, u32[]{:S(2)}) async-start(bf16[16,144,256]{2,1,0:T(8,128)(2,1)} %get-tuple-element.131), calls=%async_computation.4 | async-start | bytes 2359296 | tf_op jit(solution)/shard_map/all_to_all | solution.py:1146
  317.6 3.2 collective-permute-start.8
  324.9 27.3 %collective-permute-start.9 = (bf16[8,304,128]{2,1,0:T(8,128)(2,1)}, bf16[8,304,128]{2,1,0:T(8,128)(2,1)S(1)}, u32[]{:S(2)}, u32[]{:S(2)}) collective-permute-start(bf16[8,304,128]{2,1,0:T(8,128)(2,1)} %get-tuple-element.130), channel_id=1, source_target_pairs={{0,16},{16,0},{1,17},{17,1},{2,18},{18,2},{3,19},{19,3},{4,20},{20... | collective-permute-start | bytes 1867784 | tf_op jit(solution)/shard_map/ppermute | solution.py:1170
  356.4 29.1 %all-to-all-start.5 = ((bf16[8,304,128]{2,1,0:T(8,128)(2,1)}), bf16[8,304,128]{2,1,0:T(8,128)(2,1)S(1)}, u32[]{:S(2)}, u32[]{:S(2)}) async-start(bf16[8,304,128]{2,1,0:T(8,128)(2,1)} %add_shares.3), calls=%async_computation.5 | async-start | bytes 1245184 | tf_op jit(solution)/shard_map/all_to_all | solution.py:1359
  360.6 2.1 collective-permute-start.10
  365.5 15.8 %collective-permute-start.11 = (bf16[8,288,128]{2,1,0:T(8,128)(2,1)}, bf16[8,288,128]{2,1,0:T(8,128)(2,1)S(1)}, u32[]{:S(2)}, u32[]{:S(2)}) collective-permute-start(bf16[8,288,128]{2,1,0:T(8,128)(2,1)} %join_pair.1.own_ref), channel_id=1, source_target_pairs={{0,16},{16,0},{1,17},{17,1},{2,18},{18,2},{3,19},{19,3},{4,20},{20... | collective-permute-start | bytes 1769480 | tf_op jit(solution)/shard_map/ppermute | solution.py:1170
  365.8 20.2 %collective-permute-start.7 = (f32[1,512]{1,0:T(1,128)S(1)}, f32[1,512]{1,0:T(1,128)S(1)}, u32[]{:S(2)}, u32[]{:S(2)}) collective-permute-start(f32[1,512]{1,0:T(1,128)S(1)} %copy-done.20), channel_id=1, source_target_pairs={{0,1},{1,2},{2,3},{3,4},{4,5},{5,6},{6,7},{7,8},{8,9},{9,10},{10,1... | collective-permute-start | bytes 6152 | tf_op jit(solution)/shard_map/ppermute | solution.py:1131
  385.6 11.2 %collective-permute-start.12 = (bf16[304,128]{1,0:T(8,128)(2,1)S(1)}, bf16[304,128]{1,0:T(8,128)(2,1)S(1)}, u32[]{:S(2)}, u32[]{:S(2)}) collective-permute-start(bf16[304,128]{1,0:T(8,128)(2,1)S(1)} %reduce_sum.12), channel_id=1, source_target_pairs={{0,16},{16,0},{1,17},{17,1},{2,18},{18,2},{3,19},{19,3},{4,20},{20... | collective-permute-start | bytes 233480 | tf_op jit(solution)/shard_map/ppermute | solution.py:1170
  388.0 19.7 %all-to-all-start.6 = ((bf16[8,288,128]{2,1,0:T(8,128)(2,1)}), bf16[8,288,128]{2,1,0:T(8,128)(2,1)S(1)}, u32[]{:S(2)}, u32[]{:S(2)}) async-start(bf16[8,288,128]{2,1,0:T(8,128)(2,1)} %add_shares.2), calls=%async_computation.6 | async-start | bytes 1179648 | tf_op jit(solution)/shard_map/all_to_all | solution.py:1365
  395.0 10.0 %collective-permute-start.13 = (bf16[12,48,256]{2,1,0:T(8,128)(2,1)S(1)}, bf16[12,48,256]{2,1,0:T(8,128)(2,1)S(1)}, u32[]{:S(2)}, u32[]{:S(2)}) collective-permute-start(bf16[12,48,256]{2,1,0:T(8,128)(2,1)S(1)} %slice.180.own_ref), channel_id=1, source_target_pairs={{0,16},{16,0},{1,17},{17,1},{2,18},{18,2},{3,19},{19,3},{4,20},{20... | collective-permute-start | bytes 884744 | tf_op jit(solution)/shard_map/ppermute | solution.py:1170
  398.7 13.5 %collective-permute-start.14 = (bf16[576,384]{1,0:T(8,128)(2,1)}, bf16[576,384]{1,0:T(8,128)(2,1)S(1)}, u32[]{:S(2)}, u32[]{:S(2)}) collective-permute-start(bf16[576,384]{1,0:T(8,128)(2,1)} %bitcast.48), channel_id=1, source_target_pairs={{0,16},{16,0},{1,17},{17,1},{2,18},{18,2},{3,19},{19,3},{4,20},{20... | collective-permute-start | bytes 1327112 | tf_op jit(solution)/shard_map/ppermute | solution.py:1170
  (22 other events, 93.7 us)
Sparse Core Ops, SparseCore 0:
  99.4 62.2 all-gather.2
  268.2 106.2 reduce-scatter.1

commit v6 on v5

--- a/solution.py
+++ b/solution.py
@@ -572,6 +572,26 @@
         "split_shares",
         0,
     )
+
+
+def join_stem_kernel(clips, marks, own_ref, other_ref, heads_ref, other_heads_ref, out_ref):
+    below, rows = own_ref.shape[1], heads_ref.shape[1]
+    out_ref[:, :below] = (own_ref[...].astype(jnp.float32) + other_ref[...].astype(jnp.float32)).astype(BF)
+    first = marks[clips + CORE] == 0
+    out_ref[:, below : below + rows] = jnp.where(first, heads_ref[...], other_heads_ref[...])
+    out_ref[:, below + rows :] = jnp.where(first, other_heads_ref[...], heads_ref[...])
+
+
+def join_stem(marks, own, other, heads, other_heads, clips):
+    chips, below, lanes = own.shape
+    return call(
+        functools.partial(join_stem_kernel, clips),
+        [like((chips, below + 2 * heads.shape[1], lanes), BF)],
+        [],
+        (marks, own, other, heads, other_heads),
+        "join_stem",
+        0,
+    )[0]
 
 
 def add_below_kernel(own_ref, other_ref, _, out_ref):
@@ -924,8 +944,7 @@
     rows, width = hidden_ref.shape
     heads = width // HEAD_DIM
     if whole:
-        heads_ref, mixed_ref, conv_b_ref, groups_ref, sums_ref, grads = refs
-        groups_ref[:, 2 * width // GROUPS :] = heads_ref[...]
+        mixed_ref, conv_b_ref, groups_ref, sums_ref, grads = refs
     else:
         mixed_ref, conv_b_ref, groups_ref, sums_ref, joined_ref, grads, hidden_t = refs
     for head in range(heads):
@@ -966,16 +985,17 @@
     sums_ref[5:8] = jnp.zeros((3, width), jnp.float32)
 
 
-def after_heads(packed, grad_second, hidden, conv_sum, start, table, weight, head_grads):
+def after_heads(packed, grad_second, hidden, conv_sum, start, table, weight, whole):
     rows, width = hidden.shape
-    whole = head_grads is not None
-    lines = 2 * width // GROUPS + (width // RING if whole else 0)
-    outs = [like((rows, width)), like((rows, width), BF), like((GROUPS, lines, rows), BF), like((8, width))]
+    outs = [
+        like((rows, width)),
+        like((rows, width), BF),
+        like((GROUPS, 2 * width // GROUPS, rows), BF),
+        like((8, width)),
+    ]
     scratch = [pltpu.VMEM((3 * width, rows), BF)]
     args = (packed, grad_second, hidden, conv_sum, start, table, weight)
-    if whole:
-        args += (head_grads,)
-    else:
+    if not whole:
         outs.append(like((RING, width // RING * 3 * width // SHARE, SHARE), BF))
         scratch.append(pltpu.VMEM((width, rows), BF))
     return call(
@@ -983,7 +1003,7 @@
     )
 
 
-def head_grads_kernel(clips, marks, packed_ref, hidden_ref, other_ref, out_ref, turned):
+def head_grads_kernel(clips, marks, packed_ref, hidden_ref, other_ref, kept_ref, sent_ref, turned):
     blocks, lines, block = packed_ref.shape
     core = marks[clips + CORE]
     width = hidden_ref.shape[2]
@@ -995,8 +1015,16 @@
     total = lax.fori_loop(0, blocks // 2, one, jnp.zeros((lines, width), jnp.float32))
     turned[...] = jnp.concatenate([total, jnp.zeros((block - lines, width), jnp.float32)], axis=0).T.astype(BF)
     own = width // RING
-    for share in range(RING):
-        out_ref[share] = turned[share * own : (share + 1) * own]
+    for piece in range(block // PIECE):
+        store_pairs(
+            (kept_ref, sent_ref),
+            core == 0,
+            slice(piece * own, (piece + 1) * own),
+            [
+                turned[share * own : (share + 1) * own, piece * PIECE : (piece + 1) * PIECE]
+                for share in range(RING)
+            ],
+        )
 
 
 def head_grads(marks, packed, hidden, other, clips):
@@ -1004,21 +1032,23 @@
     width = hidden.shape[2]
     return call(
         functools.partial(head_grads_kernel, clips),
-        [like((RING, width // RING, block), BF)],
+        [like((RING // 2, block // PIECE * width // RING, PIECE), BF)] * 2,
         [pltpu.VMEM((width, block), BF)],
         (marks, packed, hidden, other),
         "head_grads",
         3 * 10**9,
-    )[0]
+    )
 
 
 def weave_heads_kernel(own_ref, other_ref, out_ref):
     heads = own_ref.shape[0]
+    rows = out_ref.shape[0]
     for part in range(3):
-        lanes = slice(part * HEAD_DIM, (part + 1) * HEAD_DIM)
+        piece, begin = divmod(part * HEAD_DIM, PIECE)
+        place = (slice(piece * rows, (piece + 1) * rows), slice(begin, begin + HEAD_DIM))
         out_ref[:, part * heads * HEAD_DIM : (part + 1) * heads * HEAD_DIM] = jnp.concatenate(
             [
-                own_ref[head, :, lanes].astype(jnp.float32) + other_ref[head, :, lanes].astype(jnp.float32)
+                own_ref[head][place].astype(jnp.float32) + other_ref[head][place].astype(jnp.float32)
                 for head in range(heads)
             ],
             axis=1,
@@ -1026,7 +1056,7 @@
 
 
 def weave_heads(own, other):
-    heads, rows, _ = own.shape
+    heads, rows = own.shape[0], own.shape[1] // 2
     return call(
         weave_heads_kernel, [like((rows, 3 * heads * HEAD_DIM))], [], (own, other), "weave_heads", 0
     )[0]
@@ -1273,31 +1303,32 @@
     back_source, _ = lax.optimization_barrier((pos_weight, hidden))
     packed = with_far_blocks(swap(packed), far)
     back_weights = conv_weights(True, back_source, 0, TURNS)
-    packed, back_weights, hidden_b = lax.optimization_barrier((packed, back_weights, hidden_b))
+    packed, back_weights = lax.optimization_barrier((packed, back_weights))
+    attended_heads, wide, log_total = attend(marks, packed, clips, far)
+    attended_heads, hidden_b = lax.optimization_barrier((attended_heads, hidden_b))
     if count == RING:
         gathered = lax.all_gather(hidden_b, "seq", axis=0, tiled=False, axis_index_groups=alike)
-    attended_heads, wide, log_total = attend(marks, packed, clips, far)
     layer_out, grad_heads, grad_pre_second, middle_sums, inner_sums, ffn_kept, ffn_sent, straight = middle(
         marks, clips, swap(attended_heads), hidden, table, attn_out, ffn_in, ffn_in_bias[None], ffn_out, out_grad[0],
         RING,
     )
     near_rows, near_chans, near_inner = width // RING, chans // RING, inner // RING
     if count == RING:
-        grad_heads, gathered = lax.optimization_barrier((grad_heads, gathered))
-        other_gathered = lax.ppermute(gathered, "seq", pairs)
         ffn_other = other_stream(ffn_sent)
     grad_heads = swap(grad_heads)
     packed_grad = attend_back(marks, packed, grad_heads, wide, log_total, clips, far)
-    own_heads = None
     if count == RING:
-        own_heads = head_grads(marks, packed_grad, gathered, other_gathered, clips)
+        packed_grad, gathered = lax.optimization_barrier((packed_grad, gathered))
+        other_gathered = lax.ppermute(gathered, "seq", pairs)
+        own_heads, sent_heads = head_grads(marks, packed_grad, gathered, other_gathered, clips)
     swapped = swap(fold_far_blocks(packed_grad, far))
     if count == RING:
+        other_heads = lax.ppermute(sent_heads, "seq", pairs)
         ffn_other, own_heads = lax.optimization_barrier((ffn_other, own_heads))
         ffn_joined = add_below(ffn_kept, ffn_other, straight)
         swapped, own_heads, ffn_joined = lax.optimization_barrier((swapped, own_heads, ffn_joined))
     grad_mixed, grad_conv_b, grad_packed, after_sums, *attn_joined = after_heads(
-        swapped, grad_pre_second, hidden, conv_sum, start_x, table, attn_in, own_heads
+        swapped, grad_pre_second, hidden, conv_sum, start_x, table, attn_in, count == RING
     )
     if count != RING:
         ffn_joined = jnp.concatenate([straight[:, : ffn_kept.shape[1]], ffn_kept, ffn_sent], axis=1)
@@ -1355,16 +1386,22 @@
         kept, sent = split_shares(marks, stem_shares[0], lax.ppermute(stem_shares[1], "seq", pairs), clips)
         other_sent = other_stream(sent)
         taps, sent_taps = taps_grad(marks, grad_groups, shape, clips, width)
-        other_sent, taps, sent_taps = lax.optimization_barrier((other_sent, taps, sent_taps))
-        received = lax.all_to_all(add_shares(kept, other_sent), "seq", 0, 0, axis_index_groups=alike)
+        sample_grad = sample_grad.at[:1].add(carried)
+        other_sent, taps, sent_taps, sample_grad = lax.optimization_barrier(
+            (other_sent, taps, sent_taps, sample_grad)
+        )
+        stem_joined = join_stem(marks, kept, other_sent, own_heads, other_heads, clips)
+        received = lax.all_to_all(stem_joined, "seq", 0, 0, axis_index_groups=alike)
         taps = join_pair(marks, taps, lax.ppermute(sent_taps, "seq", pairs), clips)
         taps = add_shares(taps, other_stream(taps))
-        taps, received, grad_groups = lax.optimization_barrier((taps, received, grad_groups))
-        by_head = grad_groups[:HEADS, 2 * group_width :]
+        taps, received = lax.optimization_barrier((taps, received))
+        by_head = received[:, kept.shape[1] :].reshape(RING, -1, PIECE)[:HEADS]
+        received = received[:, : kept.shape[1]]
         grad_attn_in = weave_heads(by_head, other_stream(by_head))
         pos_pieces = lax.all_to_all(taps, "seq", 0, 0, axis_index_groups=alike)
         pos_pieces = pos_pieces.reshape(GROUPS, -1, PIECE)
     else:
+        sample_grad = sample_grad.at[:1].add(carried)
         attn_share = over_seq(regroup(attn_joined[0], [(3 * width // SHARE, near_rows)]))
         (grad_attn_in,) = spread_out(sum_pair(attn_share), [(own, 3 * width)], SHARE)
         (taps,) = taps_grad(marks, with_far_blocks(grad_groups, 1), shape, clips, width)
@@ -1405,7 +1442,6 @@
     )
     small = stem_total[-16:]
     grad_ffn_in, grad_ffn_out, grad_attn_out = ffn_parts(ffn_share)
-    sample_grad = sample_grad.at[:1].add(carried)
     return (
         layer_out[None],
         sample_grad[None],

time: 429 us -> 421 us (0.981); the launches traced: 421 us -> 417 us
  blocking collectives: 29.7 us -> 0 us
  starting transfers between devices: 51.9 us -> 66.7 us
  Pallas kernels: 193 us -> 199 us
  waiting for transfers between devices: 107 us -> 113 us
    all_to_all x1 -> x0, blocking collectives: 29.7 us -> none  [swap(): return lax.all_to_all(value, 'seq', 0, 0, axis_index_groups=groups)]
    ppermute x6, waiting for transfers between devices: 47.1 us -> 26.9 us  [other_stream(): return lax.ppermute(share, 'rep', [(0, 1), (1, 0)])]
    all_to_all x4 -> x5, waiting for transfers between devices: 50.7 us -> 69.6 us  [swap(): return lax.all_to_all(value, 'seq', 0, 0, axis_index_groups=groups)]
    pallas_call x21, Pallas kernels: 193 us -> 199 us  [call(): pl.pallas_call(kernel, out_shape=tuple(outs), in_specs=in_specs or [SMEM_...]
    all_to_all x4 -> x5, starting transfers between devices: 21 us -> 26.5 us  [swap(): return lax.all_to_all(value, 'seq', 0, 0, axis_index_groups=groups)]
    all_to_all x1, waiting for transfers between devices: 0.01 us -> 5.32 us  [local(): pos_pieces = lax.all_to_all(taps, 'seq', 0, 0, axis_index_groups=alike)]
    ppermute x6, starting transfers between devices: 13.6 us -> 18 us  [from_behind(): lax.ppermute(value, axis, [(source, source + steps) for source in range(i...]
    unnamed x52 -> x58, local copies, waits for them, and re-layouts: 12.3 us -> 13.1 us
  transfers between devices with their start and end apart: 23 -> 25, of which waited for: 11 -> 14; matrix products, arithmetic and copies ran while one was open for 2% -> 2% of each run, Pallas kernels for 40% -> 36%
where the time goes in v6:
time: 421 us; the launch traced here: 417 us
  Pallas kernels  199 us (47%)
  waiting for transfers between devices  113 us (27%)
  starting transfers between devices  66.7 us (16%)
  local copies, waits for them, and re-layouts  18 us (4%)
  between operations  14.5 us (3%)
  other arithmetic  6.36 us (2%)
    pallas_call x21, Pallas kernels, call(): pl.pallas_call(kernel, out_shape=tuple(outs), in_specs=in_specs or [SMEM_...  199 us
    all_to_all x5, waiting for transfers between devices, swap(): return lax.all_to_all(value, 'seq', 0, 0, axis_index_groups=groups)  69.6 us
    ppermute x6, waiting for transfers between devices, other_stream(): return lax.ppermute(share, 'rep', [(0, 1), (1, 0)])  26.9 us
    all_to_all x5, starting transfers between devices, swap(): return lax.all_to_all(value, 'seq', 0, 0, axis_index_groups=groups)  26.5 us
    ppermute x6, starting transfers between devices, from_behind(): lax.ppermute(value, axis, [(source, source + steps) for source in range(i...  18 us
    unnamed x58, local copies, waits for them, and re-layouts  13.1 us
  transfers between devices with their start and end apart: 25, of which 14 were waited for; matrix products, arithmetic and copies ran while one was open for 2% of the time, Pallas kernels for 36%

profile of v6, /device:TPU:16, one launch (start us, length us, event | category | flops | bytes accessed | tf_op | source)
XLA Modules:
  0.0 417.4 jit_solution(2686269973761718511)
XLA Ops:
  11.5 5.6 %conv_weights.2.refs_0_ = bf16[16,192,768]{2,1,0:T(8,128)(2,1)} custom-call(bf16[6144,768]{1,0:T(8,128)(2,1)} %weight_ref.9), custom_call_target="tpu_custom_call" | custom-call | bytes 14155776 | tf_op jit(solution)/shard_map/conv_weights/pallas_call | solution.py:77
  30.4 5.7 %conv_weights.3.refs_1_ = bf16[16,192,768]{2,1,0:T(8,128)(2,1)} custom-call(bf16[6144,768]{1,0:T(8,128)(2,1)} %weight_ref.9), custom_call_target="tpu_custom_call" | custom-call | bytes 14155776 | tf_op jit(solution)/shard_map/conv_weights/pallas_call | solution.py:77
  36.1 16.1 %conv.1.conv_ref = f32[256,768]{1,0:T(8,128)S(1)} custom-call(s32[11]{0:T(128)S(1)} %copy-done.2, bf16[64,768]{1,0:T(8,128)(2,1)S(1)} %collective-permute-done.1.before_ref, bf16[256,768]{1,0:T(8,128)(2,1)S(1)} %copy-done.1, bf16[64,768]{1,0:T(8,128)(2,1)S(1)} %collective-permute-done.2.after_ref, bf16[16,192,768]{2,1,0:T(8,128)(2,1)S(1)} %bitcast.45, ...), custom_call_target="tpu_custom_call" | custom-call | flops 15000000512 | bytes 10813484 | tf_op jit(solution)/shard_map/conv/pallas_call | solution.py:77
  58.3 7.7 %all-to-all-start = ((bf16[16,192,256]{2,1,0:T(8,128)(2,1)}), bf16[16,192,256]{2,1,0:T(8,128)(2,1)S(1)}, u32[]{:S(2)}, u32[]{:S(2)}) async-start(bf16[16,192,256]{2,1,0:T(8,128)(2,1)} %get-tuple-element.96), calls=%async_computation | async-start | bytes 3145728 | tf_op jit(solution)/shard_map/all_to_all | solution.py:1176
  66.0 12.5 %conv_weights_back.1.refs_0_ = bf16[16,384,768]{2,1,0:T(8,128)(2,1)} custom-call(bf16[6144,768]{1,0:T(8,128)(2,1)} %weight_ref.9), custom_call_target="tpu_custom_call" | custom-call | bytes 18874368 | tf_op jit(solution)/shard_map/conv_weights_back/pallas_call | solution.py:77
  78.5 23.9 %all-to-all-done.packed_ref = bf16[16,192,256]{2,1,0:T(8,128)(2,1)S(1)} async-done(((bf16[16,192,256]{2,1,0:T(8,128)(2,1)}), bf16[16,192,256]{2,1,0:T(8,128)(2,1)S(1)}, u32[]{:S(2)}, u32[]{:S(2)}) %all-to-all-start) | async-done | bytes 1572896 | tf_op jit(solution)/shard_map/all_to_all | solution.py:1176
  103.6 22.3 %attend.1 = (bf16[16,64,256]{2,1,0:T(8,128)(2,1)}, f32[64,4096]{1,0:T(8,128)}, f32[1,4096]{1,0:T(1,128)}) custom-call(s32[11]{0:T(128)} %concatenate.23.marks, bf16[16,192,256]{2,1,0:T(8,128)(2,1)} %copy-done.8), custom_call_target="tpu_custom_call" | custom-call | flops 24999999488 | bytes 3162156 | tf_op jit(solution)/shard_map/attend/pallas_call | solution.py:77
  130.8 13.2 %all-to-all-done.1.heads_ref = bf16[16,64,256]{2,1,0:T(8,128)(2,1)S(1)} async-done(((bf16[16,64,256]{2,1,0:T(8,128)(2,1)}), bf16[16,64,256]{2,1,0:T(8,128)(2,1)S(1)}, u32[]{:S(2)}, u32[]{:S(2)}) %all-to-all-start.1) | async-done | bytes 524320 | tf_op jit(solution)/shard_map/all_to_all | solution.py:1176
  144.7 26.0 %middle.1 = (bf16[256,768]{1,0:T(8,128)(2,1)}, bf16[16,64,256]{2,1,0:T(8,128)(2,1)}, f32[256,768]{1,0:T(8,128)}, f32[8,768]{1,0:T(8,128)}, f32[1,3072]{1,0:T(1,1...) custom-call(s32[11]{0:T(128)} %concatenate.23.marks, ...), custom_call_target="tpu_custom_call" | custom-call | flops 20000000000 | bytes 28266540 | tf_op jit(solution)/shard_map/middle/pallas_call | solution.py:77
  176.0 25.2 %all-to-all-done.2.grad_ref = bf16[16,64,256]{2,1,0:T(8,128)(2,1)} async-done(((bf16[16,64,256]{2,1,0:T(8,128)(2,1)}), bf16[16,64,256]{2,1,0:T(8,128)(2,1)}, u32[]{:S(2)}, u32[]{:S(2)}) %all-to-all-start.2) | async-done | bytes 524320 | tf_op jit(solution)/shard_map/all_to_all | solution.py:1176
  201.2 28.5 %attend_back.1.packed_ref = bf16[16,192,256]{2,1,0:T(8,128)(2,1)} custom-call(s32[11]{0:T(128)} %concatenate.23.marks, bf16[16,192,256]{2,1,0:T(8,128)(2,1)} %copy-done.8, bf16[16,64,256]{2,1,0:T(8,128)(2,1)} %all-to-all-done.2.grad_ref, f32[64,4096]{1,0:T(8,128)} %get-tuple-element.105.wide_ref, f32[1,4096]{1,0:T(1,128)} %get-tuple-element.106.log_ref), custom_call_target="tpu_custom_call" | custom-call | flops 35000000512 | bytes 4735020 | tf_op jit(solution)/shard_map/attend_back/pallas_call | solution.py:77
  235.7 7.4 %head_grads.1 = (bf16[8,96,128]{2,1,0:T(8,128)(2,1)}, bf16[8,96,128]{2,1,0:T(8,128)(2,1)}) custom-call(s32[11]{0:T(128)} %concatenate.23.marks, bf16[16,192,256]{2,1,0:T(8,128)(2,1)} %attend_back.1.packed_ref, bf16[8,256,768]{2,1,0:T(8,128)(2,1)} %bitcast.55, bf16[8,256,768]{2,1,0:T(8,128)(2,1)} %collective-permute-done.4.other_ref), custom_call_target="tpu_custom_call" | custom-call | flops 3000000000 | bytes 8257580 | tf_op jit(solution)/shard_map/head_grads/pallas_call | solution.py:77
  243.1 11.2 %collective-permute-done.3.other_ref = bf16[16,288,384]{2,1,0:T(8,128)(2,1)S(1)} collective-permute-done((bf16[16,288,384]{2,1,0:T(8,128)(2,1)}, bf16[16,288,384]{2,1,0:T(8,128)(2,1)S(1)}, u32[]{:S(2)}, u32[]{:S(2)}) %collective-permute-start.3) | collective-permute-done | bytes 3538976 | tf_op jit(solution)/shard_map/ppermute | solution.py:1200
  256.1 7.2 %add_below.1 = bf16[16,576,384]{2,1,0:T(8,128)(2,1)} custom-call(bf16[16,288,384]{2,1,0:T(8,128)(2,1)} %get-tuple-element.113.own_ref, bf16[16,288,384]{2,1,0:T(8,128)(2,1)} %copy-done.6, bf16[16,576,384]{2,1,0:T(8,128)(2,1)} %get-tuple-element.115._), custom_call_target="tpu_custom_call", output_to_operand_aliasing={{}: (2, {})} | custom-call | bytes 21233664 | tf_op jit(solution)/shard_map/add_below/pallas_call | solution.py:77
  263.3 7.3 %all-to-all-done.3.packed_ref = bf16[16,192,256]{2,1,0:T(8,128)(2,1)} async-done(((bf16[16,192,256]{2,1,0:T(8,128)(2,1)}), bf16[16,192,256]{2,1,0:T(8,128)(2,1)}, u32[]{:S(2)}, u32[]{:S(2)}) %all-to-all-start.3) | async-done | bytes 1572896 | tf_op jit(solution)/shard_map/all_to_all | solution.py:1176
  270.6 6.7 %after_heads.1 = (f32[256,768]{1,0:T(8,128)}, bf16[256,768]{1,0:T(8,128)(2,1)}, bf16[16,96,256]{2,1,0:T(8,128)(2,1)}, f32[8,768]{1,0:T(8,128)}) custom-call(bf16[16,192,256]{2,1,0:T(8,128)(2,1)} %all-to-all-done.3.packed_ref, f32[256,768]{1,0:T(8,128)} %get-tuple-element.117.grad_second_ref, f32[256,768]{1,0:T(8,128)} %get-tuple-element.97.hidden_ref, ...), custom_call_target="tpu_custom_call" | custom-call | flops 5000000000 | bytes 10285056 | tf_op jit(solution)/shard_map/after_heads/pallas_call | solution.py:77
  286.9 5.5 %all-to-all-start.4 = ((bf16[16,96,256]{2,1,0:T(8,128)(2,1)}), bf16[16,96,256]{2,1,0:T(8,128)(2,1)S(1)}, u32[]{:S(2)}, u32[]{:S(2)}) async-start(bf16[16,96,256]{2,1,0:T(8,128)(2,1)} %get-tuple-element.133), calls=%async_computation.4 | async-start | bytes 1572864 | tf_op jit(solution)/shard_map/all_to_all | solution.py:1176
  293.4 19.3 %conv_back.1.input_ref = f32[256,768]{1,0:T(8,128)S(1)} custom-call(s32[11]{0:T(128)S(1)} %copy-done.3, bf16[64,768]{1,0:T(8,128)(2,1)S(1)} %collective-permute-done.5.before_ref, bf16[256,768]{1,0:T(8,128)(2,1)S(1)} %copy-done, bf16[64,768]{1,0:T(8,128)(2,1)S(1)} %collective-permute-done.6.after_ref, bf16[16,384,768]{2,1,0:T(8,128)(2,1)} %conv_weights_back.1.refs_0_), custom_call_target="tpu_custom_call" | custom-call | flops 15000000512 | bytes 10813484 | tf_op jit(solution)/shard_map/conv_back/pallas_call | solution.py:77
  313.6 6.3 %stem_back.1 = (f32[512,512]{1,0:T(8,128)}, f32[1,512]{1,0:T(1,128)}, bf16[8,608,128]{2,1,0:T(8,128)(2,1)}, bf16[8,608,128]{2,1,0:T(8,128)(2,1)}) custom-call(s32[11]{0:T(128)} %concatenate.23.marks, f32[256,768]{1,0:T(8,128)} %copy-done.5, f32[256,768]{1,0:T(8,128)} %get-tuple-element.123.mixed_ref, bf16[256,512]{1,0:T(8,128)(2,1)} %get-tuple-element.124.normed_ref, ...), custom_call_target="tpu_custom_call" | custom-call | flops 6000000000 | bytes 9109548 | tf_op jit(solution)/shard_map/stem_back/pallas_call | solution.py:77
  337.6 10.1 %taps_grad.1 = (bf16[8,144,128]{2,1,0:T(8,128)(2,1)}, bf16[8,144,128]{2,1,0:T(8,128)(2,1)}) custom-call(s32[11]{0:T(128)} %concatenate.23.marks, bf16[16,96,256]{2,1,0:T(8,128)(2,1)} %copy-done.11), custom_call_target="tpu_custom_call" | custom-call | flops 10000000000 | bytes 1376300 | tf_op jit(solution)/shard_map/taps_grad/pallas_call | solution.py:77
  351.8 5.9 %all-to-all-start.5 = ((bf16[8,496,128]{2,1,0:T(8,128)(2,1)}), bf16[8,496,128]{2,1,0:T(8,128)(2,1)S(1)}, u32[]{:S(2)}, u32[]{:S(2)}) async-start(bf16[8,496,128]{2,1,0:T(8,128)(2,1)} %join_stem.1), calls=%async_computation.5 | async-start | bytes 2031616 | tf_op jit(solution)/shard_map/all_to_all | solution.py:1394
  362.8 14.9 %collective-permute-done.11.other_ref = bf16[8,288,128]{2,1,0:T(8,128)(2,1)S(1)} collective-permute-done((bf16[8,288,128]{2,1,0:T(8,128)(2,1)}, bf16[8,288,128]{2,1,0:T(8,128)(2,1)S(1)}, u32[]{:S(2)}, u32[]{:S(2)}) %collective-permute-start.11) | collective-permute-done | bytes 589856 | tf_op jit(solution)/shard_map/ppermute | solution.py:1200
  385.7 6.8 %all-to-all-start.6 = ((bf16[8,288,128]{2,1,0:T(8,128)(2,1)}), bf16[8,288,128]{2,1,0:T(8,128)(2,1)S(1)}, u32[]{:S(2)}, u32[]{:S(2)}) async-start(bf16[8,288,128]{2,1,0:T(8,128)(2,1)} %add_shares.1), calls=%async_computation.6 | async-start | bytes 1179648 | tf_op jit(solution)/shard_map/all_to_all | solution.py:1401
  399.9 5.3 %all-to-all-done.6 = bf16[8,288,128]{2,1,0:T(8,128)(2,1)S(1)} async-done(((bf16[8,288,128]{2,1,0:T(8,128)(2,1)}), bf16[8,288,128]{2,1,0:T(8,128)(2,1)S(1)}, u32[]{:S(2)}, u32[]{:S(2)}) %all-to-all-start.6) | async-done | bytes 589856 | tf_op jit(solution)/shard_map/all_to_all | solution.py:1401
  (139 shorter events, 102.6 us)
Async XLA Ops:
  7.9 9.8 %collective-permute-start = (bf16[1,512]{1,0:T(2,128)(2,1)S(1)}, bf16[1,512]{1,0:T(2,128)(2,1)S(1)}, u32[]{:S(2)}, u32[]{:S(2)}) collective-permute-start(bf16[1,512]{1,0:T(2,128)(2,1)S(1)} %slice_bitcast_fusion.2), channel_id=1, source_target_pairs={{1,0},{2,1},{3,2},{4,3},{5,4},{6,5},{7,6},{8,7},{9,8},{10,9},{11,1... | collective-permute-start | bytes 3080 | tf_op jit(solution)/shard_map/ppermute | solution.py:1161
  23.8 12.3 %collective-permute-start.1 = (bf16[64,768]{1,0:T(8,128)(2,1)S(1)}, bf16[64,768]{1,0:T(8,128)(2,1)S(1)}, u32[]{:S(2)}, u32[]{:S(2)}) collective-permute-start(bf16[64,768]{1,0:T(8,128)(2,1)S(1)} %get-tuple-element.155), channel_id=1, source_target_pairs={{0,1},{1,2},{2,3},{3,4},{4,5},{5,6},{6,7},{7,8},{8,9},{9,10},{10,1... | collective-permute-start | bytes 294920 | tf_op jit(solution)/shard_map/ppermute | solution.py:1161
  25.9 10.3 %collective-permute-start.2 = (bf16[64,768]{1,0:T(8,128)(2,1)S(1)}, bf16[64,768]{1,0:T(8,128)(2,1)S(1)}, u32[]{:S(2)}, u32[]{:S(2)}) collective-permute-start(bf16[64,768]{1,0:T(8,128)(2,1)S(1)} %get-tuple-element.154), channel_id=1, source_target_pairs={{1,0},{2,1},{3,2},{4,3},{5,4},{6,5},{7,6},{8,7},{9,8},{10,9},{11,1... | collective-permute-start | bytes 294920 | tf_op jit(solution)/shard_map/ppermute | solution.py:1161
  58.3 44.1 %all-to-all-start = ((bf16[16,192,256]{2,1,0:T(8,128)(2,1)}), bf16[16,192,256]{2,1,0:T(8,128)(2,1)S(1)}, u32[]{:S(2)}, u32[]{:S(2)}) async-start(bf16[16,192,256]{2,1,0:T(8,128)(2,1)} %get-tuple-element.96), calls=%async_computation | async-start | bytes 3145728 | tf_op jit(solution)/shard_map/all_to_all | solution.py:1176
  125.8 18.1 %all-to-all-start.1 = ((bf16[16,64,256]{2,1,0:T(8,128)(2,1)}), bf16[16,64,256]{2,1,0:T(8,128)(2,1)S(1)}, u32[]{:S(2)}, u32[]{:S(2)}) async-start(bf16[16,64,256]{2,1,0:T(8,128)(2,1)} %get-tuple-element.102), calls=%async_computation.1 | async-start | bytes 1048576 | tf_op jit(solution)/shard_map/all_to_all | solution.py:1176
  130.0 99.7 %all-gather.3.cloned.1.call-start = ((), (), s32[]{:S(2)}) async-start(), calls=%async_computation.9 | async-start | bytes 3538944 | tf_op jit(solution)/shard_map/all_gather | solution.py:1310
  170.7 30.5 %all-to-all-start.2 = ((bf16[16,64,256]{2,1,0:T(8,128)(2,1)}), bf16[16,64,256]{2,1,0:T(8,128)(2,1)}, u32[]{:S(2)}, u32[]{:S(2)}) async-start(bf16[16,64,256]{2,1,0:T(8,128)(2,1)} %get-tuple-element.104), calls=%async_computation.2 | async-start | bytes 1048576 | tf_op jit(solution)/shard_map/all_to_all | solution.py:1176
  175.5 78.8 %collective-permute-start.3 = (bf16[16,288,384]{2,1,0:T(8,128)(2,1)}, bf16[16,288,384]{2,1,0:T(8,128)(2,1)S(1)}, u32[]{:S(2)}, u32[]{:S(2)}) collective-permute-start(bf16[16,288,384]{2,1,0:T(8,128)(2,1)} %get-tuple-element.109), channel_id=1, source_target_pairs={{0,16},{16,0},{1,17},{17,1},{2,18},{18,2},{3,19},{19,3},{4,20},{20... | collective-permute-start | bytes 10616840 | tf_op jit(solution)/shard_map/ppermute | solution.py:1200
  229.7 6.0 %collective-permute-start.4 = (bf16[8,256,768]{2,1,0:T(8,128)(2,1)}, bf16[8,256,768]{2,1,0:T(8,128)(2,1)}, u32[]{:S(2)}, u32[]{:S(2)}) collective-permute-start(bf16[8,256,768]{2,1,0:T(8,128)(2,1)} %bitcast.54), channel_id=1, source_target_pairs={{0,1},{1,0},{2,3},{3,2},{4,5},{5,4},{6,7},{7,6},{8,9},{9,8},{10,11... | collective-permute-start | bytes 9437192 | tf_op jit(solution)/shard_map/ppermute | solution.py:1322
  229.8 40.8 %all-to-all-start.3 = ((bf16[16,192,256]{2,1,0:T(8,128)(2,1)}), bf16[16,192,256]{2,1,0:T(8,128)(2,1)}, u32[]{:S(2)}, u32[]{:S(2)}) async-start(bf16[16,192,256]{2,1,0:T(8,128)(2,1)} %attend_back.1.packed_ref), calls=%async_computation.3 | async-start | bytes 3145728 | tf_op jit(solution)/shard_map/all_to_all | solution.py:1176
  234.1 160.3 %reduce-scatter.2.cloned.1.call-start = ((), (), s32[]{:S(2)}) async-start(), calls=%async_computation.8 | async-start | bytes 7520256 | tf_op jit(solution)/shard_map/reduce_scatter | solution.py:1250
  278.3 6.8 %collective-permute-start.5 = (bf16[64,768]{1,0:T(8,128)(2,1)S(1)}, bf16[64,768]{1,0:T(8,128)(2,1)S(1)}, u32[]{:S(2)}, u32[]{:S(2)}) collective-permute-start(bf16[64,768]{1,0:T(8,128)(2,1)S(1)} %get-tuple-element.153), channel_id=1, source_target_pairs={{0,1},{1,2},{2,3},{3,4},{4,5},{5,6},{6,7},{7,8},{8,9},{9,10},{10,1... | collective-permute-start | bytes 294920 | tf_op jit(solution)/shard_map/ppermute | solution.py:1161
  280.2 6.7 %collective-permute-start.6 = (bf16[64,768]{1,0:T(8,128)(2,1)S(1)}, bf16[64,768]{1,0:T(8,128)(2,1)S(1)}, u32[]{:S(2)}, u32[]{:S(2)}) collective-permute-start(bf16[64,768]{1,0:T(8,128)(2,1)S(1)} %get-tuple-element.152), channel_id=1, source_target_pairs={{1,0},{2,1},{3,2},{4,3},{5,4},{6,5},{7,6},{8,7},{9,8},{10,9},{11,1... | collective-permute-start | bytes 294920 | tf_op jit(solution)/shard_map/ppermute | solution.py:1161
  286.9 49.7 %all-to-all-start.4 = ((bf16[16,96,256]{2,1,0:T(8,128)(2,1)}), bf16[16,96,256]{2,1,0:T(8,128)(2,1)S(1)}, u32[]{:S(2)}, u32[]{:S(2)}) async-start(bf16[16,96,256]{2,1,0:T(8,128)(2,1)} %get-tuple-element.133), calls=%async_computation.4 | async-start | bytes 1572864 | tf_op jit(solution)/shard_map/all_to_all | solution.py:1176
  319.9 9.7 %collective-permute-start.7 = (bf16[8,608,128]{2,1,0:T(8,128)(2,1)}, bf16[8,608,128]{2,1,0:T(8,128)(2,1)S(1)}, u32[]{:S(2)}, u32[]{:S(2)}) collective-permute-start(bf16[8,608,128]{2,1,0:T(8,128)(2,1)} %get-tuple-element.131), channel_id=1, source_target_pairs={{0,1},{1,0},{2,3},{3,2},{4,5},{5,4},{6,7},{7,6},{8,9},{9,8},{10,11... | collective-permute-start | bytes 3735560 | tf_op jit(solution)/shard_map/ppermute | solution.py:1386
  320.1 7.5 %collective-permute-start.9 = (f32[1,512]{1,0:T(1,128)}, f32[1,512]{1,0:T(1,128)S(1)}, u32[]{:S(2)}, u32[]{:S(2)}) collective-permute-start(f32[1,512]{1,0:T(1,128)} %get-tuple-element.137), channel_id=1, source_target_pairs={{0,1},{1,2},{2,3},{3,4},{4,5},{5,6},{6,7},{7,8},{8,9},{9,10},{10,1... | collective-permute-start | bytes 6152 | tf_op jit(solution)/shard_map/ppermute | solution.py:1161
  322.3 26.1 %collective-permute-start.12 = (bf16[8,96,128]{2,1,0:T(8,128)(2,1)S(1)}, bf16[8,96,128]{2,1,0:T(8,128)(2,1)S(1)}, u32[]{:S(2)}, u32[]{:S(2)}) collective-permute-start(bf16[8,96,128]{2,1,0:T(8,128)(2,1)S(1)} %copy-done.22), channel_id=1, source_target_pairs={{0,1},{1,0},{2,3},{3,2},{4,5},{5,4},{6,7},{7,6},{8,9},{9,8},{10,11... | collective-permute-start | bytes 589832 | tf_op jit(solution)/shard_map/ppermute | solution.py:1326
  333.8 14.6 %collective-permute-start.8 = (bf16[8,304,128]{2,1,0:T(8,128)(2,1)}, bf16[8,304,128]{2,1,0:T(8,128)(2,1)S(1)}, u32[]{:S(2)}, u32[]{:S(2)}) collective-permute-start(bf16[8,304,128]{2,1,0:T(8,128)(2,1)} %get-tuple-element.132), channel_id=1, source_target_pairs={{0,16},{16,0},{1,17},{17,1},{2,18},{18,2},{3,19},{19,3},{4,20},{20... | collective-permute-start | bytes 1867784 | tf_op jit(solution)/shard_map/ppermute | solution.py:1200
  351.8 31.6 %all-to-all-start.5 = ((bf16[8,496,128]{2,1,0:T(8,128)(2,1)}), bf16[8,496,128]{2,1,0:T(8,128)(2,1)S(1)}, u32[]{:S(2)}, u32[]{:S(2)}) async-start(bf16[8,496,128]{2,1,0:T(8,128)(2,1)} %join_stem.1), calls=%async_computation.5 | async-start | bytes 2031616 | tf_op jit(solution)/shard_map/all_to_all | solution.py:1394
  362.1 15.6 %collective-permute-start.11 = (bf16[8,288,128]{2,1,0:T(8,128)(2,1)}, bf16[8,288,128]{2,1,0:T(8,128)(2,1)S(1)}, u32[]{:S(2)}, u32[]{:S(2)}) collective-permute-start(bf16[8,288,128]{2,1,0:T(8,128)(2,1)} %join_pair.1.own_ref), channel_id=1, source_target_pairs={{0,16},{16,0},{1,17},{17,1},{2,18},{18,2},{3,19},{19,3},{4,20},{20... | collective-permute-start | bytes 1769480 | tf_op jit(solution)/shard_map/ppermute | solution.py:1200
  383.5 9.0 %collective-permute-start.13 = (bf16[304,128]{1,0:T(8,128)(2,1)S(1)}, bf16[304,128]{1,0:T(8,128)(2,1)S(1)}, u32[]{:S(2)}, u32[]{:S(2)}) collective-permute-start(bf16[304,128]{1,0:T(8,128)(2,1)S(1)} %slice_reduce_fusion), channel_id=1, source_target_pairs={{0,16},{16,0},{1,17},{17,1},{2,18},{18,2},{3,19},{19,3},{4,20},{20... | collective-permute-start | bytes 233480 | tf_op jit(solution)/shard_map/ppermute | solution.py:1200
  385.1 12.1 %collective-permute-start.14 = (bf16[12,96,128]{2,1,0:T(8,128)(2,1)S(1)}, bf16[12,96,128]{2,1,0:T(8,128)(2,1)S(1)}, u32[]{:S(2)}, u32[]{:S(2)}) collective-permute-start(bf16[12,96,128]{2,1,0:T(8,128)(2,1)S(1)} %bitcast.47), channel_id=1, source_target_pairs={{0,16},{16,0},{1,17},{17,1},{2,18},{18,2},{3,19},{19,3},{4,20},{20... | collective-permute-start | bytes 884744 | tf_op jit(solution)/shard_map/ppermute | solution.py:1200
  385.7 19.5 %all-to-all-start.6 = ((bf16[8,288,128]{2,1,0:T(8,128)(2,1)}), bf16[8,288,128]{2,1,0:T(8,128)(2,1)S(1)}, u32[]{:S(2)}, u32[]{:S(2)}) async-start(bf16[8,288,128]{2,1,0:T(8,128)(2,1)} %add_shares.1), calls=%async_computation.6 | async-start | bytes 1179648 | tf_op jit(solution)/shard_map/all_to_all | solution.py:1401
  394.4 14.2 %collective-permute-start.15 = (bf16[576,384]{1,0:T(8,128)(2,1)}, bf16[576,384]{1,0:T(8,128)(2,1)S(1)}, u32[]{:S(2)}, u32[]{:S(2)}) collective-permute-start(bf16[576,384]{1,0:T(8,128)(2,1)} %bitcast.49), channel_id=1, source_target_pairs={{0,16},{16,0},{1,17},{17,1},{2,18},{18,2},{3,19},{19,3},{4,20},{20... | collective-permute-start | bytes 1327112 | tf_op jit(solution)/shard_map/ppermute | solution.py:1200
  (27 other events, 129.1 us)
Sparse Core Ops, SparseCore 0:
  133.6 66.2 all-gather.2
  270.7 97.1 reduce-scatter.1

commit v7 on v6

--- a/solution.py
+++ b/solution.py
@@ -678,7 +678,7 @@
 
 def stem_kernel(
     clips, marks, samples_ref, next_ref, weight_ref, gain_ref, bias_ref, proj_ref, gains_ref, biases_ref,
-    start_ref, start_b_ref, pre_ref, normed_ref, unfold_ref, table_ref, wide,
+    start_ref, start_b_ref, top_ref, bottom_ref, pre_ref, normed_ref, unfold_ref, table_ref, wide,
 ):
     rows, chans = pre_ref.shape
     table_ref[0:3] = gains_ref[...]
@@ -700,7 +700,11 @@
     normed_ref[...] = normed
     start = plain_dot(normed, proj_ref[...]) + table_ref[3:4]
     start_ref[...] = start
-    start_b_ref[...] = start.astype(BF)
+    start_b = start.astype(BF)
+    start_b_ref[...] = start_b
+    edge = top_ref.shape[0]
+    top_ref[...] = start_b[:edge]
+    bottom_ref[...] = start_b[rows - edge :]
 
 
 def stem(marks, samples, next_row, weight, gain, bias, proj, gains, biases, clips):
@@ -710,6 +714,7 @@
         functools.partial(stem_kernel, clips),
         [
             like((rows, width)), like((rows, width), BF),
+            like((KERNEL // 2, width), BF), like((KERNEL // 2, width), BF),
             like((rows, chans)), like((rows, chans), BF), like((rows, 3 * chans), BF), like((12, width)),
         ],
         [pltpu.VMEM((2 * rows, PIECE), jnp.float32)],
@@ -944,9 +949,9 @@
     rows, width = hidden_ref.shape
     heads = width // HEAD_DIM
     if whole:
-        mixed_ref, conv_b_ref, groups_ref, sums_ref, grads = refs
+        mixed_ref, conv_b_ref, top_ref, bottom_ref, groups_ref, sums_ref, grads = refs
     else:
-        mixed_ref, conv_b_ref, groups_ref, sums_ref, joined_ref, grads, hidden_t = refs
+        mixed_ref, conv_b_ref, top_ref, bottom_ref, groups_ref, sums_ref, joined_ref, grads, hidden_t = refs
     for head in range(heads):
         for part in range(3):
             row = part * width + head * HEAD_DIM
@@ -974,6 +979,9 @@
     conv = mixed * slope
     conv_b = conv.astype(BF)
     conv_b_ref[...] = conv_b
+    edge = top_ref.shape[0]
+    top_ref[...] = conv_b[:edge]
+    bottom_ref[...] = conv_b[rows - edge :]
     store_turned(start_ref[...].astype(BF), groups_ref, 0)
     store_turned(conv_b, groups_ref, width // GROUPS)
     sums_ref[0:1] = gain
@@ -990,6 +998,8 @@
     outs = [
         like((rows, width)),
         like((rows, width), BF),
+        like((KERNEL // 2, width), BF),
+        like((KERNEL // 2, width), BF),
         like((GROUPS, 2 * width // GROUPS, rows), BF),
         like((8, width)),
     ]
@@ -1161,9 +1171,8 @@
     return lax.ppermute(value, axis, [(source, source + steps) for source in range(initial, last)])
 
 
-def edges(value, width):
-    length = value.shape[0]
-    return from_behind(value[length - width :], "seq", 1), from_behind(value[:width], "seq", -1)
+def edges(top, bottom):
+    return from_behind(bottom, "seq", 1), from_behind(top, "seq", -1)
 
 
 def near_groups():
@@ -1276,9 +1285,9 @@
     place = lax.axis_index("seq")
     total = rows_dev * count
     begin = place * rows_dev
-    ends = jnp.cumsum(clip_lengths[0])
-    clips = ends.shape[0]
-    half = KERNEL // 2
+    clips = clip_lengths.shape[1]
+    upto = jnp.arange(clips)[:, None] >= jnp.arange(clips)[None]
+    ends = jnp.sum(jnp.where(upto, clip_lengths, 0), axis=1)
     far = 0 if count == RING else -(-MAXLEN // rows_dev)
     segment_begin = (place // RING) * RING * rows_dev
     active = jnp.where(place % RING < HEADS, 1, 0)
@@ -1288,11 +1297,11 @@
     next_row = from_behind(samples[0, :1], "seq", -1)
     one_weights = conv_weights(False, pos_weight, 0, TURNS // 2)
     next_row, one_weights = lax.optimization_barrier((next_row, one_weights))
-    start_x, start_b, stem_pre, normed_b, unfold, table = stem(
+    start_x, start_b, top, bottom, stem_pre, normed_b, unfold, table = stem(
         marks, samples[0], next_row, stem_weight, stem_gain[None], stem_bias[None], proj_weight,
         norm_gains.T, biases.T, clips,
     )
-    before, after = edges(start_b, half)
+    before, after = edges(top, bottom)
     rest_source, _ = lax.optimization_barrier((pos_weight, table))
     rest_weights = conv_weights(False, rest_source, TURNS // 2, TURNS // 2)
     before, after, rest_weights = lax.optimization_barrier((before, after, rest_weights))
@@ -1326,8 +1335,8 @@
         other_heads = lax.ppermute(sent_heads, "seq", pairs)
         ffn_other, own_heads = lax.optimization_barrier((ffn_other, own_heads))
         ffn_joined = add_below(ffn_kept, ffn_other, straight)
-        swapped, own_heads, ffn_joined = lax.optimization_barrier((swapped, own_heads, ffn_joined))
-    grad_mixed, grad_conv_b, grad_packed, after_sums, *attn_joined = after_heads(
+        swapped, own_heads, _ = lax.optimization_barrier((swapped, own_heads, ffn_joined))
+    grad_mixed, grad_conv_b, top, bottom, grad_packed, after_sums, *attn_joined = after_heads(
         swapped, grad_pre_second, hidden, conv_sum, start_x, table, attn_in, count == RING
     )
     if count != RING:
@@ -1344,7 +1353,7 @@
             ],
         )
     ffn_share = over_seq(ffn_joined)
-    before, after = edges(grad_conv_b, half)
+    before, after = edges(top, bottom)
     before, after, grad_packed = lax.optimization_barrier((before, after, grad_packed))
     grad_groups = swap(grad_packed)
     input_grad = conv_rows(True, marks, before, grad_conv_b, after, (back_weights,), clips)

time: 421 us -> 412 us (0.979)
  Pallas kernels: 199 us -> 189 us
    pallas_call x21, Pallas kernels: 199 us -> 189 us  [call(): pl.pallas_call(kernel, out_shape=tuple(outs), in_specs=in_specs or [SMEM_...]
    ppermute x6, waiting for transfers between devices: 26.9 us -> 33.5 us  [other_stream(): return lax.ppermute(share, 'rep', [(0, 1), (1, 0)])]
    all_to_all x5, waiting for transfers between devices: 69.6 us -> 64.5 us  [swap(): return lax.all_to_all(value, 'seq', 0, 0, axis_index_groups=groups)]
    unnamed x58 -> x56, local copies, waits for them, and re-layouts: 13.1 us -> 13 us
where the time goes in v7:
time: 412 us; the launch traced here: 405 us
  Pallas kernels  189 us (46%)
  waiting for transfers between devices  113 us (27%)
  starting transfers between devices  65.1 us (16%)
  local copies, waits for them, and re-layouts  15.8 us (4%)
  between operations  14.5 us (4%)
  other arithmetic  6.3 us (2%)
    pallas_call x21, Pallas kernels, call(): pl.pallas_call(kernel, out_shape=tuple(outs), in_specs=in_specs or [SMEM_...  189 us
    all_to_all x5, waiting for transfers between devices, swap(): return lax.all_to_all(value, 'seq', 0, 0, axis_index_groups=groups)  64.5 us
    ppermute x6, waiting for transfers between devices, other_stream(): return lax.ppermute(share, 'rep', [(0, 1), (1, 0)])  33.5 us
    all_to_all x5, starting transfers between devices, swap(): return lax.all_to_all(value, 'seq', 0, 0, axis_index_groups=groups)  24.2 us
    ppermute x6, starting transfers between devices, from_behind(): lax.ppermute(value, axis, [(source, source + steps) for source in range(i...  17.8 us
    unnamed x56, local copies, waits for them, and re-layouts  13 us
  transfers between devices with their start and end apart: 25, of which 14 were waited for; matrix products, arithmetic and copies ran while one was open for 2% of the time, Pallas kernels for 36%

profile of v7, /device:TPU:16, one launch (start us, length us, event | category | flops | bytes accessed | tf_op | source)
XLA Modules:
  0.0 404.5 jit_solution(1882629255713693715)
XLA Ops:
  11.4 5.6 %conv_weights.2.refs_0_ = bf16[16,192,768]{2,1,0:T(8,128)(2,1)} custom-call(bf16[6144,768]{1,0:T(8,128)(2,1)} %weight_ref.9), custom_call_target="tpu_custom_call" | custom-call | bytes 14155776 | tf_op jit(solution)/shard_map/conv_weights/pallas_call | solution.py:77
  29.2 6.1 %conv_weights.3.refs_1_ = bf16[16,192,768]{2,1,0:T(8,128)(2,1)} custom-call(bf16[6144,768]{1,0:T(8,128)(2,1)} %weight_ref.9), custom_call_target="tpu_custom_call" | custom-call | bytes 14155776 | tf_op jit(solution)/shard_map/conv_weights/pallas_call | solution.py:77
  35.4 16.1 %conv.1.conv_ref = f32[256,768]{1,0:T(8,128)S(1)} custom-call(s32[11]{0:T(128)S(1)} %copy-done.1, bf16[64,768]{1,0:T(8,128)(2,1)S(1)} %collective-permute-done.1.before_ref, bf16[256,768]{1,0:T(8,128)(2,1)S(1)} %copy-done.6, bf16[64,768]{1,0:T(8,128)(2,1)S(1)} %collective-permute-done.2.after_ref, bf16[16,192,768]{2,1,0:T(8,128)(2,1)S(1)} %copy-done, ...), custom_call_target="tpu_custom_call" | custom-call | flops 15000000512 | bytes 10813484 | tf_op jit(solution)/shard_map/conv/pallas_call | solution.py:77
  52.4 5.2 %project_heads.1 = (f32[256,768]{1,0:T(8,128)}, bf16[256,768]{1,0:T(8,128)(2,1)}, bf16[16,192,256]{2,1,0:T(8,128)(2,1)}) custom-call(f32[256,768]{1,0:T(8,128)} %copy-done.3, f32[256,768]{1,0:T(8,128)} %get-tuple-element.100.start_ref, f32[12,768]{1,0:T(8,128)} %get-tuple-element.93.table_ref, bf16[768,2304]{1,0:T(8,128)(2,1)} %weight_ref.10), custom_call_target="tpu_custom_call" | custom-call | flops 6000000000 | bytes 7901184 | tf_op jit(solution)/shard_map/project_heads/pallas_call | solution.py:77
  57.5 5.5 %all-to-all-start = ((bf16[16,192,256]{2,1,0:T(8,128)(2,1)}), bf16[16,192,256]{2,1,0:T(8,128)(2,1)S(1)}, u32[]{:S(2)}, u32[]{:S(2)}) async-start(bf16[16,192,256]{2,1,0:T(8,128)(2,1)} %get-tuple-element.101), calls=%async_computation | async-start | bytes 3145728 | tf_op jit(solution)/shard_map/all_to_all | solution.py:1185
  63.0 12.5 %conv_weights_back.1.refs_0_ = bf16[16,384,768]{2,1,0:T(8,128)(2,1)} custom-call(bf16[6144,768]{1,0:T(8,128)(2,1)} %weight_ref.9), custom_call_target="tpu_custom_call" | custom-call | bytes 18874368 | tf_op jit(solution)/shard_map/conv_weights_back/pallas_call | solution.py:77
  75.5 23.9 %all-to-all-done.packed_ref = bf16[16,192,256]{2,1,0:T(8,128)(2,1)S(1)} async-done(((bf16[16,192,256]{2,1,0:T(8,128)(2,1)}), bf16[16,192,256]{2,1,0:T(8,128)(2,1)S(1)}, u32[]{:S(2)}, u32[]{:S(2)}) %all-to-all-start) | async-done | bytes 1572896 | tf_op jit(solution)/shard_map/all_to_all | solution.py:1185
  100.6 18.0 %attend.1 = (bf16[16,64,256]{2,1,0:T(8,128)(2,1)}, f32[64,4096]{1,0:T(8,128)}, f32[1,4096]{1,0:T(1,128)}) custom-call(s32[11]{0:T(128)} %concatenate.23.marks, bf16[16,192,256]{2,1,0:T(8,128)(2,1)} %copy-done.9), custom_call_target="tpu_custom_call" | custom-call | flops 24999999488 | bytes 3162156 | tf_op jit(solution)/shard_map/attend/pallas_call | solution.py:77
  123.5 13.2 %all-to-all-done.1.heads_ref = bf16[16,64,256]{2,1,0:T(8,128)(2,1)S(1)} async-done(((bf16[16,64,256]{2,1,0:T(8,128)(2,1)}), bf16[16,64,256]{2,1,0:T(8,128)(2,1)S(1)}, u32[]{:S(2)}, u32[]{:S(2)}) %all-to-all-start.1) | async-done | bytes 524320 | tf_op jit(solution)/shard_map/all_to_all | solution.py:1185
  137.5 25.9 %middle.1 = (bf16[256,768]{1,0:T(8,128)(2,1)}, bf16[16,64,256]{2,1,0:T(8,128)(2,1)}, f32[256,768]{1,0:T(8,128)}, f32[8,768]{1,0:T(8,128)}, f32[1,3072]{1,0:T(1,1...) custom-call(s32[11]{0:T(128)} %concatenate.23.marks, ...), custom_call_target="tpu_custom_call" | custom-call | flops 20000000000 | bytes 28266540 | tf_op jit(solution)/shard_map/middle/pallas_call | solution.py:77
  169.4 24.9 %all-to-all-done.2.grad_ref = bf16[16,64,256]{2,1,0:T(8,128)(2,1)} async-done(((bf16[16,64,256]{2,1,0:T(8,128)(2,1)}), bf16[16,64,256]{2,1,0:T(8,128)(2,1)}, u32[]{:S(2)}, u32[]{:S(2)}) %all-to-all-start.2) | async-done | bytes 524320 | tf_op jit(solution)/shard_map/all_to_all | solution.py:1185
  194.3 22.9 %attend_back.1.packed_ref = bf16[16,192,256]{2,1,0:T(8,128)(2,1)} custom-call(s32[11]{0:T(128)} %concatenate.23.marks, bf16[16,192,256]{2,1,0:T(8,128)(2,1)} %copy-done.9, bf16[16,64,256]{2,1,0:T(8,128)(2,1)} %all-to-all-done.2.grad_ref, f32[64,4096]{1,0:T(8,128)} %get-tuple-element.110.wide_ref, f32[1,4096]{1,0:T(1,128)} %get-tuple-element.111.log_ref), custom_call_target="tpu_custom_call" | custom-call | flops 35000000512 | bytes 4735020 | tf_op jit(solution)/shard_map/attend_back/pallas_call | solution.py:77
  223.3 7.4 %head_grads.1 = (bf16[8,96,128]{2,1,0:T(8,128)(2,1)}, bf16[8,96,128]{2,1,0:T(8,128)(2,1)}) custom-call(s32[11]{0:T(128)} %concatenate.23.marks, bf16[16,192,256]{2,1,0:T(8,128)(2,1)} %attend_back.1.packed_ref, bf16[8,256,768]{2,1,0:T(8,128)(2,1)} %bitcast.51, bf16[8,256,768]{2,1,0:T(8,128)(2,1)} %collective-permute-done.4.other_ref), custom_call_target="tpu_custom_call" | custom-call | flops 3000000000 | bytes 8257580 | tf_op jit(solution)/shard_map/head_grads/pallas_call | solution.py:77
  230.6 16.3 %collective-permute-done.3.other_ref = bf16[16,288,384]{2,1,0:T(8,128)(2,1)S(1)} collective-permute-done((bf16[16,288,384]{2,1,0:T(8,128)(2,1)}, bf16[16,288,384]{2,1,0:T(8,128)(2,1)S(1)}, u32[]{:S(2)}, u32[]{:S(2)}) %collective-permute-start.3) | collective-permute-done | bytes 3538976 | tf_op jit(solution)/shard_map/ppermute | solution.py:1209
  248.7 7.3 %add_below.1 = bf16[16,576,384]{2,1,0:T(8,128)(2,1)} custom-call(bf16[16,288,384]{2,1,0:T(8,128)(2,1)} %get-tuple-element.118.own_ref, bf16[16,288,384]{2,1,0:T(8,128)(2,1)} %copy-done.7, bf16[16,576,384]{2,1,0:T(8,128)(2,1)} %get-tuple-element.120._), custom_call_target="tpu_custom_call", output_to_operand_aliasing={{}: (2, {})} | custom-call | bytes 21233664 | tf_op jit(solution)/shard_map/add_below/pallas_call | solution.py:77
  258.4 6.7 %after_heads.1 = (f32[256,768]{1,0:T(8,128)}, bf16[256,768]{1,0:T(8,128)(2,1)}, bf16[64,768]{1,0:T(8,128)(2,1)}, bf16[64,768]{1,0:T(8,128)(2,1)}, bf16[16,96,256]{2,1,0:T(8,128)(2,1)}, /*index=5*/f32[8,768]{1,0:T(8,128)}) custom-call(bf16[16,192,256]{2,1,0:T(8,128)(2,1)} %all-to-all-done.3.packed_ref, f32[256,768]{1,0:T(8,128)} %get-tuple-element.122.grad_second_ref, ...), custom_call_target="tpu_custom_call" | custom-call | flops 5000000000 | bytes 10481664 | tf_op jit(solution)/shard_map/after_heads/pallas_call | solution.py:77
  274.1 5.4 %all-to-all-start.4 = ((bf16[16,96,256]{2,1,0:T(8,128)(2,1)}), bf16[16,96,256]{2,1,0:T(8,128)(2,1)S(1)}, u32[]{:S(2)}, u32[]{:S(2)}) async-start(bf16[16,96,256]{2,1,0:T(8,128)(2,1)} %get-tuple-element.140), calls=%async_computation.4 | async-start | bytes 1572864 | tf_op jit(solution)/shard_map/all_to_all | solution.py:1185
  280.5 19.3 %conv_back.1.input_ref = f32[256,768]{1,0:T(8,128)S(1)} custom-call(s32[11]{0:T(128)S(1)} %copy-done.2, bf16[64,768]{1,0:T(8,128)(2,1)S(1)} %collective-permute-done.5.before_ref, bf16[256,768]{1,0:T(8,128)(2,1)S(1)} %copy-done.4, bf16[64,768]{1,0:T(8,128)(2,1)S(1)} %collective-permute-done.6.after_ref, bf16[16,384,768]{2,1,0:T(8,128)(2,1)} %conv_weights_back.1.refs_0_), custom_call_target="tpu_custom_call" | custom-call | flops 15000000512 | bytes 10813484 | tf_op jit(solution)/shard_map/conv_back/pallas_call | solution.py:77
  300.7 6.3 %stem_back.1 = (f32[512,512]{1,0:T(8,128)}, f32[1,512]{1,0:T(1,128)}, bf16[8,608,128]{2,1,0:T(8,128)(2,1)}, bf16[8,608,128]{2,1,0:T(8,128)(2,1)}) custom-call(s32[11]{0:T(128)} %concatenate.23.marks, f32[256,768]{1,0:T(8,128)} %copy-done.5, f32[256,768]{1,0:T(8,128)} %get-tuple-element.130.mixed_ref, bf16[256,512]{1,0:T(8,128)(2,1)} %get-tuple-element.131.normed_ref, ...), custom_call_target="tpu_custom_call" | custom-call | flops 6000000000 | bytes 9109548 | tf_op jit(solution)/shard_map/stem_back/pallas_call | solution.py:77
  322.0 10.1 %taps_grad.1 = (bf16[8,144,128]{2,1,0:T(8,128)(2,1)}, bf16[8,144,128]{2,1,0:T(8,128)(2,1)}) custom-call(s32[11]{0:T(128)} %concatenate.23.marks, bf16[16,96,256]{2,1,0:T(8,128)(2,1)} %copy-done.12), custom_call_target="tpu_custom_call" | custom-call | flops 10000000000 | bytes 1376300 | tf_op jit(solution)/shard_map/taps_grad/pallas_call | solution.py:77
  337.5 7.5 %all-to-all-start.5 = ((bf16[8,496,128]{2,1,0:T(8,128)(2,1)}), bf16[8,496,128]{2,1,0:T(8,128)(2,1)S(1)}, u32[]{:S(2)}, u32[]{:S(2)}) async-start(bf16[8,496,128]{2,1,0:T(8,128)(2,1)} %join_stem.1), calls=%async_computation.5 | async-start | bytes 2031616 | tf_op jit(solution)/shard_map/all_to_all | solution.py:1403
  349.6 15.2 %collective-permute-done.11.other_ref = bf16[8,288,128]{2,1,0:T(8,128)(2,1)S(1)} collective-permute-done((bf16[8,288,128]{2,1,0:T(8,128)(2,1)}, bf16[8,288,128]{2,1,0:T(8,128)(2,1)S(1)}, u32[]{:S(2)}, u32[]{:S(2)}) %collective-permute-start.11) | collective-permute-done | bytes 589856 | tf_op jit(solution)/shard_map/ppermute | solution.py:1209
  372.8 6.8 %all-to-all-start.6 = ((bf16[8,288,128]{2,1,0:T(8,128)(2,1)}), bf16[8,288,128]{2,1,0:T(8,128)(2,1)S(1)}, u32[]{:S(2)}, u32[]{:S(2)}) async-start(bf16[8,288,128]{2,1,0:T(8,128)(2,1)} %add_shares.1), calls=%async_computation.6 | async-start | bytes 1179648 | tf_op jit(solution)/shard_map/all_to_all | solution.py:1410
  387.0 5.3 %all-to-all-done.6 = bf16[8,288,128]{2,1,0:T(8,128)(2,1)S(1)} async-done(((bf16[8,288,128]{2,1,0:T(8,128)(2,1)}), bf16[8,288,128]{2,1,0:T(8,128)(2,1)S(1)}, u32[]{:S(2)}, u32[]{:S(2)}) %all-to-all-start.6) | async-done | bytes 589856 | tf_op jit(solution)/shard_map/all_to_all | solution.py:1410
  (134 shorter events, 96.8 us)
Async XLA Ops:
  7.9 9.8 %collective-permute-start = (bf16[1,512]{1,0:T(2,128)(2,1)S(1)}, bf16[1,512]{1,0:T(2,128)(2,1)S(1)}, u32[]{:S(2)}, u32[]{:S(2)}) collective-permute-start(bf16[1,512]{1,0:T(2,128)(2,1)S(1)} %slice_bitcast_fusion.2), channel_id=1, source_target_pairs={{1,0},{2,1},{3,2},{4,3},{5,4},{6,5},{7,6},{8,7},{9,8},{10,9},{11,1... | collective-permute-start | bytes 3080 | tf_op jit(solution)/shard_map/ppermute | solution.py:1171
  22.7 12.6 %collective-permute-start.1 = (bf16[64,768]{1,0:T(8,128)(2,1)}, bf16[64,768]{1,0:T(8,128)(2,1)S(1)}, u32[]{:S(2)}, u32[]{:S(2)}) collective-permute-start(bf16[64,768]{1,0:T(8,128)(2,1)} %get-tuple-element.91), channel_id=1, source_target_pairs={{0,1},{1,2},{2,3},{3,4},{4,5},{5,6},{6,7},{7,8},{8,9},{9,10},{10,1... | collective-permute-start | bytes 294920 | tf_op jit(solution)/shard_map/ppermute | solution.py:1171
  24.7 10.7 %collective-permute-start.2 = (bf16[64,768]{1,0:T(8,128)(2,1)}, bf16[64,768]{1,0:T(8,128)(2,1)S(1)}, u32[]{:S(2)}, u32[]{:S(2)}) collective-permute-start(bf16[64,768]{1,0:T(8,128)(2,1)} %get-tuple-element.92), channel_id=1, source_target_pairs={{1,0},{2,1},{3,2},{4,3},{5,4},{6,5},{7,6},{8,7},{9,8},{10,9},{11,1... | collective-permute-start | bytes 294920 | tf_op jit(solution)/shard_map/ppermute | solution.py:1171
  57.5 41.9 %all-to-all-start = ((bf16[16,192,256]{2,1,0:T(8,128)(2,1)}), bf16[16,192,256]{2,1,0:T(8,128)(2,1)S(1)}, u32[]{:S(2)}, u32[]{:S(2)}) async-start(bf16[16,192,256]{2,1,0:T(8,128)(2,1)} %get-tuple-element.101), calls=%async_computation | async-start | bytes 3145728 | tf_op jit(solution)/shard_map/all_to_all | solution.py:1185
  118.5 18.1 %all-to-all-start.1 = ((bf16[16,64,256]{2,1,0:T(8,128)(2,1)}), bf16[16,64,256]{2,1,0:T(8,128)(2,1)S(1)}, u32[]{:S(2)}, u32[]{:S(2)}) async-start(bf16[16,64,256]{2,1,0:T(8,128)(2,1)} %get-tuple-element.107), calls=%async_computation.1 | async-start | bytes 1048576 | tf_op jit(solution)/shard_map/all_to_all | solution.py:1185
  122.8 94.5 %all-gather.3.cloned.1.call-start = ((), (), s32[]{:S(2)}) async-start(), calls=%async_computation.9 | async-start | bytes 3538944 | tf_op jit(solution)/shard_map/all_gather | solution.py:1319
  163.4 30.9 %all-to-all-start.2 = ((bf16[16,64,256]{2,1,0:T(8,128)(2,1)}), bf16[16,64,256]{2,1,0:T(8,128)(2,1)}, u32[]{:S(2)}, u32[]{:S(2)}) async-start(bf16[16,64,256]{2,1,0:T(8,128)(2,1)} %get-tuple-element.109), calls=%async_computation.2 | async-start | bytes 1048576 | tf_op jit(solution)/shard_map/all_to_all | solution.py:1185
  168.1 78.8 %collective-permute-start.3 = (bf16[16,288,384]{2,1,0:T(8,128)(2,1)}, bf16[16,288,384]{2,1,0:T(8,128)(2,1)S(1)}, u32[]{:S(2)}, u32[]{:S(2)}) collective-permute-start(bf16[16,288,384]{2,1,0:T(8,128)(2,1)} %get-tuple-element.114), channel_id=1, source_target_pairs={{0,16},{16,0},{1,17},{17,1},{2,18},{18,2},{3,19},{19,3},{4,20},{20... | collective-permute-start | bytes 10616840 | tf_op jit(solution)/shard_map/ppermute | solution.py:1209
  217.2 6.0 %collective-permute-start.4 = (bf16[8,256,768]{2,1,0:T(8,128)(2,1)}, bf16[8,256,768]{2,1,0:T(8,128)(2,1)}, u32[]{:S(2)}, u32[]{:S(2)}) collective-permute-start(bf16[8,256,768]{2,1,0:T(8,128)(2,1)} %bitcast.50), channel_id=1, source_target_pairs={{0,1},{1,0},{2,3},{3,2},{4,5},{5,4},{6,7},{7,6},{8,9},{9,8},{10,11... | collective-permute-start | bytes 9437192 | tf_op jit(solution)/shard_map/ppermute | solution.py:1331
  217.3 41.2 %all-to-all-start.3 = ((bf16[16,192,256]{2,1,0:T(8,128)(2,1)}), bf16[16,192,256]{2,1,0:T(8,128)(2,1)}, u32[]{:S(2)}, u32[]{:S(2)}) async-start(bf16[16,192,256]{2,1,0:T(8,128)(2,1)} %attend_back.1.packed_ref), calls=%async_computation.3 | async-start | bytes 3145728 | tf_op jit(solution)/shard_map/all_to_all | solution.py:1185
  221.8 159.7 %reduce-scatter.2.cloned.1.call-start = ((), (), s32[]{:S(2)}) async-start(), calls=%async_computation.8 | async-start | bytes 7520256 | tf_op jit(solution)/shard_map/reduce_scatter | solution.py:1259
  265.2 7.0 %collective-permute-start.5 = (bf16[64,768]{1,0:T(8,128)(2,1)}, bf16[64,768]{1,0:T(8,128)(2,1)S(1)}, u32[]{:S(2)}, u32[]{:S(2)}) collective-permute-start(bf16[64,768]{1,0:T(8,128)(2,1)} %get-tuple-element.123), channel_id=1, source_target_pairs={{0,1},{1,2},{2,3},{3,4},{4,5},{5,6},{6,7},{7,8},{8,9},{9,10},{10,1... | collective-permute-start | bytes 294920 | tf_op jit(solution)/shard_map/ppermute | solution.py:1171
  267.1 7.1 %collective-permute-start.6 = (bf16[64,768]{1,0:T(8,128)(2,1)}, bf16[64,768]{1,0:T(8,128)(2,1)S(1)}, u32[]{:S(2)}, u32[]{:S(2)}) collective-permute-start(bf16[64,768]{1,0:T(8,128)(2,1)} %get-tuple-element.124), channel_id=1, source_target_pairs={{1,0},{2,1},{3,2},{4,3},{5,4},{6,5},{7,6},{8,7},{9,8},{10,9},{11,1... | collective-permute-start | bytes 294920 | tf_op jit(solution)/shard_map/ppermute | solution.py:1171
  274.1 47.0 %all-to-all-start.4 = ((bf16[16,96,256]{2,1,0:T(8,128)(2,1)}), bf16[16,96,256]{2,1,0:T(8,128)(2,1)S(1)}, u32[]{:S(2)}, u32[]{:S(2)}) async-start(bf16[16,96,256]{2,1,0:T(8,128)(2,1)} %get-tuple-element.140), calls=%async_computation.4 | async-start | bytes 1572864 | tf_op jit(solution)/shard_map/all_to_all | solution.py:1185
  307.0 8.4 %collective-permute-start.7 = (bf16[8,608,128]{2,1,0:T(8,128)(2,1)}, bf16[8,608,128]{2,1,0:T(8,128)(2,1)S(1)}, u32[]{:S(2)}, u32[]{:S(2)}) collective-permute-start(bf16[8,608,128]{2,1,0:T(8,128)(2,1)} %get-tuple-element.138), channel_id=1, source_target_pairs={{0,1},{1,0},{2,3},{3,2},{4,5},{5,4},{6,7},{7,6},{8,9},{9,8},{10,11... | collective-permute-start | bytes 3735560 | tf_op jit(solution)/shard_map/ppermute | solution.py:1395
  307.2 6.2 %collective-permute-start.9 = (f32[1,512]{1,0:T(1,128)}, f32[1,512]{1,0:T(1,128)S(1)}, u32[]{:S(2)}, u32[]{:S(2)}) collective-permute-start(f32[1,512]{1,0:T(1,128)} %get-tuple-element.144), channel_id=1, source_target_pairs={{0,1},{1,2},{2,3},{3,4},{4,5},{5,6},{6,7},{7,8},{8,9},{9,10},{10,1... | collective-permute-start | bytes 6152 | tf_op jit(solution)/shard_map/ppermute | solution.py:1171
  309.4 24.6 %collective-permute-start.12 = (bf16[8,96,128]{2,1,0:T(8,128)(2,1)S(1)}, bf16[8,96,128]{2,1,0:T(8,128)(2,1)S(1)}, u32[]{:S(2)}, u32[]{:S(2)}) collective-permute-start(bf16[8,96,128]{2,1,0:T(8,128)(2,1)S(1)} %copy-done.23), channel_id=1, source_target_pairs={{0,1},{1,0},{2,3},{3,2},{4,5},{5,4},{6,7},{7,6},{8,9},{9,8},{10,11... | collective-permute-start | bytes 589832 | tf_op jit(solution)/shard_map/ppermute | solution.py:1335
  319.5 14.5 %collective-permute-start.8 = (bf16[8,304,128]{2,1,0:T(8,128)(2,1)}, bf16[8,304,128]{2,1,0:T(8,128)(2,1)S(1)}, u32[]{:S(2)}, u32[]{:S(2)}) collective-permute-start(bf16[8,304,128]{2,1,0:T(8,128)(2,1)} %get-tuple-element.139), channel_id=1, source_target_pairs={{0,16},{16,0},{1,17},{17,1},{2,18},{18,2},{3,19},{19,3},{4,20},{20... | collective-permute-start | bytes 1867784 | tf_op jit(solution)/shard_map/ppermute | solution.py:1209
  337.5 33.1 %all-to-all-start.5 = ((bf16[8,496,128]{2,1,0:T(8,128)(2,1)}), bf16[8,496,128]{2,1,0:T(8,128)(2,1)S(1)}, u32[]{:S(2)}, u32[]{:S(2)}) async-start(bf16[8,496,128]{2,1,0:T(8,128)(2,1)} %join_stem.1), calls=%async_computation.5 | async-start | bytes 2031616 | tf_op jit(solution)/shard_map/all_to_all | solution.py:1403
  349.3 15.6 %collective-permute-start.11 = (bf16[8,288,128]{2,1,0:T(8,128)(2,1)}, bf16[8,288,128]{2,1,0:T(8,128)(2,1)S(1)}, u32[]{:S(2)}, u32[]{:S(2)}) collective-permute-start(bf16[8,288,128]{2,1,0:T(8,128)(2,1)} %join_pair.1.own_ref), channel_id=1, source_target_pairs={{0,16},{16,0},{1,17},{17,1},{2,18},{18,2},{3,19},{19,3},{4,20},{20... | collective-permute-start | bytes 1769480 | tf_op jit(solution)/shard_map/ppermute | solution.py:1209
  370.6 9.0 %collective-permute-start.13 = (bf16[304,128]{1,0:T(8,128)(2,1)S(1)}, bf16[304,128]{1,0:T(8,128)(2,1)S(1)}, u32[]{:S(2)}, u32[]{:S(2)}) collective-permute-start(bf16[304,128]{1,0:T(8,128)(2,1)S(1)} %slice_reduce_fusion), channel_id=1, source_target_pairs={{0,16},{16,0},{1,17},{17,1},{2,18},{18,2},{3,19},{19,3},{4,20},{20... | collective-permute-start | bytes 233480 | tf_op jit(solution)/shard_map/ppermute | solution.py:1209
  372.2 12.1 %collective-permute-start.14 = (bf16[12,96,128]{2,1,0:T(8,128)(2,1)S(1)}, bf16[12,96,128]{2,1,0:T(8,128)(2,1)S(1)}, u32[]{:S(2)}, u32[]{:S(2)}) collective-permute-start(bf16[12,96,128]{2,1,0:T(8,128)(2,1)S(1)} %bitcast.44), channel_id=1, source_target_pairs={{0,16},{16,0},{1,17},{17,1},{2,18},{18,2},{3,19},{19,3},{4,20},{20... | collective-permute-start | bytes 884744 | tf_op jit(solution)/shard_map/ppermute | solution.py:1209
  372.8 19.5 %all-to-all-start.6 = ((bf16[8,288,128]{2,1,0:T(8,128)(2,1)}), bf16[8,288,128]{2,1,0:T(8,128)(2,1)S(1)}, u32[]{:S(2)}, u32[]{:S(2)}) async-start(bf16[8,288,128]{2,1,0:T(8,128)(2,1)} %add_shares.1), calls=%async_computation.6 | async-start | bytes 1179648 | tf_op jit(solution)/shard_map/all_to_all | solution.py:1410
  381.5 14.2 %collective-permute-start.15 = (bf16[576,384]{1,0:T(8,128)(2,1)}, bf16[576,384]{1,0:T(8,128)(2,1)S(1)}, u32[]{:S(2)}, u32[]{:S(2)}) collective-permute-start(bf16[576,384]{1,0:T(8,128)(2,1)} %bitcast.46), channel_id=1, source_target_pairs={{0,16},{16,0},{1,17},{17,1},{2,18},{18,2},{3,19},{19,3},{4,20},{20... | collective-permute-start | bytes 1327112 | tf_op jit(solution)/shard_map/ppermute | solution.py:1209
  (26 other events, 119.0 us)
Sparse Core Ops, SparseCore 0:
  126.4 67.0 all-gather.2
  256.1 98.6 reduce-scatter.1
